TPU v7x, 32 devices: a whole 2x2x4 slice. The times are simulated.
32 devices in a mesh: fsdp: 2 (over x), ctx: 4 (over y, core), tp: 4 (over z).
Axes of the slice: x: 2, y: 2, z: 4, core: 2. Of those that a mesh axis runs over, the one named last changes fastest.
Arguments:
- inputs: bfloat16 [4, 1024, 2048], P('fsdp', 'ctx'), may hold values from -6 to 6
- prefix: int32 [4], P('fsdp'), may hold values from 102 to 512, as said below
- expert_ids: int32 [4, 1024, 8], P('fsdp', 'ctx'), may hold values from 0 to 15, all different within a row
- norm_gains: bfloat16 [4, 2048], P(None, ('fsdp', 'ctx')), may hold values from 0.5 to 1.5
- qkv_weight: bfloat16 [3, 2048, 2048], P(None, ('fsdp', 'ctx'), 'tp'), may hold values from -0.125 to 0.125
- out_weight: bfloat16 [2048, 2048], P(('fsdp', 'ctx'), 'tp'), may hold values from -1 to 1
- router_weight: bfloat16 [2048, 16], P(('fsdp', 'ctx')), may hold values from -0.0625 to 0.0625
- gate_up_weight: bfloat16 [16, 2, 2048, 1024], P(None, None, ('fsdp', 'ctx'), 'tp'), may hold values from -0.125 to 0.125
- down_weight: bfloat16 [16, 2048, 1024], P(None, ('fsdp', 'ctx'), 'tp'), may hold values from -1.5 to 1.5
- cotangent: bfloat16 [4, 1024, 2048], P('fsdp', 'ctx'), may hold values from -6 to 6
Outputs:
- outputs: bfloat16 [4, 1024, 2048], P('fsdp', 'ctx')
- grad_inputs: bfloat16 [4, 1024, 2048], P('fsdp', 'ctx')
- grad_norm_gains: float32 [4, 2048], P(None, ('fsdp', 'ctx'))
- grad_qkv_weight: float32 [3, 2048, 2048], P(None, ('fsdp', 'ctx'), 'tp')
- grad_out_weight: float32 [2048, 2048], P(('fsdp', 'ctx'), 'tp')
- grad_router_weight: float32 [2048, 16], P(('fsdp', 'ctx'))
- grad_gate_up_weight: float32 [16, 2, 2048, 1024], P(None, None, ('fsdp', 'ctx'), 'tp')
- grad_down_weight: float32 [16, 2048, 1024], P(None, ('fsdp', 'ctx'), 'tp')
Inputs may be any that keep to these rules, and one draw needn't show every extreme that they name: `expert_ids`: each token names 8 different experts. Some sequence has the shortest and some the longest allowed prefix.
All inputs are finite; a program needn't handle non-finite values.
Results may differ from a plain program's by a relative error of at most 0.017.
Values may be sent and summed in bfloat16 or wider, within the bound.
No kernel may reach another device: no remote copies, remote signals or barrier semaphores. Data moves between devices by JAX's collectives and lax.ppermute only.
A program may use at most 384 MiB of HBM per device.

v0:
```python
import jax
import jax.numpy as jnp
from jax import lax
from jax.sharding import PartitionSpec as P

HEAD_DIM = 128


EPSILON = 1e-05
THETA = 10000.0


def rotary_tables(positions, head_width):
    halves = jnp.arange(0, head_width, 2).astype(jnp.float32) / head_width
    inverse = 1.0 / THETA**halves
    angles = positions.astype(jnp.float32)[:, None] * inverse[None, :]
    return (jnp.cos(angles), jnp.sin(angles))


def rotate(values, cosine, sine):
    half = values.shape[-1] // 2
    first = values[..., :half]
    second = values[..., half:]
    cosine = cosine[:, None, :]
    sine = sine[:, None, :]
    return jnp.concatenate([first * cosine - second * sine, second * cosine + first * sine], -1)


def unrotate(grads, cosine, sine):
    half = grads.shape[-1] // 2
    first = grads[..., :half]
    second = grads[..., half:]
    cosine = cosine[:, None, :]
    sine = sine[:, None, :]
    return jnp.concatenate([first * cosine + second * sine, second * cosine - first * sine], -1)


def contract_rows(left, right):
    return lax.dot_general(
        left, right, (((0,), (0,)), ((), ())), preferred_element_type=jnp.float32
    )


def contract_last(left, right):
    return lax.dot_general(
        left, right, (((1,), (1,)), ((), ())), preferred_element_type=jnp.float32
    )


def body(
    inputs,
    prefix,
    expert_ids,
    norm_gains,
    qkv_weight,
    out_weight,
    router_weight,
    gate_up_weight,
    down_weight,
    cotangent,
):
    sequences, local_len, width = inputs.shape
    tokens = sequences * local_len
    full_len = local_len * lax.axis_size("ctx")
    gains_low, qkv_full, out_full = (
        lax.all_gather(norm_gains, ("fsdp", "ctx"), axis=1, tiled=True),
        lax.all_gather(qkv_weight, ("fsdp", "ctx"), axis=1, tiled=True),
        lax.all_gather(out_weight, ("fsdp", "ctx"), axis=0, tiled=True),
    )
    gains = gains_low.astype(jnp.float32)
    local_width = qkv_full.shape[2]
    head_width = HEAD_DIM
    local_heads = local_width // head_width
    head_scale = head_width ** (-0.5)
    column_start = lax.axis_index("tp") * local_width
    query_gain = lax.dynamic_slice_in_dim(gains[2], column_start, local_width)
    key_gain = lax.dynamic_slice_in_dim(gains[3], column_start, local_width)
    residual = inputs.reshape(tokens, width).astype(jnp.float32)
    scale_one = lax.rsqrt(jnp.mean(residual * residual, -1, keepdims=True) + EPSILON)
    normal_one = residual * scale_one
    normed_one = (normal_one * gains[0]).astype(jnp.bfloat16)
    projected = jnp.einsum("td,cde->cte", normed_one, qkv_full, preferred_element_type=jnp.float32)
    query_raw = projected[0]
    key_raw = projected[1]
    value_raw = projected[2]
    query_squares, key_squares = lax.psum(
        (jnp.sum(query_raw * query_raw, -1), jnp.sum(key_raw * key_raw, -1)), "tp"
    )
    query_scale = lax.rsqrt(query_squares / width + EPSILON)[:, None]
    key_scale = lax.rsqrt(key_squares / width + EPSILON)[:, None]
    query_hat = query_raw * query_scale
    key_hat = key_raw * key_scale
    positions = lax.axis_index("ctx") * local_len + jnp.arange(local_len, dtype=jnp.int32)
    cosine, sine = rotary_tables(positions, head_width)
    head_shape = (sequences, local_len, local_heads, head_width)
    queries = rotate((query_hat * query_gain).reshape(head_shape), cosine, sine).astype(
        jnp.bfloat16
    )
    keys_local = rotate((key_hat * key_gain).reshape(head_shape), cosine, sine).astype(jnp.bfloat16)
    values_local = value_raw.reshape(head_shape).astype(jnp.bfloat16)
    all_keys, all_values = (
        lax.all_gather(keys_local, "ctx", axis=1, tiled=True),
        lax.all_gather(values_local, "ctx", axis=1, tiled=True),
    )
    key_places = jnp.arange(full_len, dtype=jnp.int32)
    visible = (key_places[None, None, :] <= positions[None, :, None]) | (
        key_places[None, None, :] < prefix[:, None, None]
    )
    visible = visible[:, None]
    scores = (
        jnp.einsum("sqhd,skhd->shqk", queries, all_keys, preferred_element_type=jnp.float32)
        * head_scale
    )
    masked = jnp.where(visible, scores, -1e30)
    maxima = jnp.max(masked, -1, keepdims=True)
    expo = jnp.exp(masked - maxima)
    totals = jnp.sum(expo, -1, keepdims=True)
    probs = expo / totals
    log_total = maxima + jnp.log(totals)
    heads_out = jnp.einsum(
        "shqk,skhd->sqhd",
        probs.astype(jnp.bfloat16),
        all_values,
        preferred_element_type=jnp.float32,
    )
    heads_out = heads_out.astype(jnp.bfloat16).reshape(tokens, local_width)
    attn_total = lax.psum(contract_last(heads_out, out_full), "tp")
    mid = residual + attn_total
    scale_two = lax.rsqrt(jnp.mean(mid * mid, -1, keepdims=True) + EPSILON)
    normal_two = mid * scale_two
    normed_two = (normal_two * gains[1]).astype(jnp.bfloat16)
    gate_up_full, down_full, router_full = (
        lax.all_gather(gate_up_weight, ("fsdp", "ctx"), axis=2, tiled=True),
        lax.all_gather(down_weight, ("fsdp", "ctx"), axis=1, tiled=True),
        lax.all_gather(router_weight, ("fsdp", "ctx"), axis=0, tiled=True),
    )
    expert_count = router_full.shape[1]
    logits = jnp.dot(normed_two, router_full, preferred_element_type=jnp.float32)
    router_probs = jax.nn.softmax(logits, -1)
    chosen = jnp.sum(
        (
            expert_ids.reshape(tokens, -1)[:, :, None]
            == jnp.arange(expert_count, dtype=jnp.int32)[None, None, :]
        ).astype(jnp.float32),
        1,
    )
    gates = router_probs * chosen

    def expert_forward(carry, entries):
        pair_weights, down_one, gate_one = entries
        activations = jnp.einsum(
            "td,cdf->ctf", normed_two, pair_weights, preferred_element_type=jnp.float32
        )
        hidden = (gate_one[:, None] * jax.nn.silu(activations[0]) * activations[1]).astype(
            jnp.bfloat16
        )
        return (carry + contract_last(hidden, down_one), activations)

    moe_part, kept_activations = lax.scan(
        expert_forward, jnp.zeros((tokens, width), jnp.float32), (gate_up_full, down_full, gates.T)
    )
    moe_total = lax.psum(moe_part.astype(jnp.bfloat16), "tp").astype(jnp.float32)
    outputs = (mid + moe_total).astype(jnp.bfloat16).reshape(inputs.shape)
    grad_out = cotangent.reshape(tokens, width)
    grad_float = grad_out.astype(jnp.float32)
    gate_up_back, down_back, router_back = (
        lax.all_gather(gate_up_weight, ("fsdp", "ctx"), axis=2, tiled=True),
        lax.all_gather(down_weight, ("fsdp", "ctx"), axis=1, tiled=True),
        lax.all_gather(router_weight, ("fsdp", "ctx"), axis=0, tiled=True),
    )

    def expert_backward(carry, entries):
        pair_weights, down_one, gate_one, activations = entries
        grad_hidden = jnp.dot(grad_out, down_one, preferred_element_type=jnp.float32)
        sigma = jax.nn.sigmoid(activations[0])
        swish = jax.nn.silu(activations[0])
        hidden = (gate_one[:, None] * swish * activations[1]).astype(jnp.bfloat16)
        grad_down = contract_rows(grad_out, hidden)
        grad_gate = jnp.sum(grad_hidden * swish * activations[1], -1)
        grad_inner = grad_hidden * gate_one[:, None]
        grad_act_gate = grad_inner * activations[1] * sigma * (1.0 + activations[0] * (1.0 - sigma))
        grad_act_up = grad_inner * swish
        grad_acts = jnp.stack([grad_act_gate, grad_act_up]).astype(jnp.bfloat16)
        grad_pair = jnp.einsum(
            "td,ctf->cdf", normed_two, grad_acts, preferred_element_type=jnp.float32
        )
        carry = carry + jnp.einsum(
            "ctf,cdf->td", grad_acts, pair_weights, preferred_element_type=jnp.float32
        )
        return (carry, (grad_pair, grad_down, grad_gate))

    back_inputs = (gate_up_back, down_back, gates.T, kept_activations)
    zero_rows = jnp.zeros((tokens, width), jnp.float32)
    expert_part, (grad_gate_up, grad_down_all, grad_gates) = lax.scan(
        expert_backward, zero_rows, back_inputs
    )
    expert_grad_norm, gate_grads = lax.psum((expert_part, grad_gates.T), "tp")
    masked_grads = gate_grads * chosen
    grad_logits = (
        router_probs * (masked_grads - jnp.sum(router_probs * masked_grads, -1, keepdims=True))
    ).astype(jnp.bfloat16)
    grad_router = contract_rows(normed_two, grad_logits)
    grad_normed_two = expert_grad_norm + contract_last(grad_logits, router_back)
    owned_gate_up, owned_down, owned_router = (
        lax.psum_scatter(grad_gate_up, ("fsdp", "ctx"), scatter_dimension=2, tiled=True),
        lax.psum_scatter(grad_down_all, ("fsdp", "ctx"), scatter_dimension=1, tiled=True),
        lax.psum_scatter(grad_router, ("fsdp", "ctx"), scatter_dimension=0, tiled=True),
    )
    weighted_two = grad_normed_two * gains[1]
    grad_mid = grad_float + scale_two * (
        weighted_two - normal_two * jnp.mean(weighted_two * normal_two, -1, keepdims=True)
    )
    gain_two_grad = jnp.sum(grad_normed_two * normal_two, 0)
    grad_mid_low = grad_mid.astype(jnp.bfloat16)
    grad_out_weight = contract_rows(grad_mid_low, heads_out)
    grad_heads = (
        jnp.dot(grad_mid_low, out_full, preferred_element_type=jnp.float32)
        .astype(jnp.bfloat16)
        .reshape(head_shape)
    )
    scores_again = (
        jnp.einsum("sqhd,skhd->shqk", queries, all_keys, preferred_element_type=jnp.float32)
        * head_scale
    )
    probs_again = jnp.exp(jnp.where(visible, scores_again, -1e30) - log_total)
    grad_probs = jnp.einsum(
        "sqhd,skhd->shqk", grad_heads, all_values, preferred_element_type=jnp.float32
    )
    inner_sums = jnp.sum(probs_again * grad_probs, -1, keepdims=True)
    grad_scores = (probs_again * (grad_probs - inner_sums)).astype(jnp.bfloat16)
    grad_queries = (
        jnp.einsum("shqk,skhd->sqhd", grad_scores, all_keys, preferred_element_type=jnp.float32)
        * head_scale
    )
    grad_keys_all = (
        jnp.einsum("shqk,sqhd->skhd", grad_scores, queries, preferred_element_type=jnp.float32)
        * head_scale
    )
    grad_values_all = jnp.einsum(
        "shqk,sqhd->skhd",
        probs_again.astype(jnp.bfloat16),
        grad_heads,
        preferred_element_type=jnp.float32,
    )
    grad_keys, grad_values = (
        lax.psum_scatter(grad_keys_all, "ctx", scatter_dimension=1, tiled=True),
        lax.psum_scatter(grad_values_all, "ctx", scatter_dimension=1, tiled=True),
    )
    grad_query_hat = unrotate(grad_queries, cosine, sine).reshape(tokens, local_width)
    grad_key_hat = unrotate(grad_keys, cosine, sine).reshape(tokens, local_width)
    weighted_query = grad_query_hat * query_gain
    weighted_key = grad_key_hat * key_gain
    query_inner, key_inner = lax.psum(
        (jnp.sum(weighted_query * query_hat, -1), jnp.sum(weighted_key * key_hat, -1)), "tp"
    )
    grad_query_raw = (
        query_scale * (weighted_query - query_hat * (query_inner / width)[:, None])
    ).astype(jnp.bfloat16)
    grad_key_raw = (key_scale * (weighted_key - key_hat * (key_inner / width)[:, None])).astype(
        jnp.bfloat16
    )
    grad_value_raw = grad_values.reshape(tokens, local_width).astype(jnp.bfloat16)
    grad_projected = jnp.stack([grad_query_raw, grad_key_raw, grad_value_raw])
    grad_qkv = jnp.einsum(
        "td,cte->cde", normed_one, grad_projected, preferred_element_type=jnp.float32
    )
    grad_normed_part = jnp.einsum(
        "cte,cde->td", grad_projected, qkv_full, preferred_element_type=jnp.float32
    )
    local_gain_grads = jnp.stack(
        [jnp.sum(grad_query_hat * query_hat, 0), jnp.sum(grad_key_hat * key_hat, 0)]
    )
    placed_gains = lax.dynamic_update_slice_in_dim(
        jnp.zeros((2, width), jnp.float32), local_gain_grads, column_start, 1
    )
    grad_normed_one, qk_gain_grads = lax.psum((grad_normed_part, placed_gains), "tp")
    weighted_one = grad_normed_one * gains[0]
    grad_input = grad_mid + scale_one * (
        weighted_one - normal_one * jnp.mean(weighted_one * normal_one, -1, keepdims=True)
    )
    gain_one_grad = jnp.sum(grad_normed_one * normal_one, 0)
    grad_gains = jnp.stack([gain_one_grad, gain_two_grad, qk_gain_grads[0], qk_gain_grads[1]])
    owned_gains, owned_qkv, owned_out = (
        lax.psum_scatter(grad_gains, ("fsdp", "ctx"), scatter_dimension=1, tiled=True),
        lax.psum_scatter(grad_qkv, ("fsdp", "ctx"), scatter_dimension=1, tiled=True),
        lax.psum_scatter(grad_out_weight, ("fsdp", "ctx"), scatter_dimension=0, tiled=True),
    )
    return (
        outputs,
        grad_input.astype(jnp.bfloat16).reshape(inputs.shape),
        owned_gains,
        owned_qkv,
        owned_out,
        owned_router,
        owned_gate_up,
        owned_down,
    )


def solution(mesh):
    return jax.shard_map(
        body,
        mesh=mesh,
        in_specs=(
            P("fsdp", "ctx", None),
            P("fsdp"),
            P("fsdp", "ctx", None),
            P(None, ("fsdp", "ctx")),
            P(None, ("fsdp", "ctx"), "tp"),
            P(("fsdp", "ctx"), "tp"),
            P(("fsdp", "ctx"), None),
            P(None, None, ("fsdp", "ctx"), "tp"),
            P(None, ("fsdp", "ctx"), "tp"),
            P("fsdp", "ctx", None),
        ),
        out_specs=(
            P("fsdp", "ctx", None),
            P("fsdp", "ctx", None),
            P(None, ("fsdp", "ctx")),
            P(None, ("fsdp", "ctx"), "tp"),
            P(("fsdp", "ctx"), "tp"),
            P(("fsdp", "ctx"), None),
            P(None, None, ("fsdp", "ctx"), "tp"),
            P(None, ("fsdp", "ctx"), "tp"),
        ),
        check_vma=False,
    )
```

profile of v0, /device:TPU:0, one launch (start us, length us, event | category | flops | bytes accessed | tf_op | source)
XLA Modules:
  0.0 2617.1 jit_solution(943007271589671076)
XLA Ops:
  11.9 10.4 all_gather.27
  24.7 35.1 %all-gather.7.cloned.1.call-done = bf16[3,2048,512]{1,2,0:T(8,128)(2,1)} async-done(((bf16[3,256,512]{1,2,0:T(8,128)(2,1)}), bf16[3,2048,512]{1,2,0:T(8,128)(2,1)}) %all-gather.7.cloned.1.call-update) | async-done | bytes 6291472 | tf_op jit(solution)/shard_map/all_gather | solution.py:67
  59.9 6.2 fusion.52
  69.0 11.7 all-reduce.1
  100.7 11.7 all-gather.11.cloned.1.call-done
  121.4 16.0 all-gather.9.cloned.1.call-done
  137.4 5.8 fusion.57
  143.6 23.5 all-gather.13.cloned.1.call-done
  173.5 9.3 all_gather.32
  182.8 144.3 %all-reduce.7.cloned.1.call-done = f32[512,2048]{1,0:T(8,128)} async-done(((f32[512,2048]{1,0:T(8,128)}), f32[512,2048]{1,0:T(8,128)}) %all-reduce.7.cloned.1.call-update) | async-done | bytes 4194320 | tf_op jit(solution)/shard_map/psum | solution.py:127
  332.1 86.0 %all-gather.17.cloned.1.call-done = bf16[16,2048,256]{2,1,0:T(8,128)(2,1)} async-done(((bf16[16,256,256]{2,1,0:T(8,128)(2,1)}), bf16[16,2048,256]{2,1,0:T(8,128)(2,1)}) %all-gather.17.cloned.1.call-update) | async-done | bytes 16777232 | tf_op jit(solution)/shard_map/all_gather | solution.py:134
  418.0 162.9 %all-gather.15.cloned.1.call-done = bf16[16,2,2048,256]{3,2,1,0:T(8,128)(2,1)} async-done(((bf16[16,2,256,256]{3,2,1,0:T(8,128)(2,1)}), bf16[16,2,2048,256]{3,2,1,0:T(8,128)(2,1)}) %all-gather.15.cloned.1.call-update) | async-done | bytes 33554448 | tf_op jit(solution)/shard_map/all_gather | solution.py:133
  580.9 145.9 %while.30 = (s32[]{:T(128)}, f32[512,2048]{1,0:T(8,128)}, f32[16,2,512,256]{2,3,1,0:T(8,128)}, f32[16,512]{1,0:T(8,128)S(1)}, bf16[16,2,2048,256]{3,2,1,0:T(8,12...) while((s32[]{:T(128)}, f32[512,2048]{1,0:T(8,128)}, ...), condition=%wide.region_13.14_spmd.clone, body=%wide.region_12.13_spmd.clone.sunk | while | flops 1613627392 | bytes 50338988 | solution.py:159
  726.8 503.8 %while.31 = (s32[]{:T(128)}, f32[512,2048]{1,0:T(8,128)}, f32[16,2,2048,256]{3,2,1,0:T(8,128)}, f32[16,2048,256]{2,1,0:T(8,128)}, f32[16,512]{1,0:T(8,128)S(1)},...) while((s32[]{:T(128)}, f32[512,2048]{1,0:T(8,128)}, ...), condition=%wide.region_17.18_spmd.clone, body=%wide.region_15.17_spmd.clone.sunk | while | flops 3226992128 | bytes 86523664 | solution.py:194
  767.1 6.2 bitcast_add_fusion.4
  798.6 6.2 bitcast_add_fusion.4
  830.2 6.2 bitcast_add_fusion.4
  861.7 6.2 bitcast_add_fusion.4
  893.3 6.2 bitcast_add_fusion.4
  924.9 6.2 bitcast_add_fusion.4
  956.4 6.2 bitcast_add_fusion.4
  988.0 6.2 bitcast_add_fusion.4
  1019.6 6.2 bitcast_add_fusion.4
  1051.1 6.2 bitcast_add_fusion.4
  1082.7 6.2 bitcast_add_fusion.4
  1114.2 6.2 bitcast_add_fusion.4
  1145.8 6.2 bitcast_add_fusion.4
  1177.4 6.2 bitcast_add_fusion.4
  1208.9 6.2 bitcast_add_fusion.4
  1234.6 21.6 psum.75
  1256.3 130.5 %all-reduce.11.cloned.1.call-done = f32[512,2048]{1,0:T(8,128)} async-done(((f32[512,2048]{1,0:T(8,128)}), f32[512,2048]{1,0:T(8,128)}) %all-reduce.11.cloned.1.call-update) | async-done | bytes 4194320 | tf_op jit(solution)/shard_map/psum | solution.py:197
  1386.8 6.7 multiply_reduce_fusion.2
  1393.5 81.8 %all-reduce.9.cloned.1.call-done = bf16[512,2048]{1,0:T(8,128)(2,1)} async-done(((bf16[512,2048]{1,0:T(8,128)(2,1)}), bf16[512,2048]{1,0:T(8,128)(2,1)}) %all-reduce.9.cloned.1.call-update) | async-done | bytes 2097168 | tf_op jit(solution)/shard_map/psum | solution.py:162
  1475.3 6.7 multiply_add_fusion
  1485.7 7.0 fusion.46
  1514.6 21.7 reduce-scatter.13.cloned.1.call-done
  1541.1 42.3 %reduce-scatter.11.cloned.1.call-done = f32[2,256,4,128]{3,1,2,0:T(8,128)} async-done(((f32[2,1024,4,128]{3,1,2,0:T(8,128)}), f32[2,256,4,128]{3,1,2,0:T(8,128)}) %reduce-scatter.11.cloned.1.call-update) | async-done | bytes 1048592 | tf_op jit(solution)/shard_map/reduce_scatter | solution.py:246
  1601.4 19.0 all-reduce
  1623.7 7.8 convolution_bitcast_fusion.4
  1631.5 152.3 %all-reduce.13.cloned.1.call-done = f32[512,2048]{1,0:T(8,128)} async-done(((f32[512,2048]{1,0:T(8,128)}), f32[512,2048]{1,0:T(8,128)}) %all-reduce.13.cloned.1.call-update) | async-done | bytes 4194320 | tf_op jit(solution)/shard_map/psum | solution.py:276
  1789.5 9.8 convolution_bitcast_fusion.3
  1808.2 5.9 fusion.41
  1814.2 10.3 reduce-scatter.25.cloned.1.call-done
  1826.0 94.2 %reduce-scatter.15.cloned.1.call-done = f32[3,256,512]{1,2,0:T(8,128)} async-done(((f32[3,2048,512]{1,2,0:T(8,128)}), f32[3,256,512]{1,2,0:T(8,128)}) %reduce-scatter.15.cloned.1.call-update) | async-done | bytes 1572880 | tf_op jit(solution)/shard_map/reduce_scatter | solution.py:285
  1923.2 33.8 %reduce-scatter.19.cloned.1.call-done = f32[256,16]{0,1:T(8,128)} async-done(((f32[2048,16]{0,1:T(8,128)}), f32[256,16]{0,1:T(8,128)}) %reduce-scatter.19.cloned.1.call-update) | async-done | bytes 16400 | tf_op jit(solution)/shard_map/reduce_scatter | solution.py:207
  1957.0 55.5 %reduce-scatter.17.cloned.1.call-done = f32[256,512]{1,0:T(8,128)} async-done(((f32[2048,512]{1,0:T(8,128)}), f32[256,512]{1,0:T(8,128)}) %reduce-scatter.17.cloned.1.call-update) | async-done | bytes 524304 | tf_op jit(solution)/shard_map/reduce_scatter | solution.py:286
  2012.5 209.3 %reduce-scatter.23.cloned.1.call-done = f32[16,256,256]{2,1,0:T(8,128)} async-done(((f32[16,2048,256]{2,1,0:T(8,128)}), f32[16,256,256]{2,1,0:T(8,128)}) %reduce-scatter.23.cloned.1.call-update) | async-done | bytes 4194320 | tf_op jit(solution)/shard_map/reduce_scatter | solution.py:206
  2221.8 388.2 %reduce-scatter.21.cloned.1.call-done = f32[16,2,256,256]{3,2,1,0:T(8,128)} async-done(((f32[16,2,2048,256]{3,2,1,0:T(8,128)}), f32[16,2,256,256]{3,2,1,0:T(8,128)}) %reduce-scatter.21.cloned.1.call-update) | async-done | bytes 8388624 | tf_op jit(solution)/shard_map/reduce_scatter | solution.py:205
  (548 shorter events, 681.3 us)
Async XLA Ops:
  7.2 15.7 copy-start.8
  7.2 4.7 copy-start.42
  7.2 52.7 %all-gather.7.cloned.1.call-start = ((), (), s32[]{:S(2)}) async-start(), calls=%async_computation.8 | async-start | bytes 7077888 | tf_op jit(solution)/shard_map/all_gather | solution.py:67
  9.7 102.7 %all-gather.11.cloned.1.call-start = ((), (), s32[]{:S(2)}) async-start(), calls=%async_computation.10 | async-start | bytes 2621440 | tf_op jit(solution)/shard_map/all_gather | solution.py:102
  11.8 54.3 %copy-start.30 = (f32[1,2,2,128]{3,1,2,0:T(2,128)}, f32[1,2,2,128]{3,1,2,0:T(2,128)S(1)}, u32[]{:S(2)}) copy-start(f32[1,2,2,128]{3,1,2,0:T(2,128)S(1)} %copy.139) | copy-start | bytes 6148
  22.3 37.6 %copy-start.28 = (f32[1,2048]{1,0:T(1,128)}, f32[1,2048]{1,0:T(1,128)S(1)}, u32[]{:S(2)}) copy-start(f32[1,2048]{1,0:T(1,128)S(1)} %get-tuple-element.315) | copy-start | bytes 24580
  22.3 66.7 %copy-start.38 = (f32[1,512]{1,0:T(1,128)}, f32[1,512]{1,0:T(1,128)S(1)}, u32[]{:S(2)}) copy-start(f32[1,512]{1,0:T(1,128)S(1)} %get-tuple-element.326) | copy-start | bytes 6148
  22.3 68.0 %copy-start.36 = (f32[1,512]{1,0:T(1,128)}, f32[1,512]{1,0:T(1,128)S(1)}, u32[]{:S(2)}) copy-start(f32[1,512]{1,0:T(1,128)S(1)} %get-tuple-element.325) | copy-start | bytes 6148
  22.9 67.7 %copy-start.19 = (f32[256,64]{1,0:T(8,128)}, f32[256,64]{1,0:T(8,128)S(1)}, u32[]{:S(2)}) copy-start(f32[256,64]{1,0:T(8,128)S(1)} %get-tuple-element.316) | copy-start | bytes 196612
  22.9 67.7 %copy-start.21 = (f32[256,64]{1,0:T(8,128)}, f32[256,64]{1,0:T(8,128)S(1)}, u32[]{:S(2)}) copy-start(f32[256,64]{1,0:T(8,128)S(1)} %get-tuple-element.317) | copy-start | bytes 196612
  80.7 8.2 copy-start.32
  80.7 8.2 copy-start.34
  91.3 24.9 copy-start.14
  91.3 24.9 copy-start.16
  91.3 8.1 copy-start.43
  92.4 45.0 %all-gather.9.cloned.1.call-start = ((), (), s32[]{:S(2)}) async-start(), calls=%async_computation.9 | async-start | bytes 2621440 | tf_op jit(solution)/shard_map/all_gather | solution.py:103
  98.5 68.6 %all-gather.13.cloned.1.call-start = ((), (), s32[]{:S(2)}) async-start(), calls=%async_computation.11 | async-start | bytes 2359296 | tf_op jit(solution)/shard_map/all_gather | solution.py:68
  99.1 228.1 %all-reduce.7.cloned.1.call-start = ((), (), s32[]{:S(2)}) async-start(), calls=%async_computation.12 | async-start | bytes 8388608 | tf_op jit(solution)/shard_map/psum | solution.py:127
  143.5 28.5 %copy-start.12 = (bf16[2,256,4,128]{3,2,1,0:T(4,128)(2,1)}, bf16[2,256,4,128]{3,2,1,0:T(4,128)(2,1)S(1)}, u32[]{:S(2)}) copy-start(bf16[2,256,4,128]{3,2,1,0:T(4,128)(2,1)S(1)} %copy.90) | copy-start | bytes 1572868
  172.0 10.8 copy-start.40
  172.1 246.0 %all-gather.17.cloned.1.call-start = ((), (), s32[]{:S(2)}) async-start(), calls=%async_computation.14 | async-start | bytes 18874368 | tf_op jit(solution)/shard_map/all_gather | solution.py:134
  172.6 408.3 %all-gather.15.cloned.1.call-start = ((), (), s32[]{:S(2)}) async-start(), calls=%async_computation.13 | async-start | bytes 37748736 | tf_op jit(solution)/shard_map/all_gather | solution.py:133
  173.4 1213.4 %all-reduce.11.cloned.1.call-start = ((), (), s32[]{:S(2)}) async-start(), calls=%async_computation.16 | async-start | bytes 8388608 | tf_op jit(solution)/shard_map/psum | solution.py:197
  653.9 4.1 copy-start.2
  690.4 4.1 copy-start.2
  1230.6 244.7 %all-reduce.9.cloned.1.call-start = ((), (), s32[]{:S(2)}) async-start(), calls=%async_computation.15 | async-start | bytes 4194304 | tf_op jit(solution)/shard_map/psum | solution.py:162
  1234.5 301.8 %reduce-scatter.13.cloned.1.call-start = ((), (), s32[]{:S(2)}) async-start(), calls=%async_computation.18 | async-start | bytes 5242880 | tf_op jit(solution)/shard_map/reduce_scatter | solution.py:247
  1475.3 8.7 copy-start.18
  1492.7 90.7 %reduce-scatter.11.cloned.1.call-start = ((), (), s32[]{:S(2)}) async-start(), calls=%async_computation.17 | async-start | bytes 5242880 | tf_op jit(solution)/shard_map/reduce_scatter | solution.py:246
  1498.3 7.7 copy-start.15
  1498.3 7.7 copy-start.17
  1509.9 73.5 %copy-start.20 = (f32[256,64]{1,0:T(8,128)S(1)}, f32[256,64]{1,0:T(8,128)}, u32[]{:S(2)}) copy-start(f32[256,64]{1,0:T(8,128)} %copy-done.19) | copy-start | bytes 196612
  1509.9 73.5 %copy-start.22 = (f32[256,64]{1,0:T(8,128)S(1)}, f32[256,64]{1,0:T(8,128)}, u32[]{:S(2)}) copy-start(f32[256,64]{1,0:T(8,128)} %copy-done.21) | copy-start | bytes 196612
  1509.9 274.0 %all-reduce.13.cloned.1.call-start = ((), (), s32[]{:S(2)}) async-start(), calls=%async_computation.19 | async-start | bytes 8388608 | tf_op jit(solution)/shard_map/psum | solution.py:276
  1590.7 8.2 copy-start.33
  1590.7 8.2 copy-start.35
  1590.7 8.2 copy-start.37
  1590.7 8.2 copy-start.39
  1631.4 152.4 %copy-start.29 = (f32[1,2048]{1,0:T(1,128)S(1)}, f32[1,2048]{1,0:T(1,128)}, u32[]{:S(2)}) copy-start(f32[1,2048]{1,0:T(1,128)} %copy-done.28) | copy-start | bytes 24580
  1631.4 152.4 %copy-start.31 = (f32[1,2,2,128]{3,1,2,0:T(2,128)S(1)}, f32[1,2,2,128]{3,1,2,0:T(2,128)}, u32[]{:S(2)}) copy-start(f32[1,2,2,128]{3,1,2,0:T(2,128)} %copy-done.30) | copy-start | bytes 6148
  1631.5 158.0 %copy-start.24 = (bf16[1,512,512]{1,2,0:T(8,128)(2,1)S(1)}, bf16[1,512,512]{1,2,0:T(8,128)(2,1)}, u32[]{:S(2)}) copy-start(bf16[1,512,512]{1,2,0:T(8,128)(2,1)} %copy-done.23) | copy-start | bytes 1572868
  1631.5 158.0 %copy-start.26 = (bf16[1,512,512]{1,2,0:T(8,128)(2,1)S(1)}, bf16[1,512,512]{1,2,0:T(8,128)(2,1)}, u32[]{:S(2)}) copy-start(bf16[1,512,512]{1,2,0:T(8,128)(2,1)} %copy-done.25) | copy-start | bytes 1572868
  1631.5 192.9 %reduce-scatter.25.cloned.1.call-start = ((), (), s32[]{:S(2)}) async-start(), calls=%async_computation.25 | async-start | bytes 1179648
  1789.2 131.0 %reduce-scatter.15.cloned.1.call-start = ((), (), s32[]{:S(2)}) async-start(), calls=%async_computation.20 | async-start | bytes 14155776 | tf_op jit(solution)/shard_map/reduce_scatter | solution.py:285
  1799.3 157.7 %reduce-scatter.19.cloned.1.call-start = ((), (), s32[]{:S(2)}) async-start(), calls=%async_computation.22 | async-start | bytes 147456 | tf_op jit(solution)/shard_map/reduce_scatter | solution.py:207
  1800.4 212.1 %reduce-scatter.17.cloned.1.call-start = ((), (), s32[]{:S(2)}) async-start(), calls=%async_computation.21 | async-start | bytes 4718592 | tf_op jit(solution)/shard_map/reduce_scatter | solution.py:286
  1806.0 415.8 %reduce-scatter.23.cloned.1.call-start = ((), (), s32[]{:S(2)}) async-start(), calls=%async_computation.24 | async-start | bytes 37748736 | tf_op jit(solution)/shard_map/reduce_scatter | solution.py:206
  1806.6 803.4 %reduce-scatter.21.cloned.1.call-start = ((), (), s32[]{:S(2)}) async-start(), calls=%async_computation.23 | async-start | bytes 75497472 | tf_op jit(solution)/shard_map/reduce_scatter | solution.py:205
  (89 other events, 257.4 us)
Sparse Core Ops, SparseCore 0:
  10.5 49.3 all-gather.6
  92.6 19.8 all-gather.10
  114.6 22.8 all-gather.8
  139.2 27.8 all-gather.12
  172.2 154.9 all-reduce.6
  329.1 88.8 all-gather.16
  420.1 160.7 all-gather.14
  1230.8 155.9 all-reduce.10
  1389.7 85.5 all-reduce.8
  1492.8 43.4 reduce-scatter.12
  1538.8 44.4 reduce-scatter.10
  1631.6 152.2 all-reduce.12
  1789.4 35.0 reduce-scatter.24
  1827.8 92.3 reduce-scatter.14
  1923.6 33.3 reduce-scatter.18
  1961.2 51.3 reduce-scatter.16
  2016.5 205.2 reduce-scatter.22
  2226.2 383.7 reduce-scatter.20
where the time goes:
time: 2630 us; the launch traced here: 2620 us
  waiting for transfers between devices  1700 us (65%)
  matrix products  489 us (19%)
  local copies, waits for them, and re-layouts  282 us (11%)
  blocking collectives  71.9 us (3%)
  other arithmetic  54.7 us (2%)
    reduce_scatter x1, waiting for transfers between devices, body(): lax.psum_scatter(grad_gate_up, ('fsdp', 'ctx'), scatter_dimension=2, tile...  388 us
    reduce_scatter x1, waiting for transfers between devices, body(): lax.psum_scatter(grad_down_all, ('fsdp', 'ctx'), scatter_dimension=1, til...  209 us
    dynamic_update_slice x80, local copies, waits for them, and re-layouts, body(): lax.scan(expert_backward, zero_rows, back_inputs)  176 us
    all_gather x1, waiting for transfers between devices, body(): lax.all_gather(gate_up_weight, ('fsdp', 'ctx'), axis=2, tiled=True)  163 us
    psum x1, waiting for transfers between devices, body(): lax.psum((grad_normed_part, placed_gains), 'tp')  152 us
    psum x1, waiting for transfers between devices, body(): attn_total = lax.psum(contract_last(heads_out, out_full), 'tp')  144 us
    psum x1, waiting for transfers between devices, body(): expert_grad_norm, gate_grads = lax.psum((expert_part, grad_gates.T), 'tp')  131 us
    dot_general x16, matrix products, expert_backward(): jnp.einsum('ctf,cdf->td', grad_acts, pair_weights, preferred_element_type...  97.3 us
  transfers between devices with their start and end apart: 18, of which 18 were waited for; matrix products, arithmetic and copies ran while one was open for 3% of the time, Pallas kernels for 0%

commit v1 on v0

v1 whole, which is shorter than its diff:
```python
import functools

import jax
import jax.numpy as jnp
from jax import lax
from jax.experimental import pallas as pl
from jax.experimental.pallas import tpu as pltpu
from jax.sharding import Mesh, PartitionSpec as P

HEAD_DIM = 128
EPSILON = 1e-05
THETA = 10000.0
TILE = 256
F32 = jnp.float32
BF16 = jnp.bfloat16
FR = ("fsdp", "row")
PLANE = ("fsdp", "row", "core")
EVERY = ("fsdp", "row", "core", "tp")


def nn(a, b):
    return lax.dot_general(a, b, (((1,), (0,)), ((), ())), preferred_element_type=F32)


def nt(a, b):
    return lax.dot_general(a, b, (((1,), (1,)), ((), ())), preferred_element_type=F32)


def tn(a, b):
    return lax.dot_general(a, b, (((0,), (0,)), ((), ())), preferred_element_type=F32)


def call(kernel, name, grid, in_specs, out_specs, out_shape, flops, moved, scratch=(), prefetch=0, limit=56, aliases=None):
    return pl.pallas_call(
        kernel,
        name=name,
        out_shape=out_shape,
        grid_spec=pltpu.PrefetchScalarGridSpec(
            num_scalar_prefetch=prefetch,
            grid=grid,
            in_specs=in_specs,
            out_specs=out_specs,
            scratch_shapes=list(scratch),
        ),
        input_output_aliases=aliases or {},
        compiler_params=pltpu.CompilerParams(
            dimension_semantics=("arbitrary",) * len(grid), vmem_limit_bytes=limit << 20
        ),
        cost_estimate=pl.CostEstimate(flops=int(flops), bytes_accessed=int(moved), transcendentals=0),
    )


def fixed(shape):
    return pl.BlockSpec(shape, lambda *a: (0,) * len(shape), pipeline_mode=pl.Buffered(1))


def sds(shape, dtype):
    return jax.ShapeDtypeStruct(shape, dtype)


def qkv_kernel(x_ref, g_ref, w_ref, n_ref, raw_ref, v_ref, sq_ref):
    c = pl.program_id(0)

    @pl.when(c == 0)
    def _():
        x = x_ref[...].astype(F32)
        r = lax.rsqrt(jnp.mean(x * x, -1, keepdims=True) + EPSILON)
        n_ref[...] = (x * r * g_ref[...]).astype(BF16)

    w = w_ref[...]
    y = nn(n_ref[...], w.reshape(w.shape[0] * w.shape[2], w.shape[3]))

    @pl.when(c < 2)
    def _():
        raw_ref[0] = y
        sq_ref[0] = jnp.broadcast_to(jnp.sum(y * y, -1, keepdims=True), sq_ref.shape[1:])

    @pl.when(c == 2)
    def _():
        v_ref[...] = y.astype(BF16)


def qkv_project(x, gain, w):
    t, d = x.shape
    p, _, ds, n = w.shape
    return call(
        qkv_kernel,
        "qkv",
        (3,),
        [
            fixed((t, d)),
            fixed((1, d)),
            pl.BlockSpec((p, 1, ds, n), lambda c: (0, c, 0, 0)),
        ],
        [
            pl.BlockSpec((t, d), lambda c: (0, 0)),
            pl.BlockSpec((1, t, n), lambda c: (jnp.minimum(c, 1), 0, 0)),
            pl.BlockSpec((t, n), lambda c: (0, 0)),
            pl.BlockSpec((1, t, 128), lambda c: (jnp.minimum(c, 1), 0, 0)),
        ],
        [sds((t, d), BF16), sds((2, t, n), F32), sds((t, n), BF16), sds((2, t, 128), F32)],
        6 * t * d * n,
        2 * (3 * d * n + 2 * t * d) + 10 * t * n,
    )(x, gain, w)


def turn(v, cosine, sine):
    half = v.shape[-1] // 2
    return v * cosine + pltpu.roll(v, half, 1) * sine


def prep_kernel(raw_ref, s_ref, g_ref, cos_ref, sin_ref, q_ref, k_ref):
    reps = raw_ref.shape[1] // cos_ref.shape[0]
    cosine = jnp.concatenate([cos_ref[...]] * reps, 0)
    sine = jnp.concatenate([sin_ref[...]] * reps, 0)
    q = raw_ref[0] * s_ref[0] * g_ref[0]
    k = raw_ref[1] * s_ref[1] * g_ref[1]
    q_ref[...] = turn(q, cosine, sine).astype(BF16)
    k_ref[...] = turn(k, cosine, sine).astype(BF16)


def prepare(raw, scales, gains, cosine, sine):
    _, t, n = raw.shape
    h = HEAD_DIM
    length = cosine.shape[0]
    return call(
        prep_kernel,
        "prep",
        (n // h,),
        [
            pl.BlockSpec((2, t, h), lambda i: (0, 0, i)),
            fixed((2, t, 1)),
            pl.BlockSpec((2, 1, h), lambda i: (0, 0, i)),
            fixed((length, h)),
            fixed((length, h)),
        ],
        [pl.BlockSpec((t, h), lambda i: (0, i))] * 2,
        [sds((t, n), BF16)] * 2,
        20 * t * n,
        12 * t * n,
    )(raw, scales, gains, cosine, sine)


def masked_probs(s, scal_ref, q, ks):
    length = q.shape[0]
    prefix = scal_ref[5 + s]
    rows = lax.broadcasted_iota(jnp.int32, (length, length), 0) + scal_ref[4]
    columns = lax.broadcasted_iota(jnp.int32, (length, length), 1)
    pieces = []
    for b, k in enumerate(ks):
        place = columns + scal_ref[b]
        visible = (place <= rows) | (place < prefix)
        pieces.append(jnp.where(visible, nt(q, k) * HEAD_DIM ** (-0.5), -1e30))
    scores = jnp.concatenate(pieces, 1)
    expo = jnp.exp(scores - jnp.max(scores, -1, keepdims=True))
    return expo / jnp.sum(expo, -1, keepdims=True)


def attend_kernel(scal_ref, q_ref, *refs):
    o_ref = refs[8]
    probs = masked_probs(pl.program_id(0), scal_ref, q_ref[...], [r[...] for r in refs[:4]])
    v = jnp.concatenate([r[...] for r in refs[4:8]], 0)
    o_ref[...] = nn(probs.astype(BF16), v).astype(BF16)


def attend(scal, q, blocks, length):
    t, n = q.shape
    h = HEAD_DIM
    one = pl.BlockSpec((length, h), lambda s, i, *_: (s, i))
    return call(
        attend_kernel,
        "attend",
        (t // length, n // h),
        [one] * 9,
        one,
        sds((t, n), BF16),
        16 * t * n * length,
        24 * t * n,
        prefetch=1,
    )(scal, q, *blocks)


def attend_back_kernel(scal_ref, q_ref, *refs):
    g_ref, dq_ref, outs = refs[8], refs[9], refs[10:]
    length = q_ref.shape[0]
    q = q_ref[...]
    grad = g_ref[...]
    probs = masked_probs(pl.program_id(0), scal_ref, q, [r[...] for r in refs[:4]])
    k = jnp.concatenate([r[...] for r in refs[:4]], 0)
    v = jnp.concatenate([r[...] for r in refs[4:8]], 0)
    d_probs = nt(grad, v)
    inner = jnp.sum(probs * d_probs, -1, keepdims=True)
    d_scores = (probs * (d_probs - inner)).astype(BF16)
    scale = HEAD_DIM ** (-0.5)
    dq_ref[...] = nn(d_scores, k) * scale
    dk = (tn(d_scores, q) * scale).astype(BF16)
    dv = tn(probs.astype(BF16), grad).astype(BF16)
    for b, o in enumerate(outs):
        o[0] = dk[b * length : (b + 1) * length]
        o[1] = dv[b * length : (b + 1) * length]


def attend_back(scal, q, blocks, grad, length):
    t, n = q.shape
    h = HEAD_DIM
    one = pl.BlockSpec((length, h), lambda s, i, *_: (s, i))
    two = pl.BlockSpec((2, length, h), lambda s, i, *_: (0, s, i))
    return call(
        attend_back_kernel,
        "attend_back",
        (t // length, n // h),
        [one] * 10,
        [one] + [two] * 4,
        [sds((t, n), F32)] + [sds((2, t, n), BF16)] * 4,
        40 * t * n * length,
        48 * t * n,
        prefetch=1,
    )(scal, q, *blocks, grad)


def out_kernel(place_ref, h_ref, w_ref, *outs):
    w = w_ref[...]
    w = w.reshape(-1, w.shape[-1])
    rows = outs[0].shape[0]
    for r, o in enumerate(outs):
        start = pl.multiple_of(place_ref[r], rows)
        o[...] = nt(h_ref[pl.ds(start, rows), :], w).astype(BF16)


def project_out(places, heads, w, pieces):
    t, n = heads.shape
    p, _, ds, _ = w.shape
    pb = max(1, TILE // ds)
    return call(
        out_kernel,
        "outproj",
        (p // pb,),
        [fixed((t, n)), pl.BlockSpec((pb, 1, ds, n), lambda g, *_: (g, 3, 0, 0))],
        [pl.BlockSpec((t // pieces, pb * ds), lambda g, *_: (0, g))] * pieces,
        [sds((t // pieces, p * ds), BF16)] * pieces,
        2 * t * n * p * ds,
        2 * (t * n + n * p * ds + t * p * ds),
        prefetch=1,
    )(places, heads, w)


def d_heads_kernel(place_ref, g_ref, w_ref, o_ref, *, pieces):
    w = w_ref[...]
    y = nn(g_ref[...], w.reshape(w.shape[0] * w.shape[2], w.shape[3])).astype(BF16)
    rows = y.shape[0] // pieces
    for r in range(pieces):
        o_ref[pl.ds(pl.multiple_of(place_ref[r], rows), rows), :] = y[r * rows : (r + 1) * rows]


def heads_grad(places, grad, w, pieces):
    t, d = grad.shape
    p, _, ds, n = w.shape
    return call(
        functools.partial(d_heads_kernel, pieces=pieces),
        "dheads",
        (1,),
        [fixed((t, d)), pl.BlockSpec((p, 1, ds, n), lambda g, *_: (0, 3, 0, 0))],
        fixed((t, n)),
        sds((t, n), BF16),
        2 * t * n * d,
        2 * (t * n + n * d + t * d),
        prefetch=1,
    )(places, grad, w)


def grad_out_kernel(place_ref, g_ref, h_ref, o_ref, *, pieces):
    rows = g_ref.shape[0] // pieces
    heads = jnp.concatenate(
        [h_ref[pl.ds(pl.multiple_of(place_ref[r], rows), rows), :] for r in range(pieces)], 0
    )
    o_ref[...] = tn(g_ref[...], heads).astype(BF16).reshape(o_ref.shape)


def out_weight_grad(places, grad, heads, p, pieces):
    t, d = grad.shape
    n = heads.shape[1]
    ds = d // p
    pb = max(1, TILE // ds)
    return call(
        functools.partial(grad_out_kernel, pieces=pieces),
        "gradout",
        (p // pb,),
        [pl.BlockSpec((t, pb * ds), lambda g, *_: (0, g)), fixed((t, n))],
        pl.BlockSpec((pb, 1, ds, n), lambda g, *_: (g, 3, 0, 0)),
        sds((p, 4, ds, n), BF16),
        2 * t * n * d,
        2 * (t * n + n * d + t * d),
        prefetch=1,
    )(places, grad, heads)


def router_kernel(x_ref, w_ref, ids_ref, o_ref, *, experts):
    logits = nt(x_ref[...], w_ref[...])
    lane = lax.broadcasted_iota(jnp.int32, logits.shape, 1)
    logits = jnp.where(lane < experts, logits, -1e30)
    expo = jnp.exp(logits - jnp.max(logits, -1, keepdims=True))
    probs = expo / jnp.sum(expo, -1, keepdims=True)
    chosen = jnp.zeros_like(probs)
    for j in range(ids_ref.shape[1]):
        chosen += (ids_ref[:, j : j + 1] == lane).astype(F32)
    o_ref[...] = probs * chosen


def route(x, router, ids, experts):
    t, d = x.shape
    return call(
        functools.partial(router_kernel, experts=experts),
        "router",
        (1,),
        [fixed((t, d)), fixed(router.shape), fixed(ids.shape)],
        fixed((t, 128)),
        sds((t, 128), F32),
        2 * t * d * 128,
        2 * t * d,
    )(x, router, ids)


def expert_kernel(scal_ref, x0_ref, x1_ref, c0_ref, c1_ref, g0_ref, g1_ref, w_ref, hid_ref, dgu_ref, dg_ref):
    e = pl.program_id(0)
    t = x0_ref.shape[0]

    @pl.when(e == 0)
    def _():
        dg_ref[...] = jnp.zeros_like(dg_ref)

    width = w_ref.shape[0] * w_ref.shape[3]
    f = w_ref.shape[4]
    me = scal_ref[0] + e
    out_lane = scal_ref[1] + e
    lane = lax.broadcasted_iota(jnp.int32, (TILE, 128), 1)
    for half, (x_ref, c_ref, g_ref) in enumerate(((x0_ref, c0_ref, g0_ref), (x1_ref, c1_ref, g1_ref))):
        for tile in range(t // TILE):
            rows = pl.ds(tile * TILE, TILE)
            to = pl.ds(half * t + tile * TILE, TILE)
            x = x_ref[rows, :]
            a = nn(x, w_ref[:, 0, 0].reshape(width, f))
            b = nn(x, w_ref[:, 0, 1].reshape(width, f))
            dh = nn(c_ref[rows, :], w_ref[:, 0, 2].reshape(width, f))
            gate = jnp.sum(jnp.where(lane == me, g_ref[rows, :], 0.0), -1, keepdims=True)
            sigma = jax.nn.sigmoid(a)
            swish = a * sigma
            act = swish * b
            hid_ref[to, :] = (gate * act).astype(BF16)
            d_gate = jnp.sum(dh * act, -1, keepdims=True)
            dg_ref[to, :] += jnp.where(lane == out_lane, d_gate, 0.0)
            inner = dh * gate
            dgu_ref[to, :f] = (inner * b * sigma * (1.0 + a * (1.0 - sigma))).astype(BF16)
            dgu_ref[to, f:] = (inner * swish).astype(BF16)


def expert_up(scal, x0, x1, c0, c1, g0, g1, w):
    t, d = x0.shape
    p, e, _, ds, f = w.shape
    return call(
        expert_kernel,
        "expert_up",
        (e,),
        [fixed((t, d))] * 4
        + [fixed((t, 128))] * 2
        + [pl.BlockSpec((p, 1, 3, ds, f), lambda i, *_: (0, i, 0, 0, 0))],
        [
            pl.BlockSpec((2 * t, f), lambda i, *_: (0, i)),
            pl.BlockSpec((2 * t, 2 * f), lambda i, *_: (0, i)),
            pl.BlockSpec((2 * t, 128), lambda i, *_: (0, 0)),
        ],
        [sds((2 * t, e * f), BF16), sds((2 * t, e * 2 * f), BF16), sds((2 * t, 128), F32)],
        12 * t * d * f * e,
        2 * (3 * d * f * e + 4 * t * d + 6 * t * f * e),
        prefetch=1,
    )(scal, x0, x1, c0, c1, g0, g1, w)


def expert_grad_kernel(x0_ref, x1_ref, c0_ref, c1_ref, hid_ref, dgu_ref, o_ref):
    pb, e, _, ds, f = o_ref.shape
    t = x0_ref.shape[0]
    for i in range(e):
        both = tn(x0_ref[...], dgu_ref[:t, i * 2 * f : (i + 1) * 2 * f]) + tn(
            x1_ref[...], dgu_ref[t:, i * 2 * f : (i + 1) * 2 * f]
        )
        o_ref[:, i, 0] = both[:, :f].astype(BF16).reshape(pb, ds, f)
        o_ref[:, i, 1] = both[:, f:].astype(BF16).reshape(pb, ds, f)
        down = tn(c0_ref[...], hid_ref[:t, i * f : (i + 1) * f]) + tn(
            c1_ref[...], hid_ref[t:, i * f : (i + 1) * f]
        )
        o_ref[:, i, 2] = down.astype(BF16).reshape(pb, ds, f)


def expert_grads(x0, x1, c0, c1, hid, dgu, p, e):
    t, d = x0.shape
    ds = d // p
    f = hid.shape[1] // e
    pb = max(1, TILE // ds)
    column = pl.BlockSpec((t, pb * ds), lambda g: (0, g))
    return call(
        expert_grad_kernel,
        "expert_grad",
        (p // pb,),
        [column] * 4 + [fixed(hid.shape), fixed(dgu.shape)],
        pl.BlockSpec((pb, e, 3, ds, f), lambda g: (g, 0, 0, 0, 0)),
        sds((p, e, 3, ds, f), BF16),
        12 * t * d * f * e,
        2 * (3 * d * f * e + 4 * t * d + 6 * t * f * e),
    )(x0, x1, c0, c1, hid, dgu)


def joined(w_ref, planes):
    pb, e, _, ds, f = w_ref.shape
    return jnp.concatenate([w_ref[:, i, c].reshape(pb * ds, f) for i in range(e) for c in range(planes)], 1)


def down_kernel(*refs, planes, parts):
    acts, ws, outs = refs[:parts], refs[parts : 2 * parts], refs[2 * parts :]
    t = outs[0].shape[0]
    for half, o in enumerate(outs):
        total = None
        for a, w in zip(acts, ws):
            piece = nt(a[half * t : (half + 1) * t, :], joined(w, planes))
            total = piece if total is None else total + piece
        o[...] = total.astype(BF16)


def expert_down(acts, ws, plane, planes, name):
    t2, k = acts[0].shape
    p, e, _, ds, f = ws[0].shape
    t = t2 // 2
    pb = max(1, TILE // ds)
    parts = len(acts)
    out = pl.BlockSpec((t, pb * ds), lambda g: (0, g))
    return call(
        functools.partial(down_kernel, planes=planes, parts=parts),
        name,
        (p // pb,),
        [fixed(a.shape) for a in acts]
        + [pl.BlockSpec((pb, e, planes, ds, f), lambda g: (g, 0, plane, 0, 0))] * parts,
        [out, out],
        [sds((t, p * ds), BF16)] * 2,
        2 * t2 * k * parts * p * ds,
        2 * parts * (t2 * k + k * p * ds) + 2 * t2 * p * ds,
    )(*acts, *ws)


def unturn_kernel(dq_ref, dk_ref, raw_ref, s_ref, g_ref, cos_ref, sin_ref, u_ref, in_ref, gg_ref):
    h = pl.program_id(0)
    reps = raw_ref.shape[1] // cos_ref.shape[0]
    cosine = jnp.concatenate([cos_ref[...]] * reps, 0)
    sine = jnp.concatenate([sin_ref[...]] * reps, 0)
    for i, grad in enumerate((dq_ref[...], dk_ref[...])):
        u = turn(grad, cosine, -sine)
        hat = raw_ref[i] * s_ref[i]
        product = u * hat
        u_ref[i] = u
        gg_ref[i] = jnp.sum(product, 0, keepdims=True)
        row = jnp.broadcast_to(jnp.sum(product * g_ref[i], -1, keepdims=True), in_ref.shape[1:])

        @pl.when(h == 0)
        def _():
            in_ref[i] = row

        @pl.when(h != 0)
        def _():
            in_ref[i] += row


def unturn(dq, dk, raw, scales, gains, cosine, sine):
    _, t, n = raw.shape
    h = HEAD_DIM
    length = cosine.shape[0]
    column = pl.BlockSpec((t, h), lambda i: (0, i))
    pair = pl.BlockSpec((2, t, h), lambda i: (0, 0, i))
    return call(
        unturn_kernel,
        "unturn",
        (n // h,),
        [
            column,
            column,
            pair,
            fixed((2, t, 1)),
            pl.BlockSpec((2, 1, h), lambda i: (0, 0, i)),
            fixed((length, h)),
            fixed((length, h)),
        ],
        [
            pair,
            pl.BlockSpec((2, t, 128), lambda i: (0, 0, 0)),
            pl.BlockSpec((2, 1, h), lambda i: (0, 0, i)),
        ],
        [sds((2, t, n), F32), sds((2, t, 128), F32), sds((2, 1, n), F32)],
        30 * t * n,
        24 * t * n,
    )(dq, dk, raw, scales, gains, cosine, sine)


def raw_grads_kernel(place_ref, u_ref, raw_ref, s_ref, in_ref, g_ref, dv_ref, n_ref, w_ref, kept_ref, *refs):
    gw_ref, outs, d_ref = refs[0], refs[1:-1], refs[-1]
    t, n = dv_ref.shape

    @pl.when(pl.program_id(0) == 0)
    def _():
        for i in range(2):
            hat = raw_ref[i] * s_ref[i]
            d_ref[:, i * n : (i + 1) * n] = (
                s_ref[i] * (u_ref[i] * g_ref[i] - hat * in_ref[i])
            ).astype(BF16)
        d_ref[:, 2 * n :] = dv_ref[...]

    pb, _, ds, _ = w_ref.shape
    w = jnp.concatenate([w_ref[:, c].reshape(pb * ds, n) for c in range(3)], 1)
    rows = outs[0].shape[0]
    for r, o in enumerate(outs):
        o[...] = nt(d_ref[pl.ds(pl.multiple_of(place_ref[r], rows), rows), :], w).astype(BF16)
    grads = tn(n_ref[...], d_ref[...]).astype(BF16)
    for c in range(3):
        gw_ref[:, c] = grads[:, c * n : (c + 1) * n].reshape(pb, ds, n)


def raw_grads(places, u, raw, scales, inner, gains, dv, normed, w, kept, pieces):
    t, d = normed.shape
    p, _, ds, n = w.shape
    pb = max(1, TILE // ds)
    block = pl.BlockSpec((pb, 3, ds, n), lambda g, *_: (g, 0, 0, 0))
    return call(
        raw_grads_kernel,
        "rawgrads",
        (p // pb,),
        [
            fixed((2, t, n)),
            fixed((2, t, n)),
            fixed((2, t, 1)),
            fixed((2, t, 1)),
            fixed((2, 1, n)),
            fixed((t, n)),
            pl.BlockSpec((t, pb * ds), lambda g, *_: (0, g)),
            block,
            pl.BlockSpec(memory_space=pl.ANY),
        ],
        [block] + [pl.BlockSpec((t // pieces, pb * ds), lambda g, *_: (0, g))] * pieces,
        [sds(kept.shape, BF16)] + [sds((t // pieces, d), BF16)] * pieces,
        12 * t * d * n,
        2 * (6 * d * n + 2 * t * d) + 20 * t * n,
        scratch=[pltpu.VMEM((t, 3 * n), BF16)],
        prefetch=1,
        aliases={9: 0},
    )(places, u, raw, scales, inner, gains, dv, normed, w, kept)


def swap(value, axis):
    return lax.ppermute(value, axis, [(0, 1), (1, 0)])


def spread(value):
    rows = swap(value, "row")
    return (value, swap(value, "core"), rows, swap(rows, "core"))


def across(value, k):
    size = lax.axis_size("tp")
    return lax.ppermute(value, "tp", [(i, i ^ k) for i in range(size)])


def gather(own):
    far = across(own, 2)
    return [own, across(own, 1), far, across(far, 1)]


def scatter(chunks):
    kind = chunks[0].dtype
    near = chunks[2].astype(F32) + across(chunks[3], 1).astype(F32)
    near, beside = lax.optimization_barrier((near.astype(kind), chunks[1]))
    return [chunks[0], across(beside, 1), across(near, 2)]


def total(pieces):
    return sum(v.astype(F32) for v in pieces)


def both_cores(own, other, pieces):
    rows = own.shape[0] // pieces
    got = swap(other, "core")
    return [
        (own[r * rows : (r + 1) * rows].astype(F32) + got[r * rows : (r + 1) * rows].astype(F32)).astype(BF16)
        for r in range(pieces)
    ]


def in_place_kernel(place_ref, *refs):
    for r, piece in enumerate(refs[:-1]):

        @pl.when(pl.program_id(0) == r)
        def _():
            refs[-1][...] = piece[...]


def in_place(pieces, places):
    rows, d = pieces[0].shape
    count = len(pieces)
    return call(
        in_place_kernel,
        "inplace",
        (count,),
        [fixed((rows, d))] * count,
        pl.BlockSpec((rows, d), lambda r, place: (place[r] // rows, 0)),
        sds((rows * count, d), pieces[0].dtype),
        0,
        4 * rows * count * d,
        prefetch=1,
    )(places, *pieces)


def meet(value):
    value = value + across(value, 1)
    return value + across(value, 2)


def relative(value, places, pieces):
    rows = value.shape[0] // pieces
    return [lax.dynamic_slice_in_dim(value, places[r], rows, 0) for r in range(pieces)]


def body(
    inputs,
    prefix,
    expert_ids,
    norm_gains,
    qkv_weight,
    out_weight,
    router_weight,
    gate_up_weight,
    down_weight,
    cotangent,
    *,
    chunks,
):
    sequences, length, width = inputs.shape
    t = sequences * length
    tp = lax.axis_size("tp")
    quarter = t // tp
    column = lax.axis_index("tp")
    core = lax.axis_index("core")
    ctx = lax.axis_index("row") * 2 + core
    experts = router_weight.shape[1]
    half = experts // 2
    e = half // chunks
    x = inputs.reshape(t, width)
    places = jnp.stack([column ^ r for r in range(tp)]).astype(jnp.int32) * quarter
    cots = relative(cotangent.reshape(t, width), places, tp)
    c0 = jnp.concatenate(cots, 0)
    ids = relative(expert_ids.reshape(t, -1), places, tp)
    ids0 = jnp.concatenate(ids, 0)
    x_q = lax.dynamic_slice_in_dim(x, column * quarter, quarter, 0).astype(F32)

    attn_local = jnp.concatenate([qkv_weight, out_weight[None]], 0)
    attn_w = lax.all_gather(attn_local, PLANE, axis=0, tiled=False)
    gains_low = lax.all_gather(norm_gains, PLANE, axis=1, tiled=True)
    router = lax.all_gather(router_weight, PLANE, axis=0, tiled=True)
    triple = jnp.concatenate([gate_up_weight, down_weight[:, None]], 1)
    ds, f = triple.shape[2:]
    grouped = triple.reshape(2, chunks, e, 3, ds, f)
    ws = []
    for k in range(chunks):
        mine = lax.all_to_all(grouped[:, k], "core", 0, 0, tiled=True)
        full = lax.all_gather(mine, FR, axis=0, tiled=False)
        ws.append(full.reshape(-1, e, 3, ds, f))
    attn_w, gains_low, router = lax.optimization_barrier((attn_w, gains_low, router))
    p = attn_w.shape[0]
    c1 = swap(c0, "core")
    ids1 = swap(ids0, "core")

    gains = gains_low.astype(F32)
    n = attn_w.shape[3]
    router_rows = jnp.concatenate([router.T, jnp.zeros((128 - experts, width), BF16)], 0)

    normed_one, raw, values, squares = qkv_project(x, gains[0:1], attn_w)
    v_blocks = spread(values)
    squares = meet(squares[:, :, 0])
    scales = lax.rsqrt(squares / width + EPSILON)[:, :, None]
    own_gains = lax.dynamic_slice_in_dim(gains[2:4], column * n, n, 1)[:, None, :]
    halves = jnp.arange(0, HEAD_DIM, 2).astype(F32) / HEAD_DIM
    inverse = 1.0 / THETA**halves
    positions = ctx * length + jnp.arange(length, dtype=jnp.int32)
    angles = positions.astype(F32)[:, None] * inverse[None, :]
    cosine = jnp.concatenate([jnp.cos(angles)] * 2, 1)
    sine = jnp.concatenate([-jnp.sin(angles), jnp.sin(angles)], 1)
    queries, keys = prepare(raw, scales, own_gains, cosine, sine)
    blocks = spread(keys) + v_blocks
    offsets = jnp.stack([ctx, ctx ^ 1, ctx ^ 2, ctx ^ 3, ctx]).astype(jnp.int32) * length
    scal = jnp.concatenate([offsets, prefix.astype(jnp.int32)])
    heads = attend(scal, queries, blocks, length)
    mid = x_q + total(scatter(project_out(places, heads, attn_w, tp)))
    scale_two = lax.rsqrt(jnp.mean(mid * mid, -1, keepdims=True) + EPSILON)
    normal_two = mid * scale_two
    two_low = (normal_two * gains[1]).astype(BF16)
    x0 = jnp.concatenate(gather(two_low), 0)
    x1 = swap(x0, "core")

    g0 = route(x0, router_rows, ids0, experts)
    g1 = route(x1, router_rows, ids1, experts)
    hids, dgus, d_gates, grads = [], [], None, []
    for k in range(chunks):
        where = jnp.stack([core * half + k * e, k * e]).astype(jnp.int32)
        hid, dgu, dg = expert_up(where, x0, x1, c0, c1, g0, g1, ws[k])
        hids.append(hid)
        dgus.append(dgu)
        d_gates = dg if d_gates is None else d_gates + dg
        if k < chunks - 1:
            grad = expert_grads(x0, x1, c0, c1, hid, dgu, p, e)
            grad, x0, x1 = lax.optimization_barrier((grad, x0, x1))
            grads.append(grad)
    dx0, dx1 = expert_down(dgus, ws, 0, 2, "expert_dx")
    dx0, dx1, hids, dgus = lax.optimization_barrier((dx0, dx1, hids, dgus))
    dx, hids, dgus = lax.optimization_barrier((both_cores(dx0, dx1, tp), hids, dgus))
    d_normed = scatter(dx)
    gates_all = d_gates[:, :half]
    away = swap(gates_all[t:], "core")
    gates_own = jnp.where(
        core == 0,
        jnp.concatenate([gates_all[:t], away], 1),
        jnp.concatenate([away, gates_all[:t]], 1),
    )
    gate_grads = scatter([gates_own[r * quarter : (r + 1) * quarter] for r in range(tp)])
    grads.append(expert_grads(x0, x1, c0, c1, hids[-1], dgus[-1], p, e))
    last, hids = lax.optimization_barrier((grads[-1], hids))
    grads[-1] = last
    m0, m1 = expert_down(hids, ws, 2, 1, "expert_out")
    d_normed, gate_grads, m0, m1 = lax.optimization_barrier((d_normed, gate_grads, m0, m1))
    d_normed = total(d_normed)
    gate_grads = total(gate_grads)
    grads = [
        lax.psum_scatter(g.reshape(p // 2, 2, e, 3, ds, f), FR, scatter_dimension=0, tiled=False)
        for g in grads
    ]

    chosen = jnp.sum((ids[0][:, :, None] == jnp.arange(experts, dtype=jnp.int32)).astype(F32), 1)
    router_probs = jax.nn.softmax(jnp.dot(two_low, router, preferred_element_type=F32), -1)
    masked = gate_grads * chosen
    d_logits = (router_probs * (masked - jnp.sum(router_probs * masked, -1, keepdims=True))).astype(BF16)
    grad_router = tn(d_logits, two_low)
    d_normed = d_normed + nt(d_logits, router)
    weighted = d_normed * gains[1]
    d_mid = cots[0].astype(F32) + scale_two * (
        weighted - normal_two * jnp.mean(weighted * normal_two, -1, keepdims=True)
    )
    gain_two = jnp.sum(d_normed * normal_two, 0)
    d_mid_low = jnp.concatenate(gather(d_mid.astype(BF16)), 0)

    m0, m1, d_mid_low = lax.optimization_barrier((m0, m1, d_mid_low))
    d_heads = heads_grad(places, d_mid_low, attn_w, tp)
    grad_out = out_weight_grad(places, d_mid_low, heads, p, tp)
    moe = scatter(both_cores(m0, m1, tp))
    dq, b0, b1, b2, b3 = attend_back(scal, queries, blocks, d_heads, length)
    r1 = swap(b1, "core")
    r3 = swap(b3, "core")
    r2 = swap((b2.astype(F32) + r3.astype(F32)).astype(BF16), "row")
    d_kv = b0.astype(F32) + r1.astype(F32) + r2.astype(F32)
    dq, d_kv, moe, grads[0] = lax.optimization_barrier((dq, d_kv, moe, grads[0]))
    out_pieces = gather((mid + total(moe)).astype(BF16))
    u, inner, gain_qk = unturn(dq, d_kv[0], raw, scales, own_gains, cosine, sine)
    inner = (meet(inner[:, :, 0]) / width)[:, :, None]
    placed = lax.dynamic_update_slice_in_dim(
        jnp.zeros((2, width), F32), gain_qk[:, 0, :], column * n, 1
    )
    grad_attn, *d_one = raw_grads(
        places, u, raw, scales, inner, own_gains, d_kv[1].astype(BF16), normed_one, attn_w, grad_out, tp
    )
    grad_attn, grads[-1] = lax.optimization_barrier((grad_attn, grads[-1]))
    grad_attn = lax.psum_scatter(grad_attn, PLANE, scatter_dimension=0, tiled=False)
    d_one = total(scatter(d_one))
    scale_one = lax.rsqrt(jnp.mean(x_q * x_q, -1, keepdims=True) + EPSILON)
    normal_one = x_q * scale_one
    weighted_one = d_one * gains[0]
    grad_in = d_mid + scale_one * (
        weighted_one - normal_one * jnp.mean(weighted_one * normal_one, -1, keepdims=True)
    )
    gain_one = jnp.sum(d_one * normal_one, 0)
    grad_inputs = in_place(gather(grad_in.astype(BF16)), places).reshape(inputs.shape)
    outputs = in_place(out_pieces, places).reshape(inputs.shape)

    small = jnp.concatenate([grad_router, gain_one[None], gain_two[None], placed], 0)
    rows = small.shape[0]
    small = small.reshape(rows, p, ds).transpose(1, 0, 2)
    small = jnp.sum(lax.all_to_all(small, PLANE, 0, 0, tiled=True), 0)
    small = meet(small)
    owned_gains = small[experts:]
    owned_router = small[:experts].T

    owned = []
    for g in grads:
        owned.append(lax.all_to_all(g, "core", 0, 0, tiled=True))
    stacked = jnp.stack(owned, 1).astype(F32)
    owned_gate_up = stacked[:, :, :, :2].reshape(experts, 2, ds, f)
    owned_down = stacked[:, :, :, 2].reshape(experts, ds, f)
    grad_attn = grad_attn.astype(F32)
    return (
        outputs,
        grad_inputs,
        owned_gains,
        grad_attn[:3],
        grad_attn[3],
        owned_router,
        owned_gate_up,
        owned_down,
    )


def solution(mesh):
    fsdp, ctx, tp = (mesh.shape[a] for a in ("fsdp", "ctx", "tp"))
    fine = Mesh(mesh.devices.reshape(fsdp, ctx // 2, 2, tp), EVERY)
    tokens = P("fsdp", ("row", "core"), None)
    weights = (
        P(None, PLANE),
        P(None, PLANE, "tp"),
        P(PLANE, "tp"),
        P(PLANE, None),
        P(None, None, PLANE, "tp"),
        P(None, PLANE, "tp"),
    )
    return jax.shard_map(
        functools.partial(body, chunks=2),
        mesh=fine,
        in_specs=(tokens, P("fsdp"), tokens) + weights + (tokens,),
        out_specs=(tokens, tokens) + weights,
        check_vma=False,
    )
```

time: 2630 us -> 765 us (0.29)
  waiting for transfers between devices: 1700 us -> 357 us
  matrix products: 489 us -> 0.76 us
  local copies, waits for them, and re-layouts: 282 us -> 26.9 us
  Pallas kernels: 0 us -> 220 us
  starting transfers between devices: 1.37 us -> 45.5 us
    reduce_scatter x7 -> x1, waiting for transfers between devices: 845 us -> 0.01 us  [body(): lax.psum_scatter(grad_attn, PLANE, scatter_dimension=0, tiled=False)]
    psum x4 -> x0, waiting for transfers between devices: 509 us -> none  [the longest x1 152 us: body(): lax.psum((grad_normed_part, placed_gains), 'tp')]
    dot_general x111 -> x3, matrix products: 489 us -> 0.76 us  [the longest x1 0.32 us: nt(): lax.dot_general(a, b, (((1,), (1,)), ((), ())), preferred_element_type=F32)]
    ppermute x0 -> x48, waiting for transfers between devices: none -> 290 us  [the longest x33 216 us: across(): return lax.ppermute(value, 'tp', [(i, i ^ k) for i in range(size)])]
    all_gather x6 -> x3, waiting for transfers between devices: 335 us -> 66.5 us  [the longest x2 47 us: body(): full = lax.all_gather(mine, FR, axis=0, tiled=False)]
    pallas_call x0 -> x19, Pallas kernels: none -> 220 us  [the longest x2 43 us: expert_up(): call(expert_kernel, 'expert_up', (e,), [fixed((t, d))] * 4 + [fixed((t, 1...]
    dynamic_update_slice x80 -> x1, local copies, waits for them, and re-layouts: 176 us -> 0.02 us  [body(): lax.dynamic_update_slice_in_dim(jnp.zeros((2, width), F32), gain_qk[:, 0,...]
    while x160 -> x0, local copies, waits for them, and re-layouts: 57.7 us -> none
  transfers between devices with their start and end apart: 18 -> 55, of which waited for: 18 -> 30; matrix products, arithmetic and copies ran while one was open for 3% -> 7% of each run, Pallas kernels for 0% -> 29%
where the time goes in v1:
time: 765 us; the launch traced here: 760 us
  waiting for transfers between devices  357 us (47%)
  Pallas kernels  220 us (29%)
  blocking collectives  50.1 us (7%)
  starting transfers between devices  45.5 us (6%)
  other arithmetic  37.4 us (5%)
  local copies, waits for them, and re-layouts  26.9 us (4%)
  between operations  22.2 us (3%)
    ppermute x33, waiting for transfers between devices, across(): return lax.ppermute(value, 'tp', [(i, i ^ k) for i in range(size)])  216 us
    ppermute x15, waiting for transfers between devices, swap(): return lax.ppermute(value, axis, [(0, 1), (1, 0)])  73.7 us
    all_gather x2, waiting for transfers between devices, body(): full = lax.all_gather(mine, FR, axis=0, tiled=False)  47 us
    pallas_call x2, Pallas kernels, expert_up(): call(expert_kernel, 'expert_up', (e,), [fixed((t, d))] * 4 + [fixed((t, 1...  43 us
    pallas_call x2, Pallas kernels, expert_grads(): call(expert_grad_kernel, 'expert_grad', (p // pb,), [column] * 4 + [fixed...  39.8 us
    pallas_call x2, Pallas kernels, expert_down(): call(functools.partial(down_kernel, planes=planes, parts=parts), name, (p...  39.3 us
    ppermute x33, starting transfers between devices, across(): return lax.ppermute(value, 'tp', [(i, i ^ k) for i in range(size)])  34.6 us
    all_gather x1, waiting for transfers between devices, body(): attn_w = lax.all_gather(attn_local, PLANE, axis=0, tiled=False)  19.5 us
  transfers between devices with their start and end apart: 55, of which 30 were waited for; matrix products, arithmetic and copies ran while one was open for 7% of the time, Pallas kernels for 29%

profile of v1, /device:TPU:0, one launch (start us, length us, event | category | flops | bytes accessed | tf_op | source)
XLA Modules:
  0.0 759.9 jit_solution(12580682087064493098)
XLA Ops:
  12.7 7.2 all_to_all.25
  20.0 7.2 all_to_all.26
  27.9 10.3 %all_gather.26 = bf16[4,2048]{1,0:T(4,128)(2,1)S(1)} all-gather(bf16[4,256]{1,0:T(4,128)(2,1)S(1)} %copy-done.26), channel_id=1, replica_groups=mesh['fsdp'=2,'row'=2,'core'=2,'tp'=4] {'fsdp','row','core'}, dimensions={1}, use_global_device_ids=true | all-gather | bytes 18432 | tf_op jit(solution)/shard_map/all_gather | solution.py:659
  38.3 9.4 %all_gather.27 = bf16[2048,16]{0,1:T(8,128)(2,1)S(1)} all-gather(bf16[256,16]{0,1:T(8,128)(2,1)S(1)} %copy-done.24), channel_id=1, replica_groups=mesh['fsdp'=2,'row'=2,'core'=2,'tp'=4] {'fsdp','row','core'}, dimensions={0}, use_global_device_ids=true | all-gather | bytes 73728 | tf_op jit(solution)/shard_map/all_gather | solution.py:660
  48.2 19.5 %all-gather.7.cloned.1.call-done = bf16[32,256,512]{2,1,0:T(8,128)(2,1)} async-done(((bf16[4,256,512]{2,1,0:T(8,128)(2,1)}), bf16[32,256,512]{2,1,0:T(8,128)(2,1)}) %all-gather.7.cloned.1.call-update) | async-done | bytes 8388624 | tf_op jit(solution)/shard_map/all_gather | solution.py:658
  68.3 10.3 %qkv.1 = (bf16[512,2048]{1,0:T(8,128)(2,1)}, f32[2,512,512]{2,1,0:T(8,128)}, bf16[512,512]{1,0:T(8,128)(2,1)}, f32[2,512,128]{2,1,0:T(8,128)}) custom-call(bf16[512,2048]{1,0:T(8,128)(2,1)} %bitcast.91, f32[1,2048]{1,0:T(1,128)} %get-tuple-element.209.g_ref, bf16[8,4,256,512]{3,2,1,0:T(8,128)(2,1)} %bitcast.72), custom_call_target="tpu_custom_call" | custom-call | flops 3221225472 | bytes 13107200 | tf_op jit(solution)/shard_map/qkv/pallas_call | solution.py:86
  89.3 4.4 prep.1
  95.6 17.3 %collective-permute-done.6.refs_6_ = bf16[512,512]{1,0:T(8,128)(2,1)S(1)} collective-permute-done((bf16[512,512]{1,0:T(8,128)(2,1)}, bf16[512,512]{1,0:T(8,128)(2,1)S(1)}, u32[]{:S(2)}, u32[]{:S(2)}) %collective-permute-start.6) | collective-permute-done | bytes 524320 | tf_op jit(solution)/shard_map/ppermute | solution.py:553
  112.9 21.8 %collective-permute-done.3.refs_2_ = bf16[512,512]{1,0:T(8,128)(2,1)S(1)} collective-permute-done((bf16[512,512]{1,0:T(8,128)(2,1)}, bf16[512,512]{1,0:T(8,128)(2,1)S(1)}, u32[]{:S(2)}, u32[]{:S(2)}) %collective-permute-start.3) | collective-permute-done | bytes 524320 | tf_op jit(solution)/shard_map/ppermute | solution.py:553
  137.0 10.1 %attend.1.h_ref = bf16[512,512]{1,0:T(8,128)(2,1)} custom-call(s32[7]{0:T(128)} %pad_add_fusion.1.scal_ref, bf16[512,512]{1,0:T(8,128)(2,1)} %get-tuple-element.95.q_ref, bf16[512,512]{1,0:T(8,128)(2,1)} %get-tuple-element.96.refs_0_, bf16[512,512]{1,0:T(8,128)(2,1)} %copy-done.16, bf16[512,512]{1,0:T(8,128)(2,1)} %copy-done.14, ...), custom_call_target="tpu_custom_call" | custom-call | flops 1073741824 | bytes 6291456 | tf_op jit(solution)/shard_map/attend/pallas_call | solution.py:170
  147.0 8.3 %outproj.1 = (bf16[128,2048]{1,0:T(8,128)(2,1)}, bf16[128,2048]{1,0:T(8,128)(2,1)}, bf16[128,2048]{1,0:T(8,128)(2,1)}, bf16[128,2048]{1,0:T(8,128)(2,1)}) custom-call(s32[4]{0:T(128)} %add_multiply_fusion.1.place_ref, bf16[512,512]{1,0:T(8,128)(2,1)} %attend.1.h_ref, bf16[8,4,256,512]{3,2,1,0:T(8,128)(2,1)} %bitcast.73), custom_call_target="tpu_custom_call" | custom-call | flops 1073741824 | bytes 4718592 | tf_op jit(solution)/shard_map/outproj/pallas_call | solution.py:234
  156.8 13.0 %collective-permute-done.8 = bf16[128,2048]{1,0:T(8,128)(2,1)S(1)} collective-permute-done((bf16[128,2048]{1,0:T(8,128)(2,1)}, bf16[128,2048]{1,0:T(8,128)(2,1)S(1)}, u32[]{:S(2)}, u32[]{:S(2)}) %collective-permute-start.8) | collective-permute-done | bytes 524320 | tf_op jit(solution)/shard_map/ppermute | solution.py:563
  173.0 21.0 %collective-permute-done.9 = bf16[128,2048]{1,0:T(8,128)(2,1)S(1)} collective-permute-done((bf16[128,2048]{1,0:T(8,128)(2,1)}, bf16[128,2048]{1,0:T(8,128)(2,1)S(1)}, u32[]{:S(2)}, u32[]{:S(2)}) %collective-permute-start.9) | collective-permute-done | bytes 524320 | tf_op jit(solution)/shard_map/ppermute | solution.py:563
  194.0 4.1 collective-permute-done.10
  200.5 22.5 %collective-permute-done.12 = bf16[128,2048]{1,0:T(8,128)(2,1)S(1)} collective-permute-done((bf16[128,2048]{1,0:T(8,128)(2,1)S(1)}, bf16[128,2048]{1,0:T(8,128)(2,1)S(1)}, u32[]{:S(2)}, u32[]{:S(2)}) %collective-permute-start.12) | collective-permute-done | bytes 524320 | tf_op jit(solution)/shard_map/ppermute | solution.py:563
  242.9 3.4 router.2.g0_ref
  246.2 3.4 router.3.g1_ref
  249.6 21.5 %expert_up.2 = (bf16[1024,1024]{1,0:T(8,128)(2,1)}, bf16[1024,2048]{1,0:T(8,128)(2,1)}, f32[1024,128]{1,0:T(8,128)}) custom-call(s32[2]{0:T(128)} %pad_add_fusion.2.scal_ref, bf16[512,2048]{1,0:T(8,128)(2,1)} %copy-done, bf16[512,2048]{1,0:T(8,128)(2,1)} %collective-permute-done.14.x_ref.x1_ref, bf16[512,2048]{1,0:T(8,128)(2,1)} %pad_maximum_fusion.2.c0_ref, ...), custom_call_target="tpu_custom_call" | custom-call | flops 12884901888 | bytes 27262976 | tf_op jit(solution)/shard_map/expert_up/pallas_call | solution.py:359
  271.1 20.1 %expert_grad.2 = bf16[8,4,3,256,256]{4,3,2,1,0:T(8,128)(2,1)} custom-call(bf16[512,2048]{1,0:T(8,128)(2,1)} %copy-done, bf16[512,2048]{1,0:T(8,128)(2,1)} %collective-permute-done.14.x_ref.x1_ref, bf16[512,2048]{1,0:T(8,128)(2,1)} %pad_maximum_fusion.2.c0_ref, bf16[512,2048]{1,0:T(8,128)(2,1)} %collective-permute-done.15.c1_ref, ...), custom_call_target="tpu_custom_call" | custom-call | flops 12884901888 | bytes 27262976 | tf_op jit(solution)/shard_map/expert_grad/pallas_call | solution.py:399
  292.0 47.0 %all-gather.11.cloned.1.call-done.w_ref.refs_3_ = bf16[8,4,3,256,256]{4,3,2,1,0:T(8,128)(2,1)} async-done(((bf16[2,4,3,256,256]{4,3,2,1,0:T(8,128)(2,1)}), bf16[8,4,3,256,256]{4,3,2,1,0:T(8,128)(2,1)}) %all-gather.11.cloned.1.call-update) | async-done | bytes 12582928 | tf_op jit(solution)/shard_map/all_gather | solution.py:667
  339.0 21.5 %expert_up.3 = (bf16[1024,1024]{1,0:T(8,128)(2,1)}, bf16[1024,2048]{1,0:T(8,128)(2,1)}, f32[1024,128]{1,0:T(8,128)}) custom-call(s32[2]{0:T(128)} %pad_add_fusion.3.scal_ref, bf16[512,2048]{1,0:T(8,128)(2,1)} %copy-done, bf16[512,2048]{1,0:T(8,128)(2,1)} %collective-permute-done.14.x_ref.x1_ref, bf16[512,2048]{1,0:T(8,128)(2,1)} %pad_maximum_fusion.2.c0_ref, ...), custom_call_target="tpu_custom_call" | custom-call | flops 12884901888 | bytes 27262976 | tf_op jit(solution)/shard_map/expert_up/pallas_call | solution.py:359
  360.4 24.2 %expert_dx.1 = (bf16[512,2048]{1,0:T(8,128)(2,1)}, bf16[512,2048]{1,0:T(8,128)(2,1)}) custom-call(bf16[1024,2048]{1,0:T(8,128)(2,1)} %get-tuple-element.105.dgu_ref.refs_0_, bf16[1024,2048]{1,0:T(8,128)(2,1)} %get-tuple-element.129.refs_1_.dgu_ref, bf16[8,4,3,256,256]{4,3,2,1,0:T(8,128)(2,1)} %all-gather.9.cloned.1.call-done.w_ref.refs_2_, ...), custom_call_target="tpu_custom_call" | custom-call | flops 17179869184 | bytes 29360128 | tf_op jit(solution)/shard_map/expert_dx/pallas_call | solution.py:434
  384.6 4.4 collective-permute-done.17
  392.2 19.7 %expert_grad.3 = bf16[8,4,3,256,256]{4,3,2,1,0:T(8,128)(2,1)} custom-call(bf16[512,2048]{1,0:T(8,128)(2,1)} %copy-done, bf16[512,2048]{1,0:T(8,128)(2,1)} %collective-permute-done.14.x_ref.x1_ref, bf16[512,2048]{1,0:T(8,128)(2,1)} %pad_maximum_fusion.2.c0_ref, bf16[512,2048]{1,0:T(8,128)(2,1)} %collective-permute-done.15.c1_ref, ...), custom_call_target="tpu_custom_call" | custom-call | flops 12884901888 | bytes 27262976 | tf_op jit(solution)/shard_map/expert_grad/pallas_call | solution.py:399
  419.1 12.3 %collective-permute-done.22 = f32[128,16]{0,1:T(8,128)S(1)} collective-permute-done((f32[128,16]{0,1:T(8,128)S(1)}, f32[128,16]{0,1:T(8,128)S(1)}, u32[]{:S(2)}, u32[]{:S(2)}) %collective-permute-start.22) | collective-permute-done | bytes 8224 | tf_op jit(solution)/shard_map/ppermute | solution.py:563
  436.6 15.1 %expert_out.1 = (bf16[512,2048]{1,0:T(8,128)(2,1)}, bf16[512,2048]{1,0:T(8,128)(2,1)}) custom-call(bf16[1024,1024]{1,0:T(8,128)(2,1)} %get-tuple-element.131.hid_ref.refs_0_, bf16[1024,1024]{1,0:T(8,128)(2,1)} %get-tuple-element.132.hid_ref.refs_1_, bf16[8,4,3,256,256]{4,3,2,1,0:T(8,128)(2,1)} %all-gather.9.cloned.1.call-done.w_ref.refs_2_, ...), custom_call_target="tpu_custom_call" | custom-call | flops 8589934592 | bytes 16777216 | tf_op jit(solution)/shard_map/expert_out/pallas_call | solution.py:434
  451.7 7.0 collective-permute-done.19
  464.8 20.7 %collective-permute-done.26 = bf16[128,2048]{1,0:T(8,128)(2,1)S(1)} collective-permute-done((bf16[128,2048]{1,0:T(8,128)(2,1)S(1)}, bf16[128,2048]{1,0:T(8,128)(2,1)S(1)}, u32[]{:S(2)}, u32[]{:S(2)}) %collective-permute-start.26) | collective-permute-done | bytes 524320 | tf_op jit(solution)/shard_map/ppermute | solution.py:563
  485.6 13.2 %collective-permute-done.27 = bf16[128,2048]{1,0:T(8,128)(2,1)S(1)} collective-permute-done((bf16[128,2048]{1,0:T(8,128)(2,1)S(1)}, bf16[128,2048]{1,0:T(8,128)(2,1)S(1)}, u32[]{:S(2)}, u32[]{:S(2)}) %collective-permute-start.27) | collective-permute-done | bytes 524320 | tf_op jit(solution)/shard_map/ppermute | solution.py:563
  500.4 5.2 dheads.1.refs_8_
  505.6 13.4 %attend_back.1 = (f32[512,512]{1,0:T(8,128)}, bf16[2,512,512]{2,1,0:T(8,128)(2,1)}, bf16[2,512,512]{2,1,0:T(8,128)(2,1)}, bf16[2,512,512]{2,1,0:T(8,128)(2,1)}, bf16[2,512,512]{2,1,0:T(8,128)(2,1)}) custom-call(s32[7]{0:T(128)} %pad_add_fusion.1.scal_ref, bf16[512,512]{1,0:T(8,128)(2,1)} %get-tuple-element.95.q_ref, ...), custom_call_target="tpu_custom_call" | custom-call | flops 2684354560 | bytes 12582912 | tf_op jit(solution)/shard_map/attend_back/pallas_call | solution.py:208
  523.8 11.4 %collective-permute-done.32 = bf16[128,2048]{1,0:T(8,128)(2,1)S(1)} collective-permute-done((bf16[128,2048]{1,0:T(8,128)(2,1)S(1)}, bf16[128,2048]{1,0:T(8,128)(2,1)S(1)}, u32[]{:S(2)}, u32[]{:S(2)}) %collective-permute-start.32) | collective-permute-done | bytes 524320 | tf_op jit(solution)/shard_map/ppermute | solution.py:563
  535.9 28.2 %collective-permute-done.30 = bf16[2,512,512]{2,1,0:T(8,128)(2,1)S(1)} collective-permute-done((bf16[2,512,512]{2,1,0:T(8,128)(2,1)S(1)}, bf16[2,512,512]{2,1,0:T(8,128)(2,1)S(1)}, u32[]{:S(2)}, u32[]{:S(2)}) %collective-permute-start.30) | collective-permute-done | bytes 1048608 | tf_op jit(solution)/shard_map/ppermute | solution.py:553
  568.9 6.1 unturn.1
  578.1 7.7 %gradout.1.kept_ref = bf16[8,4,256,512]{3,2,1,0:T(8,128)(2,1)} custom-call(s32[4]{0:T(128)} %add_multiply_fusion.1.place_ref, bf16[512,2048]{1,0:T(8,128)(2,1)} %pad_maximum_fusion.3.g_ref, bf16[512,512]{1,0:T(8,128)(2,1)} %attend.1.h_ref), custom_call_target="tpu_custom_call" | custom-call | flops 1073741824 | bytes 4718592 | tf_op jit(solution)/shard_map/gradout/pallas_call | solution.py:284
  591.3 17.9 %rawgrads.1 = (bf16[8,4,256,512]{3,2,1,0:T(8,128)(2,1)}, bf16[128,2048]{1,0:T(8,128)(2,1)}, bf16[128,2048]{1,0:T(8,128)(2,1)}, bf16[128,2048]{1,0:T(8,128)(2,1)}, bf16[128,2048]{1,0:T(8,128)(2,1)}) custom-call(s32[4]{0:T(128)} %add_multiply_fusion.1.place_ref, f32[2,512,512]{2,1,0:T(8,128)} %get-tuple-element.159.u_ref, ...), custom_call_target="tpu_custom_call", output_to_operand_aliasing={{0}: (9, {})} | custom-call | flops 6442450944 | bytes 22020096 | tf_op jit(solution)/shard_map/rawgrads/pallas_call | solution.py:527
  609.9 13.0 %collective-permute-done.40 = bf16[128,2048]{1,0:T(8,128)(2,1)S(1)} collective-permute-done((bf16[128,2048]{1,0:T(8,128)(2,1)}, bf16[128,2048]{1,0:T(8,128)(2,1)S(1)}, u32[]{:S(2)}, u32[]{:S(2)}) %collective-permute-start.40) | collective-permute-done | bytes 524320 | tf_op jit(solution)/shard_map/ppermute | solution.py:563
  626.6 20.9 %collective-permute-done.41 = bf16[128,2048]{1,0:T(8,128)(2,1)S(1)} collective-permute-done((bf16[128,2048]{1,0:T(8,128)(2,1)}, bf16[128,2048]{1,0:T(8,128)(2,1)S(1)}, u32[]{:S(2)}, u32[]{:S(2)}) %collective-permute-start.41) | collective-permute-done | bytes 524320 | tf_op jit(solution)/shard_map/ppermute | solution.py:563
  657.0 8.3 %all_to_all.27 = f32[8,20,256]{2,1,0:T(8,128)S(1)} all-to-all(f32[8,20,256]{2,1,0:T(8,128)S(1)} %maximum_bitcast_fusion), channel_id=1, replica_groups=mesh['fsdp'=2,'row'=2,'core'=2,'tp'=4] {'fsdp','row','core'}, dimensions={0} | all-to-all | bytes 327680 | tf_op jit(solution)/shard_map/all_to_all | solution.py:786
  665.4 10.3 %collective-permute-done.46 = f32[20,256]{1,0:T(8,128)S(1)} collective-permute-done((f32[20,256]{1,0:T(8,128)S(1)}, f32[20,256]{1,0:T(8,128)S(1)}, u32[]{:S(2)}, u32[]{:S(2)}) %collective-permute-start.46) | collective-permute-done | bytes 20512 | tf_op jit(solution)/shard_map/ppermute | solution.py:563
  677.8 4.2 all-to-all-start.3
  684.1 16.2 %collective-permute-done.47 = f32[20,256]{1,0:T(8,128)S(1)} collective-permute-done((f32[20,256]{1,0:T(8,128)S(1)}, f32[20,256]{1,0:T(8,128)S(1)}, u32[]{:S(2)}, u32[]{:S(2)}) %collective-permute-start.47) | collective-permute-done | bytes 20512 | tf_op jit(solution)/shard_map/ppermute | solution.py:563
  703.5 7.5 all_to_all.28
  711.9 4.3 slice.204
  718.5 15.5 %collective-permute-done.45.refs_3_ = bf16[128,2048]{1,0:T(8,128)(2,1)} collective-permute-done((bf16[128,2048]{1,0:T(8,128)(2,1)}, bf16[128,2048]{1,0:T(8,128)(2,1)}, u32[]{:S(2)}, u32[]{:S(2)}) %collective-permute-start.45) | collective-permute-done | bytes 524320 | tf_op jit(solution)/shard_map/ppermute | solution.py:563
  734.0 4.1 inplace.3
  738.1 7.1 collective-permute-done.37.refs_3_
  745.2 4.1 inplace.2
  (231 shorter events, 112.5 us)
Async XLA Ops:
  7.2 60.5 %all-gather.7.cloned.1.call-start = ((), (), s32[]{:S(2)}) async-start(), calls=%async_computation.9 | async-start | bytes 9437184 | tf_op jit(solution)/shard_map/all_gather | solution.py:658
  9.5 240.1 %all-gather.9.cloned.1.call-start = ((), (), s32[]{:S(2)}) async-start(), calls=%async_computation.10 | async-start | bytes 15728640 | tf_op jit(solution)/shard_map/all_gather | solution.py:667
  20.0 319.0 %all-gather.11.cloned.1.call-start = ((), (), s32[]{:S(2)}) async-start(), calls=%async_computation.11 | async-start | bytes 15728640 | tf_op jit(solution)/shard_map/all_gather | solution.py:667
  27.3 539.4 %reduce-scatter.10.cloned.1.call-start = ((), (), s32[]{:S(2)}) async-start(), calls=%async_computation.12 | async-start | bytes 15728640
  86.7 26.2 %collective-permute-start.6 = (bf16[512,512]{1,0:T(8,128)(2,1)}, bf16[512,512]{1,0:T(8,128)(2,1)S(1)}, u32[]{:S(2)}, u32[]{:S(2)}) collective-permute-start(bf16[512,512]{1,0:T(8,128)(2,1)} %get-tuple-element.97.refs_4_), channel_id=1, source_target_pairs={{0,8},{8,0},{1,9},{9,1},{2,10},{10,2},{3,11},{11,3},{4,12},{12,4},... | collective-permute-start | bytes 1572872 | tf_op jit(solution)/shard_map/ppermute | solution.py:553
  93.7 41.0 %collective-permute-start.3 = (bf16[512,512]{1,0:T(8,128)(2,1)}, bf16[512,512]{1,0:T(8,128)(2,1)S(1)}, u32[]{:S(2)}, u32[]{:S(2)}) collective-permute-start(bf16[512,512]{1,0:T(8,128)(2,1)} %get-tuple-element.96.refs_0_), channel_id=1, source_target_pairs={{0,8},{8,0},{1,9},{9,1},{2,10},{10,2},{3,11},{11,3},{4,12},{12,4},... | collective-permute-start | bytes 1572872 | tf_op jit(solution)/shard_map/ppermute | solution.py:553
  95.0 40.9 %collective-permute-start.5 = (bf16[512,512]{1,0:T(8,128)(2,1)S(1)}, bf16[512,512]{1,0:T(8,128)(2,1)S(1)}, u32[]{:S(2)}, u32[]{:S(2)}) collective-permute-start(bf16[512,512]{1,0:T(8,128)(2,1)S(1)} %copy-done.12), channel_id=1, source_target_pairs={{0,4},{4,0},{1,5},{5,1},{2,6},{6,2},{3,7},{7,3},{8,12},{12,8},{9,1... | collective-permute-start | bytes 1572872 | tf_op jit(solution)/shard_map/ppermute | solution.py:553
  95.1 40.9 %collective-permute-start.2 = (bf16[512,512]{1,0:T(8,128)(2,1)}, bf16[512,512]{1,0:T(8,128)(2,1)S(1)}, u32[]{:S(2)}, u32[]{:S(2)}) collective-permute-start(bf16[512,512]{1,0:T(8,128)(2,1)} %get-tuple-element.96.refs_0_), channel_id=1, source_target_pairs={{0,4},{4,0},{1,5},{5,1},{2,6},{6,2},{3,7},{7,3},{8,12},{12,8},{9,1... | collective-permute-start | bytes 1572872 | tf_op jit(solution)/shard_map/ppermute | solution.py:553
  112.9 23.1 %collective-permute-start.7 = (bf16[512,512]{1,0:T(8,128)(2,1)S(1)}, bf16[512,512]{1,0:T(8,128)(2,1)}, u32[]{:S(2)}, u32[]{:S(2)}) collective-permute-start(bf16[512,512]{1,0:T(8,128)(2,1)S(1)} %collective-permute-done.6.refs_6_), channel_id=1, source_target_pairs={{0,4},{4,0},{1,5},{5,1},{2,6},{6,2},{3,7},{7,3},{8,12},{12,8},{9,1... | collective-permute-start | bytes 1572872 | tf_op jit(solution)/shard_map/ppermute | solution.py:553
  155.3 14.5 %collective-permute-start.8 = (bf16[128,2048]{1,0:T(8,128)(2,1)}, bf16[128,2048]{1,0:T(8,128)(2,1)S(1)}, u32[]{:S(2)}, u32[]{:S(2)}) collective-permute-start(bf16[128,2048]{1,0:T(8,128)(2,1)} %get-tuple-element.100), channel_id=1, source_target_pairs={{0,1},{1,0},{2,3},{3,2},{4,5},{5,4},{6,7},{7,6},{8,9},{9,8},{10,11... | collective-permute-start | bytes 1572872 | tf_op jit(solution)/shard_map/ppermute | solution.py:563
  170.9 23.1 %collective-permute-start.9 = (bf16[128,2048]{1,0:T(8,128)(2,1)}, bf16[128,2048]{1,0:T(8,128)(2,1)S(1)}, u32[]{:S(2)}, u32[]{:S(2)}) collective-permute-start(bf16[128,2048]{1,0:T(8,128)(2,1)} %get-tuple-element.102), channel_id=1, source_target_pairs={{0,1},{1,0},{2,3},{3,2},{4,5},{5,4},{6,7},{7,6},{8,9},{9,8},{10,11... | collective-permute-start | bytes 1572872 | tf_op jit(solution)/shard_map/ppermute | solution.py:563
  172.6 25.6 %collective-permute-start.10 = (bf16[128,2048]{1,0:T(8,128)(2,1)S(1)}, bf16[128,2048]{1,0:T(8,128)(2,1)S(1)}, u32[]{:S(2)}, u32[]{:S(2)}) collective-permute-start(bf16[128,2048]{1,0:T(8,128)(2,1)S(1)} %add_convert_fusion.13), channel_id=1, source_target_pairs={{0,2},{1,3},{2,0},{3,1},{4,6},{5,7},{6,4},{7,5},{8,10},{9,11},{10,... | collective-permute-start | bytes 1572872 | tf_op jit(solution)/shard_map/ppermute | solution.py:563
  200.0 23.0 %collective-permute-start.12 = (bf16[128,2048]{1,0:T(8,128)(2,1)S(1)}, bf16[128,2048]{1,0:T(8,128)(2,1)S(1)}, u32[]{:S(2)}, u32[]{:S(2)}) collective-permute-start(bf16[128,2048]{1,0:T(8,128)(2,1)S(1)} %multiply_convert_fusion), channel_id=1, source_target_pairs={{0,2},{1,3},{2,0},{3,1},{4,6},{5,7},{6,4},{7,5},{8,10},{9,11},{10,... | collective-permute-start | bytes 1572872 | tf_op jit(solution)/shard_map/ppermute | solution.py:563
  200.5 32.8 %collective-permute-start.11 = (bf16[128,2048]{1,0:T(8,128)(2,1)S(1)}, bf16[128,2048]{1,0:T(8,128)(2,1)S(1)}, u32[]{:S(2)}, u32[]{:S(2)}) collective-permute-start(bf16[128,2048]{1,0:T(8,128)(2,1)S(1)} %multiply_convert_fusion), channel_id=1, source_target_pairs={{0,1},{1,0},{2,3},{3,2},{4,5},{5,4},{6,7},{7,6},{8,9},{9,8},{10,11... | collective-permute-start | bytes 1572872 | tf_op jit(solution)/shard_map/ppermute | solution.py:563
  223.0 13.9 %collective-permute-start.13 = (bf16[128,2048]{1,0:T(8,128)(2,1)S(1)}, bf16[128,2048]{1,0:T(8,128)(2,1)}, u32[]{:S(2)}, u32[]{:S(2)}) collective-permute-start(bf16[128,2048]{1,0:T(8,128)(2,1)S(1)} %collective-permute-done.12), channel_id=1, source_target_pairs={{0,1},{1,0},{2,3},{3,2},{4,5},{5,4},{6,7},{7,6},{8,9},{9,8},{10,11... | collective-permute-start | bytes 1572872 | tf_op jit(solution)/shard_map/ppermute | solution.py:563
  238.6 7.7 %collective-permute-start.14 = (bf16[512,2048]{1,0:T(8,128)(2,1)S(1)}, bf16[512,2048]{1,0:T(8,128)(2,1)}, u32[]{:S(2)}, u32[]{:S(2)}) collective-permute-start(bf16[512,2048]{1,0:T(8,128)(2,1)S(1)} %pad_maximum_fusion.1.x_ref.x0_ref), channel_id=1, source_target_pairs={{0,4},{4,0},{1,5},{5,1},{2,6},{6,2},{3,7},{7,3},{8,12},{12,8},{9,1... | collective-permute-start | bytes 6291464 | tf_op jit(solution)/shard_map/ppermute | solution.py:553
  240.6 9.1 %collective-permute-start.15 = (bf16[512,2048]{1,0:T(8,128)(2,1)}, bf16[512,2048]{1,0:T(8,128)(2,1)}, u32[]{:S(2)}, u32[]{:S(2)}) collective-permute-start(bf16[512,2048]{1,0:T(8,128)(2,1)} %pad_maximum_fusion.2.c0_ref), channel_id=1, source_target_pairs={{0,4},{4,0},{1,5},{5,1},{2,6},{6,2},{3,7},{7,3},{8,12},{12,8},{9,1... | collective-permute-start | bytes 6291464 | tf_op jit(solution)/shard_map/ppermute | solution.py:553
  241.0 5.3 collective-permute-start.16
  291.3 318.0 %reduce-scatter.12.cloned.1.call-start = ((), (), s32[]{:S(2)}) async-start(), calls=%async_computation.13 | async-start | bytes 15728640
  411.9 337.4 %reduce-scatter.8.cloned.1.call-start = ((), (), s32[]{:S(2)}) async-start(), calls=%async_computation.8 | async-start | bytes 9437184 | tf_op jit(solution)/shard_map/reduce_scatter | solution.py:771
  417.0 18.3 %collective-permute-start.18 = (bf16[128,2048]{1,0:T(8,128)(2,1)S(1)}, bf16[128,2048]{1,0:T(8,128)(2,1)S(1)}, u32[]{:S(2)}, u32[]{:S(2)}) collective-permute-start(bf16[128,2048]{1,0:T(8,128)(2,1)S(1)} %get-tuple-element.120), channel_id=1, source_target_pairs={{0,1},{1,0},{2,3},{3,2},{4,5},{5,4},{6,7},{7,6},{8,9},{9,8},{10,11... | collective-permute-start | bytes 1572872 | tf_op jit(solution)/shard_map/ppermute | solution.py:563
  418.5 12.9 %collective-permute-start.22 = (f32[128,16]{0,1:T(8,128)S(1)}, f32[128,16]{0,1:T(8,128)S(1)}, u32[]{:S(2)}, u32[]{:S(2)}) collective-permute-start(f32[128,16]{0,1:T(8,128)S(1)} %get-tuple-element.202), channel_id=1, source_target_pairs={{0,1},{1,0},{2,3},{3,2},{4,5},{5,4},{6,7},{7,6},{8,9},{9,8},{10,11... | collective-permute-start | bytes 24584 | tf_op jit(solution)/shard_map/ppermute | solution.py:563
  431.4 20.3 %collective-permute-start.23 = (f32[128,16]{0,1:T(8,128)S(1)}, f32[128,16]{0,1:T(8,128)S(1)}, u32[]{:S(2)}, u32[]{:S(2)}) collective-permute-start(f32[128,16]{0,1:T(8,128)S(1)} %get-tuple-element.126), channel_id=1, source_target_pairs={{0,1},{1,0},{2,3},{3,2},{4,5},{5,4},{6,7},{7,6},{8,9},{9,8},{10,11... | collective-permute-start | bytes 24584 | tf_op jit(solution)/shard_map/ppermute | solution.py:563
  432.9 18.8 %collective-permute-start.24 = (f32[128,16]{0,1:T(8,128)S(1)}, f32[128,16]{0,1:T(8,128)S(1)}, u32[]{:S(2)}, u32[]{:S(2)}) collective-permute-start(f32[128,16]{0,1:T(8,128)S(1)} %slice_add_fusion), channel_id=1, source_target_pairs={{0,2},{1,3},{2,0},{3,1},{4,6},{5,7},{6,4},{7,5},{8,10},{9,11},{10,... | collective-permute-start | bytes 24584 | tf_op jit(solution)/shard_map/ppermute | solution.py:563
  435.5 23.2 %collective-permute-start.19 = (bf16[128,2048]{1,0:T(8,128)(2,1)S(1)}, bf16[128,2048]{1,0:T(8,128)(2,1)S(1)}, u32[]{:S(2)}, u32[]{:S(2)}) collective-permute-start(bf16[128,2048]{1,0:T(8,128)(2,1)S(1)} %get-tuple-element.122), channel_id=1, source_target_pairs={{0,1},{1,0},{2,3},{3,2},{4,5},{5,4},{6,7},{7,6},{8,9},{9,8},{10,11... | collective-permute-start | bytes 1572872 | tf_op jit(solution)/shard_map/ppermute | solution.py:563
  436.1 24.8 %collective-permute-start.20 = (bf16[128,2048]{1,0:T(8,128)(2,1)S(1)}, bf16[128,2048]{1,0:T(8,128)(2,1)S(1)}, u32[]{:S(2)}, u32[]{:S(2)}) collective-permute-start(bf16[128,2048]{1,0:T(8,128)(2,1)S(1)} %add_convert_fusion.8), channel_id=1, source_target_pairs={{0,2},{1,3},{2,0},{3,1},{4,6},{5,7},{6,4},{7,5},{8,10},{9,11},{10,... | collective-permute-start | bytes 1572872 | tf_op jit(solution)/shard_map/ppermute | solution.py:563
  462.6 22.9 %collective-permute-start.26 = (bf16[128,2048]{1,0:T(8,128)(2,1)S(1)}, bf16[128,2048]{1,0:T(8,128)(2,1)S(1)}, u32[]{:S(2)}, u32[]{:S(2)}) collective-permute-start(bf16[128,2048]{1,0:T(8,128)(2,1)S(1)} %fusion.17), channel_id=1, source_target_pairs={{0,2},{1,3},{2,0},{3,1},{4,6},{5,7},{6,4},{7,5},{8,10},{9,11},{10,... | collective-permute-start | bytes 1572872 | tf_op jit(solution)/shard_map/ppermute | solution.py:563
  463.1 22.5 %collective-permute-start.25 = (bf16[128,2048]{1,0:T(8,128)(2,1)S(1)}, bf16[128,2048]{1,0:T(8,128)(2,1)S(1)}, u32[]{:S(2)}, u32[]{:S(2)}) collective-permute-start(bf16[128,2048]{1,0:T(8,128)(2,1)S(1)} %fusion.17), channel_id=1, source_target_pairs={{0,1},{1,0},{2,3},{3,2},{4,5},{5,4},{6,7},{7,6},{8,9},{9,8},{10,11... | collective-permute-start | bytes 1572872 | tf_op jit(solution)/shard_map/ppermute | solution.py:563
  485.5 13.3 %collective-permute-start.27 = (bf16[128,2048]{1,0:T(8,128)(2,1)S(1)}, bf16[128,2048]{1,0:T(8,128)(2,1)S(1)}, u32[]{:S(2)}, u32[]{:S(2)}) collective-permute-start(bf16[128,2048]{1,0:T(8,128)(2,1)S(1)} %collective-permute-done.26), channel_id=1, source_target_pairs={{0,1},{1,0},{2,3},{3,2},{4,5},{5,4},{6,7},{7,6},{8,9},{9,8},{10,11... | collective-permute-start | bytes 1572872 | tf_op jit(solution)/shard_map/ppermute | solution.py:563
  500.4 19.1 %collective-permute-start.31 = (bf16[512,2048]{1,0:T(8,128)(2,1)}, bf16[512,2048]{1,0:T(8,128)(2,1)S(1)}, u32[]{:S(2)}, u32[]{:S(2)}) collective-permute-start(bf16[512,2048]{1,0:T(8,128)(2,1)} %get-tuple-element.150), channel_id=1, source_target_pairs={{0,4},{4,0},{1,5},{5,1},{2,6},{6,2},{3,7},{7,3},{8,12},{12,8},{9,1... | collective-permute-start | bytes 6291464 | tf_op jit(solution)/shard_map/ppermute | solution.py:553
  519.3 16.6 %collective-permute-start.28 = (bf16[2,512,512]{2,1,0:T(8,128)(2,1)}, bf16[2,512,512]{2,1,0:T(8,128)(2,1)S(1)}, u32[]{:S(2)}, u32[]{:S(2)}) collective-permute-start(bf16[2,512,512]{2,1,0:T(8,128)(2,1)} %get-tuple-element.146), channel_id=1, source_target_pairs={{0,4},{4,0},{1,5},{5,1},{2,6},{6,2},{3,7},{7,3},{8,12},{12,8},{9,1... | collective-permute-start | bytes 3145736 | tf_op jit(solution)/shard_map/ppermute | solution.py:553
  520.9 14.2 %collective-permute-start.32 = (bf16[128,2048]{1,0:T(8,128)(2,1)S(1)}, bf16[128,2048]{1,0:T(8,128)(2,1)S(1)}, u32[]{:S(2)}, u32[]{:S(2)}) collective-permute-start(bf16[128,2048]{1,0:T(8,128)(2,1)S(1)} %get-tuple-element.186), channel_id=1, source_target_pairs={{0,1},{1,0},{2,3},{3,2},{4,5},{5,4},{6,7},{7,6},{8,9},{9,8},{10,11... | collective-permute-start | bytes 1572872 | tf_op jit(solution)/shard_map/ppermute | solution.py:563
  522.1 41.9 %collective-permute-start.30 = (bf16[2,512,512]{2,1,0:T(8,128)(2,1)S(1)}, bf16[2,512,512]{2,1,0:T(8,128)(2,1)S(1)}, u32[]{:S(2)}, u32[]{:S(2)}) collective-permute-start(bf16[2,512,512]{2,1,0:T(8,128)(2,1)S(1)} %add_convert_fusion), channel_id=1, source_target_pairs={{0,8},{8,0},{1,9},{9,1},{2,10},{10,2},{3,11},{11,3},{4,12},{12,4},... | collective-permute-start | bytes 3145736 | tf_op jit(solution)/shard_map/ppermute | solution.py:553
  535.4 30.5 %collective-permute-start.33 = (bf16[128,2048]{1,0:T(8,128)(2,1)S(1)}, bf16[128,2048]{1,0:T(8,128)(2,1)S(1)}, u32[]{:S(2)}, u32[]{:S(2)}) collective-permute-start(bf16[128,2048]{1,0:T(8,128)(2,1)S(1)} %get-tuple-element.151), channel_id=1, source_target_pairs={{0,1},{1,0},{2,3},{3,2},{4,5},{5,4},{6,7},{7,6},{8,9},{9,8},{10,11... | collective-permute-start | bytes 1572872 | tf_op jit(solution)/shard_map/ppermute | solution.py:563
  535.9 30.7 %collective-permute-start.34 = (bf16[128,2048]{1,0:T(8,128)(2,1)S(1)}, bf16[128,2048]{1,0:T(8,128)(2,1)}, u32[]{:S(2)}, u32[]{:S(2)}) collective-permute-start(bf16[128,2048]{1,0:T(8,128)(2,1)S(1)} %add_convert_fusion.4), channel_id=1, source_target_pairs={{0,2},{1,3},{2,0},{3,1},{4,6},{5,7},{6,4},{7,5},{8,10},{9,11},{10,... | collective-permute-start | bytes 1572872 | tf_op jit(solution)/shard_map/ppermute | solution.py:563
  576.3 9.4 %collective-permute-start.38 = (f32[2,512]{1,0:T(2,128)S(1)}, f32[2,512]{1,0:T(2,128)S(1)}, u32[]{:S(2)}, u32[]{:S(2)}) collective-permute-start(f32[2,512]{1,0:T(2,128)S(1)} %slice_reduce_fusion), channel_id=1, source_target_pairs={{0,1},{1,0},{2,3},{3,2},{4,5},{5,4},{6,7},{7,6},{8,9},{9,8},{10,11... | collective-permute-start | bytes 12296 | tf_op jit(solution)/shard_map/ppermute | solution.py:563
  609.4 13.6 %collective-permute-start.40 = (bf16[128,2048]{1,0:T(8,128)(2,1)}, bf16[128,2048]{1,0:T(8,128)(2,1)S(1)}, u32[]{:S(2)}, u32[]{:S(2)}) collective-permute-start(bf16[128,2048]{1,0:T(8,128)(2,1)} %get-tuple-element.164), channel_id=1, source_target_pairs={{0,1},{1,0},{2,3},{3,2},{4,5},{5,4},{6,7},{7,6},{8,9},{9,8},{10,11... | collective-permute-start | bytes 1572872 | tf_op jit(solution)/shard_map/ppermute | solution.py:563
  624.3 23.2 %collective-permute-start.41 = (bf16[128,2048]{1,0:T(8,128)(2,1)}, bf16[128,2048]{1,0:T(8,128)(2,1)S(1)}, u32[]{:S(2)}, u32[]{:S(2)}) collective-permute-start(bf16[128,2048]{1,0:T(8,128)(2,1)} %get-tuple-element.166), channel_id=1, source_target_pairs={{0,1},{1,0},{2,3},{3,2},{4,5},{5,4},{6,7},{7,6},{8,9},{9,8},{10,11... | collective-permute-start | bytes 1572872 | tf_op jit(solution)/shard_map/ppermute | solution.py:563
  624.9 24.2 %collective-permute-start.42 = (bf16[128,2048]{1,0:T(8,128)(2,1)S(1)}, bf16[128,2048]{1,0:T(8,128)(2,1)S(1)}, u32[]{:S(2)}, u32[]{:S(2)}) collective-permute-start(bf16[128,2048]{1,0:T(8,128)(2,1)S(1)} %add_convert_fusion.1), channel_id=1, source_target_pairs={{0,2},{1,3},{2,0},{3,1},{4,6},{5,7},{6,4},{7,5},{8,10},{9,11},{10,... | collective-permute-start | bytes 1572872 | tf_op jit(solution)/shard_map/ppermute | solution.py:563
  654.0 47.5 %collective-permute-start.44 = (bf16[128,2048]{1,0:T(8,128)(2,1)}, bf16[128,2048]{1,0:T(8,128)(2,1)}, u32[]{:S(2)}, u32[]{:S(2)}) collective-permute-start(bf16[128,2048]{1,0:T(8,128)(2,1)} %get-tuple-element.197.refs_0_), channel_id=1, source_target_pairs={{0,2},{1,3},{2,0},{3,1},{4,6},{5,7},{6,4},{7,5},{8,10},{9,11},{10,... | collective-permute-start | bytes 1572872 | tf_op jit(solution)/shard_map/ppermute | solution.py:563
  654.6 46.8 %collective-permute-start.36 = (bf16[128,2048]{1,0:T(8,128)(2,1)}, bf16[128,2048]{1,0:T(8,128)(2,1)}, u32[]{:S(2)}, u32[]{:S(2)}) collective-permute-start(bf16[128,2048]{1,0:T(8,128)(2,1)} %get-tuple-element.198.refs_0_), channel_id=1, source_target_pairs={{0,2},{1,3},{2,0},{3,1},{4,6},{5,7},{6,4},{7,5},{8,10},{9,11},{10,... | collective-permute-start | bytes 1572872 | tf_op jit(solution)/shard_map/ppermute | solution.py:563
  665.3 10.3 %collective-permute-start.46 = (f32[20,256]{1,0:T(8,128)S(1)}, f32[20,256]{1,0:T(8,128)S(1)}, u32[]{:S(2)}, u32[]{:S(2)}) collective-permute-start(f32[20,256]{1,0:T(8,128)S(1)} %reduce_sum.99), channel_id=1, source_target_pairs={{0,1},{1,0},{2,3},{3,2},{4,5},{5,4},{6,7},{7,6},{8,9},{9,8},{10,11... | collective-permute-start | bytes 61448 | tf_op jit(solution)/shard_map/ppermute | solution.py:563
  675.7 24.6 %collective-permute-start.47 = (f32[20,256]{1,0:T(8,128)S(1)}, f32[20,256]{1,0:T(8,128)S(1)}, u32[]{:S(2)}, u32[]{:S(2)}) collective-permute-start(f32[20,256]{1,0:T(8,128)S(1)} %add.233), channel_id=1, source_target_pairs={{0,2},{1,3},{2,0},{3,1},{4,6},{5,7},{6,4},{7,5},{8,10},{9,11},{10,... | collective-permute-start | bytes 61448 | tf_op jit(solution)/shard_map/ppermute | solution.py:563
  677.8 25.7 %all-to-all-start.3 = ((bf16[2,4,3,256,256]{4,3,2,1,0:T(8,128)(2,1)}), bf16[2,4,3,256,256]{4,3,2,1,0:T(8,128)(2,1)S(1)}, u32[]{:S(2)}, u32[]{:S(2)}) async-start(bf16[2,4,3,256,256]{4,3,2,1,0:T(8,128)(2,1)} %bitcast.85), calls=%async_computation.4 | async-start | bytes 6291456 | tf_op jit(solution)/shard_map/all_to_all | solution.py:793
  682.0 36.5 %collective-permute-start.43 = (bf16[128,2048]{1,0:T(8,128)(2,1)}, bf16[128,2048]{1,0:T(8,128)(2,1)}, u32[]{:S(2)}, u32[]{:S(2)}) collective-permute-start(bf16[128,2048]{1,0:T(8,128)(2,1)} %get-tuple-element.197.refs_0_), channel_id=1, source_target_pairs={{0,1},{1,0},{2,3},{3,2},{4,5},{5,4},{6,7},{7,6},{8,9},{9,8},{10,11... | collective-permute-start | bytes 1572872 | tf_op jit(solution)/shard_map/ppermute | solution.py:563
  682.4 55.7 %collective-permute-start.35 = (bf16[128,2048]{1,0:T(8,128)(2,1)}, bf16[128,2048]{1,0:T(8,128)(2,1)}, u32[]{:S(2)}, u32[]{:S(2)}) collective-permute-start(bf16[128,2048]{1,0:T(8,128)(2,1)} %get-tuple-element.198.refs_0_), channel_id=1, source_target_pairs={{0,1},{1,0},{2,3},{3,2},{4,5},{5,4},{6,7},{7,6},{8,9},{9,8},{10,11... | collective-permute-start | bytes 1572872 | tf_op jit(solution)/shard_map/ppermute | solution.py:563
  701.5 32.5 %collective-permute-start.45 = (bf16[128,2048]{1,0:T(8,128)(2,1)}, bf16[128,2048]{1,0:T(8,128)(2,1)}, u32[]{:S(2)}, u32[]{:S(2)}) collective-permute-start(bf16[128,2048]{1,0:T(8,128)(2,1)} %collective-permute-done.44.refs_2_), channel_id=1, source_target_pairs={{0,1},{1,0},{2,3},{3,2},{4,5},{5,4},{6,7},{7,6},{8,9},{9,8},{10,11... | collective-permute-start | bytes 1572872 | tf_op jit(solution)/shard_map/ppermute | solution.py:563
  701.5 43.7 %collective-permute-start.37 = (bf16[128,2048]{1,0:T(8,128)(2,1)}, bf16[128,2048]{1,0:T(8,128)(2,1)}, u32[]{:S(2)}, u32[]{:S(2)}) collective-permute-start(bf16[128,2048]{1,0:T(8,128)(2,1)} %collective-permute-done.36.refs_2_), channel_id=1, source_target_pairs={{0,1},{1,0},{2,3},{3,2},{4,5},{5,4},{6,7},{7,6},{8,9},{9,8},{10,11... | collective-permute-start | bytes 1572872 | tf_op jit(solution)/shard_map/ppermute | solution.py:563
  (35 other events, 453.5 us)
Sparse Core Ops, SparseCore 0:
  10.5 57.1 all-gather.6
  69.5 145.0 all-gather.8
  216.4 122.4 all-gather.10
  341.9 120.7 reduce-scatter.9
  465.6 140.5 reduce-scatter.11
  609.5 71.2 reduce-scatter.7

commit v2 on v1

v2 whole, which is shorter than its diff:
```python
import functools

import jax
import jax.numpy as jnp
from jax import lax
from jax.experimental import pallas as pl
from jax.experimental.pallas import tpu as pltpu
from jax.sharding import Mesh, PartitionSpec as P

HEAD_DIM = 128
EPSILON = 1e-05
THETA = 10000.0
TILE = 256
F32 = jnp.float32
BF16 = jnp.bfloat16
FR = ("fsdp", "row")
LANES = 128
PLANE = ("fsdp", "row", "core")
EVERY = ("fsdp", "row", "core", "tp")


def nn(a, b):
    return lax.dot_general(a, b, (((1,), (0,)), ((), ())), preferred_element_type=F32)


def nt(a, b):
    return lax.dot_general(a, b, (((1,), (1,)), ((), ())), preferred_element_type=F32)


def tn(a, b):
    return lax.dot_general(a, b, (((0,), (0,)), ((), ())), preferred_element_type=F32)


def call(kernel, name, grid, in_specs, out_specs, out_shape, flops, moved, scratch=(), prefetch=0, limit=56, aliases=None):
    return pl.pallas_call(
        kernel,
        name=name,
        out_shape=out_shape,
        grid_spec=pltpu.PrefetchScalarGridSpec(
            num_scalar_prefetch=prefetch,
            grid=grid,
            in_specs=in_specs,
            out_specs=out_specs,
            scratch_shapes=list(scratch),
        ),
        input_output_aliases=aliases or {},
        compiler_params=pltpu.CompilerParams(
            dimension_semantics=("arbitrary",) * len(grid), vmem_limit_bytes=limit << 20
        ),
        cost_estimate=pl.CostEstimate(flops=int(flops), bytes_accessed=int(moved), transcendentals=0),
    )


def fixed(shape):
    return pl.BlockSpec(shape, lambda *a: (0,) * len(shape), pipeline_mode=pl.Buffered(1))


def sds(shape, dtype):
    return jax.ShapeDtypeStruct(shape, dtype)


def qkv_kernel(x_ref, g_ref, w_ref, n_ref, raw_ref, v_ref, sq_ref):
    c = pl.program_id(0)

    @pl.when(c == 0)
    def _():
        x = x_ref[...].astype(F32)
        r = lax.rsqrt(jnp.mean(x * x, -1, keepdims=True) + EPSILON)
        n_ref[...] = (x * r * g_ref[...]).astype(BF16)

    w = w_ref[...]
    y = nn(n_ref[...], w.reshape(w.shape[0] * w.shape[2], w.shape[3]))

    @pl.when(c < 2)
    def _():
        raw_ref[0] = y
        sq_ref[0] = jnp.broadcast_to(jnp.sum(y * y, -1, keepdims=True), sq_ref.shape[1:])

    @pl.when(c == 2)
    def _():
        v_ref[...] = y.astype(BF16)


def qkv_project(x, gain, w):
    t, d = x.shape
    p, _, ds, n = w.shape
    return call(
        qkv_kernel,
        "qkv",
        (3,),
        [
            fixed((t, d)),
            fixed((1, d)),
            pl.BlockSpec((p, 1, ds, n), lambda c: (0, c, 0, 0)),
        ],
        [
            pl.BlockSpec((t, d), lambda c: (0, 0)),
            pl.BlockSpec((1, t, n), lambda c: (jnp.minimum(c, 1), 0, 0)),
            pl.BlockSpec((t, n), lambda c: (0, 0)),
            pl.BlockSpec((1, t, 128), lambda c: (jnp.minimum(c, 1), 0, 0)),
        ],
        [sds((t, d), BF16), sds((2, t, n), F32), sds((t, n), BF16), sds((2, t, 128), F32)],
        6 * t * d * n,
        2 * (3 * d * n + 2 * t * d) + 10 * t * n,
    )(x, gain, w)


def turn(v, cosine, sine):
    half = v.shape[-1] // 2
    return v * cosine + pltpu.roll(v, half, 1) * sine


def prep_kernel(raw_ref, s_ref, g_ref, cos_ref, sin_ref, q_ref, k_ref):
    reps = raw_ref.shape[1] // cos_ref.shape[0]
    cosine = jnp.concatenate([cos_ref[...]] * reps, 0)
    sine = jnp.concatenate([sin_ref[...]] * reps, 0)
    q = raw_ref[0] * s_ref[0] * g_ref[0]
    k = raw_ref[1] * s_ref[1] * g_ref[1]
    q_ref[...] = turn(q, cosine, sine).astype(BF16)
    k_ref[...] = turn(k, cosine, sine).astype(BF16)


def prepare(raw, scales, gains, cosine, sine):
    _, t, n = raw.shape
    h = HEAD_DIM
    length = cosine.shape[0]
    return call(
        prep_kernel,
        "prep",
        (n // h,),
        [
            pl.BlockSpec((2, t, h), lambda i: (0, 0, i)),
            fixed((2, t, 1)),
            pl.BlockSpec((2, 1, h), lambda i: (0, 0, i)),
            fixed((length, h)),
            fixed((length, h)),
        ],
        [pl.BlockSpec((t, h), lambda i: (0, i))] * 2,
        [sds((t, n), BF16)] * 2,
        20 * t * n,
        12 * t * n,
    )(raw, scales, gains, cosine, sine)


def masked_probs(s, scal_ref, q, ks):
    length = q.shape[0]
    prefix = scal_ref[5 + s]
    rows = lax.broadcasted_iota(jnp.int32, (length, length), 0) + scal_ref[4]
    columns = lax.broadcasted_iota(jnp.int32, (length, length), 1)
    pieces = []
    for b, k in enumerate(ks):
        place = columns + scal_ref[b]
        visible = (place <= rows) | (place < prefix)
        pieces.append(jnp.where(visible, nt(q, k) * HEAD_DIM ** (-0.5), -1e30))
    scores = jnp.concatenate(pieces, 1)
    expo = jnp.exp(scores - jnp.max(scores, -1, keepdims=True))
    return expo / jnp.sum(expo, -1, keepdims=True)


def attend_kernel(scal_ref, q_ref, *refs):
    o_ref = refs[8]
    probs = masked_probs(pl.program_id(0), scal_ref, q_ref[...], [r[...] for r in refs[:4]])
    v = jnp.concatenate([r[...] for r in refs[4:8]], 0)
    o_ref[...] = nn(probs.astype(BF16), v).astype(BF16)


def attend(scal, q, blocks, length):
    t, n = q.shape
    h = HEAD_DIM
    one = pl.BlockSpec((length, h), lambda s, i, *_: (s, i))
    return call(
        attend_kernel,
        "attend",
        (t // length, n // h),
        [one] * 9,
        one,
        sds((t, n), BF16),
        16 * t * n * length,
        24 * t * n,
        prefetch=1,
    )(scal, q, *blocks)


def attend_back_kernel(scal_ref, q_ref, *refs):
    g_ref, dq_ref, outs = refs[8], refs[9], refs[10:]
    length = q_ref.shape[0]
    q = q_ref[...]
    grad = g_ref[...]
    probs = masked_probs(pl.program_id(0), scal_ref, q, [r[...] for r in refs[:4]])
    k = jnp.concatenate([r[...] for r in refs[:4]], 0)
    v = jnp.concatenate([r[...] for r in refs[4:8]], 0)
    d_probs = nt(grad, v)
    inner = jnp.sum(probs * d_probs, -1, keepdims=True)
    d_scores = (probs * (d_probs - inner)).astype(BF16)
    scale = HEAD_DIM ** (-0.5)
    dq_ref[...] = nn(d_scores, k) * scale
    dk = (tn(d_scores, q) * scale).astype(BF16)
    dv = tn(probs.astype(BF16), grad).astype(BF16)
    for b, o in enumerate(outs):
        o[0] = dk[b * length : (b + 1) * length]
        o[1] = dv[b * length : (b + 1) * length]


def attend_back(scal, q, blocks, grad, length):
    t, n = q.shape
    h = HEAD_DIM
    one = pl.BlockSpec((length, h), lambda s, i, *_: (s, i))
    two = pl.BlockSpec((2, length, h), lambda s, i, *_: (0, s, i))
    return call(
        attend_back_kernel,
        "attend_back",
        (t // length, n // h),
        [one] * 10,
        [one] + [two] * 4,
        [sds((t, n), F32)] + [sds((2, t, n), BF16)] * 4,
        40 * t * n * length,
        48 * t * n,
        prefetch=1,
    )(scal, q, *blocks, grad)


def out_kernel(place_ref, h_ref, w_ref, *outs):
    w = w_ref[...]
    w = w.reshape(-1, w.shape[-1])
    rows = outs[0].shape[0]
    heads = jnp.concatenate(
        [h_ref[pl.ds(pl.multiple_of(place_ref[r], rows), rows), :] for r in range(len(outs))], 0
    )
    y = nt(heads, w).astype(BF16)
    for r, o in enumerate(outs):
        o[...] = y[r * rows : (r + 1) * rows]


def project_out(places, heads, w, pieces):
    t, n = heads.shape
    p, _, ds, _ = w.shape
    pb = max(1, 2 * TILE // ds)
    return call(
        out_kernel,
        "outproj",
        (p // pb,),
        [fixed((t, n)), pl.BlockSpec((pb, 1, ds, n), lambda g, *_: (g, 3, 0, 0))],
        [pl.BlockSpec((t // pieces, pb * ds), lambda g, *_: (0, g))] * pieces,
        [sds((t // pieces, p * ds), BF16)] * pieces,
        2 * t * n * p * ds,
        2 * (t * n + n * p * ds + t * p * ds),
        prefetch=1,
    )(places, heads, w)


def d_heads_kernel(place_ref, g_ref, w_ref, o_ref, *, pieces):
    w = w_ref[...]
    y = nn(g_ref[...], w.reshape(w.shape[0] * w.shape[2], w.shape[3])).astype(BF16)
    rows = y.shape[0] // pieces
    for r in range(pieces):
        o_ref[pl.ds(pl.multiple_of(place_ref[r], rows), rows), :] = y[r * rows : (r + 1) * rows]


def heads_grad(places, grad, w, pieces):
    t, d = grad.shape
    p, _, ds, n = w.shape
    return call(
        functools.partial(d_heads_kernel, pieces=pieces),
        "dheads",
        (1,),
        [fixed((t, d)), pl.BlockSpec((p, 1, ds, n), lambda g, *_: (0, 3, 0, 0), pipeline_mode=pl.Buffered(1))],
        fixed((t, n)),
        sds((t, n), BF16),
        2 * t * n * d,
        2 * (t * n + n * d + t * d),
        prefetch=1,
    )(places, grad, w)


def grad_out_kernel(place_ref, g_ref, h_ref, o_ref, *, pieces):
    rows = g_ref.shape[0] // pieces
    heads = jnp.concatenate(
        [h_ref[pl.ds(pl.multiple_of(place_ref[r], rows), rows), :] for r in range(pieces)], 0
    )
    o_ref[...] = tn(g_ref[...], heads).astype(BF16).reshape(o_ref.shape)


def out_weight_grad(places, grad, heads, p, pieces):
    t, d = grad.shape
    n = heads.shape[1]
    ds = d // p
    pb = max(1, TILE // ds)
    return call(
        functools.partial(grad_out_kernel, pieces=pieces),
        "gradout",
        (p // pb,),
        [pl.BlockSpec((t, pb * ds), lambda g, *_: (0, g)), fixed((t, n))],
        pl.BlockSpec((pb, ds, n), lambda g, *_: (g, 0, 0)),
        sds((p, ds, n), BF16),
        2 * t * n * d,
        2 * (t * n + n * d + t * d),
        prefetch=1,
    )(places, grad, heads)


def norm_two_kernel(x_ref, a_ref, b_ref, c_ref, g_ref, w_ref, ids_ref, mid_ref, ext_ref, probs_ref, chosen_ref, *, experts):
    mid = x_ref[...].astype(F32) + a_ref[...].astype(F32) + b_ref[...].astype(F32) + c_ref[...].astype(F32)
    mid_ref[...] = mid
    d = mid.shape[1]
    r = lax.rsqrt(jnp.mean(mid * mid, -1, keepdims=True) + EPSILON)
    low = (mid * r * g_ref[...]).astype(BF16)
    ext_ref[:, :d] = low
    logits = nt(low, w_ref[...])
    lane = lax.broadcasted_iota(jnp.int32, logits.shape, 1)
    logits = jnp.where(lane < experts, logits, -1e30)
    expo = jnp.exp(logits - jnp.max(logits, -1, keepdims=True))
    probs = expo / jnp.sum(expo, -1, keepdims=True)
    chosen = jnp.zeros_like(probs)
    for j in range(ids_ref.shape[1]):
        chosen += (ids_ref[:, j : j + 1] == lane).astype(F32)
    probs_ref[...] = probs
    chosen_ref[...] = chosen
    gates = probs * chosen
    high = gates.astype(BF16)
    rest = (gates - high.astype(F32)).astype(BF16)
    ext_ref[:, d:] = jnp.concatenate([high[:, : LANES // 2], rest[:, : LANES // 2]], 1)


def norm_two(x, sums, gain, router, ids, experts):
    t, d = x.shape
    return call(
        functools.partial(norm_two_kernel, experts=experts),
        "norm_two",
        (1,),
        [fixed((t, d))] * 4 + [fixed((1, d)), fixed(router.shape), fixed(ids.shape)],
        [fixed((t, d)), fixed((t, d + LANES)), fixed((t, LANES)), fixed((t, LANES))],
        [sds((t, d), F32), sds((t, d + LANES), BF16), sds((t, LANES), F32), sds((t, LANES), F32)],
        2 * t * d * LANES,
        14 * t * d,
    )(x, *sums, gain, router, ids)


def norm_two_back_kernel(a_ref, b_ref, c_ref, mid_ref, ext_ref, probs_ref, chosen_ref, cot_ref, g_ref, w_ref, *outs):
    mid_grad_ref, low_ref, gain_ref, router_ref = outs
    d = mid_ref.shape[1]
    du = a_ref[...].astype(F32) + b_ref[...].astype(F32) + c_ref[...].astype(F32)
    probs = probs_ref[...]
    masked = du[:, d:] * chosen_ref[...]
    d_logits = (probs * (masked - jnp.sum(probs * masked, -1, keepdims=True))).astype(BF16)
    router_ref[...] = tn(d_logits, ext_ref[:, :d])
    u = du[:, :d] + nn(d_logits, w_ref[...])
    mid = mid_ref[...]
    r = lax.rsqrt(jnp.mean(mid * mid, -1, keepdims=True) + EPSILON)
    hat = mid * r
    gain_ref[...] = jnp.sum(u * hat, 0, keepdims=True)
    w = u * g_ref[...]
    grad = cot_ref[...].astype(F32) + r * (w - hat * jnp.mean(w * hat, -1, keepdims=True))
    mid_grad_ref[...] = grad
    low_ref[...] = grad.astype(BF16)


def norm_two_back(sums, mid, ext, probs, chosen, cot, gain, router):
    t, d = mid.shape
    wide = fixed((t, d + LANES))
    return call(
        norm_two_back_kernel,
        "norm_two_back",
        (1,),
        [wide] * 3
        + [fixed((t, d)), wide, fixed((t, LANES)), fixed((t, LANES)), fixed((t, d)), fixed((1, d)), fixed(router.shape)],
        [fixed((t, d)), fixed((t, d)), fixed((1, d)), fixed((LANES, d))],
        [sds((t, d), F32), sds((t, d), BF16), sds((1, d), F32), sds((LANES, d), F32)],
        4 * t * d * LANES,
        20 * t * d,
    )(*sums, mid, ext, probs, chosen, cot, gain, router)


def norm_one_back_kernel(a_ref, b_ref, c_ref, x_ref, mid_grad_ref, g_ref, o_ref, gain_ref):
    u = a_ref[...].astype(F32) + b_ref[...].astype(F32) + c_ref[...].astype(F32)
    x = x_ref[...].astype(F32)
    r = lax.rsqrt(jnp.mean(x * x, -1, keepdims=True) + EPSILON)
    hat = x * r
    gain_ref[...] = jnp.sum(u * hat, 0, keepdims=True)
    w = u * g_ref[...]
    o_ref[...] = (mid_grad_ref[...] + r * (w - hat * jnp.mean(w * hat, -1, keepdims=True))).astype(BF16)


def norm_one_back(sums, x, mid_grad, gain):
    t, d = x.shape
    return call(
        norm_one_back_kernel,
        "norm_one_back",
        (1,),
        [fixed((t, d))] * 5 + [fixed((1, d))],
        [fixed((t, d)), fixed((1, d))],
        [sds((t, d), BF16), sds((1, d), F32)],
        20 * t * d,
        14 * t * d,
    )(*sums, x, mid_grad, gain)


def expert_kernel(first_ref, *refs, parts):
    xs, cs, w_ref = refs[:parts], refs[parts : 2 * parts], refs[2 * parts]
    hid_ref, dgu_ref, dg_ref = refs[2 * parts + 1 :]
    e = pl.program_id(0)
    t = cs[0].shape[0]
    d = cs[0].shape[1]

    @pl.when(e == 0)
    def _():
        dg_ref[...] = jnp.zeros_like(dg_ref)

    f = w_ref.shape[4]
    me = first_ref[0] + e
    lane = lax.broadcasted_iota(jnp.int32, (t, LANES), 1)
    for part, (x_ref, c_ref) in enumerate(zip(xs, cs)):

        def block(x_ref=x_ref, c_ref=c_ref, to=slice(part * t, (part + 1) * t)):
            x = x_ref[:, :d]
            a = nn(x, w_ref[:, 0, 0].reshape(d, f))
            b = nn(x, w_ref[:, 0, 1].reshape(d, f))
            dh = nn(c_ref[...], w_ref[:, 0, 2].reshape(d, f))
            mine = (lane == me) | (lane == me + LANES // 2)
            gate = jnp.sum(jnp.where(mine, x_ref[:, d:].astype(F32), 0.0), -1, keepdims=True)
            sigma = jax.nn.sigmoid(a)
            swish = a * sigma
            act = swish * b
            hid_ref[to, :] = (gate * act).astype(BF16)
            d_gate = jnp.sum(dh * act, -1, keepdims=True)
            dg_ref[to, :] += jnp.where(lane == me, d_gate, 0.0)
            inner = dh * gate
            dgu_ref[to, :f] = (inner * b * sigma * (1.0 + a * (1.0 - sigma))).astype(BF16)
            dgu_ref[to, f:] = (inner * swish).astype(BF16)

        block()


def expert_up(first, xs, cs, w):
    t, d = cs[0].shape
    parts = len(cs)
    p, e, _, ds, f = w.shape
    every = parts * t
    return call(
        functools.partial(expert_kernel, parts=parts),
        "expert_up",
        (e,),
        [fixed(x.shape) for x in xs]
        + [fixed((t, d))] * parts
        + [pl.BlockSpec((p, 1, 3, ds, f), lambda i, *_: (0, i, 0, 0, 0))],
        [
            pl.BlockSpec((every, f), lambda i, *_: (0, i)),
            pl.BlockSpec((every, 2 * f), lambda i, *_: (0, i)),
            pl.BlockSpec((every, LANES), lambda i, *_: (0, 0)),
        ],
        [sds((every, e * f), BF16), sds((every, e * 2 * f), BF16), sds((every, LANES), F32)],
        6 * every * d * f * e,
        2 * (3 * d * f * e + 2 * every * d + 3 * every * f * e),
        prefetch=1,
    )(first, *xs, *cs, w)


def expert_grad_kernel(col_ref, *refs, parts, groups, sides):
    xs, cs = refs[:parts], refs[parts : 2 * parts]
    hids, dgus = refs[2 * parts : 2 * parts + groups], refs[2 * parts + groups : 2 * parts + 2 * groups]
    outs = refs[2 * parts + 2 * groups :]
    pb, e, _, ds, f = outs[0].shape
    x = jnp.concatenate([r[...] for r in xs], 0)
    c = jnp.concatenate([r[...] for r in cs], 0)
    share = x.shape[0] // groups
    step = pl.program_id(0)
    each = pl.num_programs(0) // sides

    def product(left, refs):
        return sum(tn(left[g * share : (g + 1) * share], r[...]) for g, r in enumerate(refs)).astype(BF16)

    both = product(x, dgus)
    down = product(c, hids)
    for side, o in enumerate(outs):

        @pl.when(step // each == side)
        def _():
            for i in range(e):
                o[:, i, 0] = both[:, 2 * i * f : (2 * i + 1) * f].reshape(pb, ds, f)
                o[:, i, 1] = both[:, (2 * i + 1) * f : (2 * i + 2) * f].reshape(pb, ds, f)
                o[:, i, 2] = down[:, i * f : (i + 1) * f].reshape(pb, ds, f)


def expert_grads(columns, xs, cs, hids, dgus, p, e, sides):
    t, d = cs[0].shape
    parts = len(cs)
    groups = len(hids)
    ds = d // p
    f = hids[0].shape[1] // e
    pb = max(1, TILE // ds)
    steps = p // pb
    each = steps // sides
    column = pl.BlockSpec((t, pb * ds), lambda g, col: (0, col[g]))

    def out(side):
        return pl.BlockSpec(
            (pb, e, 3, ds, f), lambda g, col: (jnp.clip(g - side * each, 0, each - 1), 0, 0, 0, 0)
        )

    return call(
        functools.partial(expert_grad_kernel, parts=parts, groups=groups, sides=sides),
        "expert_grad",
        (steps,),
        [column] * (2 * parts) + [fixed(h.shape) for h in hids] + [fixed(g.shape) for g in dgus],
        [out(side) for side in range(sides)],
        [sds((p // sides, e, 3, ds, f), BF16)] * sides,
        6 * parts * t * d * f * e,
        2 * (3 * d * f * e + 2 * parts * t * d + 3 * parts * t * f * e),
        prefetch=1,
    )(columns, *xs, *cs, *hids, *dgus)


def settle_kernel(spot_ref, *refs, pieces):
    gate_up_ref, down_ref = refs[-2:]
    each = pl.num_programs(0) // pieces
    for r in range(pieces):

        @pl.when(pl.program_id(0) // each == r)
        def _():
            gate_up_ref[...] = refs[r][:, :2].astype(F32)
            down_ref[...] = refs[r][:, 2].astype(F32)


def settle(spots, pieces, kept, experts):
    e, _, ds, f = pieces[0].shape
    count = len(pieces)
    each = e // 2

    def piece(r):
        return pl.BlockSpec((2, 3, ds, f), lambda g, spot: (jnp.clip(g - r * each, 0, each - 1), 0, 0, 0))

    return call(
        functools.partial(settle_kernel, pieces=count),
        "settle",
        (count * each,),
        [piece(r) for r in range(count)] + [pl.BlockSpec(memory_space=pl.ANY)] * len(kept),
        [
            pl.BlockSpec((2, 2, ds, f), lambda g, spot: (spot[g], 0, 0, 0)),
            pl.BlockSpec((2, ds, f), lambda g, spot: (spot[g], 0, 0)),
        ],
        [sds((experts, 2, ds, f), F32), sds((experts, ds, f), F32)],
        0,
        18 * count * e * ds * f,
        prefetch=1,
        aliases={1 + count + i: i for i in range(len(kept))},
    )(spots, *pieces, *kept)


def down_kernel(*refs, planes, chunks, sides, begun):
    acts, ws = refs[:chunks], refs[chunks : 2 * chunks]
    gates = refs[2 * chunks : 2 * chunks + sides]
    before = refs[2 * chunks + sides : 2 * chunks + sides + begun]
    outs = refs[2 * chunks + sides + begun :]
    g = pl.program_id(0)
    pb, _, _, ds, f = ws[0].shape
    wide = pb * ds
    rows = outs[0].shape[0]
    joined = [
        jnp.concatenate([w[:, i, c].reshape(wide, f) for i in range(w.shape[1]) for c in range(planes)], 1)
        for w in ws
    ]
    to = pl.ds(pl.multiple_of(g * wide, wide), wide)
    for part, o in enumerate(outs):
        own = slice(part * rows, (part + 1) * rows)
        value = sum(nt(a[own, :], w) for a, w in zip(acts, joined))
        if begun:
            value += before[part][...].astype(F32)
        o[:, to] = value.astype(BF16)
    if sides:

        @pl.when(g == 0)
        def _():
            for part, o in enumerate(outs):
                own = slice(part * rows, (part + 1) * rows)
                o[:, o.shape[1] - LANES :] = sum(s[own, :] for s in gates).astype(BF16)


def expert_down(acts, ws, plane, planes, gates, before, parts, name):
    every = acts[0].shape[0]
    p, _, _, ds, f = ws[0].shape
    k = sum(a.shape[1] for a in acts)
    t = every // parts
    chunks = len(acts)
    d = p * ds + (LANES if gates else 0)
    pb = max(1, 2 * TILE // ds)
    return call(
        functools.partial(down_kernel, planes=planes, chunks=chunks, sides=len(gates), begun=len(before)),
        name,
        (p // pb,),
        [fixed(a.shape) for a in acts]
        + [pl.BlockSpec((pb, w.shape[1], planes, ds, f), lambda g: (g, 0, plane, 0, 0)) for w in ws]
        + [fixed((every, LANES))] * len(gates)
        + [pl.BlockSpec((t, pb * ds), lambda g: (0, g))] * len(before),
        [pl.BlockSpec((t, d), lambda g: (0, 0))] * parts,
        [sds((t, d), BF16)] * parts,
        2 * every * k * p * ds,
        2 * (every * k + k * p * ds) + 2 * every * d,
    )(*acts, *ws, *gates, *before)


def unturn_kernel(dq_ref, dk_ref, raw_ref, s_ref, g_ref, cos_ref, sin_ref, u_ref, in_ref, gg_ref):
    h = pl.program_id(0)
    reps = raw_ref.shape[1] // cos_ref.shape[0]
    cosine = jnp.concatenate([cos_ref[...]] * reps, 0)
    sine = jnp.concatenate([sin_ref[...]] * reps, 0)
    for i, grad in enumerate((dq_ref[...], dk_ref[...])):
        u = turn(grad, cosine, -sine)
        hat = raw_ref[i] * s_ref[i]
        product = u * hat
        u_ref[i] = u
        gg_ref[i] = jnp.sum(product, 0, keepdims=True)
        row = jnp.broadcast_to(jnp.sum(product * g_ref[i], -1, keepdims=True), in_ref.shape[1:])

        @pl.when(h == 0)
        def _():
            in_ref[i] = row

        @pl.when(h != 0)
        def _():
            in_ref[i] += row


def unturn(dq, dk, raw, scales, gains, cosine, sine):
    _, t, n = raw.shape
    h = HEAD_DIM
    length = cosine.shape[0]
    column = pl.BlockSpec((t, h), lambda i: (0, i))
    pair = pl.BlockSpec((2, t, h), lambda i: (0, 0, i))
    return call(
        unturn_kernel,
        "unturn",
        (n // h,),
        [
            column,
            column,
            pair,
            fixed((2, t, 1)),
            pl.BlockSpec((2, 1, h), lambda i: (0, 0, i)),
            fixed((length, h)),
            fixed((length, h)),
        ],
        [
            pair,
            pl.BlockSpec((2, t, 128), lambda i: (0, 0, 0)),
            pl.BlockSpec((2, 1, h), lambda i: (0, 0, i)),
        ],
        [sds((2, t, n), F32), sds((2, t, 128), F32), sds((2, 1, n), F32)],
        30 * t * n,
        24 * t * n,
    )(dq, dk, raw, scales, gains, cosine, sine)


def raw_back_kernel(place_ref, u_ref, raw_ref, s_ref, in_ref, g_ref, dv_ref, w_ref, d_ref, *outs):
    t, n = dv_ref.shape

    @pl.when(pl.program_id(0) == 0)
    def _():
        for i in range(2):
            hat = raw_ref[i] * s_ref[i]
            d_ref[:, i * n : (i + 1) * n] = (
                s_ref[i] * (u_ref[i] * g_ref[i] - hat * in_ref[i])
            ).astype(BF16)
        d_ref[:, 2 * n :] = dv_ref[...]

    pb, _, ds, _ = w_ref.shape
    w = jnp.concatenate([w_ref[:, c].reshape(pb * ds, n) for c in range(3)], 1)
    y = nt(d_ref[...], w).astype(BF16)
    rows = outs[0].shape[0]
    outs[0][...] = y[:rows]
    for r, o in enumerate(outs):
        for q in range(len(outs)):

            @pl.when(place_ref[r] == q * rows)
            def _():
                o[...] = y[q * rows : (q + 1) * rows]


def raw_back(places, u, raw, scales, inner, gains, dv, w, pieces):
    t, n = dv.shape
    p, _, ds, _ = w.shape
    d = p * ds
    pb = max(1, 2 * TILE // ds)
    return call(
        raw_back_kernel,
        "raw_back",
        (p // pb,),
        [
            fixed((2, t, n)),
            fixed((2, t, n)),
            fixed((2, t, 1)),
            fixed((2, t, 1)),
            fixed((2, 1, n)),
            fixed((t, n)),
            pl.BlockSpec((pb, 3, ds, n), lambda g, *_: (g, 0, 0, 0)),
        ],
        [pl.BlockSpec((t, 3 * n), lambda g, *_: (0, 0))]
        + [pl.BlockSpec((t // pieces, pb * ds), lambda g, *_: (0, g))] * pieces,
        [sds((t, 3 * n), BF16)] + [sds((t // pieces, d), BF16)] * pieces,
        6 * t * d * n,
        2 * (3 * d * n + t * d) + 20 * t * n,
        prefetch=1,
    )(places, u, raw, scales, inner, gains, dv, w)


def qkv_grad_kernel(n_ref, d_ref, o_ref):
    pb, _, ds, n = o_ref.shape
    grads = tn(n_ref[...], d_ref[...]).astype(BF16)
    for c in range(3):
        o_ref[:, c] = grads[:, c * n : (c + 1) * n].reshape(pb, ds, n)


def qkv_grads(normed, grad, p):
    t, d = normed.shape
    n = grad.shape[1] // 3
    ds = d // p
    pb = max(1, TILE // ds)
    return call(
        qkv_grad_kernel,
        "qkv_grad",
        (p // pb,),
        [pl.BlockSpec((t, pb * ds), lambda g: (0, g)), fixed((t, 3 * n))],
        pl.BlockSpec((pb, 3, ds, n), lambda g: (g, 0, 0, 0)),
        sds((p, 3, ds, n), BF16),
        6 * t * d * n,
        2 * (3 * d * n + t * d + 3 * t * n),
    )(normed, grad)


def swap(value, axis):
    return lax.ppermute(value, axis, [(0, 1), (1, 0)])


def spread(value):
    rows = swap(value, "row")
    return (value, swap(value, "core"), rows, swap(rows, "core"))


def across(value, k):
    size = lax.axis_size("tp")
    return lax.ppermute(value, "tp", [(i, i ^ k) for i in range(size)])


def total(pieces):
    return sum(v.astype(F32) for v in pieces)


def add(*values):
    return total(values).astype(values[0].dtype)


def cut(value, pieces):
    rows = value.shape[0] // pieces
    return [value[r * rows : (r + 1) * rows] for r in range(pieces)]


def join(*pieces):
    return jnp.concatenate(pieces, 0)


class Crossing:
    def __init__(self, first, second):
        self.one, self.two = first, second
        self.far = swap(first[3], "row"), swap(second[3], "fsdp")
        self.near = swap(first[1], "row"), swap(second[2], "fsdp")

    def half(self, line):
        sums = line(
            lambda a, b, c, d, e, f, g, h: (add(a, b), add(c, d), add(e, f), add(g, h)),
            self.one[2],
            self.far[0],
            self.two[1],
            self.far[1],
            self.one[0],
            self.near[0],
            self.two[0],
            self.near[1],
        )
        self.last = swap(sums[0], "fsdp"), swap(sums[1], "row")
        self.kept = sums[2:]

    def done(self, line):
        return line(lambda a, b, c, d: (add(a, b), add(c, d)), self.kept[0], self.last[0], self.kept[1], self.last[1])


class Line:
    def __init__(self):
        self.last = None

    def __call__(self, step, *operands):
        leaves, form = jax.tree.flatten(operands)
        spots = [i for i, v in enumerate(leaves) if isinstance(v, jax.Array)]
        if self.last is not None:
            kept, self.last = lax.optimization_barrier(([leaves[i] for i in spots], self.last))
            for i, v in zip(spots, kept):
                leaves[i] = v
        result = step(*jax.tree.unflatten(form, leaves))
        self.last = min(jax.tree.leaves(result), key=lambda v: v.size)
        return result

    def sums(self, own, core, pieces, first=None):
        mine, theirs = cut(own, pieces), cut(swap(core, "core"), pieces)
        last = across(self(add, mine[3], theirs[3]), 1)
        near = self(add, mine[2], theirs[2], last)
        beside, first = self(lambda a, b, c, d: (add(a, b), add(c, d)), mine[1], theirs[1], mine[0], theirs[0])
        return [first, across(beside, 1), across(near, 2)]


def in_place_kernel(place_ref, *refs):
    for r, piece in enumerate(refs[:-1]):

        @pl.when(pl.program_id(0) == r)
        def _():
            refs[-1][...] = piece[...]


def in_place(pieces, places):
    rows, d = pieces[0].shape
    count = len(pieces)
    return call(
        in_place_kernel,
        "inplace",
        (count,),
        [fixed((rows, d))] * count,
        pl.BlockSpec((rows, d), lambda r, place: (place[r] // rows, 0)),
        sds((rows * count, d), pieces[0].dtype),
        0,
        4 * rows * count * d,
        prefetch=1,
    )(places, *pieces)


def meet(value):
    value = value + across(value, 1)
    return value + across(value, 2)


def relative(value, places, pieces):
    rows = value.shape[0] // pieces
    return [lax.dynamic_slice_in_dim(value, places[r], rows, 0) for r in range(pieces)]


def body(
    inputs,
    prefix,
    expert_ids,
    norm_gains,
    qkv_weight,
    out_weight,
    router_weight,
    gate_up_weight,
    down_weight,
    cotangent,
    *,
    chunks,
):
    sequences, length, width = inputs.shape
    t = sequences * length
    tp = lax.axis_size("tp")
    quarter = t // tp
    column = lax.axis_index("tp")
    core = lax.axis_index("core")
    ctx = lax.axis_index("row") * 2 + core
    experts = router_weight.shape[1]
    group = experts // 2
    starts = [sum(chunks[:k]) for k in range(len(chunks))]
    x = inputs.reshape(t, width)
    places = jnp.stack([column ^ r for r in range(tp)]).astype(jnp.int32) * quarter
    x_q = lax.dynamic_slice_in_dim(x, column * quarter, quarter, 0)

    line = Line()
    attn_local = jnp.concatenate([qkv_weight, out_weight[None]], 0)
    attn_w = lax.all_gather(attn_local, PLANE, axis=0, tiled=False)
    triple = jnp.concatenate([gate_up_weight, down_weight[:, None]], 1)
    ds, f = triple.shape[2:]
    grouped = triple.reshape(2, group, 3, ds, f)
    ws = []
    for begin, e in zip(starts, chunks):
        mine = lax.all_to_all(grouped[:, begin : begin + e], "core", 0, 0, tiled=True)
        ws.append(lax.all_gather(mine, FR, axis=0, tiled=False).reshape(-1, e, 3, ds, f))
    gains_low = lax.all_gather(norm_gains, PLANE, axis=1, tiled=True)
    router = lax.all_gather(router_weight, PLANE, axis=0, tiled=True)
    cots = relative(cotangent.reshape(t, width), places, tp)
    c0 = join(*cots)
    c1 = swap(c0, "core")
    attn_w, gains_low, router, c0 = lax.optimization_barrier((attn_w, gains_low, router, c0))
    p = attn_w.shape[0]

    gains = gains_low.astype(F32)
    n = attn_w.shape[3]
    router_rows = jnp.concatenate([router.T, jnp.zeros((128 - experts, width), BF16)], 0)

    own_gains = lax.dynamic_slice_in_dim(gains[2:4], column * n, n, 1)[:, None, :]
    halves = jnp.arange(0, HEAD_DIM, 2).astype(F32) / HEAD_DIM
    inverse = 1.0 / THETA**halves
    positions = ctx * length + jnp.arange(length, dtype=jnp.int32)
    angles = positions.astype(F32)[:, None] * inverse[None, :]
    cosine = jnp.concatenate([jnp.cos(angles)] * 2, 1)
    sine = jnp.concatenate([-jnp.sin(angles), jnp.sin(angles)], 1)
    offsets = jnp.stack([ctx, ctx ^ 1, ctx ^ 2, ctx ^ 3, ctx]).astype(jnp.int32) * length
    scal = jnp.concatenate([offsets, prefix.astype(jnp.int32)])
    ids_q = lax.dynamic_slice_in_dim(expert_ids.reshape(t, -1), column * quarter, quarter, 0)
    normed_one, raw, values, squares = line(qkv_project, x, gains[0:1], attn_w)
    v_blocks = spread(values)
    scales = lax.rsqrt(meet(squares[:, :, 0]) / width + EPSILON)[:, :, None]
    queries, keys = line(prepare, raw, scales, own_gains, cosine, sine)
    k_blocks = spread(keys)
    blocks = k_blocks + v_blocks
    heads = line(attend, scal, queries, blocks, length)
    sums = line(project_out, places, heads, attn_w, tp)
    near = line(add, sums[2], across(sums[3], 1))
    sums = [sums[0], across(sums[1], 1), across(near, 2)]
    mid, ext, probs, chosen = line(norm_two, x_q, sums, gains[1:2], router_rows, ids_q, experts)
    far = across(ext, 2)
    near = across(ext, 1)
    x0 = line(join, ext, near, far, across(far, 1))
    x1 = swap(x0, "core")

    xs, cs = [x0, x1], [c0, c1]
    blocks_in = jnp.arange(width // TILE, dtype=jnp.int32)
    square = lax.axis_size("fsdp") == 2 and lax.axis_size("row") == 2
    chip = lax.axis_index("fsdp") * 2 + lax.axis_index("row")
    by_chip = blocks_in
    if square:
        share = width // TILE // 8
        chips, cores, inner = jnp.meshgrid(jnp.arange(4), jnp.arange(2), jnp.arange(share), indexing="ij")
        by_chip = (((chips ^ chip) * 2 + cores) * share + inner).reshape(-1).astype(jnp.int32)
    hid, dgu, side, grads = [], [], [], []
    dx = []

    def up(k):
        first = (core * group + starts[k]).astype(jnp.int32)[None]
        for kept, made in zip((hid, dgu, side), line(expert_up, first, xs, cs, ws[k])):
            kept.append(made)

    def back(k, before):
        gates = side if k == len(chunks) - 1 else []
        return line(expert_down, [dgu[k]], [ws[k]], 0, 2, gates, before, 2, "expert_dx")

    def weight_grad(k, relative_chips):
        sides = 4 if relative_chips else 1
        columns = by_chip if relative_chips else blocks_in
        made = line(expert_grads, columns, xs, cs, [hid[k]], [dgu[k]], p, chunks[k], sides)
        if relative_chips:
            return made
        made = made[0].reshape(-1, 2, chunks[k], 3, ds, f)
        return lax.optimization_barrier(lax.psum_scatter(made, FR, scatter_dimension=0, tiled=False))

    for k in range(len(chunks)):
        up(k)
        dx = back(k, dx)
        if k < len(chunks) - 1:
            grads.append(weight_grad(k, False))
    d_normed = line.sums(*dx, tp)
    moe = line(expert_down, hid, ws, 2, 1, [], [], 2, "expert_out")
    tail = weight_grad(len(chunks) - 1, square)
    if square:
        middle = chunks[-1] // 2
        tail = Crossing([v[:, :middle] for v in tail], [v[:, middle:] for v in tail])

    d_mid, d_mid_low, gain_two, grad_router = line(
        norm_two_back, d_normed, mid, ext, probs, chosen, cots[0], gains[1:2], router_rows
    )
    far = across(d_mid_low, 2)
    near = across(d_mid_low, 1)
    d_mid_low = line(join, d_mid_low, near, far, across(far, 1))
    own, beside = cut(moe[0], tp), cut(swap(moe[1], "core"), tp)
    last = across(line(add, own[3], beside[3]), 1)

    d_heads = line(heads_grad, places, d_mid_low, attn_w, tp)
    near = line(add, own[2], beside[2], last)
    next_one = line(add, own[1], beside[1])
    moe = [across(next_one, 1), across(near, 2)]
    dq, b0, b1, b2, b3 = line(attend_back, scal, queries, blocks, d_heads, length)
    r1 = swap(b1, "core")
    r2 = swap(line(add, b2, swap(b3, "core")), "row")
    out = line(lambda *v: total(v).astype(BF16), mid, own[0], beside[0], *moe)
    out_far = across(out, 2)
    out_near = across(out, 1)
    grad_out = line(out_weight_grad, places, d_mid_low, heads, p, tp)
    d_kv = line(lambda *v: total(v), b0, r1, r2)
    u, inner, gain_qk = line(unturn, dq, d_kv[0], raw, scales, own_gains, cosine, sine)
    grad_out, grads[0], u = lax.optimization_barrier((grad_out, grads[0], u))
    grad_out = lax.psum_scatter(grad_out, PLANE, scatter_dimension=0, tiled=False)
    if square:
        tail.half(line)

    def parted(k):
        own, other = line(
            lambda v: [lax.dynamic_index_in_dim(v, c, 0, keepdims=False) for c in (core, core ^ 1)], grads[k]
        )
        return own, swap(other, "core")

    def settled(k, pair, kept):
        steps = jnp.arange(chunks[k] // 2, dtype=jnp.int32)
        spots = jnp.concatenate([(c * group + starts[k]) // 2 + steps for c in (core, core ^ 1)])
        return line(settle, spots.astype(jnp.int32), pair, kept, experts)

    pairs = [parted(0)]
    inner = (meet(inner[:, :, 0]) / width)[:, :, None]
    out_both = across(out_far, 1)
    outputs = line(in_place, [out, out_near, out_far, out_both], places).reshape(inputs.shape)
    d_raw, *d_one = line(
        raw_back, places, u, raw, scales, inner, own_gains, d_kv[1].astype(BF16), attn_w, tp
    )
    last = across(d_one[3], 1)
    near = line(add, d_one[2], last)
    d_one = [d_one[0], across(d_one[1], 1), across(near, 2)]
    grad_qkv = line(qkv_grads, normed_one, d_raw, p)
    grad_in, gain_one = line(norm_one_back, d_one, x_q, d_mid, gains[0:1])
    far = across(grad_in, 2)
    near = across(grad_in, 1)
    grad_qkv, gain_one = lax.optimization_barrier((grad_qkv, gain_one))
    grad_qkv = lax.psum_scatter(grad_qkv, PLANE, scatter_dimension=0, tiled=False)
    placed = lax.dynamic_update_slice_in_dim(
        jnp.zeros((2, width), F32), gain_qk[:, 0, :], column * n, 1
    )

    small = line(lambda *v: jnp.concatenate(v, 0), grad_router[:experts], gain_one, gain_two, placed)
    rows = small.shape[0]
    small = small.reshape(rows, p, ds).transpose(1, 0, 2)
    small = jnp.sum(lax.all_to_all(small, PLANE, 0, 0, tiled=True), 0)
    other = across(small, 1)
    both = across(far, 1)
    kept = settled(0, pairs[0], [])
    grads.append(jnp.concatenate(tail.done(line), 1) if square else tail)
    pairs.append(parted(1))
    owned_gate_up, owned_down = settled(1, pairs[1], kept)
    small = line(lambda a, b: a + b, small, other)
    other = across(small, 2)
    grad_inputs = line(in_place, [grad_in, near, far, both], places).reshape(inputs.shape)
    small = line(lambda a, b: a + b, small, other)
    owned_gains = small[experts:]
    owned_router = small[:experts].T
    return (
        outputs,
        grad_inputs,
        owned_gains,
        grad_qkv.astype(F32),
        grad_out.astype(F32),
        owned_router,
        owned_gate_up,
        owned_down,
    )


def solution(mesh):
    fsdp, ctx, tp = (mesh.shape[a] for a in ("fsdp", "ctx", "tp"))
    fine = Mesh(mesh.devices.reshape(fsdp, ctx // 2, 2, tp), EVERY)
    tokens = P("fsdp", ("row", "core"), None)
    weights = (
        P(None, PLANE),
        P(None, PLANE, "tp"),
        P(PLANE, "tp"),
        P(PLANE, None),
        P(None, None, PLANE, "tp"),
        P(None, PLANE, "tp"),
    )
    return jax.shard_map(
        functools.partial(body, chunks=(6, 2)),
        mesh=fine,
        in_specs=(tokens, P("fsdp"), tokens) + weights + (tokens,),
        out_specs=(tokens, tokens) + weights,
        check_vma=False,
    )
```

time: 765 us -> 739 us (0.966)
  waiting for transfers between devices: 357 us -> 312 us
  Pallas kernels: 220 us -> 244 us
  local copies, waits for them, and re-layouts: 26.9 us -> 43.4 us
  blocking collectives: 50.1 us -> 34.2 us
    all_gather x2, waiting for transfers between devices: 47 us -> 15.2 us  [body(): lax.all_gather(mine, FR, axis=0, tiled=False).reshape(-1, e, 3, ds, f)]
    pallas_call x9 -> x14, Pallas kernels: 147 us -> 174 us  [the longest x2 45.1 us: expert_grads(): call(functools.partial(expert_grad_kernel, parts=parts, groups=groups, si...]
    all_to_all x4 -> x2, blocking collectives: 30.3 us -> 14.5 us  [body(): mine = lax.all_to_all(grouped[:, begin:begin + e], 'core', 0, 0, tiled=True)]
    ppermute x33 -> x30, starting transfers between devices: 34.6 us -> 24 us  [across(): return lax.ppermute(value, 'tp', [(i, i ^ k) for i in range(size)])]
    ppermute x15 -> x21, waiting for transfers between devices: 73.7 us -> 63.4 us  [swap(): return lax.ppermute(value, axis, [(0, 1), (1, 0)])]
    convert_element_type x13 -> x19, other arithmetic: 13.8 us -> 22.4 us  [the longest x16 17.7 us: add(): return total(values).astype(values[0].dtype)]
    ppermute x33 -> x30, waiting for transfers between devices: 216 us -> 212 us  [across(): return lax.ppermute(value, 'tp', [(i, i ^ k) for i in range(size)])]
  transfers between devices with their start and end apart: 55 -> 58, of which waited for: 30 -> 33; matrix products, arithmetic and copies ran while one was open for 7% -> 9% of each run, Pallas kernels for 29% -> 33%
where the time goes in v2:
time: 739 us; the launch traced here: 730 us
  waiting for transfers between devices  312 us (42%)
  Pallas kernels  244 us (33%)
  local copies, waits for them, and re-layouts  43.4 us (6%)
  starting transfers between devices  38.4 us (5%)
  other arithmetic  34.5 us (5%)
  blocking collectives  34.2 us (5%)
  between operations  23.1 us (3%)
    ppermute x30, waiting for transfers between devices, across(): return lax.ppermute(value, 'tp', [(i, i ^ k) for i in range(size)])  212 us
    ppermute x21, waiting for transfers between devices, swap(): return lax.ppermute(value, axis, [(0, 1), (1, 0)])  63.4 us
    pallas_call x2, Pallas kernels, expert_grads(): call(functools.partial(expert_grad_kernel, parts=parts, groups=groups, si...  45.1 us
    pallas_call x3, Pallas kernels, expert_down(): call(functools.partial(down_kernel, planes=planes, chunks=chunks, sides=l...  43.4 us
    pallas_call x2, Pallas kernels, expert_up(): call(functools.partial(expert_kernel, parts=parts), 'expert_up', (e,), [f...  41.3 us
    ppermute x30, starting transfers between devices, across(): return lax.ppermute(value, 'tp', [(i, i ^ k) for i in range(size)])  24 us
    convert_element_type x16, other arithmetic, add(): return total(values).astype(values[0].dtype)  17.7 us
    all_gather x2, waiting for transfers between devices, body(): lax.all_gather(mine, FR, axis=0, tiled=False).reshape(-1, e, 3, ds, f)  15.2 us
  transfers between devices with their start and end apart: 58, of which 33 were waited for; matrix products, arithmetic and copies ran while one was open for 9% of the time, Pallas kernels for 33%

profile of v2, /device:TPU:0, one launch (start us, length us, event | category | flops | bytes accessed | tf_op | source)
XLA Modules:
  0.0 729.9 jit_solution(2223877316022591114)
XLA Ops:
  11.9 8.6 %all_to_all.15 = bf16[2,6,3,256,256]{4,3,2,1,0:T(8,128)(2,1)} all-to-all(bf16[2,6,3,256,256]{4,3,2,1,0:T(8,128)(2,1)S(1)} %fusion), channel_id=1, replica_groups=mesh['fsdp'=2,'row'=2,'core'=2,'tp'=4] {'core'}, dimensions={0} | all-to-all | bytes 9437184 | tf_op jit(solution)/shard_map/all_to_all | solution.py:877
  29.0 10.4 %all_gather.26 = bf16[4,2048]{1,0:T(4,128)(2,1)S(1)} all-gather(bf16[4,256]{1,0:T(4,128)(2,1)S(1)} %copy-done.37), channel_id=1, replica_groups=mesh['fsdp'=2,'row'=2,'core'=2,'tp'=4] {'fsdp','row','core'}, dimensions={1}, use_global_device_ids=true | all-gather | bytes 18432 | tf_op jit(solution)/shard_map/all_gather | solution.py:879
  39.4 9.4 %all_gather.27 = bf16[2048,16]{0,1:T(8,128)(2,1)S(1)} all-gather(bf16[256,16]{0,1:T(8,128)(2,1)S(1)} %copy-done.33), channel_id=1, replica_groups=mesh['fsdp'=2,'row'=2,'core'=2,'tp'=4] {'fsdp','row','core'}, dimensions={0}, use_global_device_ids=true | all-gather | bytes 73728 | tf_op jit(solution)/shard_map/all_gather | solution.py:880
  53.1 14.6 %all-gather.7.cloned.1.call-done = bf16[32,256,512]{2,1,0:T(8,128)(2,1)} async-done(((bf16[4,256,512]{2,1,0:T(8,128)(2,1)}), bf16[32,256,512]{2,1,0:T(8,128)(2,1)}) %all-gather.7.cloned.1.call-update) | async-done | bytes 8388624 | tf_op jit(solution)/shard_map/all_gather | solution.py:871
  68.4 10.4 %qkv.1 = (bf16[512,2048]{1,0:T(8,128)(2,1)}, f32[2,512,512]{2,1,0:T(8,128)}, bf16[512,512]{1,0:T(8,128)(2,1)}, f32[2,512,128]{2,1,0:T(8,128)}) custom-call(bf16[512,2048]{1,0:T(8,128)(2,1)} %bitcast.79, f32[1,2048]{1,0:T(1,128)} %get-tuple-element.471.g_ref, bf16[8,4,256,512]{3,2,1,0:T(8,128)(2,1)} %bitcast.61), custom_call_target="tpu_custom_call" | custom-call | flops 3221225472 | bytes 13107200 | tf_op jit(solution)/shard_map/qkv/pallas_call | solution.py:87
  95.7 17.4 %collective-permute-done.6.refs_6_ = bf16[512,512]{1,0:T(8,128)(2,1)S(1)} collective-permute-done((bf16[512,512]{1,0:T(8,128)(2,1)}, bf16[512,512]{1,0:T(8,128)(2,1)S(1)}, u32[]{:S(2)}, u32[]{:S(2)}) %collective-permute-start.6) | collective-permute-done | bytes 524320 | tf_op jit(solution)/shard_map/ppermute | solution.py:729
  113.1 21.9 %collective-permute-done.3.refs_2_ = bf16[512,512]{1,0:T(8,128)(2,1)} collective-permute-done((bf16[512,512]{1,0:T(8,128)(2,1)}, bf16[512,512]{1,0:T(8,128)(2,1)}, u32[]{:S(2)}, u32[]{:S(2)}) %collective-permute-start.3) | collective-permute-done | bytes 524320 | tf_op jit(solution)/shard_map/ppermute | solution.py:729
  137.2 9.9 %attend.1.h_ref = bf16[512,512]{1,0:T(8,128)(2,1)} custom-call(s32[7]{0:T(128)} %pad_add_fusion.scal_ref, bf16[512,512]{1,0:T(8,128)(2,1)} %get-tuple-element.396.q_ref, bf16[512,512]{1,0:T(8,128)(2,1)} %get-tuple-element.397.refs_0_, bf16[512,512]{1,0:T(8,128)(2,1)} %collective-permute-done.2.refs_1_, bf16[512,512]{1,0:T(8,128)(2,1)} %collective-permute-done.3.refs_2_, ...), custom_call_target="tpu_custom_call" | custom-call | flops 1073741824 | bytes 6291456 | tf_op jit(solution)/shard_map/attend/pallas_call | solution.py:171
  147.1 5.4 outproj.1
  154.6 13.0 %collective-permute-done.9 = bf16[128,2048]{1,0:T(8,128)(2,1)S(1)} collective-permute-done((bf16[128,2048]{1,0:T(8,128)(2,1)}, bf16[128,2048]{1,0:T(8,128)(2,1)S(1)}, u32[]{:S(2)}, u32[]{:S(2)}) %collective-permute-start.9) | collective-permute-done | bytes 524320 | tf_op jit(solution)/shard_map/ppermute | solution.py:739
  172.9 11.9 %collective-permute-done.8.b_ref = bf16[128,2048]{1,0:T(8,128)(2,1)S(1)} collective-permute-done((bf16[128,2048]{1,0:T(8,128)(2,1)}, bf16[128,2048]{1,0:T(8,128)(2,1)S(1)}, u32[]{:S(2)}, u32[]{:S(2)}) %collective-permute-start.8) | collective-permute-done | bytes 524320 | tf_op jit(solution)/shard_map/ppermute | solution.py:739
  184.8 8.7 %collective-permute-done.10.c_ref = bf16[128,2048]{1,0:T(8,128)(2,1)} collective-permute-done((bf16[128,2048]{1,0:T(8,128)(2,1)S(1)}, bf16[128,2048]{1,0:T(8,128)(2,1)}, u32[]{:S(2)}, u32[]{:S(2)}) %collective-permute-start.10) | collective-permute-done | bytes 524320 | tf_op jit(solution)/shard_map/ppermute | solution.py:739
  197.1 5.9 all_to_all.16
  205.1 14.4 %collective-permute-done.12 = bf16[128,2176]{1,0:T(8,128)(2,1)S(1)} collective-permute-done((bf16[128,2176]{1,0:T(8,128)(2,1)}, bf16[128,2176]{1,0:T(8,128)(2,1)S(1)}, u32[]{:S(2)}, u32[]{:S(2)}) %collective-permute-start.12) | collective-permute-done | bytes 557088 | tf_op jit(solution)/shard_map/ppermute | solution.py:739
  219.6 11.1 %collective-permute-done.11 = bf16[128,2176]{1,0:T(8,128)(2,1)S(1)} collective-permute-done((bf16[128,2176]{1,0:T(8,128)(2,1)S(1)}, bf16[128,2176]{1,0:T(8,128)(2,1)S(1)}, u32[]{:S(2)}, u32[]{:S(2)}) %collective-permute-start.11) | collective-permute-done | bytes 557088 | tf_op jit(solution)/shard_map/ppermute | solution.py:739
  230.7 11.1 %collective-permute-done.13 = bf16[128,2176]{1,0:T(8,128)(2,1)S(1)} collective-permute-done((bf16[128,2176]{1,0:T(8,128)(2,1)S(1)}, bf16[128,2176]{1,0:T(8,128)(2,1)S(1)}, u32[]{:S(2)}, u32[]{:S(2)}) %collective-permute-start.13) | collective-permute-done | bytes 557088 | tf_op jit(solution)/shard_map/ppermute | solution.py:739
  245.8 6.8 collective-permute-done.15.refs_3_
  252.9 15.2 %all-gather.9.cloned.1.call-done.refs_4_.refs_1_.refs_2_ = bf16[8,6,3,256,256]{4,3,2,1,0:T(8,128)(2,1)} async-done(((bf16[2,6,3,256,256]{4,3,2,1,0:T(8,128)(2,1)}), bf16[8,6,3,256,256]{4,3,2,1,0:T(8,128)(2,1)}) %all-gather.9.cloned.1.call-update) | async-done | bytes 18874384 | tf_op jit(solution)/shard_map/all_gather | solution.py:878
  268.1 28.1 %expert_up.2 = (bf16[1024,1536]{1,0:T(8,128)(2,1)}, bf16[1024,3072]{1,0:T(8,128)(2,1)}, f32[1024,128]{1,0:T(8,128)}) custom-call(s32[1]{0:T(128)} %bitcast.19.first_ref, bf16[512,2176]{1,0:T(8,128)(2,1)} %constant_dynamic-update-slice_fusion.refs_0_, bf16[512,2176]{1,0:T(8,128)(2,1)} %collective-permute-done.14.refs_1_, ...), custom_call_target="tpu_custom_call" | custom-call | flops 19327352832 | bytes 36700160 | tf_op jit(solution)/shard_map/expert_up/pallas_call | solution.py:438
  296.2 18.9 %expert_dx.2 = (bf16[512,2048]{1,0:T(8,128)(2,1)}, bf16[512,2048]{1,0:T(8,128)(2,1)}) custom-call(bf16[1024,3072]{1,0:T(8,128)(2,1)} %get-tuple-element.326.refs_0_.refs_5_, bf16[8,6,3,256,256]{4,3,2,1,0:T(8,128)(2,1)} %all-gather.9.cloned.1.call-done.refs_4_.refs_1_.refs_2_), custom_call_target="tpu_custom_call" | custom-call | flops 12884901888 | bytes 23068672 | tf_op jit(solution)/shard_map/expert_dx/pallas_call | solution.py:585
  315.7 29.9 %expert_grad.2 = bf16[8,6,3,256,256]{4,3,2,1,0:T(8,128)(2,1)} custom-call(s32[8]{0:T(128)} %iota.27.col_ref, bf16[512,2176]{1,0:T(8,128)(2,1)} %constant_dynamic-update-slice_fusion.refs_0_, bf16[512,2176]{1,0:T(8,128)(2,1)} %collective-permute-done.14.refs_1_, bf16[512,2048]{1,0:T(8,128)(2,1)} %pad_maximum_fusion.refs_2_, ...), custom_call_target="tpu_custom_call" | custom-call | flops 19327352832 | bytes 36700160 | tf_op jit(solution)/shard_map/expert_grad/pallas_call | solution.py:499
  345.9 13.2 %expert_up.3 = (bf16[1024,512]{1,0:T(8,128)(2,1)}, bf16[1024,1024]{1,0:T(8,128)(2,1)}, f32[1024,128]{1,0:T(8,128)}) custom-call(s32[1]{0:T(128)} %bitcast.22.first_ref, bf16[512,2176]{1,0:T(8,128)(2,1)} %constant_dynamic-update-slice_fusion.refs_0_, bf16[512,2176]{1,0:T(8,128)(2,1)} %collective-permute-done.14.refs_1_, ...), custom_call_target="tpu_custom_call" | custom-call | flops 6442450944 | bytes 17825792 | tf_op jit(solution)/shard_map/expert_up/pallas_call | solution.py:438
  359.1 10.5 %expert_dx.3 = (bf16[512,2176]{1,0:T(8,128)(2,1)}, bf16[512,2176]{1,0:T(8,128)(2,1)}) custom-call(bf16[1024,1024]{1,0:T(8,128)(2,1)} %get-tuple-element.367.refs_0_.refs_5_, bf16[8,2,3,256,256]{4,3,2,1,0:T(8,128)(2,1)} %all-gather.11.cloned.1.call-done.refs_4_.refs_1_.refs_3_, f32[1024,128]{1,0:T(8,128)} %get-tuple-element.339.refs_2_, ...), custom_call_target="tpu_custom_call" | custom-call | flops 4294967296 | bytes 10747904 | tf_op jit(solution)/shard_map/expert_dx/pallas_call | solution.py:585
  377.4 12.8 %collective-permute-done.17 = bf16[128,2176]{1,0:T(8,128)(2,1)} collective-permute-done((bf16[128,2176]{1,0:T(8,128)(2,1)}, bf16[128,2176]{1,0:T(8,128)(2,1)}, u32[]{:S(2)}, u32[]{:S(2)}) %collective-permute-start.17) | collective-permute-done | bytes 557088 | tf_op jit(solution)/shard_map/ppermute | solution.py:739
  395.7 14.0 %expert_out.1 = (bf16[512,2048]{1,0:T(8,128)(2,1)}, bf16[512,2048]{1,0:T(8,128)(2,1)}) custom-call(bf16[1024,1536]{1,0:T(8,128)(2,1)} %get-tuple-element.352.refs_4_.refs_0_, bf16[1024,512]{1,0:T(8,128)(2,1)} %get-tuple-element.366.refs_1_.refs_4_, bf16[8,6,3,256,256]{4,3,2,1,0:T(8,128)(2,1)} %all-gather.9.cloned.1.call-done.refs_4_.refs_1_.refs_2_, ...), custom_call_target="tpu_custom_call" | custom-call | flops 8589934592 | bytes 16777216 | tf_op jit(solution)/shard_map/expert_out/pallas_call | solution.py:585
  410.6 15.2 %expert_grad.3 = (bf16[2,2,3,256,256]{4,3,2,1,0:T(8,128)(2,1)}, bf16[2,2,3,256,256]{4,3,2,1,0:T(8,128)(2,1)}, bf16[2,2,3,256,256]{4,3,2,1,0:T(8,128)(2,1)}, bf16[2,2,3,256,256]{4,3,2,1,0:T(8,128)(2,1)}) custom-call(s32[8]{0:T(128)} %add.210.col_ref, bf16[512,2176]{1,0:T(8,128)(2,1)} %constant_dynamic-update-slice_fusion.refs_0_, ...), custom_call_target="tpu_custom_call" | custom-call | flops 6442450944 | bytes 17825792 | tf_op jit(solution)/shard_map/expert_grad/pallas_call | solution.py:499
  426.9 4.8 norm_two_back.1
  433.0 24.9 %collective-permute-done.22 = bf16[128,2048]{1,0:T(8,128)(2,1)S(1)} collective-permute-done((bf16[128,2048]{1,0:T(8,128)(2,1)}, bf16[128,2048]{1,0:T(8,128)(2,1)S(1)}, u32[]{:S(2)}, u32[]{:S(2)}) %collective-permute-start.22) | collective-permute-done | bytes 524320 | tf_op jit(solution)/shard_map/ppermute | solution.py:739
  458.1 13.7 %collective-permute-done.23 = bf16[128,2048]{1,0:T(8,128)(2,1)S(1)} collective-permute-done((bf16[128,2048]{1,0:T(8,128)(2,1)S(1)}, bf16[128,2048]{1,0:T(8,128)(2,1)S(1)}, u32[]{:S(2)}, u32[]{:S(2)}) %collective-permute-start.23) | collective-permute-done | bytes 524320 | tf_op jit(solution)/shard_map/ppermute | solution.py:739
  473.8 5.3 dheads.1.refs_8_
  479.0 7.6 %collective-permute-done.24 = bf16[128,2048]{1,0:T(8,128)(2,1)S(1)} collective-permute-done((bf16[128,2048]{1,0:T(8,128)(2,1)S(1)}, bf16[128,2048]{1,0:T(8,128)(2,1)S(1)}, u32[]{:S(2)}, u32[]{:S(2)}) %collective-permute-start.24) | collective-permute-done | bytes 524320 | tf_op jit(solution)/shard_map/ppermute | solution.py:739
  488.7 13.4 %attend_back.1 = (f32[512,512]{1,0:T(8,128)}, bf16[2,512,512]{2,1,0:T(8,128)(2,1)}, bf16[2,512,512]{2,1,0:T(8,128)(2,1)}, bf16[2,512,512]{2,1,0:T(8,128)(2,1)}, bf16[2,512,512]{2,1,0:T(8,128)(2,1)}) custom-call(s32[7]{0:T(128)} %pad_add_fusion.scal_ref, bf16[512,512]{1,0:T(8,128)(2,1)} %get-tuple-element.396.q_ref, ...), custom_call_target="tpu_custom_call" | custom-call | flops 2684354560 | bytes 12582912 | tf_op jit(solution)/shard_map/attend_back/pallas_call | solution.py:209
  512.3 17.9 %collective-permute-done.25 = bf16[128,2048]{1,0:T(8,128)(2,1)S(1)} collective-permute-done((bf16[128,2048]{1,0:T(8,128)(2,1)}, bf16[128,2048]{1,0:T(8,128)(2,1)S(1)}, u32[]{:S(2)}, u32[]{:S(2)}) %collective-permute-start.25) | collective-permute-done | bytes 524320 | tf_op jit(solution)/shard_map/ppermute | solution.py:739
  534.0 7.6 %gradout.1 = bf16[8,256,512]{2,1,0:T(8,128)(2,1)} custom-call(s32[4]{0:T(128)} %copy-done.31, bf16[512,2048]{1,0:T(8,128)(2,1)} %copy-done.1, bf16[512,512]{1,0:T(8,128)(2,1)} %attend.1.h_ref), custom_call_target="tpu_custom_call" | custom-call | flops 1073741824 | bytes 4718592 | tf_op jit(solution)/shard_map/gradout/pallas_call | solution.py:288
  548.0 6.0 unturn.1
  558.4 7.9 %collective-permute-done.29.refs_2_ = bf16[128,2048]{1,0:T(8,128)(2,1)} collective-permute-done((bf16[128,2048]{1,0:T(8,128)(2,1)S(1)}, bf16[128,2048]{1,0:T(8,128)(2,1)}, u32[]{:S(2)}, u32[]{:S(2)}) %collective-permute-start.29) | collective-permute-done | bytes 524320 | tf_op jit(solution)/shard_map/ppermute | solution.py:739
  566.3 5.0 collective-permute-done.35
  576.7 12.0 %collective-permute-done.37 = f32[2,512]{1,0:T(2,128)S(1)} collective-permute-done((f32[2,512]{1,0:T(2,128)S(1)}, f32[2,512]{1,0:T(2,128)S(1)}, u32[]{:S(2)}, u32[]{:S(2)}) %collective-permute-start.37) | collective-permute-done | bytes 4128 | tf_op jit(solution)/shard_map/ppermute | solution.py:739
  602.8 10.9 %raw_back.1 = (bf16[512,1536]{1,0:T(8,128)(2,1)}, bf16[128,2048]{1,0:T(8,128)(2,1)}, bf16[128,2048]{1,0:T(8,128)(2,1)}, bf16[128,2048]{1,0:T(8,128)(2,1)}, bf16[128,2048]{1,0:T(8,128)(2,1)}) custom-call(s32[4]{0:T(128)} %copy-done.31, f32[2,512,512]{2,1,0:T(8,128)} %get-tuple-element.448.u_ref, f32[2,512,512]{2,1,0:T(8,128)} %get-tuple-element.449.raw_ref, ...), custom_call_target="tpu_custom_call" | custom-call | flops 3221225472 | bytes 13631488 | tf_op jit(solution)/shard_map/raw_back/pallas_call | solution.py:682
  615.7 13.0 %collective-permute-done.40 = bf16[128,2048]{1,0:T(8,128)(2,1)S(1)} collective-permute-done((bf16[128,2048]{1,0:T(8,128)(2,1)}, bf16[128,2048]{1,0:T(8,128)(2,1)S(1)}, u32[]{:S(2)}, u32[]{:S(2)}) %collective-permute-start.40) | collective-permute-done | bytes 524320 | tf_op jit(solution)/shard_map/ppermute | solution.py:739
  630.0 9.2 %qkv_grad.1 = bf16[8,3,256,512]{3,2,1,0:T(8,128)(2,1)} custom-call(bf16[512,2048]{1,0:T(8,128)(2,1)} %get-tuple-element.464.n_ref, bf16[512,1536]{1,0:T(8,128)(2,1)} %get-tuple-element.465.d_ref), custom_call_target="tpu_custom_call" | custom-call | flops 3221225472 | bytes 9961472 | tf_op jit(solution)/shard_map/qkv_grad/pallas_call | solution.py:716
  639.2 6.9 collective-permute-done.39.b_ref
  646.1 5.9 collective-permute-done.41.c_ref
  664.9 8.3 %settle.2 = (f32[16,2,256,256]{3,2,1,0:T(8,128)}, f32[16,256,256]{2,1,0:T(8,128)}) custom-call(s32[6]{0:T(128)} %pad_add_fusion.2.spot_ref, bf16[6,3,256,256]{3,2,1,0:T(8,128)(2,1)} %get-tuple-element.487.refs_0_, bf16[6,3,256,256]{3,2,1,0:T(8,128)(2,1)} %collective-permute-done.48.refs_1_), custom_call_target="tpu_custom_call" | custom-call | bytes 14155776 | tf_op jit(solution)/shard_map/settle/pallas_call | solution.py:531
  673.3 7.6 %collective-permute-done.47 = bf16[2,1,3,256,256]{4,3,2,1,0:T(8,128)(2,1)S(1)} collective-permute-done((bf16[2,1,3,256,256]{4,3,2,1,0:T(8,128)(2,1)S(1)}, bf16[2,1,3,256,256]{4,3,2,1,0:T(8,128)(2,1)S(1)}, u32[]{:S(2)}, u32[]{:S(2)}) %collective-permute-start.47) | collective-permute-done | bytes 786464 | tf_op jit(solution)/shard_map/ppermute | solution.py:729
  682.5 6.1 collective-permute-done.43.refs_2_
  692.8 6.1 all-to-all-done.2
  705.8 5.7 collective-permute-done.45
  (272 shorter events, 152.4 us)
Async XLA Ops:
  7.2 60.6 %all-gather.7.cloned.1.call-start = ((), (), s32[]{:S(2)}) async-start(), calls=%async_computation.8 | async-start | bytes 9437184 | tf_op jit(solution)/shard_map/all_gather | solution.py:871
  9.7 258.4 %all-gather.9.cloned.1.call-start = ((), (), s32[]{:S(2)}) async-start(), calls=%async_computation.9 | async-start | bytes 23592960 | tf_op jit(solution)/shard_map/all_gather | solution.py:878
  20.5 325.4 %all-gather.11.cloned.1.call-start = ((), (), s32[]{:S(2)}) async-start(), calls=%async_computation.10 | async-start | bytes 7864320 | tf_op jit(solution)/shard_map/all_gather | solution.py:878
  86.9 26.2 %collective-permute-start.6 = (bf16[512,512]{1,0:T(8,128)(2,1)}, bf16[512,512]{1,0:T(8,128)(2,1)S(1)}, u32[]{:S(2)}, u32[]{:S(2)}) collective-permute-start(bf16[512,512]{1,0:T(8,128)(2,1)} %get-tuple-element.401.refs_4_), channel_id=1, source_target_pairs={{0,8},{8,0},{1,9},{9,1},{2,10},{10,2},{3,11},{11,3},{4,12},{12,4},... | collective-permute-start | bytes 1572872 | tf_op jit(solution)/shard_map/ppermute | solution.py:729
  93.8 41.1 %collective-permute-start.3 = (bf16[512,512]{1,0:T(8,128)(2,1)}, bf16[512,512]{1,0:T(8,128)(2,1)}, u32[]{:S(2)}, u32[]{:S(2)}) collective-permute-start(bf16[512,512]{1,0:T(8,128)(2,1)} %get-tuple-element.397.refs_0_), channel_id=1, source_target_pairs={{0,8},{8,0},{1,9},{9,1},{2,10},{10,2},{3,11},{11,3},{4,12},{12,4},... | collective-permute-start | bytes 1572872 | tf_op jit(solution)/shard_map/ppermute | solution.py:729
  95.1 40.6 %collective-permute-start.5 = (bf16[512,512]{1,0:T(8,128)(2,1)S(1)}, bf16[512,512]{1,0:T(8,128)(2,1)}, u32[]{:S(2)}, u32[]{:S(2)}) collective-permute-start(bf16[512,512]{1,0:T(8,128)(2,1)S(1)} %copy-done.29), channel_id=1, source_target_pairs={{0,4},{4,0},{1,5},{5,1},{2,6},{6,2},{3,7},{7,3},{8,12},{12,8},{9,1... | collective-permute-start | bytes 1572872 | tf_op jit(solution)/shard_map/ppermute | solution.py:729
  95.1 40.6 %collective-permute-start.2 = (bf16[512,512]{1,0:T(8,128)(2,1)}, bf16[512,512]{1,0:T(8,128)(2,1)}, u32[]{:S(2)}, u32[]{:S(2)}) collective-permute-start(bf16[512,512]{1,0:T(8,128)(2,1)} %get-tuple-element.397.refs_0_), channel_id=1, source_target_pairs={{0,4},{4,0},{1,5},{5,1},{2,6},{6,2},{3,7},{7,3},{8,12},{12,8},{9,1... | collective-permute-start | bytes 1572872 | tf_op jit(solution)/shard_map/ppermute | solution.py:729
  113.1 22.6 %collective-permute-start.7 = (bf16[512,512]{1,0:T(8,128)(2,1)S(1)}, bf16[512,512]{1,0:T(8,128)(2,1)}, u32[]{:S(2)}, u32[]{:S(2)}) collective-permute-start(bf16[512,512]{1,0:T(8,128)(2,1)S(1)} %collective-permute-done.6.refs_6_), channel_id=1, source_target_pairs={{0,4},{4,0},{1,5},{5,1},{2,6},{6,2},{3,7},{7,3},{8,12},{12,8},{9,1... | collective-permute-start | bytes 1572872 | tf_op jit(solution)/shard_map/ppermute | solution.py:729
  152.5 15.0 %collective-permute-start.9 = (bf16[128,2048]{1,0:T(8,128)(2,1)}, bf16[128,2048]{1,0:T(8,128)(2,1)S(1)}, u32[]{:S(2)}, u32[]{:S(2)}) collective-permute-start(bf16[128,2048]{1,0:T(8,128)(2,1)} %get-tuple-element.289), channel_id=1, source_target_pairs={{0,1},{1,0},{2,3},{3,2},{4,5},{5,4},{6,7},{7,6},{8,9},{9,8},{10,11... | collective-permute-start | bytes 1572872 | tf_op jit(solution)/shard_map/ppermute | solution.py:739
  154.0 30.8 %collective-permute-start.8 = (bf16[128,2048]{1,0:T(8,128)(2,1)}, bf16[128,2048]{1,0:T(8,128)(2,1)S(1)}, u32[]{:S(2)}, u32[]{:S(2)}) collective-permute-start(bf16[128,2048]{1,0:T(8,128)(2,1)} %get-tuple-element.287), channel_id=1, source_target_pairs={{0,1},{1,0},{2,3},{3,2},{4,5},{5,4},{6,7},{7,6},{8,9},{9,8},{10,11... | collective-permute-start | bytes 1572872 | tf_op jit(solution)/shard_map/ppermute | solution.py:739
  168.8 24.7 %collective-permute-start.10 = (bf16[128,2048]{1,0:T(8,128)(2,1)S(1)}, bf16[128,2048]{1,0:T(8,128)(2,1)}, u32[]{:S(2)}, u32[]{:S(2)}) collective-permute-start(bf16[128,2048]{1,0:T(8,128)(2,1)S(1)} %add_convert_fusion.16), channel_id=1, source_target_pairs={{0,2},{1,3},{2,0},{3,1},{4,6},{5,7},{6,4},{7,5},{8,10},{9,11},{10,... | collective-permute-start | bytes 1572872 | tf_op jit(solution)/shard_map/ppermute | solution.py:739
  197.0 22.6 %collective-permute-start.12 = (bf16[128,2176]{1,0:T(8,128)(2,1)}, bf16[128,2176]{1,0:T(8,128)(2,1)S(1)}, u32[]{:S(2)}, u32[]{:S(2)}) collective-permute-start(bf16[128,2176]{1,0:T(8,128)(2,1)} %get-tuple-element.373.ext_ref), channel_id=1, source_target_pairs={{0,2},{1,3},{2,0},{3,1},{4,6},{5,7},{6,4},{7,5},{8,10},{9,11},{10,... | collective-permute-start | bytes 1671176 | tf_op jit(solution)/shard_map/ppermute | solution.py:739
  203.1 350.9 %reduce-scatter.10.cloned.1.call-start = ((), (), s32[]{:S(2)}) async-start(), calls=%async_computation.11 | async-start | bytes 23592960
  203.3 27.4 %collective-permute-start.11 = (bf16[128,2176]{1,0:T(8,128)(2,1)S(1)}, bf16[128,2176]{1,0:T(8,128)(2,1)S(1)}, u32[]{:S(2)}, u32[]{:S(2)}) collective-permute-start(bf16[128,2176]{1,0:T(8,128)(2,1)S(1)} %copy-done.8), channel_id=1, source_target_pairs={{0,1},{1,0},{2,3},{3,2},{4,5},{5,4},{6,7},{7,6},{8,9},{9,8},{10,11... | collective-permute-start | bytes 1671176 | tf_op jit(solution)/shard_map/ppermute | solution.py:739
  219.6 22.3 %collective-permute-start.13 = (bf16[128,2176]{1,0:T(8,128)(2,1)S(1)}, bf16[128,2176]{1,0:T(8,128)(2,1)S(1)}, u32[]{:S(2)}, u32[]{:S(2)}) collective-permute-start(bf16[128,2176]{1,0:T(8,128)(2,1)S(1)} %collective-permute-done.12), channel_id=1, source_target_pairs={{0,1},{1,0},{2,3},{3,2},{4,5},{5,4},{6,7},{7,6},{8,9},{9,8},{10,11... | collective-permute-start | bytes 1671176 | tf_op jit(solution)/shard_map/ppermute | solution.py:739
  345.6 371.5 %reduce-scatter.8.cloned.1.call-start = ((), (), s32[]{:S(2)}) async-start(), calls=%async_computation.7 | async-start | bytes 2359296 | tf_op jit(solution)/shard_map/reduce_scatter | solution.py:982
  375.2 15.0 %collective-permute-start.17 = (bf16[128,2176]{1,0:T(8,128)(2,1)}, bf16[128,2176]{1,0:T(8,128)(2,1)}, u32[]{:S(2)}, u32[]{:S(2)}) collective-permute-start(bf16[128,2176]{1,0:T(8,128)(2,1)} %add_convert_fusion.10), channel_id=1, source_target_pairs={{0,1},{1,0},{2,3},{3,2},{4,5},{5,4},{6,7},{7,6},{8,9},{9,8},{10,11... | collective-permute-start | bytes 1671176 | tf_op jit(solution)/shard_map/ppermute | solution.py:739
  391.5 34.3 %collective-permute-start.20 = (bf16[128,2176]{1,0:T(8,128)(2,1)S(1)}, bf16[128,2176]{1,0:T(8,128)(2,1)S(1)}, u32[]{:S(2)}, u32[]{:S(2)}) collective-permute-start(bf16[128,2176]{1,0:T(8,128)(2,1)S(1)} %add_convert_fusion.9), channel_id=1, source_target_pairs={{0,2},{1,3},{2,0},{3,1},{4,6},{5,7},{6,4},{7,5},{8,10},{9,11},{10,... | collective-permute-start | bytes 1671176 | tf_op jit(solution)/shard_map/ppermute | solution.py:739
  394.2 31.7 %collective-permute-start.19 = (bf16[128,2176]{1,0:T(8,128)(2,1)S(1)}, bf16[128,2176]{1,0:T(8,128)(2,1)S(1)}, u32[]{:S(2)}, u32[]{:S(2)}) collective-permute-start(bf16[128,2176]{1,0:T(8,128)(2,1)S(1)} %add_convert_fusion.8), channel_id=1, source_target_pairs={{0,1},{1,0},{2,3},{3,2},{4,5},{5,4},{6,7},{7,6},{8,9},{9,8},{10,11... | collective-permute-start | bytes 1671176 | tf_op jit(solution)/shard_map/ppermute | solution.py:739
  409.7 62.3 %collective-permute-start.18 = (bf16[512,2048]{1,0:T(8,128)(2,1)}, bf16[512,2048]{1,0:T(8,128)(2,1)S(1)}, u32[]{:S(2)}, u32[]{:S(2)}) collective-permute-start(bf16[512,2048]{1,0:T(8,128)(2,1)} %get-tuple-element.357), channel_id=1, source_target_pairs={{0,4},{4,0},{1,5},{5,1},{2,6},{6,2},{3,7},{7,3},{8,12},{12,8},{9,1... | collective-permute-start | bytes 6291464 | tf_op jit(solution)/shard_map/ppermute | solution.py:729
  431.7 26.2 %collective-permute-start.22 = (bf16[128,2048]{1,0:T(8,128)(2,1)}, bf16[128,2048]{1,0:T(8,128)(2,1)S(1)}, u32[]{:S(2)}, u32[]{:S(2)}) collective-permute-start(bf16[128,2048]{1,0:T(8,128)(2,1)} %get-tuple-element.381), channel_id=1, source_target_pairs={{0,2},{1,3},{2,0},{3,1},{4,6},{5,7},{6,4},{7,5},{8,10},{9,11},{10,... | collective-permute-start | bytes 1572872 | tf_op jit(solution)/shard_map/ppermute | solution.py:739
  432.1 26.0 %collective-permute-start.21 = (bf16[128,2048]{1,0:T(8,128)(2,1)}, bf16[128,2048]{1,0:T(8,128)(2,1)S(1)}, u32[]{:S(2)}, u32[]{:S(2)}) collective-permute-start(bf16[128,2048]{1,0:T(8,128)(2,1)} %get-tuple-element.381), channel_id=1, source_target_pairs={{0,1},{1,0},{2,3},{3,2},{4,5},{5,4},{6,7},{7,6},{8,9},{9,8},{10,11... | collective-permute-start | bytes 1572872 | tf_op jit(solution)/shard_map/ppermute | solution.py:739
  457.8 13.9 %collective-permute-start.23 = (bf16[128,2048]{1,0:T(8,128)(2,1)S(1)}, bf16[128,2048]{1,0:T(8,128)(2,1)S(1)}, u32[]{:S(2)}, u32[]{:S(2)}) collective-permute-start(bf16[128,2048]{1,0:T(8,128)(2,1)S(1)} %collective-permute-done.22), channel_id=1, source_target_pairs={{0,1},{1,0},{2,3},{3,2},{4,5},{5,4},{6,7},{7,6},{8,9},{9,8},{10,11... | collective-permute-start | bytes 1572872 | tf_op jit(solution)/shard_map/ppermute | solution.py:739
  473.4 13.2 %collective-permute-start.24 = (bf16[128,2048]{1,0:T(8,128)(2,1)S(1)}, bf16[128,2048]{1,0:T(8,128)(2,1)S(1)}, u32[]{:S(2)}, u32[]{:S(2)}) collective-permute-start(bf16[128,2048]{1,0:T(8,128)(2,1)S(1)} %add_convert_fusion.15), channel_id=1, source_target_pairs={{0,1},{1,0},{2,3},{3,2},{4,5},{5,4},{6,7},{7,6},{8,9},{9,8},{10,11... | collective-permute-start | bytes 1572872 | tf_op jit(solution)/shard_map/ppermute | solution.py:739
  504.9 52.0 %collective-permute-start.36 = (bf16[2,1,3,256,256]{4,3,2,1,0:T(8,128)(2,1)}, bf16[2,1,3,256,256]{4,3,2,1,0:T(8,128)(2,1)}, u32[]{:S(2)}, u32[]{:S(2)}) collective-permute-start(bf16[2,1,3,256,256]{4,3,2,1,0:T(8,128)(2,1)} %get-tuple-element.538), channel_id=1, source_target_pairs={{0,16},{16,0},{1,17},{17,1},{2,18},{18,2},{3,19},{19,3},{4,20},{20... | collective-permute-start | bytes 2359304 | tf_op jit(solution)/shard_map/ppermute | solution.py:729
  506.5 23.7 %collective-permute-start.25 = (bf16[128,2048]{1,0:T(8,128)(2,1)}, bf16[128,2048]{1,0:T(8,128)(2,1)S(1)}, u32[]{:S(2)}, u32[]{:S(2)}) collective-permute-start(bf16[128,2048]{1,0:T(8,128)(2,1)} %add_convert_fusion.13), channel_id=1, source_target_pairs={{0,1},{1,0},{2,3},{3,2},{4,5},{5,4},{6,7},{7,6},{8,9},{9,8},{10,11... | collective-permute-start | bytes 1572872 | tf_op jit(solution)/shard_map/ppermute | solution.py:739
  507.2 26.1 %collective-permute-start.26 = (bf16[128,2048]{1,0:T(8,128)(2,1)}, bf16[128,2048]{1,0:T(8,128)(2,1)S(1)}, u32[]{:S(2)}, u32[]{:S(2)}) collective-permute-start(bf16[128,2048]{1,0:T(8,128)(2,1)} %add_convert_fusion.14), channel_id=1, source_target_pairs={{0,2},{1,3},{2,0},{3,1},{4,6},{5,7},{6,4},{7,5},{8,10},{9,11},{10,... | collective-permute-start | bytes 1572872 | tf_op jit(solution)/shard_map/ppermute | solution.py:739
  507.2 34.4 %collective-permute-start.31 = (bf16[2,512,512]{2,1,0:T(8,128)(2,1)}, bf16[2,512,512]{2,1,0:T(8,128)(2,1)S(1)}, u32[]{:S(2)}, u32[]{:S(2)}) collective-permute-start(bf16[2,512,512]{2,1,0:T(8,128)(2,1)} %get-tuple-element.420), channel_id=1, source_target_pairs={{0,4},{4,0},{1,5},{5,1},{2,6},{6,2},{3,7},{7,3},{8,12},{12,8},{9,1... | collective-permute-start | bytes 3145736 | tf_op jit(solution)/shard_map/ppermute | solution.py:729
  509.7 33.6 %collective-permute-start.32 = (bf16[2,512,512]{2,1,0:T(8,128)(2,1)}, bf16[2,512,512]{2,1,0:T(8,128)(2,1)}, u32[]{:S(2)}, u32[]{:S(2)}) collective-permute-start(bf16[2,512,512]{2,1,0:T(8,128)(2,1)} %add_convert_fusion), channel_id=1, source_target_pairs={{0,8},{8,0},{1,9},{9,1},{2,10},{10,2},{3,11},{11,3},{4,12},{12,4},... | collective-permute-start | bytes 3145736 | tf_op jit(solution)/shard_map/ppermute | solution.py:729
  530.2 36.1 %collective-permute-start.34 = (bf16[2,1,3,256,256]{4,3,2,1,0:T(8,128)(2,1)}, bf16[2,1,3,256,256]{4,3,2,1,0:T(8,128)(2,1)}, u32[]{:S(2)}, u32[]{:S(2)}) collective-permute-start(bf16[2,1,3,256,256]{4,3,2,1,0:T(8,128)(2,1)} %get-tuple-element.544), channel_id=1, source_target_pairs={{0,16},{16,0},{1,17},{17,1},{2,18},{18,2},{3,19},{19,3},{4,20},{20... | collective-permute-start | bytes 2359304 | tf_op jit(solution)/shard_map/ppermute | solution.py:729
  533.3 33.0 %collective-permute-start.33 = (bf16[2,1,3,256,256]{4,3,2,1,0:T(8,128)(2,1)}, bf16[2,1,3,256,256]{4,3,2,1,0:T(8,128)(2,1)}, u32[]{:S(2)}, u32[]{:S(2)}) collective-permute-start(bf16[2,1,3,256,256]{4,3,2,1,0:T(8,128)(2,1)} %get-tuple-element.545), channel_id=1, source_target_pairs={{0,8},{8,0},{1,9},{9,1},{2,10},{10,2},{3,11},{11,3},{4,12},{12,4},... | collective-permute-start | bytes 2359304 | tf_op jit(solution)/shard_map/ppermute | solution.py:729
  541.6 29.6 %collective-permute-start.35 = (bf16[2,1,3,256,256]{4,3,2,1,0:T(8,128)(2,1)}, bf16[2,1,3,256,256]{4,3,2,1,0:T(8,128)(2,1)}, u32[]{:S(2)}, u32[]{:S(2)}) collective-permute-start(bf16[2,1,3,256,256]{4,3,2,1,0:T(8,128)(2,1)} %get-tuple-element.542), channel_id=1, source_target_pairs={{0,8},{8,0},{1,9},{9,1},{2,10},{10,2},{3,11},{11,3},{4,12},{12,4},... | collective-permute-start | bytes 2359304 | tf_op jit(solution)/shard_map/ppermute | solution.py:729
  543.3 22.9 %collective-permute-start.29 = (bf16[128,2048]{1,0:T(8,128)(2,1)S(1)}, bf16[128,2048]{1,0:T(8,128)(2,1)}, u32[]{:S(2)}, u32[]{:S(2)}) collective-permute-start(bf16[128,2048]{1,0:T(8,128)(2,1)S(1)} %add_convert_fusion.12.refs_0_), channel_id=1, source_target_pairs={{0,2},{1,3},{2,0},{3,1},{4,6},{5,7},{6,4},{7,5},{8,10},{9,11},{10,... | collective-permute-start | bytes 1572872 | tf_op jit(solution)/shard_map/ppermute | solution.py:739
  554.1 166.1 %reduce-scatter.6.cloned.1.call-start = ((), (), s32[]{:S(2)}) async-start(), calls=%async_computation.6 | async-start | bytes 7077888 | tf_op jit(solution)/shard_map/reduce_scatter | solution.py:1012
  556.9 38.8 %collective-permute-start.28 = (bf16[128,2048]{1,0:T(8,128)(2,1)S(1)}, bf16[128,2048]{1,0:T(8,128)(2,1)S(1)}, u32[]{:S(2)}, u32[]{:S(2)}) collective-permute-start(bf16[128,2048]{1,0:T(8,128)(2,1)S(1)} %add_convert_fusion.12.refs_0_), channel_id=1, source_target_pairs={{0,1},{1,0},{2,3},{3,2},{4,5},{5,4},{6,7},{7,6},{8,9},{9,8},{10,11... | collective-permute-start | bytes 1572872 | tf_op jit(solution)/shard_map/ppermute | solution.py:739
  566.3 29.4 %collective-permute-start.30 = (bf16[128,2048]{1,0:T(8,128)(2,1)}, bf16[128,2048]{1,0:T(8,128)(2,1)S(1)}, u32[]{:S(2)}, u32[]{:S(2)}) collective-permute-start(bf16[128,2048]{1,0:T(8,128)(2,1)} %collective-permute-done.29.refs_2_), channel_id=1, source_target_pairs={{0,1},{1,0},{2,3},{3,2},{4,5},{5,4},{6,7},{7,6},{8,9},{9,8},{10,11... | collective-permute-start | bytes 1572872 | tf_op jit(solution)/shard_map/ppermute | solution.py:739
  572.5 16.1 %collective-permute-start.37 = (f32[2,512]{1,0:T(2,128)S(1)}, f32[2,512]{1,0:T(2,128)S(1)}, u32[]{:S(2)}, u32[]{:S(2)}) collective-permute-start(f32[2,512]{1,0:T(2,128)S(1)} %slice_reduce_fusion), channel_id=1, source_target_pairs={{0,1},{1,0},{2,3},{3,2},{4,5},{5,4},{6,7},{7,6},{8,9},{9,8},{10,11... | collective-permute-start | bytes 12296 | tf_op jit(solution)/shard_map/ppermute | solution.py:739
  613.7 15.1 %collective-permute-start.40 = (bf16[128,2048]{1,0:T(8,128)(2,1)}, bf16[128,2048]{1,0:T(8,128)(2,1)S(1)}, u32[]{:S(2)}, u32[]{:S(2)}) collective-permute-start(bf16[128,2048]{1,0:T(8,128)(2,1)} %get-tuple-element.458), channel_id=1, source_target_pairs={{0,1},{1,0},{2,3},{3,2},{4,5},{5,4},{6,7},{7,6},{8,9},{9,8},{10,11... | collective-permute-start | bytes 1572872 | tf_op jit(solution)/shard_map/ppermute | solution.py:739
  613.7 32.4 %collective-permute-start.39 = (bf16[128,2048]{1,0:T(8,128)(2,1)}, bf16[128,2048]{1,0:T(8,128)(2,1)S(1)}, u32[]{:S(2)}, u32[]{:S(2)}) collective-permute-start(bf16[128,2048]{1,0:T(8,128)(2,1)} %get-tuple-element.456), channel_id=1, source_target_pairs={{0,1},{1,0},{2,3},{3,2},{4,5},{5,4},{6,7},{7,6},{8,9},{9,8},{10,11... | collective-permute-start | bytes 1572872 | tf_op jit(solution)/shard_map/ppermute | solution.py:739
  629.9 22.0 %collective-permute-start.41 = (bf16[128,2048]{1,0:T(8,128)(2,1)S(1)}, bf16[128,2048]{1,0:T(8,128)(2,1)S(1)}, u32[]{:S(2)}, u32[]{:S(2)}) collective-permute-start(bf16[128,2048]{1,0:T(8,128)(2,1)S(1)} %add_convert_fusion.11), channel_id=1, source_target_pairs={{0,2},{1,3},{2,0},{3,1},{4,6},{5,7},{6,4},{7,5},{8,10},{9,11},{10,... | collective-permute-start | bytes 1572872 | tf_op jit(solution)/shard_map/ppermute | solution.py:739
  658.1 22.8 %collective-permute-start.46 = (bf16[2,1,3,256,256]{4,3,2,1,0:T(8,128)(2,1)S(1)}, bf16[2,1,3,256,256]{4,3,2,1,0:T(8,128)(2,1)S(1)}, u32[]{:S(2)}, u32[]{:S(2)}) collective-permute-start(bf16[2,1,3,256,256]{4,3,2,1,0:T(8,128)(2,1)S(1)} %copy-done.17), channel_id=1, source_target_pairs={{0,16},{16,0},{1,17},{17,1},{2,18},{18,2},{3,19},{19,3},{4,20},{20... | collective-permute-start | bytes 2359304 | tf_op jit(solution)/shard_map/ppermute | solution.py:729
  660.1 20.8 %collective-permute-start.47 = (bf16[2,1,3,256,256]{4,3,2,1,0:T(8,128)(2,1)S(1)}, bf16[2,1,3,256,256]{4,3,2,1,0:T(8,128)(2,1)S(1)}, u32[]{:S(2)}, u32[]{:S(2)}) collective-permute-start(bf16[2,1,3,256,256]{4,3,2,1,0:T(8,128)(2,1)S(1)} %add_convert_fusion.3), channel_id=1, source_target_pairs={{0,8},{8,0},{1,9},{9,1},{2,10},{10,2},{3,11},{11,3},{4,12},{12,4},... | collective-permute-start | bytes 2359304 | tf_op jit(solution)/shard_map/ppermute | solution.py:729
  664.8 23.8 %collective-permute-start.43 = (bf16[128,2048]{1,0:T(8,128)(2,1)S(1)}, bf16[128,2048]{1,0:T(8,128)(2,1)S(1)}, u32[]{:S(2)}, u32[]{:S(2)}) collective-permute-start(bf16[128,2048]{1,0:T(8,128)(2,1)S(1)} %copy-done.20), channel_id=1, source_target_pairs={{0,2},{1,3},{2,0},{3,1},{4,6},{5,7},{6,4},{7,5},{8,10},{9,11},{10,... | collective-permute-start | bytes 1572872 | tf_op jit(solution)/shard_map/ppermute | solution.py:739
  682.4 18.6 %collective-permute-start.49 = (bf16[2,3,256,256]{3,2,1,0:T(8,128)(2,1)S(1)}, bf16[2,3,256,256]{3,2,1,0:T(8,128)(2,1)S(1)}, u32[]{:S(2)}, u32[]{:S(2)}) collective-permute-start(bf16[2,3,256,256]{3,2,1,0:T(8,128)(2,1)S(1)} %get-tuple-element.536), channel_id=1, source_target_pairs={{0,4},{4,0},{1,5},{5,1},{2,6},{6,2},{3,7},{7,3},{8,12},{12,8},{9,1... | collective-permute-start | bytes 2359304 | tf_op jit(solution)/shard_map/ppermute | solution.py:729
  682.5 29.8 %collective-permute-start.42 = (bf16[128,2048]{1,0:T(8,128)(2,1)S(1)}, bf16[128,2048]{1,0:T(8,128)(2,1)S(1)}, u32[]{:S(2)}, u32[]{:S(2)}) collective-permute-start(bf16[128,2048]{1,0:T(8,128)(2,1)S(1)} %copy-done.20), channel_id=1, source_target_pairs={{0,1},{1,0},{2,3},{3,2},{4,5},{5,4},{6,7},{7,6},{8,9},{9,8},{10,11... | collective-permute-start | bytes 1572872 | tf_op jit(solution)/shard_map/ppermute | solution.py:739
  688.6 23.7 %collective-permute-start.44 = (bf16[128,2048]{1,0:T(8,128)(2,1)S(1)}, bf16[128,2048]{1,0:T(8,128)(2,1)}, u32[]{:S(2)}, u32[]{:S(2)}) collective-permute-start(bf16[128,2048]{1,0:T(8,128)(2,1)S(1)} %collective-permute-done.43.refs_2_), channel_id=1, source_target_pairs={{0,1},{1,0},{2,3},{3,2},{4,5},{5,4},{6,7},{7,6},{8,9},{9,8},{10,11... | collective-permute-start | bytes 1572872 | tf_op jit(solution)/shard_map/ppermute | solution.py:739
  689.4 9.5 %all-to-all-start.2 = ((f32[8,20,256]{2,1,0:T(8,128)}), f32[8,20,256]{2,1,0:T(8,128)S(1)}, u32[]{:S(2)}, u32[]{:S(2)}) async-start(f32[8,20,256]{2,1,0:T(8,128)} %bitcast.60), calls=%async_computation.2 | async-start | bytes 393216 | tf_op jit(solution)/shard_map/all_to_all | solution.py:1020
  699.0 12.5 %collective-permute-start.45 = (f32[20,256]{1,0:T(8,128)S(1)}, f32[20,256]{1,0:T(8,128)S(1)}, u32[]{:S(2)}, u32[]{:S(2)}) collective-permute-start(f32[20,256]{1,0:T(8,128)S(1)} %reduce_sum.9), channel_id=1, source_target_pairs={{0,1},{1,0},{2,3},{3,2},{4,5},{5,4},{6,7},{7,6},{8,9},{9,8},{10,11... | collective-permute-start | bytes 61448 | tf_op jit(solution)/shard_map/ppermute | solution.py:739
  (49 other events, 505.9 us)
Sparse Core Ops, SparseCore 0:
  10.5 57.2 all-gather.6
  69.6 198.3 all-gather.8
  269.9 70.1 all-gather.10
  345.7 177.6 reduce-scatter.9
  554.2 40.4 reduce-scatter.7
  656.5 61.0 reduce-scatter.5

commit v3 on v2

--- a/solution.py
+++ b/solution.py
@@ -290,8 +290,8 @@
         "gradout",
         (p // pb,),
         [pl.BlockSpec((t, pb * ds), lambda g, *_: (0, g)), fixed((t, n))],
-        pl.BlockSpec((pb, ds, n), lambda g, *_: (g, 0, 0)),
-        sds((p, ds, n), BF16),
+        pl.BlockSpec((pb, 1, ds, n), lambda g, *_: (g, 3, 0, 0)),
+        sds((p, 4, ds, n), BF16),
         2 * t * n * d,
         2 * (t * n + n * d + t * d),
         prefetch=1,
@@ -454,59 +454,36 @@
     )(first, *xs, *cs, w)
 
 
-def expert_grad_kernel(col_ref, *refs, parts, groups, sides):
-    xs, cs = refs[:parts], refs[parts : 2 * parts]
-    hids, dgus = refs[2 * parts : 2 * parts + groups], refs[2 * parts + groups : 2 * parts + 2 * groups]
-    outs = refs[2 * parts + 2 * groups :]
-    pb, e, _, ds, f = outs[0].shape
+def expert_grad_kernel(*refs, parts):
+    xs, cs, hid_ref, dgu_ref, o_ref = refs[:parts], refs[parts : 2 * parts], *refs[2 * parts :]
+    pb, e, _, ds, f = o_ref.shape
     x = jnp.concatenate([r[...] for r in xs], 0)
     c = jnp.concatenate([r[...] for r in cs], 0)
-    share = x.shape[0] // groups
-    step = pl.program_id(0)
-    each = pl.num_programs(0) // sides
-
-    def product(left, refs):
-        return sum(tn(left[g * share : (g + 1) * share], r[...]) for g, r in enumerate(refs)).astype(BF16)
-
-    both = product(x, dgus)
-    down = product(c, hids)
-    for side, o in enumerate(outs):
-
-        @pl.when(step // each == side)
-        def _():
-            for i in range(e):
-                o[:, i, 0] = both[:, 2 * i * f : (2 * i + 1) * f].reshape(pb, ds, f)
-                o[:, i, 1] = both[:, (2 * i + 1) * f : (2 * i + 2) * f].reshape(pb, ds, f)
-                o[:, i, 2] = down[:, i * f : (i + 1) * f].reshape(pb, ds, f)
-
-
-def expert_grads(columns, xs, cs, hids, dgus, p, e, sides):
+    both = tn(x, dgu_ref[...]).astype(BF16)
+    down = tn(c, hid_ref[...]).astype(BF16)
+    for i in range(e):
+        o_ref[:, i, 0] = both[:, 2 * i * f : (2 * i + 1) * f].reshape(pb, ds, f)
+        o_ref[:, i, 1] = both[:, (2 * i + 1) * f : (2 * i + 2) * f].reshape(pb, ds, f)
+        o_ref[:, i, 2] = down[:, i * f : (i + 1) * f].reshape(pb, ds, f)
+
+
+def expert_grads(xs, cs, hid, dgu, p, e):
     t, d = cs[0].shape
     parts = len(cs)
-    groups = len(hids)
     ds = d // p
-    f = hids[0].shape[1] // e
+    f = hid.shape[1] // e
     pb = max(1, TILE // ds)
-    steps = p // pb
-    each = steps // sides
-    column = pl.BlockSpec((t, pb * ds), lambda g, col: (0, col[g]))
-
-    def out(side):
-        return pl.BlockSpec(
-            (pb, e, 3, ds, f), lambda g, col: (jnp.clip(g - side * each, 0, each - 1), 0, 0, 0, 0)
-        )
-
-    return call(
-        functools.partial(expert_grad_kernel, parts=parts, groups=groups, sides=sides),
+    column = pl.BlockSpec((t, pb * ds), lambda g: (0, g))
+    return call(
+        functools.partial(expert_grad_kernel, parts=parts),
         "expert_grad",
-        (steps,),
-        [column] * (2 * parts) + [fixed(h.shape) for h in hids] + [fixed(g.shape) for g in dgus],
-        [out(side) for side in range(sides)],
-        [sds((p // sides, e, 3, ds, f), BF16)] * sides,
+        (p // pb,),
+        [column] * (2 * parts) + [fixed(hid.shape), fixed(dgu.shape)],
+        pl.BlockSpec((pb, e, 3, ds, f), lambda g: (g, 0, 0, 0, 0)),
+        sds((p, e, 3, ds, f), BF16),
         6 * parts * t * d * f * e,
         2 * (3 * d * f * e + 2 * parts * t * d + 3 * parts * t * f * e),
-        prefetch=1,
-    )(columns, *xs, *cs, *hids, *dgus)
+    )(*xs, *cs, hid, dgu)
 
 
 def settle_kernel(spot_ref, *refs, pieces):
@@ -701,14 +678,14 @@
     )(places, u, raw, scales, inner, gains, dv, w)
 
 
-def qkv_grad_kernel(n_ref, d_ref, o_ref):
+def qkv_grad_kernel(n_ref, d_ref, kept_ref, o_ref):
     pb, _, ds, n = o_ref.shape
     grads = tn(n_ref[...], d_ref[...]).astype(BF16)
     for c in range(3):
         o_ref[:, c] = grads[:, c * n : (c + 1) * n].reshape(pb, ds, n)
 
 
-def qkv_grads(normed, grad, p):
+def qkv_grads(normed, grad, kept, p):
     t, d = normed.shape
     n = grad.shape[1] // 3
     ds = d // p
@@ -717,12 +694,17 @@
         qkv_grad_kernel,
         "qkv_grad",
         (p // pb,),
-        [pl.BlockSpec((t, pb * ds), lambda g: (0, g)), fixed((t, 3 * n))],
+        [
+            pl.BlockSpec((t, pb * ds), lambda g: (0, g)),
+            fixed((t, 3 * n)),
+            pl.BlockSpec(memory_space=pl.ANY),
+        ],
         pl.BlockSpec((pb, 3, ds, n), lambda g: (g, 0, 0, 0)),
-        sds((p, 3, ds, n), BF16),
+        sds(kept.shape, BF16),
         6 * t * d * n,
         2 * (3 * d * n + t * d + 3 * t * n),
-    )(normed, grad)
+        aliases={2: 0},
+    )(normed, grad, kept)
 
 
 def swap(value, axis):
@@ -754,31 +736,6 @@
 
 def join(*pieces):
     return jnp.concatenate(pieces, 0)
-
-
-class Crossing:
-    def __init__(self, first, second):
-        self.one, self.two = first, second
-        self.far = swap(first[3], "row"), swap(second[3], "fsdp")
-        self.near = swap(first[1], "row"), swap(second[2], "fsdp")
-
-    def half(self, line):
-        sums = line(
-            lambda a, b, c, d, e, f, g, h: (add(a, b), add(c, d), add(e, f), add(g, h)),
-            self.one[2],
-            self.far[0],
-            self.two[1],
-            self.far[1],
-            self.one[0],
-            self.near[0],
-            self.two[0],
-            self.near[1],
-        )
-        self.last = swap(sums[0], "fsdp"), swap(sums[1], "row")
-        self.kept = sums[2:]
-
-    def done(self, line):
-        return line(lambda a, b, c, d: (add(a, b), add(c, d)), self.kept[0], self.last[0], self.kept[1], self.last[1])
 
 
 class Line:
@@ -793,7 +750,7 @@
             for i, v in zip(spots, kept):
                 leaves[i] = v
         result = step(*jax.tree.unflatten(form, leaves))
-        self.last = min(jax.tree.leaves(result), key=lambda v: v.size)
+        self.last = jax.tree.leaves(result)
         return result
 
     def sums(self, own, core, pieces, first=None):
@@ -804,28 +761,29 @@
         return [first, across(beside, 1), across(near, 2)]
 
 
-def in_place_kernel(place_ref, *refs):
-    for r, piece in enumerate(refs[:-1]):
+def in_place_kernel(place_ref, *refs, count):
+    for r, piece in enumerate(refs[:count]):
 
         @pl.when(pl.program_id(0) == r)
         def _():
             refs[-1][...] = piece[...]
 
 
-def in_place(pieces, places):
+def in_place(places, pieces, kept, total_rows):
     rows, d = pieces[0].shape
     count = len(pieces)
     return call(
-        in_place_kernel,
+        functools.partial(in_place_kernel, count=count),
         "inplace",
         (count,),
-        [fixed((rows, d))] * count,
+        [fixed((rows, d))] * count + [pl.BlockSpec(memory_space=pl.ANY)] * len(kept),
         pl.BlockSpec((rows, d), lambda r, place: (place[r] // rows, 0)),
-        sds((rows * count, d), pieces[0].dtype),
+        sds((total_rows, d), pieces[0].dtype),
         0,
         4 * rows * count * d,
         prefetch=1,
-    )(places, *pieces)
+        aliases={1 + count: 0} if kept else None,
+    )(places, *pieces, *kept)
 
 
 def meet(value):
@@ -916,13 +874,6 @@
 
     xs, cs = [x0, x1], [c0, c1]
     blocks_in = jnp.arange(width // TILE, dtype=jnp.int32)
-    square = lax.axis_size("fsdp") == 2 and lax.axis_size("row") == 2
-    chip = lax.axis_index("fsdp") * 2 + lax.axis_index("row")
-    by_chip = blocks_in
-    if square:
-        share = width // TILE // 8
-        chips, cores, inner = jnp.meshgrid(jnp.arange(4), jnp.arange(2), jnp.arange(share), indexing="ij")
-        by_chip = (((chips ^ chip) * 2 + cores) * share + inner).reshape(-1).astype(jnp.int32)
     hid, dgu, side, grads = [], [], [], []
     dx = []
 
@@ -935,26 +886,23 @@
         gates = side if k == len(chunks) - 1 else []
         return line(expert_down, [dgu[k]], [ws[k]], 0, 2, gates, before, 2, "expert_dx")
 
-    def weight_grad(k, relative_chips):
-        sides = 4 if relative_chips else 1
-        columns = by_chip if relative_chips else blocks_in
-        made = line(expert_grads, columns, xs, cs, [hid[k]], [dgu[k]], p, chunks[k], sides)
-        if relative_chips:
-            return made
-        made = made[0].reshape(-1, 2, chunks[k], 3, ds, f)
+    def weight_grad(k):
+        return line(expert_grads, xs, cs, hid[k], dgu[k], p, chunks[k])
+
+    def to_owners(made, k, after):
+        made, after = lax.optimization_barrier((made, after))
+        made = made.reshape(-1, 2, chunks[k], 3, ds, f)
         return lax.optimization_barrier(lax.psum_scatter(made, FR, scatter_dimension=0, tiled=False))
 
     for k in range(len(chunks)):
         up(k)
         dx = back(k, dx)
         if k < len(chunks) - 1:
-            grads.append(weight_grad(k, False))
+            made = weight_grad(k)
+            grads.append(to_owners(made, k, ()))
     d_normed = line.sums(*dx, tp)
     moe = line(expert_down, hid, ws, 2, 1, [], [], 2, "expert_out")
-    tail = weight_grad(len(chunks) - 1, square)
-    if square:
-        middle = chunks[-1] // 2
-        tail = Crossing([v[:, :middle] for v in tail], [v[:, middle:] for v in tail])
+    late = weight_grad(len(chunks) - 1)
 
     d_mid, d_mid_low, gain_two, grad_router = line(
         norm_two_back, d_normed, mid, ext, probs, chosen, cots[0], gains[1:2], router_rows
@@ -966,22 +914,23 @@
     last = across(line(add, own[3], beside[3]), 1)
 
     d_heads = line(heads_grad, places, d_mid_low, attn_w, tp)
+    grads.append(to_owners(late, len(chunks) - 1, d_heads))
+    dq, b0, b1, b2, b3 = line(attend_back, scal, queries, blocks, d_heads, length)
+    r1 = swap(b1, "core")
+    r3 = swap(b3, "core")
     near = line(add, own[2], beside[2], last)
     next_one = line(add, own[1], beside[1])
     moe = [across(next_one, 1), across(near, 2)]
-    dq, b0, b1, b2, b3 = line(attend_back, scal, queries, blocks, d_heads, length)
-    r1 = swap(b1, "core")
-    r2 = swap(line(add, b2, swap(b3, "core")), "row")
+    r2 = swap(line(add, b2, r3), "row")
+    grad_attn = line(out_weight_grad, places, d_mid_low, heads, p, tp)
     out = line(lambda *v: total(v).astype(BF16), mid, own[0], beside[0], *moe)
     out_far = across(out, 2)
     out_near = across(out, 1)
-    grad_out = line(out_weight_grad, places, d_mid_low, heads, p, tp)
     d_kv = line(lambda *v: total(v), b0, r1, r2)
+    out_far, d_kv = lax.optimization_barrier((out_far, d_kv))
+    out_both = across(out_far, 1)
     u, inner, gain_qk = line(unturn, dq, d_kv[0], raw, scales, own_gains, cosine, sine)
-    grad_out, grads[0], u = lax.optimization_barrier((grad_out, grads[0], u))
-    grad_out = lax.psum_scatter(grad_out, PLANE, scatter_dimension=0, tiled=False)
-    if square:
-        tail.half(line)
+    outputs = line(in_place, places, [out, out_near, out_far, out_both], [], t).reshape(inputs.shape)
 
     def parted(k):
         own, other = line(
@@ -994,22 +943,20 @@
         spots = jnp.concatenate([(c * group + starts[k]) // 2 + steps for c in (core, core ^ 1)])
         return line(settle, spots.astype(jnp.int32), pair, kept, experts)
 
-    pairs = [parted(0)]
     inner = (meet(inner[:, :, 0]) / width)[:, :, None]
-    out_both = across(out_far, 1)
-    outputs = line(in_place, [out, out_near, out_far, out_both], places).reshape(inputs.shape)
     d_raw, *d_one = line(
         raw_back, places, u, raw, scales, inner, own_gains, d_kv[1].astype(BF16), attn_w, tp
     )
     last = across(d_one[3], 1)
     near = line(add, d_one[2], last)
     d_one = [d_one[0], across(d_one[1], 1), across(near, 2)]
-    grad_qkv = line(qkv_grads, normed_one, d_raw, p)
+    grad_attn = line(qkv_grads, normed_one, d_raw, grad_attn, p)
+    pairs = [parted(0)]
     grad_in, gain_one = line(norm_one_back, d_one, x_q, d_mid, gains[0:1])
     far = across(grad_in, 2)
     near = across(grad_in, 1)
-    grad_qkv, gain_one = lax.optimization_barrier((grad_qkv, gain_one))
-    grad_qkv = lax.psum_scatter(grad_qkv, PLANE, scatter_dimension=0, tiled=False)
+    grad_attn, gain_one = lax.optimization_barrier((grad_attn, gain_one))
+    grad_attn = lax.psum_scatter(grad_attn, PLANE, scatter_dimension=0, tiled=False)
     placed = lax.dynamic_update_slice_in_dim(
         jnp.zeros((2, width), F32), gain_qk[:, 0, :], column * n, 1
     )
@@ -1021,12 +968,12 @@
     other = across(small, 1)
     both = across(far, 1)
     kept = settled(0, pairs[0], [])
-    grads.append(jnp.concatenate(tail.done(line), 1) if square else tail)
+    placed_in = line(in_place, places[:2], [grad_in, near], [], t)
     pairs.append(parted(1))
     owned_gate_up, owned_down = settled(1, pairs[1], kept)
     small = line(lambda a, b: a + b, small, other)
     other = across(small, 2)
-    grad_inputs = line(in_place, [grad_in, near, far, both], places).reshape(inputs.shape)
+    grad_inputs = line(in_place, places[2:], [far, both], [placed_in], t).reshape(inputs.shape)
     small = line(lambda a, b: a + b, small, other)
     owned_gains = small[experts:]
     owned_router = small[:experts].T
@@ -1034,8 +981,8 @@
         outputs,
         grad_inputs,
         owned_gains,
-        grad_qkv.astype(F32),
-        grad_out.astype(F32),
+        grad_attn[:3].astype(F32),
+        grad_attn[3].astype(F32),
         owned_router,
         owned_gate_up,
         owned_down,

time: 739 us -> 714 us (0.966)
  other arithmetic: 34.5 us -> 22.5 us
  waiting for transfers between devices: 312 us -> 302 us
    ppermute x30, waiting for transfers between devices: 212 us -> 179 us  [across(): return lax.ppermute(value, 'tp', [(i, i ^ k) for i in range(size)])]
    reduce_scatter x2 -> x1, waiting for transfers between devices: 0.01 us -> 17.6 us  [body(): lax.psum_scatter(grad_attn, PLANE, scatter_dimension=0, tiled=False)]
    convert_element_type x16 -> x10, other arithmetic: 17.7 us -> 7.13 us  [add(): return total(values).astype(values[0].dtype)]
    ppermute x30, starting transfers between devices: 24 us -> 34.2 us  [across(): return lax.ppermute(value, 'tp', [(i, i ^ k) for i in range(size)])]
    ppermute x21 -> x15, waiting for transfers between devices: 63.4 us -> 67.6 us  [swap(): return lax.ppermute(value, axis, [(0, 1), (1, 0)])]
    pallas_call x4 -> x5, Pallas kernels: 53.3 us -> 50 us  [the longest x2 40.1 us: expert_grads(): call(functools.partial(expert_grad_kernel, parts=parts), 'expert_grad', (...]
  transfers between devices with their start and end apart: 58 -> 52, of which waited for: 33 -> 32; matrix products, arithmetic and copies ran while one was open for 9% -> 7% of each run, Pallas kernels for 33% -> 34%
where the time goes in v3:
time: 714 us; the launch traced here: 704 us
  waiting for transfers between devices  302 us (42%)
  Pallas kernels  241 us (34%)
  starting transfers between devices  44.3 us (6%)
  local copies, waits for them, and re-layouts  37.6 us (5%)
  blocking collectives  34.3 us (5%)
  between operations  22.9 us (3%)
  other arithmetic  22.5 us (3%)
    ppermute x30, waiting for transfers between devices, across(): return lax.ppermute(value, 'tp', [(i, i ^ k) for i in range(size)])  179 us
    ppermute x15, waiting for transfers between devices, swap(): return lax.ppermute(value, axis, [(0, 1), (1, 0)])  67.6 us
    pallas_call x3, Pallas kernels, expert_down(): call(functools.partial(down_kernel, planes=planes, chunks=chunks, sides=l...  43.1 us
    pallas_call x2, Pallas kernels, expert_up(): call(functools.partial(expert_kernel, parts=parts), 'expert_up', (e,), [f...  41.4 us
    pallas_call x2, Pallas kernels, expert_grads(): call(functools.partial(expert_grad_kernel, parts=parts), 'expert_grad', (...  40.1 us
    ppermute x30, starting transfers between devices, across(): return lax.ppermute(value, 'tp', [(i, i ^ k) for i in range(size)])  34.2 us
    reduce_scatter x1, waiting for transfers between devices, body(): lax.psum_scatter(grad_attn, PLANE, scatter_dimension=0, tiled=False)  17.6 us
    all_gather x2, waiting for transfers between devices, body(): lax.all_gather(mine, FR, axis=0, tiled=False).reshape(-1, e, 3, ds, f)  15.1 us
  transfers between devices with their start and end apart: 52, of which 32 were waited for; matrix products, arithmetic and copies ran while one was open for 7% of the time, Pallas kernels for 34%

profile of v3, /device:TPU:0, one launch (start us, length us, event | category | flops | bytes accessed | tf_op | source)
XLA Modules:
  0.0 704.3 jit_solution(6287658027079064337)
XLA Ops:
  11.9 8.6 %all_to_all.15 = bf16[2,6,3,256,256]{4,3,2,1,0:T(8,128)(2,1)} all-to-all(bf16[2,6,3,256,256]{4,3,2,1,0:T(8,128)(2,1)S(1)} %fusion), channel_id=1, replica_groups=mesh['fsdp'=2,'row'=2,'core'=2,'tp'=4] {'core'}, dimensions={0} | all-to-all | bytes 9437184 | tf_op jit(solution)/shard_map/all_to_all | solution.py:835
  29.0 10.4 %all_gather.26 = bf16[4,2048]{1,0:T(4,128)(2,1)S(1)} all-gather(bf16[4,256]{1,0:T(4,128)(2,1)S(1)} %copy-done.28), channel_id=1, replica_groups=mesh['fsdp'=2,'row'=2,'core'=2,'tp'=4] {'fsdp','row','core'}, dimensions={1}, use_global_device_ids=true | all-gather | bytes 18432 | tf_op jit(solution)/shard_map/all_gather | solution.py:837
  39.4 9.4 %all_gather.27 = bf16[2048,16]{0,1:T(8,128)(2,1)S(1)} all-gather(bf16[256,16]{0,1:T(8,128)(2,1)S(1)} %copy-done.27), channel_id=1, replica_groups=mesh['fsdp'=2,'row'=2,'core'=2,'tp'=4] {'fsdp','row','core'}, dimensions={0}, use_global_device_ids=true | all-gather | bytes 73728 | tf_op jit(solution)/shard_map/all_gather | solution.py:838
  53.1 14.7 %all-gather.7.cloned.1.call-done = bf16[32,256,512]{2,1,0:T(8,128)(2,1)} async-done(((bf16[4,256,512]{2,1,0:T(8,128)(2,1)}), bf16[32,256,512]{2,1,0:T(8,128)(2,1)}) %all-gather.7.cloned.1.call-update) | async-done | bytes 8388624 | tf_op jit(solution)/shard_map/all_gather | solution.py:829
  68.4 10.4 %qkv.1 = (bf16[512,2048]{1,0:T(8,128)(2,1)}, f32[2,512,512]{2,1,0:T(8,128)}, bf16[512,512]{1,0:T(8,128)(2,1)}, f32[2,512,128]{2,1,0:T(8,128)}) custom-call(bf16[512,2048]{1,0:T(8,128)(2,1)} %bitcast.87, f32[1,2048]{1,0:T(1,128)} %get-tuple-element.450.g_ref, bf16[8,4,256,512]{3,2,1,0:T(8,128)(2,1)} %bitcast.67), custom_call_target="tpu_custom_call" | custom-call | flops 3221225472 | bytes 13107200 | tf_op jit(solution)/shard_map/qkv/pallas_call | solution.py:87
  89.4 4.4 prep.1
  95.7 17.4 %collective-permute-done.6.refs_6_ = bf16[512,512]{1,0:T(8,128)(2,1)S(1)} collective-permute-done((bf16[512,512]{1,0:T(8,128)(2,1)}, bf16[512,512]{1,0:T(8,128)(2,1)S(1)}, u32[]{:S(2)}, u32[]{:S(2)}) %collective-permute-start.6) | collective-permute-done | bytes 524320 | tf_op jit(solution)/shard_map/ppermute | solution.py:711
  113.1 21.9 %collective-permute-done.3.refs_2_ = bf16[512,512]{1,0:T(8,128)(2,1)} collective-permute-done((bf16[512,512]{1,0:T(8,128)(2,1)}, bf16[512,512]{1,0:T(8,128)(2,1)}, u32[]{:S(2)}, u32[]{:S(2)}) %collective-permute-start.3) | collective-permute-done | bytes 524320 | tf_op jit(solution)/shard_map/ppermute | solution.py:711
  137.2 9.9 %attend.1.h_ref = bf16[512,512]{1,0:T(8,128)(2,1)} custom-call(s32[7]{0:T(128)} %pad_add_fusion.scal_ref, bf16[512,512]{1,0:T(8,128)(2,1)} %get-tuple-element.376.q_ref, bf16[512,512]{1,0:T(8,128)(2,1)} %get-tuple-element.377.refs_0_, bf16[512,512]{1,0:T(8,128)(2,1)} %collective-permute-done.2.refs_1_, bf16[512,512]{1,0:T(8,128)(2,1)} %collective-permute-done.3.refs_2_, ...), custom_call_target="tpu_custom_call" | custom-call | flops 1073741824 | bytes 6291456 | tf_op jit(solution)/shard_map/attend/pallas_call | solution.py:171
  147.1 5.4 outproj.1
  154.6 12.9 %collective-permute-done.9 = bf16[128,2048]{1,0:T(8,128)(2,1)S(1)} collective-permute-done((bf16[128,2048]{1,0:T(8,128)(2,1)}, bf16[128,2048]{1,0:T(8,128)(2,1)S(1)}, u32[]{:S(2)}, u32[]{:S(2)}) %collective-permute-start.9) | collective-permute-done | bytes 524320 | tf_op jit(solution)/shard_map/ppermute | solution.py:721
  172.9 11.9 %collective-permute-done.8.b_ref = bf16[128,2048]{1,0:T(8,128)(2,1)S(1)} collective-permute-done((bf16[128,2048]{1,0:T(8,128)(2,1)}, bf16[128,2048]{1,0:T(8,128)(2,1)S(1)}, u32[]{:S(2)}, u32[]{:S(2)}) %collective-permute-start.8) | collective-permute-done | bytes 524320 | tf_op jit(solution)/shard_map/ppermute | solution.py:721
  184.8 8.7 %collective-permute-done.10.c_ref = bf16[128,2048]{1,0:T(8,128)(2,1)} collective-permute-done((bf16[128,2048]{1,0:T(8,128)(2,1)S(1)}, bf16[128,2048]{1,0:T(8,128)(2,1)}, u32[]{:S(2)}, u32[]{:S(2)}) %collective-permute-start.10) | collective-permute-done | bytes 524320 | tf_op jit(solution)/shard_map/ppermute | solution.py:721
  197.1 6.0 all_to_all.16
  205.2 14.4 %collective-permute-done.12 = bf16[128,2176]{1,0:T(8,128)(2,1)S(1)} collective-permute-done((bf16[128,2176]{1,0:T(8,128)(2,1)}, bf16[128,2176]{1,0:T(8,128)(2,1)S(1)}, u32[]{:S(2)}, u32[]{:S(2)}) %collective-permute-start.12) | collective-permute-done | bytes 557088 | tf_op jit(solution)/shard_map/ppermute | solution.py:721
  219.5 11.2 %collective-permute-done.11 = bf16[128,2176]{1,0:T(8,128)(2,1)S(1)} collective-permute-done((bf16[128,2176]{1,0:T(8,128)(2,1)S(1)}, bf16[128,2176]{1,0:T(8,128)(2,1)S(1)}, u32[]{:S(2)}, u32[]{:S(2)}) %collective-permute-start.11) | collective-permute-done | bytes 557088 | tf_op jit(solution)/shard_map/ppermute | solution.py:721
  230.7 11.2 %collective-permute-done.13 = bf16[128,2176]{1,0:T(8,128)(2,1)S(1)} collective-permute-done((bf16[128,2176]{1,0:T(8,128)(2,1)S(1)}, bf16[128,2176]{1,0:T(8,128)(2,1)S(1)}, u32[]{:S(2)}, u32[]{:S(2)}) %collective-permute-start.13) | collective-permute-done | bytes 557088 | tf_op jit(solution)/shard_map/ppermute | solution.py:721
  245.9 6.8 collective-permute-done.15.refs_3_
  253.0 15.1 %all-gather.9.cloned.1.call-done.refs_4_.refs_1_.refs_2_ = bf16[8,6,3,256,256]{4,3,2,1,0:T(8,128)(2,1)} async-done(((bf16[2,6,3,256,256]{4,3,2,1,0:T(8,128)(2,1)}), bf16[8,6,3,256,256]{4,3,2,1,0:T(8,128)(2,1)}) %all-gather.9.cloned.1.call-update) | async-done | bytes 18874384 | tf_op jit(solution)/shard_map/all_gather | solution.py:836
  268.1 28.1 %expert_up.2 = (bf16[1024,1536]{1,0:T(8,128)(2,1)}, bf16[1024,3072]{1,0:T(8,128)(2,1)}, f32[1024,128]{1,0:T(8,128)}) custom-call(s32[1]{0:T(128)} %bitcast.19.first_ref, bf16[512,2176]{1,0:T(8,128)(2,1)} %constant_dynamic-update-slice_fusion.refs_0_, bf16[512,2176]{1,0:T(8,128)(2,1)} %collective-permute-done.14.refs_1_, ...), custom_call_target="tpu_custom_call" | custom-call | flops 19327352832 | bytes 36700160 | tf_op jit(solution)/shard_map/expert_up/pallas_call | solution.py:438
  296.2 18.9 %expert_dx.2 = (bf16[512,2048]{1,0:T(8,128)(2,1)}, bf16[512,2048]{1,0:T(8,128)(2,1)}) custom-call(bf16[1024,3072]{1,0:T(8,128)(2,1)} %get-tuple-element.313.refs_0_.refs_5_, bf16[8,6,3,256,256]{4,3,2,1,0:T(8,128)(2,1)} %all-gather.9.cloned.1.call-done.refs_4_.refs_1_.refs_2_), custom_call_target="tpu_custom_call" | custom-call | flops 12884901888 | bytes 23068672 | tf_op jit(solution)/shard_map/expert_dx/pallas_call | solution.py:562
  315.1 27.0 %expert_grad.2 = bf16[8,6,3,256,256]{4,3,2,1,0:T(8,128)(2,1)} custom-call(bf16[512,2176]{1,0:T(8,128)(2,1)} %constant_dynamic-update-slice_fusion.refs_0_, bf16[512,2176]{1,0:T(8,128)(2,1)} %collective-permute-done.14.refs_1_, bf16[512,2048]{1,0:T(8,128)(2,1)} %pad_maximum_fusion.refs_2_, bf16[512,2048]{1,0:T(8,128)(2,1)} %collective-permute-done.15.refs_3_, ...), custom_call_target="tpu_custom_call" | custom-call | flops 19327352832 | bytes 36700160 | tf_op jit(solution)/shard_map/expert_grad/pallas_call | solution.py:477
  342.4 13.3 %expert_up.3 = (bf16[1024,512]{1,0:T(8,128)(2,1)}, bf16[1024,1024]{1,0:T(8,128)(2,1)}, f32[1024,128]{1,0:T(8,128)}) custom-call(s32[1]{0:T(128)} %bitcast.22.first_ref, bf16[512,2176]{1,0:T(8,128)(2,1)} %constant_dynamic-update-slice_fusion.refs_0_, bf16[512,2176]{1,0:T(8,128)(2,1)} %collective-permute-done.14.refs_1_, ...), custom_call_target="tpu_custom_call" | custom-call | flops 6442450944 | bytes 17825792 | tf_op jit(solution)/shard_map/expert_up/pallas_call | solution.py:438
  355.8 10.5 %expert_dx.3 = (bf16[512,2176]{1,0:T(8,128)(2,1)}, bf16[512,2176]{1,0:T(8,128)(2,1)}) custom-call(bf16[1024,1024]{1,0:T(8,128)(2,1)} %get-tuple-element.351.refs_0_.refs_5_, bf16[8,2,3,256,256]{4,3,2,1,0:T(8,128)(2,1)} %all-gather.11.cloned.1.call-done.refs_4_.refs_1_.refs_3_, f32[1024,128]{1,0:T(8,128)} %get-tuple-element.325.refs_2_, ...), custom_call_target="tpu_custom_call" | custom-call | flops 4294967296 | bytes 10747904 | tf_op jit(solution)/shard_map/expert_dx/pallas_call | solution.py:562
  372.6 13.2 %collective-permute-done.17 = bf16[128,2176]{1,0:T(8,128)(2,1)S(1)} collective-permute-done((bf16[128,2176]{1,0:T(8,128)(2,1)S(1)}, bf16[128,2176]{1,0:T(8,128)(2,1)S(1)}, u32[]{:S(2)}, u32[]{:S(2)}) %collective-permute-start.17) | collective-permute-done | bytes 557088 | tf_op jit(solution)/shard_map/ppermute | solution.py:721
  391.1 13.7 %expert_out.1 = (bf16[512,2048]{1,0:T(8,128)(2,1)}, bf16[512,2048]{1,0:T(8,128)(2,1)}) custom-call(bf16[1024,1536]{1,0:T(8,128)(2,1)} %get-tuple-element.340.refs_4_.refs_0_, bf16[1024,512]{1,0:T(8,128)(2,1)} %get-tuple-element.350.refs_1_.refs_4_, bf16[8,6,3,256,256]{4,3,2,1,0:T(8,128)(2,1)} %all-gather.9.cloned.1.call-done.refs_4_.refs_1_.refs_2_, ...), custom_call_target="tpu_custom_call" | custom-call | flops 8589934592 | bytes 16777216 | tf_op jit(solution)/shard_map/expert_out/pallas_call | solution.py:562
  404.9 13.1 %expert_grad.3 = bf16[8,2,3,256,256]{4,3,2,1,0:T(8,128)(2,1)} custom-call(bf16[512,2176]{1,0:T(8,128)(2,1)} %constant_dynamic-update-slice_fusion.refs_0_, bf16[512,2176]{1,0:T(8,128)(2,1)} %collective-permute-done.14.refs_1_, bf16[512,2048]{1,0:T(8,128)(2,1)} %pad_maximum_fusion.refs_2_, bf16[512,2048]{1,0:T(8,128)(2,1)} %collective-permute-done.15.refs_3_, ...), custom_call_target="tpu_custom_call" | custom-call | flops 6442450944 | bytes 17825792 | tf_op jit(solution)/shard_map/expert_grad/pallas_call | solution.py:477
  419.6 4.5 norm_two_back.1
  425.3 25.6 %collective-permute-done.22 = bf16[128,2048]{1,0:T(8,128)(2,1)S(1)} collective-permute-done((bf16[128,2048]{1,0:T(8,128)(2,1)}, bf16[128,2048]{1,0:T(8,128)(2,1)S(1)}, u32[]{:S(2)}, u32[]{:S(2)}) %collective-permute-start.22) | collective-permute-done | bytes 524320 | tf_op jit(solution)/shard_map/ppermute | solution.py:721
  451.2 13.7 %collective-permute-done.23 = bf16[128,2048]{1,0:T(8,128)(2,1)S(1)} collective-permute-done((bf16[128,2048]{1,0:T(8,128)(2,1)S(1)}, bf16[128,2048]{1,0:T(8,128)(2,1)S(1)}, u32[]{:S(2)}, u32[]{:S(2)}) %collective-permute-start.23) | collective-permute-done | bytes 524320 | tf_op jit(solution)/shard_map/ppermute | solution.py:721
  467.4 5.0 dheads.1.refs_8_
  473.0 13.2 %attend_back.1 = (f32[512,512]{1,0:T(8,128)}, bf16[2,512,512]{2,1,0:T(8,128)(2,1)}, bf16[2,512,512]{2,1,0:T(8,128)(2,1)}, bf16[2,512,512]{2,1,0:T(8,128)(2,1)}, bf16[2,512,512]{2,1,0:T(8,128)(2,1)}) custom-call(s32[7]{0:T(128)} %pad_add_fusion.scal_ref, bf16[512,512]{1,0:T(8,128)(2,1)} %get-tuple-element.376.q_ref, ...), custom_call_target="tpu_custom_call" | custom-call | flops 2684354560 | bytes 12582912 | tf_op jit(solution)/shard_map/attend_back/pallas_call | solution.py:209
  492.5 7.7 %gradout.1.kept_ref = bf16[8,4,256,512]{3,2,1,0:T(8,128)(2,1)} custom-call(s32[4]{0:T(128)} %copy-done.24, bf16[512,2048]{1,0:T(8,128)(2,1)} %copy-done.1, bf16[512,512]{1,0:T(8,128)(2,1)} %attend.1.h_ref), custom_call_target="tpu_custom_call" | custom-call | flops 1073741824 | bytes 4718592 | tf_op jit(solution)/shard_map/gradout/pallas_call | solution.py:288
  500.1 12.2 %collective-permute-done.25 = bf16[128,2048]{1,0:T(8,128)(2,1)S(1)} collective-permute-done((bf16[128,2048]{1,0:T(8,128)(2,1)}, bf16[128,2048]{1,0:T(8,128)(2,1)S(1)}, u32[]{:S(2)}, u32[]{:S(2)}) %collective-permute-start.25) | collective-permute-done | bytes 524320 | tf_op jit(solution)/shard_map/ppermute | solution.py:721
  518.1 16.7 %collective-permute-done.31 = bf16[2,512,512]{2,1,0:T(8,128)(2,1)S(1)} collective-permute-done((bf16[2,512,512]{2,1,0:T(8,128)(2,1)S(1)}, bf16[2,512,512]{2,1,0:T(8,128)(2,1)S(1)}, u32[]{:S(2)}, u32[]{:S(2)}) %collective-permute-start.31) | collective-permute-done | bytes 1048608 | tf_op jit(solution)/shard_map/ppermute | solution.py:711
  535.3 4.6 collective-permute-done.29.refs_2_
  542.0 6.0 unturn.1
  558.1 4.1 inplace.3
  564.3 10.9 %raw_back.1 = (bf16[512,1536]{1,0:T(8,128)(2,1)}, bf16[128,2048]{1,0:T(8,128)(2,1)}, bf16[128,2048]{1,0:T(8,128)(2,1)}, bf16[128,2048]{1,0:T(8,128)(2,1)}, bf16[128,2048]{1,0:T(8,128)(2,1)}) custom-call(s32[4]{0:T(128)} %copy-done.24, f32[2,512,512]{2,1,0:T(8,128)} %get-tuple-element.427.u_ref, f32[2,512,512]{2,1,0:T(8,128)} %get-tuple-element.428.raw_ref, ...), custom_call_target="tpu_custom_call" | custom-call | flops 3221225472 | bytes 13631488 | tf_op jit(solution)/shard_map/raw_back/pallas_call | solution.py:659
  577.2 18.7 %collective-permute-done.36 = bf16[128,2048]{1,0:T(8,128)(2,1)S(1)} collective-permute-done((bf16[128,2048]{1,0:T(8,128)(2,1)}, bf16[128,2048]{1,0:T(8,128)(2,1)S(1)}, u32[]{:S(2)}, u32[]{:S(2)}) %collective-permute-start.36) | collective-permute-done | bytes 524320 | tf_op jit(solution)/shard_map/ppermute | solution.py:721
  598.2 9.3 %qkv_grad.1 = bf16[8,4,256,512]{3,2,1,0:T(8,128)(2,1)} custom-call(bf16[512,2048]{1,0:T(8,128)(2,1)} %get-tuple-element.441.n_ref, bf16[512,1536]{1,0:T(8,128)(2,1)} %get-tuple-element.442.d_ref, bf16[8,4,256,512]{3,2,1,0:T(8,128)(2,1)} %gradout.1.kept_ref), custom_call_target="tpu_custom_call", output_to_operand_aliasing={{}: (2, {})} | custom-call | flops 3221225472 | bytes 9961472 | tf_op jit(solution)/shard_map/qkv_grad/pallas_call | solution.py:693
  607.4 4.2 dynamic-slice_bitcast_fusion
  611.6 5.1 collective-permute-done.37.c_ref
  627.3 8.7 %settle.2 = (f32[16,2,256,256]{3,2,1,0:T(8,128)}, f32[16,256,256]{2,1,0:T(8,128)}) custom-call(s32[6]{0:T(128)} %pad_add_fusion.1.spot_ref, bf16[6,3,256,256]{3,2,1,0:T(8,128)(2,1)} %get-tuple-element.459.refs_0_, bf16[6,3,256,256]{3,2,1,0:T(8,128)(2,1)} %collective-permute-done.41.refs_1_), custom_call_target="tpu_custom_call" | custom-call | bytes 14155776 | tf_op jit(solution)/shard_map/settle/pallas_call | solution.py:508
  636.0 8.0 %collective-permute-done.40.refs_1_ = bf16[128,2048]{1,0:T(8,128)(2,1)S(1)} collective-permute-done((bf16[128,2048]{1,0:T(8,128)(2,1)S(1)}, bf16[128,2048]{1,0:T(8,128)(2,1)S(1)}, u32[]{:S(2)}, u32[]{:S(2)}) %collective-permute-start.40) | collective-permute-done | bytes 524320 | tf_op jit(solution)/shard_map/ppermute | solution.py:721
  654.1 7.6 %all-to-all-done.2 = f32[8,20,256]{2,1,0:T(8,128)S(1)} async-done(((f32[8,20,256]{2,1,0:T(8,128)}), f32[8,20,256]{2,1,0:T(8,128)S(1)}, u32[]{:S(2)}, u32[]{:S(2)}) %all-to-all-start.2) | async-done | bytes 163872 | tf_op jit(solution)/shard_map/all_to_all | solution.py:967
  665.3 3.8 settle.3
  675.2 17.6 %reduce-scatter.8.cloned.1.call-done = bf16[1,4,256,512]{3,2,1,0:T(8,128)(2,1)} async-done(((bf16[8,4,256,512]{3,2,1,0:T(8,128)(2,1)}), bf16[1,4,256,512]{3,2,1,0:T(8,128)(2,1)}) %reduce-scatter.8.cloned.1.call-update) | async-done | bytes 1048592 | tf_op jit(solution)/shard_map/reduce_scatter | solution.py:959
  (229 shorter events, 125.9 us)
Async XLA Ops:
  7.2 60.6 %all-gather.7.cloned.1.call-start = ((), (), s32[]{:S(2)}) async-start(), calls=%async_computation.7 | async-start | bytes 9437184 | tf_op jit(solution)/shard_map/all_gather | solution.py:829
  9.7 258.4 %all-gather.9.cloned.1.call-start = ((), (), s32[]{:S(2)}) async-start(), calls=%async_computation.8 | async-start | bytes 23592960 | tf_op jit(solution)/shard_map/all_gather | solution.py:836
  20.5 322.0 %all-gather.11.cloned.1.call-start = ((), (), s32[]{:S(2)}) async-start(), calls=%async_computation.9 | async-start | bytes 7864320 | tf_op jit(solution)/shard_map/all_gather | solution.py:836
  83.9 4.5 collective-permute-start.1
  86.9 26.2 %collective-permute-start.6 = (bf16[512,512]{1,0:T(8,128)(2,1)}, bf16[512,512]{1,0:T(8,128)(2,1)S(1)}, u32[]{:S(2)}, u32[]{:S(2)}) collective-permute-start(bf16[512,512]{1,0:T(8,128)(2,1)} %get-tuple-element.381.refs_4_), channel_id=1, source_target_pairs={{0,8},{8,0},{1,9},{9,1},{2,10},{10,2},{3,11},{11,3},{4,12},{12,4},... | collective-permute-start | bytes 1572872 | tf_op jit(solution)/shard_map/ppermute | solution.py:711
  93.8 41.1 %collective-permute-start.3 = (bf16[512,512]{1,0:T(8,128)(2,1)}, bf16[512,512]{1,0:T(8,128)(2,1)}, u32[]{:S(2)}, u32[]{:S(2)}) collective-permute-start(bf16[512,512]{1,0:T(8,128)(2,1)} %get-tuple-element.377.refs_0_), channel_id=1, source_target_pairs={{0,8},{8,0},{1,9},{9,1},{2,10},{10,2},{3,11},{11,3},{4,12},{12,4},... | collective-permute-start | bytes 1572872 | tf_op jit(solution)/shard_map/ppermute | solution.py:711
  95.1 40.6 %collective-permute-start.5 = (bf16[512,512]{1,0:T(8,128)(2,1)S(1)}, bf16[512,512]{1,0:T(8,128)(2,1)}, u32[]{:S(2)}, u32[]{:S(2)}) collective-permute-start(bf16[512,512]{1,0:T(8,128)(2,1)S(1)} %copy-done.21), channel_id=1, source_target_pairs={{0,4},{4,0},{1,5},{5,1},{2,6},{6,2},{3,7},{7,3},{8,12},{12,8},{9,1... | collective-permute-start | bytes 1572872 | tf_op jit(solution)/shard_map/ppermute | solution.py:711
  95.1 40.6 %collective-permute-start.2 = (bf16[512,512]{1,0:T(8,128)(2,1)}, bf16[512,512]{1,0:T(8,128)(2,1)}, u32[]{:S(2)}, u32[]{:S(2)}) collective-permute-start(bf16[512,512]{1,0:T(8,128)(2,1)} %get-tuple-element.377.refs_0_), channel_id=1, source_target_pairs={{0,4},{4,0},{1,5},{5,1},{2,6},{6,2},{3,7},{7,3},{8,12},{12,8},{9,1... | collective-permute-start | bytes 1572872 | tf_op jit(solution)/shard_map/ppermute | solution.py:711
  113.1 22.6 %collective-permute-start.7 = (bf16[512,512]{1,0:T(8,128)(2,1)S(1)}, bf16[512,512]{1,0:T(8,128)(2,1)}, u32[]{:S(2)}, u32[]{:S(2)}) collective-permute-start(bf16[512,512]{1,0:T(8,128)(2,1)S(1)} %collective-permute-done.6.refs_6_), channel_id=1, source_target_pairs={{0,4},{4,0},{1,5},{5,1},{2,6},{6,2},{3,7},{7,3},{8,12},{12,8},{9,1... | collective-permute-start | bytes 1572872 | tf_op jit(solution)/shard_map/ppermute | solution.py:711
  152.5 15.0 %collective-permute-start.9 = (bf16[128,2048]{1,0:T(8,128)(2,1)}, bf16[128,2048]{1,0:T(8,128)(2,1)S(1)}, u32[]{:S(2)}, u32[]{:S(2)}) collective-permute-start(bf16[128,2048]{1,0:T(8,128)(2,1)} %get-tuple-element.275), channel_id=1, source_target_pairs={{0,1},{1,0},{2,3},{3,2},{4,5},{5,4},{6,7},{7,6},{8,9},{9,8},{10,11... | collective-permute-start | bytes 1572872 | tf_op jit(solution)/shard_map/ppermute | solution.py:721
  154.0 30.8 %collective-permute-start.8 = (bf16[128,2048]{1,0:T(8,128)(2,1)}, bf16[128,2048]{1,0:T(8,128)(2,1)S(1)}, u32[]{:S(2)}, u32[]{:S(2)}) collective-permute-start(bf16[128,2048]{1,0:T(8,128)(2,1)} %get-tuple-element.273), channel_id=1, source_target_pairs={{0,1},{1,0},{2,3},{3,2},{4,5},{5,4},{6,7},{7,6},{8,9},{9,8},{10,11... | collective-permute-start | bytes 1572872 | tf_op jit(solution)/shard_map/ppermute | solution.py:721
  168.8 24.7 %collective-permute-start.10 = (bf16[128,2048]{1,0:T(8,128)(2,1)S(1)}, bf16[128,2048]{1,0:T(8,128)(2,1)}, u32[]{:S(2)}, u32[]{:S(2)}) collective-permute-start(bf16[128,2048]{1,0:T(8,128)(2,1)S(1)} %add_convert_fusion.10), channel_id=1, source_target_pairs={{0,2},{1,3},{2,0},{3,1},{4,6},{5,7},{6,4},{7,5},{8,10},{9,11},{10,... | collective-permute-start | bytes 1572872 | tf_op jit(solution)/shard_map/ppermute | solution.py:721
  196.9 22.6 %collective-permute-start.12 = (bf16[128,2176]{1,0:T(8,128)(2,1)}, bf16[128,2176]{1,0:T(8,128)(2,1)S(1)}, u32[]{:S(2)}, u32[]{:S(2)}) collective-permute-start(bf16[128,2176]{1,0:T(8,128)(2,1)} %get-tuple-element.356.ext_ref), channel_id=1, source_target_pairs={{0,2},{1,3},{2,0},{3,1},{4,6},{5,7},{6,4},{7,5},{8,10},{9,11},{10,... | collective-permute-start | bytes 1671176 | tf_op jit(solution)/shard_map/ppermute | solution.py:721
  203.1 404.3 %reduce-scatter.10.cloned.1.call-start = ((), (), s32[]{:S(2)}) async-start(), calls=%async_computation.10 | async-start | bytes 23592960
  203.4 27.4 %collective-permute-start.11 = (bf16[128,2176]{1,0:T(8,128)(2,1)S(1)}, bf16[128,2176]{1,0:T(8,128)(2,1)S(1)}, u32[]{:S(2)}, u32[]{:S(2)}) collective-permute-start(bf16[128,2176]{1,0:T(8,128)(2,1)S(1)} %copy-done.5), channel_id=1, source_target_pairs={{0,1},{1,0},{2,3},{3,2},{4,5},{5,4},{6,7},{7,6},{8,9},{9,8},{10,11... | collective-permute-start | bytes 1671176 | tf_op jit(solution)/shard_map/ppermute | solution.py:721
  219.5 22.3 %collective-permute-start.13 = (bf16[128,2176]{1,0:T(8,128)(2,1)S(1)}, bf16[128,2176]{1,0:T(8,128)(2,1)S(1)}, u32[]{:S(2)}, u32[]{:S(2)}) collective-permute-start(bf16[128,2176]{1,0:T(8,128)(2,1)S(1)} %collective-permute-done.12), channel_id=1, source_target_pairs={{0,1},{1,0},{2,3},{3,2},{4,5},{5,4},{6,7},{7,6},{8,9},{9,8},{10,11... | collective-permute-start | bytes 1671176 | tf_op jit(solution)/shard_map/ppermute | solution.py:721
  245.3 7.7 %collective-permute-start.14 = (bf16[512,2176]{1,0:T(8,128)(2,1)}, bf16[512,2176]{1,0:T(8,128)(2,1)}, u32[]{:S(2)}, u32[]{:S(2)}) collective-permute-start(bf16[512,2176]{1,0:T(8,128)(2,1)} %constant_dynamic-update-slice_fusion.refs_0_), channel_id=1, source_target_pairs={{0,4},{4,0},{1,5},{5,1},{2,6},{6,2},{3,7},{7,3},{8,12},{12,8},{9,1... | collective-permute-start | bytes 6684680 | tf_op jit(solution)/shard_map/ppermute | solution.py:711
  245.3 7.3 %collective-permute-start.15 = (bf16[512,2048]{1,0:T(8,128)(2,1)S(1)}, bf16[512,2048]{1,0:T(8,128)(2,1)}, u32[]{:S(2)}, u32[]{:S(2)}) collective-permute-start(bf16[512,2048]{1,0:T(8,128)(2,1)S(1)} %copy-done.7), channel_id=1, source_target_pairs={{0,4},{4,0},{1,5},{5,1},{2,6},{6,2},{3,7},{7,3},{8,12},{12,8},{9,1... | collective-permute-start | bytes 6291464 | tf_op jit(solution)/shard_map/ppermute | solution.py:711
  342.1 281.6 %reduce-scatter.12.cloned.1.call-start = ((), (), s32[]{:S(2)}) async-start(), calls=%async_computation.11 | async-start | bytes 7864320
  366.2 4.6 collective-permute-start.16
  371.1 14.7 %collective-permute-start.17 = (bf16[128,2176]{1,0:T(8,128)(2,1)S(1)}, bf16[128,2176]{1,0:T(8,128)(2,1)S(1)}, u32[]{:S(2)}, u32[]{:S(2)}) collective-permute-start(bf16[128,2176]{1,0:T(8,128)(2,1)S(1)} %add_convert_fusion.4), channel_id=1, source_target_pairs={{0,1},{1,0},{2,3},{3,2},{4,5},{5,4},{6,7},{7,6},{8,9},{9,8},{10,11... | collective-permute-start | bytes 1671176 | tf_op jit(solution)/shard_map/ppermute | solution.py:721
  386.0 32.0 %collective-permute-start.20 = (bf16[128,2176]{1,0:T(8,128)(2,1)S(1)}, bf16[128,2176]{1,0:T(8,128)(2,1)S(1)}, u32[]{:S(2)}, u32[]{:S(2)}) collective-permute-start(bf16[128,2176]{1,0:T(8,128)(2,1)S(1)} %add_convert_fusion.3), channel_id=1, source_target_pairs={{0,2},{1,3},{2,0},{3,1},{4,6},{5,7},{6,4},{7,5},{8,10},{9,11},{10,... | collective-permute-start | bytes 1671176 | tf_op jit(solution)/shard_map/ppermute | solution.py:721
  388.6 29.3 %collective-permute-start.19 = (bf16[128,2176]{1,0:T(8,128)(2,1)S(1)}, bf16[128,2176]{1,0:T(8,128)(2,1)S(1)}, u32[]{:S(2)}, u32[]{:S(2)}) collective-permute-start(bf16[128,2176]{1,0:T(8,128)(2,1)S(1)} %add_convert_fusion.2), channel_id=1, source_target_pairs={{0,1},{1,0},{2,3},{3,2},{4,5},{5,4},{6,7},{7,6},{8,9},{9,8},{10,11... | collective-permute-start | bytes 1671176 | tf_op jit(solution)/shard_map/ppermute | solution.py:721
  404.9 60.2 %collective-permute-start.18 = (bf16[512,2048]{1,0:T(8,128)(2,1)}, bf16[512,2048]{1,0:T(8,128)(2,1)S(1)}, u32[]{:S(2)}, u32[]{:S(2)}) collective-permute-start(bf16[512,2048]{1,0:T(8,128)(2,1)} %get-tuple-element.345), channel_id=1, source_target_pairs={{0,4},{4,0},{1,5},{5,1},{2,6},{6,2},{3,7},{7,3},{8,12},{12,8},{9,1... | collective-permute-start | bytes 6291464 | tf_op jit(solution)/shard_map/ppermute | solution.py:711
  424.1 26.9 %collective-permute-start.22 = (bf16[128,2048]{1,0:T(8,128)(2,1)}, bf16[128,2048]{1,0:T(8,128)(2,1)S(1)}, u32[]{:S(2)}, u32[]{:S(2)}) collective-permute-start(bf16[128,2048]{1,0:T(8,128)(2,1)} %get-tuple-element.366), channel_id=1, source_target_pairs={{0,2},{1,3},{2,0},{3,1},{4,6},{5,7},{6,4},{7,5},{8,10},{9,11},{10,... | collective-permute-start | bytes 1572872 | tf_op jit(solution)/shard_map/ppermute | solution.py:721
  425.3 25.8 %collective-permute-start.21 = (bf16[128,2048]{1,0:T(8,128)(2,1)}, bf16[128,2048]{1,0:T(8,128)(2,1)S(1)}, u32[]{:S(2)}, u32[]{:S(2)}) collective-permute-start(bf16[128,2048]{1,0:T(8,128)(2,1)} %get-tuple-element.366), channel_id=1, source_target_pairs={{0,1},{1,0},{2,3},{3,2},{4,5},{5,4},{6,7},{7,6},{8,9},{9,8},{10,11... | collective-permute-start | bytes 1572872 | tf_op jit(solution)/shard_map/ppermute | solution.py:721
  451.0 13.9 %collective-permute-start.23 = (bf16[128,2048]{1,0:T(8,128)(2,1)S(1)}, bf16[128,2048]{1,0:T(8,128)(2,1)S(1)}, u32[]{:S(2)}, u32[]{:S(2)}) collective-permute-start(bf16[128,2048]{1,0:T(8,128)(2,1)S(1)} %collective-permute-done.22), channel_id=1, source_target_pairs={{0,1},{1,0},{2,3},{3,2},{4,5},{5,4},{6,7},{7,6},{8,9},{9,8},{10,11... | collective-permute-start | bytes 1572872 | tf_op jit(solution)/shard_map/ppermute | solution.py:721
  472.4 220.3 %reduce-scatter.8.cloned.1.call-start = ((), (), s32[]{:S(2)}) async-start(), calls=%async_computation.6 | async-start | bytes 9437184 | tf_op jit(solution)/shard_map/reduce_scatter | solution.py:959
  472.7 14.0 %collective-permute-start.24 = (bf16[128,2048]{1,0:T(8,128)(2,1)}, bf16[128,2048]{1,0:T(8,128)(2,1)S(1)}, u32[]{:S(2)}, u32[]{:S(2)}) collective-permute-start(bf16[128,2048]{1,0:T(8,128)(2,1)} %add_convert_fusion.9), channel_id=1, source_target_pairs={{0,1},{1,0},{2,3},{3,2},{4,5},{5,4},{6,7},{7,6},{8,9},{9,8},{10,11... | collective-permute-start | bytes 1572872 | tf_op jit(solution)/shard_map/ppermute | solution.py:721
  486.3 31.8 %collective-permute-start.30 = (bf16[2,512,512]{2,1,0:T(8,128)(2,1)}, bf16[2,512,512]{2,1,0:T(8,128)(2,1)S(1)}, u32[]{:S(2)}, u32[]{:S(2)}) collective-permute-start(bf16[2,512,512]{2,1,0:T(8,128)(2,1)} %get-tuple-element.388), channel_id=1, source_target_pairs={{0,4},{4,0},{1,5},{5,1},{2,6},{6,2},{3,7},{7,3},{8,12},{12,8},{9,1... | collective-permute-start | bytes 3145736 | tf_op jit(solution)/shard_map/ppermute | solution.py:711
  487.8 26.3 %collective-permute-start.26 = (bf16[128,2048]{1,0:T(8,128)(2,1)}, bf16[128,2048]{1,0:T(8,128)(2,1)S(1)}, u32[]{:S(2)}, u32[]{:S(2)}) collective-permute-start(bf16[128,2048]{1,0:T(8,128)(2,1)} %add_convert_fusion.8), channel_id=1, source_target_pairs={{0,2},{1,3},{2,0},{3,1},{4,6},{5,7},{6,4},{7,5},{8,10},{9,11},{10,... | collective-permute-start | bytes 1572872 | tf_op jit(solution)/shard_map/ppermute | solution.py:721
  490.3 22.1 %collective-permute-start.25 = (bf16[128,2048]{1,0:T(8,128)(2,1)}, bf16[128,2048]{1,0:T(8,128)(2,1)S(1)}, u32[]{:S(2)}, u32[]{:S(2)}) collective-permute-start(bf16[128,2048]{1,0:T(8,128)(2,1)} %add_convert_fusion.7), channel_id=1, source_target_pairs={{0,1},{1,0},{2,3},{3,2},{4,5},{5,4},{6,7},{7,6},{8,9},{9,8},{10,11... | collective-permute-start | bytes 1572872 | tf_op jit(solution)/shard_map/ppermute | solution.py:721
  490.9 43.9 %collective-permute-start.31 = (bf16[2,512,512]{2,1,0:T(8,128)(2,1)S(1)}, bf16[2,512,512]{2,1,0:T(8,128)(2,1)S(1)}, u32[]{:S(2)}, u32[]{:S(2)}) collective-permute-start(bf16[2,512,512]{2,1,0:T(8,128)(2,1)S(1)} %add_convert_fusion), channel_id=1, source_target_pairs={{0,8},{8,0},{1,9},{9,1},{2,10},{10,2},{3,11},{11,3},{4,12},{12,4},... | collective-permute-start | bytes 3145736 | tf_op jit(solution)/shard_map/ppermute | solution.py:711
  514.5 25.4 %collective-permute-start.29 = (bf16[128,2048]{1,0:T(8,128)(2,1)S(1)}, bf16[128,2048]{1,0:T(8,128)(2,1)S(1)}, u32[]{:S(2)}, u32[]{:S(2)}) collective-permute-start(bf16[128,2048]{1,0:T(8,128)(2,1)S(1)} %add_convert_fusion.6.refs_0_), channel_id=1, source_target_pairs={{0,2},{1,3},{2,0},{3,1},{4,6},{5,7},{6,4},{7,5},{8,10},{9,11},{10,... | collective-permute-start | bytes 1572872 | tf_op jit(solution)/shard_map/ppermute | solution.py:721
  516.4 41.7 %collective-permute-start.28 = (bf16[128,2048]{1,0:T(8,128)(2,1)S(1)}, bf16[128,2048]{1,0:T(8,128)(2,1)}, u32[]{:S(2)}, u32[]{:S(2)}) collective-permute-start(bf16[128,2048]{1,0:T(8,128)(2,1)S(1)} %add_convert_fusion.6.refs_0_), channel_id=1, source_target_pairs={{0,1},{1,0},{2,3},{3,2},{4,5},{5,4},{6,7},{7,6},{8,9},{9,8},{10,11... | collective-permute-start | bytes 1572872 | tf_op jit(solution)/shard_map/ppermute | solution.py:721
  539.8 18.2 %collective-permute-start.32 = (bf16[128,2048]{1,0:T(8,128)(2,1)S(1)}, bf16[128,2048]{1,0:T(8,128)(2,1)}, u32[]{:S(2)}, u32[]{:S(2)}) collective-permute-start(bf16[128,2048]{1,0:T(8,128)(2,1)S(1)} %collective-permute-done.29.refs_2_), channel_id=1, source_target_pairs={{0,1},{1,0},{2,3},{3,2},{4,5},{5,4},{6,7},{7,6},{8,9},{9,8},{10,11... | collective-permute-start | bytes 1572872 | tf_op jit(solution)/shard_map/ppermute | solution.py:721
  553.6 4.5 collective-permute-start.34
  575.2 20.7 %collective-permute-start.36 = (bf16[128,2048]{1,0:T(8,128)(2,1)}, bf16[128,2048]{1,0:T(8,128)(2,1)S(1)}, u32[]{:S(2)}, u32[]{:S(2)}) collective-permute-start(bf16[128,2048]{1,0:T(8,128)(2,1)} %get-tuple-element.437), channel_id=1, source_target_pairs={{0,1},{1,0},{2,3},{3,2},{4,5},{5,4},{6,7},{7,6},{8,9},{9,8},{10,11... | collective-permute-start | bytes 1572872 | tf_op jit(solution)/shard_map/ppermute | solution.py:721
  576.5 35.1 %collective-permute-start.35 = (bf16[128,2048]{1,0:T(8,128)(2,1)}, bf16[128,2048]{1,0:T(8,128)(2,1)S(1)}, u32[]{:S(2)}, u32[]{:S(2)}) collective-permute-start(bf16[128,2048]{1,0:T(8,128)(2,1)} %get-tuple-element.435), channel_id=1, source_target_pairs={{0,1},{1,0},{2,3},{3,2},{4,5},{5,4},{6,7},{7,6},{8,9},{9,8},{10,11... | collective-permute-start | bytes 1572872 | tf_op jit(solution)/shard_map/ppermute | solution.py:721
  597.0 19.6 %collective-permute-start.37 = (bf16[128,2048]{1,0:T(8,128)(2,1)S(1)}, bf16[128,2048]{1,0:T(8,128)(2,1)}, u32[]{:S(2)}, u32[]{:S(2)}) collective-permute-start(bf16[128,2048]{1,0:T(8,128)(2,1)S(1)} %add_convert_fusion.5), channel_id=1, source_target_pairs={{0,2},{1,3},{2,0},{3,1},{4,6},{5,7},{6,4},{7,5},{8,10},{9,11},{10,... | collective-permute-start | bytes 1572872 | tf_op jit(solution)/shard_map/ppermute | solution.py:721
  620.3 7.0 collective-permute-start.41
  621.6 22.4 %collective-permute-start.40 = (bf16[128,2048]{1,0:T(8,128)(2,1)S(1)}, bf16[128,2048]{1,0:T(8,128)(2,1)S(1)}, u32[]{:S(2)}, u32[]{:S(2)}) collective-permute-start(bf16[128,2048]{1,0:T(8,128)(2,1)S(1)} %copy-done.17), channel_id=1, source_target_pairs={{0,1},{1,0},{2,3},{3,2},{4,5},{5,4},{6,7},{7,6},{8,9},{9,8},{10,11... | collective-permute-start | bytes 1572872 | tf_op jit(solution)/shard_map/ppermute | solution.py:721
  623.8 26.1 %collective-permute-start.38 = (bf16[128,2048]{1,0:T(8,128)(2,1)S(1)}, bf16[128,2048]{1,0:T(8,128)(2,1)}, u32[]{:S(2)}, u32[]{:S(2)}) collective-permute-start(bf16[128,2048]{1,0:T(8,128)(2,1)S(1)} %copy-done.17), channel_id=1, source_target_pairs={{0,2},{1,3},{2,0},{3,1},{4,6},{5,7},{6,4},{7,5},{8,10},{9,11},{10,... | collective-permute-start | bytes 1572872 | tf_op jit(solution)/shard_map/ppermute | solution.py:721
  648.7 15.8 %collective-permute-start.43 = (bf16[2,3,256,256]{3,2,1,0:T(8,128)(2,1)S(1)}, bf16[2,3,256,256]{3,2,1,0:T(8,128)(2,1)S(1)}, u32[]{:S(2)}, u32[]{:S(2)}) collective-permute-start(bf16[2,3,256,256]{3,2,1,0:T(8,128)(2,1)S(1)} %get-tuple-element.506), channel_id=1, source_target_pairs={{0,4},{4,0},{1,5},{5,1},{2,6},{6,2},{3,7},{7,3},{8,12},{12,8},{9,1... | collective-permute-start | bytes 2359304 | tf_op jit(solution)/shard_map/ppermute | solution.py:711
  649.8 20.1 %collective-permute-start.39 = (bf16[128,2048]{1,0:T(8,128)(2,1)}, bf16[128,2048]{1,0:T(8,128)(2,1)S(1)}, u32[]{:S(2)}, u32[]{:S(2)}) collective-permute-start(bf16[128,2048]{1,0:T(8,128)(2,1)} %collective-permute-done.38.refs_0_), channel_id=1, source_target_pairs={{0,1},{1,0},{2,3},{3,2},{4,5},{5,4},{6,7},{7,6},{8,9},{9,8},{10,11... | collective-permute-start | bytes 1572872 | tf_op jit(solution)/shard_map/ppermute | solution.py:721
  650.6 11.1 %all-to-all-start.2 = ((f32[8,20,256]{2,1,0:T(8,128)}), f32[8,20,256]{2,1,0:T(8,128)S(1)}, u32[]{:S(2)}, u32[]{:S(2)}) async-start(f32[8,20,256]{2,1,0:T(8,128)} %bitcast.66), calls=%async_computation.2 | async-start | bytes 393216 | tf_op jit(solution)/shard_map/all_to_all | solution.py:967
  661.7 7.4 %collective-permute-start.42 = (f32[20,256]{1,0:T(8,128)S(1)}, f32[20,256]{1,0:T(8,128)S(1)}, u32[]{:S(2)}, u32[]{:S(2)}) collective-permute-start(f32[20,256]{1,0:T(8,128)S(1)} %reduce_sum.9), channel_id=1, source_target_pairs={{0,1},{1,0},{2,3},{3,2},{4,5},{5,4},{6,7},{7,6},{8,9},{9,8},{10,11... | collective-permute-start | bytes 61448 | tf_op jit(solution)/shard_map/ppermute | solution.py:721
  669.2 4.8 collective-permute-start.44
  (34 other events, 427.9 us)
Sparse Core Ops, SparseCore 0:
  10.5 57.2 all-gather.6
  69.6 198.4 all-gather.8
  269.9 70.1 all-gather.10
  343.1 189.5 reduce-scatter.9
  536.4 71.0 reduce-scatter.11
  620.5 72.2 reduce-scatter.7

commit v4 on v3

--- a/solution.py
+++ b/solution.py
@@ -859,6 +859,8 @@
     normed_one, raw, values, squares = line(qkv_project, x, gains[0:1], attn_w)
     v_blocks = spread(values)
     scales = lax.rsqrt(meet(squares[:, :, 0]) / width + EPSILON)[:, :, None]
+    scales, values = lax.optimization_barrier((scales, v_blocks[2]))
+    v_blocks = v_blocks[:2] + (values,) + v_blocks[3:]
     queries, keys = line(prepare, raw, scales, own_gains, cosine, sine)
     k_blocks = spread(keys)
     blocks = k_blocks + v_blocks
@@ -948,15 +950,14 @@
         raw_back, places, u, raw, scales, inner, own_gains, d_kv[1].astype(BF16), attn_w, tp
     )
     last = across(d_one[3], 1)
+    grad_attn = line(qkv_grads, normed_one, d_raw, grad_attn, p)
+    grad_attn = lax.psum_scatter(grad_attn, PLANE, scatter_dimension=0, tiled=False)
+    pairs = [parted(0)]
     near = line(add, d_one[2], last)
     d_one = [d_one[0], across(d_one[1], 1), across(near, 2)]
-    grad_attn = line(qkv_grads, normed_one, d_raw, grad_attn, p)
-    pairs = [parted(0)]
     grad_in, gain_one = line(norm_one_back, d_one, x_q, d_mid, gains[0:1])
     far = across(grad_in, 2)
     near = across(grad_in, 1)
-    grad_attn, gain_one = lax.optimization_barrier((grad_attn, gain_one))
-    grad_attn = lax.psum_scatter(grad_attn, PLANE, scatter_dimension=0, tiled=False)
     placed = lax.dynamic_update_slice_in_dim(
         jnp.zeros((2, width), F32), gain_qk[:, 0, :], column * n, 1
     )
@@ -974,6 +975,7 @@
     small = line(lambda a, b: a + b, small, other)
     other = across(small, 2)
     grad_inputs = line(in_place, places[2:], [far, both], [placed_in], t).reshape(inputs.shape)
+    grad_attn, grad_inputs = lax.optimization_barrier((grad_attn, grad_inputs))
     small = line(lambda a, b: a + b, small, other)
     owned_gains = small[experts:]
     owned_router = small[:experts].T

time: 714 us -> 701 us (0.982)
  waiting for transfers between devices: 302 us -> 281 us
  starting transfers between devices: 44.3 us -> 51.9 us
    reduce_scatter x1, waiting for transfers between devices: 17.6 us -> 0.69 us  [body(): lax.psum_scatter(grad_attn, PLANE, scatter_dimension=0, tiled=False)]
    ppermute x15, waiting for transfers between devices: 67.6 us -> 60.3 us  [swap(): return lax.ppermute(value, axis, [(0, 1), (1, 0)])]
  transfers between devices with their start and end apart: 52 -> 52, of which waited for: 32 -> 32; matrix products, arithmetic and copies ran while one was open for 7% -> 7% of each run, Pallas kernels for 34% -> 35%
where the time goes in v4:
time: 701 us; the launch traced here: 691 us
  waiting for transfers between devices  281 us (40%)
  Pallas kernels  240 us (34%)
  starting transfers between devices  51.9 us (7%)
  local copies, waits for them, and re-layouts  37.6 us (5%)
  blocking collectives  35.3 us (5%)
  between operations  22.9 us (3%)
  other arithmetic  22.8 us (3%)
    ppermute x30, waiting for transfers between devices, across(): return lax.ppermute(value, 'tp', [(i, i ^ k) for i in range(size)])  185 us
    ppermute x15, waiting for transfers between devices, swap(): return lax.ppermute(value, axis, [(0, 1), (1, 0)])  60.3 us
    pallas_call x3, Pallas kernels, expert_down(): call(functools.partial(down_kernel, planes=planes, chunks=chunks, sides=l...  43.1 us
    pallas_call x2, Pallas kernels, expert_up(): call(functools.partial(expert_kernel, parts=parts), 'expert_up', (e,), [f...  41.4 us
    ppermute x30, starting transfers between devices, across(): return lax.ppermute(value, 'tp', [(i, i ^ k) for i in range(size)])  41.2 us
    pallas_call x2, Pallas kernels, expert_grads(): call(functools.partial(expert_grad_kernel, parts=parts), 'expert_grad', (...  40.1 us
    all_gather x2, waiting for transfers between devices, body(): lax.all_gather(mine, FR, axis=0, tiled=False).reshape(-1, e, 3, ds, f)  15.7 us
    all_to_all x2, blocking collectives, body(): mine = lax.all_to_all(grouped[:, begin:begin + e], 'core', 0, 0, tiled=True)  14.5 us
  transfers between devices with their start and end apart: 52, of which 32 were waited for; matrix products, arithmetic and copies ran while one was open for 7% of the time, Pallas kernels for 35%

profile of v4, /device:TPU:0, one launch (start us, length us, event | category | flops | bytes accessed | tf_op | source)
XLA Modules:
  0.0 691.2 jit_solution(13510081817455019406)
XLA Ops:
  11.9 8.6 %all_to_all.15 = bf16[2,6,3,256,256]{4,3,2,1,0:T(8,128)(2,1)} all-to-all(bf16[2,6,3,256,256]{4,3,2,1,0:T(8,128)(2,1)S(1)} %fusion), channel_id=1, replica_groups=mesh['fsdp'=2,'row'=2,'core'=2,'tp'=4] {'core'}, dimensions={0} | all-to-all | bytes 9437184 | tf_op jit(solution)/shard_map/all_to_all | solution.py:835
  29.5 10.3 %all_gather.26 = bf16[4,2048]{1,0:T(4,128)(2,1)S(1)} all-gather(bf16[4,256]{1,0:T(4,128)(2,1)S(1)} %copy-done.31), channel_id=1, replica_groups=mesh['fsdp'=2,'row'=2,'core'=2,'tp'=4] {'fsdp','row','core'}, dimensions={1}, use_global_device_ids=true | all-gather | bytes 18432 | tf_op jit(solution)/shard_map/all_gather | solution.py:837
  39.9 10.4 %all_gather.27 = bf16[2048,16]{0,1:T(8,128)(2,1)} all-gather(bf16[256,16]{0,1:T(8,128)(2,1)S(1)} %copy-done.29), channel_id=1, replica_groups=mesh['fsdp'=2,'row'=2,'core'=2,'tp'=4] {'fsdp','row','core'}, dimensions={0}, use_global_device_ids=true | all-gather | bytes 73728 | tf_op jit(solution)/shard_map/all_gather | solution.py:838
  54.6 13.2 %all-gather.7.cloned.1.call-done = bf16[32,256,512]{2,1,0:T(8,128)(2,1)} async-done(((bf16[4,256,512]{2,1,0:T(8,128)(2,1)}), bf16[32,256,512]{2,1,0:T(8,128)(2,1)}) %all-gather.7.cloned.1.call-update) | async-done | bytes 8388624 | tf_op jit(solution)/shard_map/all_gather | solution.py:829
  68.4 10.4 %qkv.1 = (bf16[512,2048]{1,0:T(8,128)(2,1)}, f32[2,512,512]{2,1,0:T(8,128)}, bf16[512,512]{1,0:T(8,128)(2,1)}, f32[2,512,128]{2,1,0:T(8,128)}) custom-call(bf16[512,2048]{1,0:T(8,128)(2,1)} %bitcast.83, f32[1,2048]{1,0:T(1,128)} %get-tuple-element.454.g_ref, bf16[8,4,256,512]{3,2,1,0:T(8,128)(2,1)} %bitcast.61), custom_call_target="tpu_custom_call" | custom-call | flops 3221225472 | bytes 13107200 | tf_op jit(solution)/shard_map/qkv/pallas_call | solution.py:87
  91.1 9.7 %collective-permute-done.2.refs_6_ = bf16[512,512]{1,0:T(8,128)(2,1)S(1)} collective-permute-done((bf16[512,512]{1,0:T(8,128)(2,1)}, bf16[512,512]{1,0:T(8,128)(2,1)S(1)}, u32[]{:S(2)}, u32[]{:S(2)}) %collective-permute-start.2) | collective-permute-done | bytes 524320 | tf_op jit(solution)/shard_map/ppermute | solution.py:711
  101.8 4.4 prep.1
  108.8 22.9 %collective-permute-done.4.refs_2_ = bf16[512,512]{1,0:T(8,128)(2,1)} collective-permute-done((bf16[512,512]{1,0:T(8,128)(2,1)}, bf16[512,512]{1,0:T(8,128)(2,1)}, u32[]{:S(2)}, u32[]{:S(2)}) %collective-permute-start.4) | collective-permute-done | bytes 524320 | tf_op jit(solution)/shard_map/ppermute | solution.py:711
  134.0 9.9 %attend.1.h_ref = bf16[512,512]{1,0:T(8,128)(2,1)} custom-call(s32[7]{0:T(128)} %pad_add_fusion.scal_ref, bf16[512,512]{1,0:T(8,128)(2,1)} %get-tuple-element.380.q_ref, bf16[512,512]{1,0:T(8,128)(2,1)} %get-tuple-element.381.refs_0_, bf16[512,512]{1,0:T(8,128)(2,1)} %collective-permute-done.3.refs_1_, bf16[512,512]{1,0:T(8,128)(2,1)} %collective-permute-done.4.refs_2_, ...), custom_call_target="tpu_custom_call" | custom-call | flops 1073741824 | bytes 6291456 | tf_op jit(solution)/shard_map/attend/pallas_call | solution.py:171
  143.9 5.4 outproj.1
  151.4 12.9 %collective-permute-done.9 = bf16[128,2048]{1,0:T(8,128)(2,1)S(1)} collective-permute-done((bf16[128,2048]{1,0:T(8,128)(2,1)}, bf16[128,2048]{1,0:T(8,128)(2,1)S(1)}, u32[]{:S(2)}, u32[]{:S(2)}) %collective-permute-start.9) | collective-permute-done | bytes 524320 | tf_op jit(solution)/shard_map/ppermute | solution.py:721
  171.6 11.9 %collective-permute-done.8.b_ref = bf16[128,2048]{1,0:T(8,128)(2,1)S(1)} collective-permute-done((bf16[128,2048]{1,0:T(8,128)(2,1)}, bf16[128,2048]{1,0:T(8,128)(2,1)S(1)}, u32[]{:S(2)}, u32[]{:S(2)}) %collective-permute-start.8) | collective-permute-done | bytes 524320 | tf_op jit(solution)/shard_map/ppermute | solution.py:721
  183.5 6.8 collective-permute-done.10.c_ref
  193.9 6.0 all_to_all.16
  203.9 12.2 %collective-permute-done.12 = bf16[128,2176]{1,0:T(8,128)(2,1)S(1)} collective-permute-done((bf16[128,2176]{1,0:T(8,128)(2,1)}, bf16[128,2176]{1,0:T(8,128)(2,1)S(1)}, u32[]{:S(2)}, u32[]{:S(2)}) %collective-permute-start.12) | collective-permute-done | bytes 557088 | tf_op jit(solution)/shard_map/ppermute | solution.py:721
  216.9 8.8 %collective-permute-done.11 = bf16[128,2176]{1,0:T(8,128)(2,1)S(1)} collective-permute-done((bf16[128,2176]{1,0:T(8,128)(2,1)S(1)}, bf16[128,2176]{1,0:T(8,128)(2,1)S(1)}, u32[]{:S(2)}, u32[]{:S(2)}) %collective-permute-start.11) | collective-permute-done | bytes 557088 | tf_op jit(solution)/shard_map/ppermute | solution.py:721
  225.7 11.5 %collective-permute-done.13 = bf16[128,2176]{1,0:T(8,128)(2,1)S(1)} collective-permute-done((bf16[128,2176]{1,0:T(8,128)(2,1)S(1)}, bf16[128,2176]{1,0:T(8,128)(2,1)S(1)}, u32[]{:S(2)}, u32[]{:S(2)}) %collective-permute-start.13) | collective-permute-done | bytes 557088 | tf_op jit(solution)/shard_map/ppermute | solution.py:721
  241.1 6.8 collective-permute-done.15.refs_3_
  248.2 15.7 %all-gather.9.cloned.1.call-done.refs_4_.refs_1_.refs_2_ = bf16[8,6,3,256,256]{4,3,2,1,0:T(8,128)(2,1)} async-done(((bf16[2,6,3,256,256]{4,3,2,1,0:T(8,128)(2,1)}), bf16[8,6,3,256,256]{4,3,2,1,0:T(8,128)(2,1)}) %all-gather.9.cloned.1.call-update) | async-done | bytes 18874384 | tf_op jit(solution)/shard_map/all_gather | solution.py:836
  264.0 28.1 %expert_up.2 = (bf16[1024,1536]{1,0:T(8,128)(2,1)}, bf16[1024,3072]{1,0:T(8,128)(2,1)}, f32[1024,128]{1,0:T(8,128)}) custom-call(s32[1]{0:T(128)} %bitcast.19.first_ref, bf16[512,2176]{1,0:T(8,128)(2,1)} %constant_dynamic-update-slice_fusion.refs_0_, bf16[512,2176]{1,0:T(8,128)(2,1)} %collective-permute-done.14.refs_1_, ...), custom_call_target="tpu_custom_call" | custom-call | flops 19327352832 | bytes 36700160 | tf_op jit(solution)/shard_map/expert_up/pallas_call | solution.py:438
  292.0 18.9 %expert_dx.2 = (bf16[512,2048]{1,0:T(8,128)(2,1)}, bf16[512,2048]{1,0:T(8,128)(2,1)}) custom-call(bf16[1024,3072]{1,0:T(8,128)(2,1)} %get-tuple-element.317.refs_0_.refs_5_, bf16[8,6,3,256,256]{4,3,2,1,0:T(8,128)(2,1)} %all-gather.9.cloned.1.call-done.refs_4_.refs_1_.refs_2_), custom_call_target="tpu_custom_call" | custom-call | flops 12884901888 | bytes 23068672 | tf_op jit(solution)/shard_map/expert_dx/pallas_call | solution.py:562
  311.0 27.0 %expert_grad.2 = bf16[8,6,3,256,256]{4,3,2,1,0:T(8,128)(2,1)} custom-call(bf16[512,2176]{1,0:T(8,128)(2,1)} %constant_dynamic-update-slice_fusion.refs_0_, bf16[512,2176]{1,0:T(8,128)(2,1)} %collective-permute-done.14.refs_1_, bf16[512,2048]{1,0:T(8,128)(2,1)} %pad_maximum_fusion.refs_2_, bf16[512,2048]{1,0:T(8,128)(2,1)} %collective-permute-done.15.refs_3_, ...), custom_call_target="tpu_custom_call" | custom-call | flops 19327352832 | bytes 36700160 | tf_op jit(solution)/shard_map/expert_grad/pallas_call | solution.py:477
  338.3 13.3 %expert_up.3 = (bf16[1024,512]{1,0:T(8,128)(2,1)}, bf16[1024,1024]{1,0:T(8,128)(2,1)}, f32[1024,128]{1,0:T(8,128)}) custom-call(s32[1]{0:T(128)} %bitcast.22.first_ref, bf16[512,2176]{1,0:T(8,128)(2,1)} %constant_dynamic-update-slice_fusion.refs_0_, bf16[512,2176]{1,0:T(8,128)(2,1)} %collective-permute-done.14.refs_1_, ...), custom_call_target="tpu_custom_call" | custom-call | flops 6442450944 | bytes 17825792 | tf_op jit(solution)/shard_map/expert_up/pallas_call | solution.py:438
  351.6 10.5 %expert_dx.3 = (bf16[512,2176]{1,0:T(8,128)(2,1)}, bf16[512,2176]{1,0:T(8,128)(2,1)}) custom-call(bf16[1024,1024]{1,0:T(8,128)(2,1)} %get-tuple-element.355.refs_0_.refs_5_, bf16[8,2,3,256,256]{4,3,2,1,0:T(8,128)(2,1)} %all-gather.11.cloned.1.call-done.refs_4_.refs_1_.refs_3_, f32[1024,128]{1,0:T(8,128)} %get-tuple-element.329.refs_2_, ...), custom_call_target="tpu_custom_call" | custom-call | flops 4294967296 | bytes 10747904 | tf_op jit(solution)/shard_map/expert_dx/pallas_call | solution.py:562
  368.5 13.2 %collective-permute-done.17 = bf16[128,2176]{1,0:T(8,128)(2,1)S(1)} collective-permute-done((bf16[128,2176]{1,0:T(8,128)(2,1)S(1)}, bf16[128,2176]{1,0:T(8,128)(2,1)S(1)}, u32[]{:S(2)}, u32[]{:S(2)}) %collective-permute-start.17) | collective-permute-done | bytes 557088 | tf_op jit(solution)/shard_map/ppermute | solution.py:721
  387.0 13.7 %expert_out.1 = (bf16[512,2048]{1,0:T(8,128)(2,1)}, bf16[512,2048]{1,0:T(8,128)(2,1)}) custom-call(bf16[1024,1536]{1,0:T(8,128)(2,1)} %get-tuple-element.344.refs_4_.refs_0_, bf16[1024,512]{1,0:T(8,128)(2,1)} %get-tuple-element.354.refs_1_.refs_4_, bf16[8,6,3,256,256]{4,3,2,1,0:T(8,128)(2,1)} %all-gather.9.cloned.1.call-done.refs_4_.refs_1_.refs_2_, ...), custom_call_target="tpu_custom_call" | custom-call | flops 8589934592 | bytes 16777216 | tf_op jit(solution)/shard_map/expert_out/pallas_call | solution.py:562
  400.7 13.1 %expert_grad.3 = bf16[8,2,3,256,256]{4,3,2,1,0:T(8,128)(2,1)} custom-call(bf16[512,2176]{1,0:T(8,128)(2,1)} %constant_dynamic-update-slice_fusion.refs_0_, bf16[512,2176]{1,0:T(8,128)(2,1)} %collective-permute-done.14.refs_1_, bf16[512,2048]{1,0:T(8,128)(2,1)} %pad_maximum_fusion.refs_2_, bf16[512,2048]{1,0:T(8,128)(2,1)} %collective-permute-done.15.refs_3_, ...), custom_call_target="tpu_custom_call" | custom-call | flops 6442450944 | bytes 17825792 | tf_op jit(solution)/shard_map/expert_grad/pallas_call | solution.py:477
  415.4 4.5 norm_two_back.1
  421.1 25.6 %collective-permute-done.22 = bf16[128,2048]{1,0:T(8,128)(2,1)S(1)} collective-permute-done((bf16[128,2048]{1,0:T(8,128)(2,1)}, bf16[128,2048]{1,0:T(8,128)(2,1)S(1)}, u32[]{:S(2)}, u32[]{:S(2)}) %collective-permute-start.22) | collective-permute-done | bytes 524320 | tf_op jit(solution)/shard_map/ppermute | solution.py:721
  446.9 13.7 %collective-permute-done.23 = bf16[128,2048]{1,0:T(8,128)(2,1)S(1)} collective-permute-done((bf16[128,2048]{1,0:T(8,128)(2,1)S(1)}, bf16[128,2048]{1,0:T(8,128)(2,1)S(1)}, u32[]{:S(2)}, u32[]{:S(2)}) %collective-permute-start.23) | collective-permute-done | bytes 524320 | tf_op jit(solution)/shard_map/ppermute | solution.py:721
  463.2 5.0 dheads.1.refs_8_
  468.8 13.2 %attend_back.1 = (f32[512,512]{1,0:T(8,128)}, bf16[2,512,512]{2,1,0:T(8,128)(2,1)}, bf16[2,512,512]{2,1,0:T(8,128)(2,1)}, bf16[2,512,512]{2,1,0:T(8,128)(2,1)}, bf16[2,512,512]{2,1,0:T(8,128)(2,1)}) custom-call(s32[7]{0:T(128)} %pad_add_fusion.scal_ref, bf16[512,512]{1,0:T(8,128)(2,1)} %get-tuple-element.380.q_ref, ...), custom_call_target="tpu_custom_call" | custom-call | flops 2684354560 | bytes 12582912 | tf_op jit(solution)/shard_map/attend_back/pallas_call | solution.py:209
  488.2 7.7 %gradout.1.kept_ref = bf16[8,4,256,512]{3,2,1,0:T(8,128)(2,1)} custom-call(s32[4]{0:T(128)} %copy-done.26, bf16[512,2048]{1,0:T(8,128)(2,1)} %copy-done.1, bf16[512,512]{1,0:T(8,128)(2,1)} %attend.1.h_ref), custom_call_target="tpu_custom_call" | custom-call | flops 1073741824 | bytes 4718592 | tf_op jit(solution)/shard_map/gradout/pallas_call | solution.py:288
  495.9 12.3 %collective-permute-done.25 = bf16[128,2048]{1,0:T(8,128)(2,1)S(1)} collective-permute-done((bf16[128,2048]{1,0:T(8,128)(2,1)}, bf16[128,2048]{1,0:T(8,128)(2,1)S(1)}, u32[]{:S(2)}, u32[]{:S(2)}) %collective-permute-start.25) | collective-permute-done | bytes 524320 | tf_op jit(solution)/shard_map/ppermute | solution.py:721
  513.9 16.8 %collective-permute-done.31 = bf16[2,512,512]{2,1,0:T(8,128)(2,1)S(1)} collective-permute-done((bf16[2,512,512]{2,1,0:T(8,128)(2,1)S(1)}, bf16[2,512,512]{2,1,0:T(8,128)(2,1)S(1)}, u32[]{:S(2)}, u32[]{:S(2)}) %collective-permute-start.31) | collective-permute-done | bytes 1048608 | tf_op jit(solution)/shard_map/ppermute | solution.py:711
  531.1 4.5 collective-permute-done.29.refs_2_
  537.8 6.0 unturn.1
  553.9 4.1 inplace.3
  560.1 10.9 %raw_back.1 = (bf16[512,1536]{1,0:T(8,128)(2,1)}, bf16[128,2048]{1,0:T(8,128)(2,1)}, bf16[128,2048]{1,0:T(8,128)(2,1)}, bf16[128,2048]{1,0:T(8,128)(2,1)}, bf16[128,2048]{1,0:T(8,128)(2,1)}) custom-call(s32[4]{0:T(128)} %copy-done.26, f32[2,512,512]{2,1,0:T(8,128)} %get-tuple-element.431.u_ref, f32[2,512,512]{2,1,0:T(8,128)} %get-tuple-element.432.raw_ref, ...), custom_call_target="tpu_custom_call" | custom-call | flops 3221225472 | bytes 13631488 | tf_op jit(solution)/shard_map/raw_back/pallas_call | solution.py:659
  571.0 9.1 %qkv_grad.1 = bf16[8,4,256,512]{3,2,1,0:T(8,128)(2,1)} custom-call(bf16[512,2048]{1,0:T(8,128)(2,1)} %get-tuple-element.443.n_ref, bf16[512,1536]{1,0:T(8,128)(2,1)} %get-tuple-element.444.d_ref, bf16[8,4,256,512]{3,2,1,0:T(8,128)(2,1)} %gradout.1.kept_ref), custom_call_target="tpu_custom_call", output_to_operand_aliasing={{}: (2, {})} | custom-call | flops 3221225472 | bytes 9961472 | tf_op jit(solution)/shard_map/qkv_grad/pallas_call | solution.py:693
  580.2 4.3 dynamic-slice_bitcast_fusion
  586.5 12.7 %collective-permute-done.36 = bf16[128,2048]{1,0:T(8,128)(2,1)S(1)} collective-permute-done((bf16[128,2048]{1,0:T(8,128)(2,1)S(1)}, bf16[128,2048]{1,0:T(8,128)(2,1)S(1)}, u32[]{:S(2)}, u32[]{:S(2)}) %collective-permute-start.36) | collective-permute-done | bytes 524320 | tf_op jit(solution)/shard_map/ppermute | solution.py:721
  602.6 17.2 %collective-permute-done.35.b_ref = bf16[128,2048]{1,0:T(8,128)(2,1)S(1)} collective-permute-done((bf16[128,2048]{1,0:T(8,128)(2,1)}, bf16[128,2048]{1,0:T(8,128)(2,1)S(1)}, u32[]{:S(2)}, u32[]{:S(2)}) %collective-permute-start.35) | collective-permute-done | bytes 524320 | tf_op jit(solution)/shard_map/ppermute | solution.py:721
  619.8 5.2 collective-permute-done.37.c_ref
  634.5 7.9 %settle.2 = (f32[16,2,256,256]{3,2,1,0:T(8,128)}, f32[16,256,256]{2,1,0:T(8,128)}) custom-call(s32[6]{0:T(128)} %pad_add_fusion.1.spot_ref, bf16[6,3,256,256]{3,2,1,0:T(8,128)(2,1)} %get-tuple-element.462.refs_0_, bf16[6,3,256,256]{3,2,1,0:T(8,128)(2,1)} %collective-permute-done.41.refs_1_), custom_call_target="tpu_custom_call" | custom-call | bytes 14155776 | tf_op jit(solution)/shard_map/settle/pallas_call | solution.py:508
  642.4 6.8 collective-permute-done.40.refs_1_
  660.0 5.6 all-to-all-done.2
  669.1 3.8 settle.3
  (235 shorter events, 135.6 us)
Async XLA Ops:
  7.2 60.6 %all-gather.7.cloned.1.call-start = ((), (), s32[]{:S(2)}) async-start(), calls=%async_computation.7 | async-start | bytes 9437184 | tf_op jit(solution)/shard_map/all_gather | solution.py:829
  9.7 254.3 %all-gather.9.cloned.1.call-start = ((), (), s32[]{:S(2)}) async-start(), calls=%async_computation.8 | async-start | bytes 23592960 | tf_op jit(solution)/shard_map/all_gather | solution.py:836
  20.5 317.8 %all-gather.11.cloned.1.call-start = ((), (), s32[]{:S(2)}) async-start(), calls=%async_computation.9 | async-start | bytes 7864320 | tf_op jit(solution)/shard_map/all_gather | solution.py:836
  78.8 22.0 %collective-permute-start.2 = (bf16[512,512]{1,0:T(8,128)(2,1)}, bf16[512,512]{1,0:T(8,128)(2,1)S(1)}, u32[]{:S(2)}, u32[]{:S(2)}) collective-permute-start(bf16[512,512]{1,0:T(8,128)(2,1)} %get-tuple-element.385.refs_4_), channel_id=1, source_target_pairs={{0,8},{8,0},{1,9},{9,1},{2,10},{10,2},{3,11},{11,3},{4,12},{12,4},... | collective-permute-start | bytes 1572872 | tf_op jit(solution)/shard_map/ppermute | solution.py:711
  86.6 4.5 collective-permute-start.1
  106.2 25.5 %collective-permute-start.4 = (bf16[512,512]{1,0:T(8,128)(2,1)}, bf16[512,512]{1,0:T(8,128)(2,1)}, u32[]{:S(2)}, u32[]{:S(2)}) collective-permute-start(bf16[512,512]{1,0:T(8,128)(2,1)} %get-tuple-element.381.refs_0_), channel_id=1, source_target_pairs={{0,8},{8,0},{1,9},{9,1},{2,10},{10,2},{3,11},{11,3},{4,12},{12,4},... | collective-permute-start | bytes 1572872 | tf_op jit(solution)/shard_map/ppermute | solution.py:711
  108.3 24.7 %collective-permute-start.6 = (bf16[512,512]{1,0:T(8,128)(2,1)S(1)}, bf16[512,512]{1,0:T(8,128)(2,1)}, u32[]{:S(2)}, u32[]{:S(2)}) collective-permute-start(bf16[512,512]{1,0:T(8,128)(2,1)S(1)} %copy-done.21), channel_id=1, source_target_pairs={{0,4},{4,0},{1,5},{5,1},{2,6},{6,2},{3,7},{7,3},{8,12},{12,8},{9,1... | collective-permute-start | bytes 1572872 | tf_op jit(solution)/shard_map/ppermute | solution.py:711
  108.3 24.7 %collective-permute-start.3 = (bf16[512,512]{1,0:T(8,128)(2,1)}, bf16[512,512]{1,0:T(8,128)(2,1)}, u32[]{:S(2)}, u32[]{:S(2)}) collective-permute-start(bf16[512,512]{1,0:T(8,128)(2,1)} %get-tuple-element.381.refs_0_), channel_id=1, source_target_pairs={{0,4},{4,0},{1,5},{5,1},{2,6},{6,2},{3,7},{7,3},{8,12},{12,8},{9,1... | collective-permute-start | bytes 1572872 | tf_op jit(solution)/shard_map/ppermute | solution.py:711
  108.8 24.2 %collective-permute-start.7 = (bf16[512,512]{1,0:T(8,128)(2,1)S(1)}, bf16[512,512]{1,0:T(8,128)(2,1)}, u32[]{:S(2)}, u32[]{:S(2)}) collective-permute-start(bf16[512,512]{1,0:T(8,128)(2,1)S(1)} %collective-permute-done.2.refs_6_), channel_id=1, source_target_pairs={{0,4},{4,0},{1,5},{5,1},{2,6},{6,2},{3,7},{7,3},{8,12},{12,8},{9,1... | collective-permute-start | bytes 1572872 | tf_op jit(solution)/shard_map/ppermute | solution.py:711
  149.3 15.0 %collective-permute-start.9 = (bf16[128,2048]{1,0:T(8,128)(2,1)}, bf16[128,2048]{1,0:T(8,128)(2,1)S(1)}, u32[]{:S(2)}, u32[]{:S(2)}) collective-permute-start(bf16[128,2048]{1,0:T(8,128)(2,1)} %get-tuple-element.279), channel_id=1, source_target_pairs={{0,1},{1,0},{2,3},{3,2},{4,5},{5,4},{6,7},{7,6},{8,9},{9,8},{10,11... | collective-permute-start | bytes 1572872 | tf_op jit(solution)/shard_map/ppermute | solution.py:721
  150.7 32.9 %collective-permute-start.8 = (bf16[128,2048]{1,0:T(8,128)(2,1)}, bf16[128,2048]{1,0:T(8,128)(2,1)S(1)}, u32[]{:S(2)}, u32[]{:S(2)}) collective-permute-start(bf16[128,2048]{1,0:T(8,128)(2,1)} %get-tuple-element.277), channel_id=1, source_target_pairs={{0,1},{1,0},{2,3},{3,2},{4,5},{5,4},{6,7},{7,6},{8,9},{9,8},{10,11... | collective-permute-start | bytes 1572872 | tf_op jit(solution)/shard_map/ppermute | solution.py:721
  165.7 24.7 %collective-permute-start.10 = (bf16[128,2048]{1,0:T(8,128)(2,1)S(1)}, bf16[128,2048]{1,0:T(8,128)(2,1)}, u32[]{:S(2)}, u32[]{:S(2)}) collective-permute-start(bf16[128,2048]{1,0:T(8,128)(2,1)S(1)} %add_convert_fusion.10), channel_id=1, source_target_pairs={{0,2},{1,3},{2,0},{3,1},{4,6},{5,7},{6,4},{7,5},{8,10},{9,11},{10,... | collective-permute-start | bytes 1572872 | tf_op jit(solution)/shard_map/ppermute | solution.py:721
  193.7 22.4 %collective-permute-start.12 = (bf16[128,2176]{1,0:T(8,128)(2,1)}, bf16[128,2176]{1,0:T(8,128)(2,1)S(1)}, u32[]{:S(2)}, u32[]{:S(2)}) collective-permute-start(bf16[128,2176]{1,0:T(8,128)(2,1)} %get-tuple-element.360.ext_ref), channel_id=1, source_target_pairs={{0,2},{1,3},{2,0},{3,1},{4,6},{5,7},{6,4},{7,5},{8,10},{9,11},{10,... | collective-permute-start | bytes 1671176 | tf_op jit(solution)/shard_map/ppermute | solution.py:721
  199.9 380.3 %reduce-scatter.10.cloned.1.call-start = ((), (), s32[]{:S(2)}) async-start(), calls=%async_computation.10 | async-start | bytes 23592960
  200.1 25.6 %collective-permute-start.11 = (bf16[128,2176]{1,0:T(8,128)(2,1)S(1)}, bf16[128,2176]{1,0:T(8,128)(2,1)S(1)}, u32[]{:S(2)}, u32[]{:S(2)}) collective-permute-start(bf16[128,2176]{1,0:T(8,128)(2,1)S(1)} %copy-done.5), channel_id=1, source_target_pairs={{0,1},{1,0},{2,3},{3,2},{4,5},{5,4},{6,7},{7,6},{8,9},{9,8},{10,11... | collective-permute-start | bytes 1671176 | tf_op jit(solution)/shard_map/ppermute | solution.py:721
  216.1 21.0 %collective-permute-start.13 = (bf16[128,2176]{1,0:T(8,128)(2,1)S(1)}, bf16[128,2176]{1,0:T(8,128)(2,1)S(1)}, u32[]{:S(2)}, u32[]{:S(2)}) collective-permute-start(bf16[128,2176]{1,0:T(8,128)(2,1)S(1)} %collective-permute-done.12), channel_id=1, source_target_pairs={{0,1},{1,0},{2,3},{3,2},{4,5},{5,4},{6,7},{7,6},{8,9},{9,8},{10,11... | collective-permute-start | bytes 1671176 | tf_op jit(solution)/shard_map/ppermute | solution.py:721
  240.6 7.7 %collective-permute-start.14 = (bf16[512,2176]{1,0:T(8,128)(2,1)}, bf16[512,2176]{1,0:T(8,128)(2,1)}, u32[]{:S(2)}, u32[]{:S(2)}) collective-permute-start(bf16[512,2176]{1,0:T(8,128)(2,1)} %constant_dynamic-update-slice_fusion.refs_0_), channel_id=1, source_target_pairs={{0,4},{4,0},{1,5},{5,1},{2,6},{6,2},{3,7},{7,3},{8,12},{12,8},{9,1... | collective-permute-start | bytes 6684680 | tf_op jit(solution)/shard_map/ppermute | solution.py:711
  240.6 7.3 %collective-permute-start.15 = (bf16[512,2048]{1,0:T(8,128)(2,1)S(1)}, bf16[512,2048]{1,0:T(8,128)(2,1)}, u32[]{:S(2)}, u32[]{:S(2)}) collective-permute-start(bf16[512,2048]{1,0:T(8,128)(2,1)S(1)} %copy-done.7), channel_id=1, source_target_pairs={{0,4},{4,0},{1,5},{5,1},{2,6},{6,2},{3,7},{7,3},{8,12},{12,8},{9,1... | collective-permute-start | bytes 6291464 | tf_op jit(solution)/shard_map/ppermute | solution.py:711
  338.0 292.3 %reduce-scatter.12.cloned.1.call-start = ((), (), s32[]{:S(2)}) async-start(), calls=%async_computation.11 | async-start | bytes 7864320
  362.1 4.6 collective-permute-start.16
  366.9 14.7 %collective-permute-start.17 = (bf16[128,2176]{1,0:T(8,128)(2,1)S(1)}, bf16[128,2176]{1,0:T(8,128)(2,1)S(1)}, u32[]{:S(2)}, u32[]{:S(2)}) collective-permute-start(bf16[128,2176]{1,0:T(8,128)(2,1)S(1)} %add_convert_fusion.4), channel_id=1, source_target_pairs={{0,1},{1,0},{2,3},{3,2},{4,5},{5,4},{6,7},{7,6},{8,9},{9,8},{10,11... | collective-permute-start | bytes 1671176 | tf_op jit(solution)/shard_map/ppermute | solution.py:721
  381.9 31.9 %collective-permute-start.20 = (bf16[128,2176]{1,0:T(8,128)(2,1)S(1)}, bf16[128,2176]{1,0:T(8,128)(2,1)S(1)}, u32[]{:S(2)}, u32[]{:S(2)}) collective-permute-start(bf16[128,2176]{1,0:T(8,128)(2,1)S(1)} %add_convert_fusion.3), channel_id=1, source_target_pairs={{0,2},{1,3},{2,0},{3,1},{4,6},{5,7},{6,4},{7,5},{8,10},{9,11},{10,... | collective-permute-start | bytes 1671176 | tf_op jit(solution)/shard_map/ppermute | solution.py:721
  384.5 29.3 %collective-permute-start.19 = (bf16[128,2176]{1,0:T(8,128)(2,1)S(1)}, bf16[128,2176]{1,0:T(8,128)(2,1)S(1)}, u32[]{:S(2)}, u32[]{:S(2)}) collective-permute-start(bf16[128,2176]{1,0:T(8,128)(2,1)S(1)} %add_convert_fusion.2), channel_id=1, source_target_pairs={{0,1},{1,0},{2,3},{3,2},{4,5},{5,4},{6,7},{7,6},{8,9},{9,8},{10,11... | collective-permute-start | bytes 1671176 | tf_op jit(solution)/shard_map/ppermute | solution.py:721
  400.7 60.2 %collective-permute-start.18 = (bf16[512,2048]{1,0:T(8,128)(2,1)}, bf16[512,2048]{1,0:T(8,128)(2,1)S(1)}, u32[]{:S(2)}, u32[]{:S(2)}) collective-permute-start(bf16[512,2048]{1,0:T(8,128)(2,1)} %get-tuple-element.349), channel_id=1, source_target_pairs={{0,4},{4,0},{1,5},{5,1},{2,6},{6,2},{3,7},{7,3},{8,12},{12,8},{9,1... | collective-permute-start | bytes 6291464 | tf_op jit(solution)/shard_map/ppermute | solution.py:711
  419.9 26.8 %collective-permute-start.22 = (bf16[128,2048]{1,0:T(8,128)(2,1)}, bf16[128,2048]{1,0:T(8,128)(2,1)S(1)}, u32[]{:S(2)}, u32[]{:S(2)}) collective-permute-start(bf16[128,2048]{1,0:T(8,128)(2,1)} %get-tuple-element.370), channel_id=1, source_target_pairs={{0,2},{1,3},{2,0},{3,1},{4,6},{5,7},{6,4},{7,5},{8,10},{9,11},{10,... | collective-permute-start | bytes 1572872 | tf_op jit(solution)/shard_map/ppermute | solution.py:721
  421.1 25.8 %collective-permute-start.21 = (bf16[128,2048]{1,0:T(8,128)(2,1)}, bf16[128,2048]{1,0:T(8,128)(2,1)S(1)}, u32[]{:S(2)}, u32[]{:S(2)}) collective-permute-start(bf16[128,2048]{1,0:T(8,128)(2,1)} %get-tuple-element.370), channel_id=1, source_target_pairs={{0,1},{1,0},{2,3},{3,2},{4,5},{5,4},{6,7},{7,6},{8,9},{9,8},{10,11... | collective-permute-start | bytes 1572872 | tf_op jit(solution)/shard_map/ppermute | solution.py:721
  446.7 13.9 %collective-permute-start.23 = (bf16[128,2048]{1,0:T(8,128)(2,1)S(1)}, bf16[128,2048]{1,0:T(8,128)(2,1)S(1)}, u32[]{:S(2)}, u32[]{:S(2)}) collective-permute-start(bf16[128,2048]{1,0:T(8,128)(2,1)S(1)} %collective-permute-done.22), channel_id=1, source_target_pairs={{0,1},{1,0},{2,3},{3,2},{4,5},{5,4},{6,7},{7,6},{8,9},{9,8},{10,11... | collective-permute-start | bytes 1572872 | tf_op jit(solution)/shard_map/ppermute | solution.py:721
  468.2 210.2 %reduce-scatter.8.cloned.1.call-start = ((), (), s32[]{:S(2)}) async-start(), calls=%async_computation.6 | async-start | bytes 9437184 | tf_op jit(solution)/shard_map/reduce_scatter | solution.py:954
  468.5 14.1 %collective-permute-start.24 = (bf16[128,2048]{1,0:T(8,128)(2,1)}, bf16[128,2048]{1,0:T(8,128)(2,1)S(1)}, u32[]{:S(2)}, u32[]{:S(2)}) collective-permute-start(bf16[128,2048]{1,0:T(8,128)(2,1)} %add_convert_fusion.9), channel_id=1, source_target_pairs={{0,1},{1,0},{2,3},{3,2},{4,5},{5,4},{6,7},{7,6},{8,9},{9,8},{10,11... | collective-permute-start | bytes 1572872 | tf_op jit(solution)/shard_map/ppermute | solution.py:721
  482.1 31.8 %collective-permute-start.30 = (bf16[2,512,512]{2,1,0:T(8,128)(2,1)}, bf16[2,512,512]{2,1,0:T(8,128)(2,1)S(1)}, u32[]{:S(2)}, u32[]{:S(2)}) collective-permute-start(bf16[2,512,512]{2,1,0:T(8,128)(2,1)} %get-tuple-element.392), channel_id=1, source_target_pairs={{0,4},{4,0},{1,5},{5,1},{2,6},{6,2},{3,7},{7,3},{8,12},{12,8},{9,1... | collective-permute-start | bytes 3145736 | tf_op jit(solution)/shard_map/ppermute | solution.py:711
  483.6 26.3 %collective-permute-start.26 = (bf16[128,2048]{1,0:T(8,128)(2,1)}, bf16[128,2048]{1,0:T(8,128)(2,1)S(1)}, u32[]{:S(2)}, u32[]{:S(2)}) collective-permute-start(bf16[128,2048]{1,0:T(8,128)(2,1)} %add_convert_fusion.8), channel_id=1, source_target_pairs={{0,2},{1,3},{2,0},{3,1},{4,6},{5,7},{6,4},{7,5},{8,10},{9,11},{10,... | collective-permute-start | bytes 1572872 | tf_op jit(solution)/shard_map/ppermute | solution.py:721
  486.1 22.1 %collective-permute-start.25 = (bf16[128,2048]{1,0:T(8,128)(2,1)}, bf16[128,2048]{1,0:T(8,128)(2,1)S(1)}, u32[]{:S(2)}, u32[]{:S(2)}) collective-permute-start(bf16[128,2048]{1,0:T(8,128)(2,1)} %add_convert_fusion.7), channel_id=1, source_target_pairs={{0,1},{1,0},{2,3},{3,2},{4,5},{5,4},{6,7},{7,6},{8,9},{9,8},{10,11... | collective-permute-start | bytes 1572872 | tf_op jit(solution)/shard_map/ppermute | solution.py:721
  486.7 44.0 %collective-permute-start.31 = (bf16[2,512,512]{2,1,0:T(8,128)(2,1)S(1)}, bf16[2,512,512]{2,1,0:T(8,128)(2,1)S(1)}, u32[]{:S(2)}, u32[]{:S(2)}) collective-permute-start(bf16[2,512,512]{2,1,0:T(8,128)(2,1)S(1)} %add_convert_fusion), channel_id=1, source_target_pairs={{0,8},{8,0},{1,9},{9,1},{2,10},{10,2},{3,11},{11,3},{4,12},{12,4},... | collective-permute-start | bytes 3145736 | tf_op jit(solution)/shard_map/ppermute | solution.py:711
  510.3 25.4 %collective-permute-start.29 = (bf16[128,2048]{1,0:T(8,128)(2,1)S(1)}, bf16[128,2048]{1,0:T(8,128)(2,1)S(1)}, u32[]{:S(2)}, u32[]{:S(2)}) collective-permute-start(bf16[128,2048]{1,0:T(8,128)(2,1)S(1)} %add_convert_fusion.6.refs_0_), channel_id=1, source_target_pairs={{0,2},{1,3},{2,0},{3,1},{4,6},{5,7},{6,4},{7,5},{8,10},{9,11},{10,... | collective-permute-start | bytes 1572872 | tf_op jit(solution)/shard_map/ppermute | solution.py:721
  512.2 41.7 %collective-permute-start.28 = (bf16[128,2048]{1,0:T(8,128)(2,1)S(1)}, bf16[128,2048]{1,0:T(8,128)(2,1)}, u32[]{:S(2)}, u32[]{:S(2)}) collective-permute-start(bf16[128,2048]{1,0:T(8,128)(2,1)S(1)} %add_convert_fusion.6.refs_0_), channel_id=1, source_target_pairs={{0,1},{1,0},{2,3},{3,2},{4,5},{5,4},{6,7},{7,6},{8,9},{9,8},{10,11... | collective-permute-start | bytes 1572872 | tf_op jit(solution)/shard_map/ppermute | solution.py:721
  535.7 18.3 %collective-permute-start.32 = (bf16[128,2048]{1,0:T(8,128)(2,1)S(1)}, bf16[128,2048]{1,0:T(8,128)(2,1)}, u32[]{:S(2)}, u32[]{:S(2)}) collective-permute-start(bf16[128,2048]{1,0:T(8,128)(2,1)S(1)} %collective-permute-done.29.refs_2_), channel_id=1, source_target_pairs={{0,1},{1,0},{2,3},{3,2},{4,5},{5,4},{6,7},{7,6},{8,9},{9,8},{10,11... | collective-permute-start | bytes 1572872 | tf_op jit(solution)/shard_map/ppermute | solution.py:721
  549.4 4.5 collective-permute-start.34
  584.5 50.0 %collective-permute-start.41 = (bf16[6,3,256,256]{3,2,1,0:T(8,128)(2,1)S(1)}, bf16[6,3,256,256]{3,2,1,0:T(8,128)(2,1)}, u32[]{:S(2)}, u32[]{:S(2)}) collective-permute-start(bf16[6,3,256,256]{3,2,1,0:T(8,128)(2,1)S(1)} %get-tuple-element.488), channel_id=1, source_target_pairs={{0,4},{4,0},{1,5},{5,1},{2,6},{6,2},{3,7},{7,3},{8,12},{12,8},{9,1... | collective-permute-start | bytes 7077896 | tf_op jit(solution)/shard_map/ppermute | solution.py:711
  584.5 14.7 %collective-permute-start.36 = (bf16[128,2048]{1,0:T(8,128)(2,1)S(1)}, bf16[128,2048]{1,0:T(8,128)(2,1)S(1)}, u32[]{:S(2)}, u32[]{:S(2)}) collective-permute-start(bf16[128,2048]{1,0:T(8,128)(2,1)S(1)} %copy-done.32), channel_id=1, source_target_pairs={{0,1},{1,0},{2,3},{3,2},{4,5},{5,4},{6,7},{7,6},{8,9},{9,8},{10,11... | collective-permute-start | bytes 1572872 | tf_op jit(solution)/shard_map/ppermute | solution.py:721
  585.8 34.0 %collective-permute-start.35 = (bf16[128,2048]{1,0:T(8,128)(2,1)}, bf16[128,2048]{1,0:T(8,128)(2,1)S(1)}, u32[]{:S(2)}, u32[]{:S(2)}) collective-permute-start(bf16[128,2048]{1,0:T(8,128)(2,1)} %get-tuple-element.440), channel_id=1, source_target_pairs={{0,1},{1,0},{2,3},{3,2},{4,5},{5,4},{6,7},{7,6},{8,9},{9,8},{10,11... | collective-permute-start | bytes 1572872 | tf_op jit(solution)/shard_map/ppermute | solution.py:721
  599.4 25.6 %collective-permute-start.37 = (bf16[128,2048]{1,0:T(8,128)(2,1)S(1)}, bf16[128,2048]{1,0:T(8,128)(2,1)}, u32[]{:S(2)}, u32[]{:S(2)}) collective-permute-start(bf16[128,2048]{1,0:T(8,128)(2,1)S(1)} %add_convert_fusion.5), channel_id=1, source_target_pairs={{0,2},{1,3},{2,0},{3,1},{4,6},{5,7},{6,4},{7,5},{8,10},{9,11},{10,... | collective-permute-start | bytes 1572872 | tf_op jit(solution)/shard_map/ppermute | solution.py:721
  628.6 20.6 %collective-permute-start.40 = (bf16[128,2048]{1,0:T(8,128)(2,1)}, bf16[128,2048]{1,0:T(8,128)(2,1)S(1)}, u32[]{:S(2)}, u32[]{:S(2)}) collective-permute-start(bf16[128,2048]{1,0:T(8,128)(2,1)} %get-tuple-element.467.refs_0_), channel_id=1, source_target_pairs={{0,1},{1,0},{2,3},{3,2},{4,5},{5,4},{6,7},{7,6},{8,9},{9,8},{10,11... | collective-permute-start | bytes 1572872 | tf_op jit(solution)/shard_map/ppermute | solution.py:721
  630.3 25.4 %collective-permute-start.38 = (bf16[128,2048]{1,0:T(8,128)(2,1)}, bf16[128,2048]{1,0:T(8,128)(2,1)S(1)}, u32[]{:S(2)}, u32[]{:S(2)}) collective-permute-start(bf16[128,2048]{1,0:T(8,128)(2,1)} %get-tuple-element.467.refs_0_), channel_id=1, source_target_pairs={{0,2},{1,3},{2,0},{3,1},{4,6},{5,7},{6,4},{7,5},{8,10},{9,11},{10,... | collective-permute-start | bytes 1572872 | tf_op jit(solution)/shard_map/ppermute | solution.py:721
  653.9 14.4 %collective-permute-start.43 = (bf16[2,3,256,256]{3,2,1,0:T(8,128)(2,1)S(1)}, bf16[2,3,256,256]{3,2,1,0:T(8,128)(2,1)S(1)}, u32[]{:S(2)}, u32[]{:S(2)}) collective-permute-start(bf16[2,3,256,256]{3,2,1,0:T(8,128)(2,1)S(1)} %get-tuple-element.510), channel_id=1, source_target_pairs={{0,4},{4,0},{1,5},{5,1},{2,6},{6,2},{3,7},{7,3},{8,12},{12,8},{9,1... | collective-permute-start | bytes 2359304 | tf_op jit(solution)/shard_map/ppermute | solution.py:711
  655.8 18.2 %collective-permute-start.39 = (bf16[128,2048]{1,0:T(8,128)(2,1)S(1)}, bf16[128,2048]{1,0:T(8,128)(2,1)S(1)}, u32[]{:S(2)}, u32[]{:S(2)}) collective-permute-start(bf16[128,2048]{1,0:T(8,128)(2,1)S(1)} %collective-permute-done.38.refs_0_), channel_id=1, source_target_pairs={{0,1},{1,0},{2,3},{3,2},{4,5},{5,4},{6,7},{7,6},{8,9},{9,8},{10,11... | collective-permute-start | bytes 1572872 | tf_op jit(solution)/shard_map/ppermute | solution.py:721
  656.6 9.0 %all-to-all-start.2 = ((f32[8,20,256]{2,1,0:T(8,128)}), f32[8,20,256]{2,1,0:T(8,128)S(1)}, u32[]{:S(2)}, u32[]{:S(2)}) async-start(f32[8,20,256]{2,1,0:T(8,128)} %bitcast.60), calls=%async_computation.3 | async-start | bytes 393216 | tf_op jit(solution)/shard_map/all_to_all | solution.py:968
  665.6 7.4 %collective-permute-start.42 = (f32[20,256]{1,0:T(8,128)S(1)}, f32[20,256]{1,0:T(8,128)S(1)}, u32[]{:S(2)}, u32[]{:S(2)}) collective-permute-start(f32[20,256]{1,0:T(8,128)S(1)} %reduce_sum.9), channel_id=1, source_target_pairs={{0,1},{1,0},{2,3},{3,2},{4,5},{5,4},{6,7},{7,6},{8,9},{9,8},{10,11... | collective-permute-start | bytes 61448 | tf_op jit(solution)/shard_map/ppermute | solution.py:721
  673.0 9.7 %collective-permute-start.44 = (f32[20,256]{1,0:T(8,128)S(1)}, f32[20,256]{1,0:T(8,128)S(1)}, u32[]{:S(2)}, u32[]{:S(2)}) collective-permute-start(f32[20,256]{1,0:T(8,128)S(1)} %add.201), channel_id=1, source_target_pairs={{0,2},{1,3},{2,0},{3,1},{4,6},{5,7},{6,4},{7,5},{8,10},{9,11},{10,... | collective-permute-start | bytes 61448 | tf_op jit(solution)/shard_map/ppermute | solution.py:721
  (37 other events, 474.3 us)
Sparse Core Ops, SparseCore 0:
  10.5 57.2 all-gather.6
  69.6 194.2 all-gather.8
  265.8 70.1 all-gather.10
  339.0 189.5 reduce-scatter.9
  532.3 71.0 reduce-scatter.11
  607.1 71.2 reduce-scatter.7

commit v5 on v4

--- a/solution.py
+++ b/solution.py
@@ -928,22 +928,23 @@
     out = line(lambda *v: total(v).astype(BF16), mid, own[0], beside[0], *moe)
     out_far = across(out, 2)
     out_near = across(out, 1)
+    def parted(k):
+        own, other = line(
+            lambda v: [lax.dynamic_index_in_dim(v, c, 0, keepdims=False) for c in (core, core ^ 1)], grads[k]
+        )
+        return own, swap(other, "core")
+
+    def settled(k, pair, kept):
+        steps = jnp.arange(chunks[k] // 2, dtype=jnp.int32)
+        spots = jnp.concatenate([(c * group + starts[k]) // 2 + steps for c in (core, core ^ 1)])
+        return line(settle, spots.astype(jnp.int32), pair, kept, experts)
+
+    pairs = [parted(0)]
     d_kv = line(lambda *v: total(v), b0, r1, r2)
     out_far, d_kv = lax.optimization_barrier((out_far, d_kv))
     out_both = across(out_far, 1)
     u, inner, gain_qk = line(unturn, dq, d_kv[0], raw, scales, own_gains, cosine, sine)
     outputs = line(in_place, places, [out, out_near, out_far, out_both], [], t).reshape(inputs.shape)
-
-    def parted(k):
-        own, other = line(
-            lambda v: [lax.dynamic_index_in_dim(v, c, 0, keepdims=False) for c in (core, core ^ 1)], grads[k]
-        )
-        return own, swap(other, "core")
-
-    def settled(k, pair, kept):
-        steps = jnp.arange(chunks[k] // 2, dtype=jnp.int32)
-        spots = jnp.concatenate([(c * group + starts[k]) // 2 + steps for c in (core, core ^ 1)])
-        return line(settle, spots.astype(jnp.int32), pair, kept, experts)
 
     inner = (meet(inner[:, :, 0]) / width)[:, :, None]
     d_raw, *d_one = line(
@@ -951,18 +952,25 @@
     )
     last = across(d_one[3], 1)
     grad_attn = line(qkv_grads, normed_one, d_raw, grad_attn, p)
-    grad_attn = lax.psum_scatter(grad_attn, PLANE, scatter_dimension=0, tiled=False)
-    pairs = [parted(0)]
+    grad_attn = grad_attn.reshape((-1, 2) + grad_attn.shape[1:])
+    theirs = line(lambda v: lax.dynamic_index_in_dim(v, core ^ 1, 1, keepdims=False), grad_attn)
+    theirs = swap(theirs, "core")
     near = line(add, d_one[2], last)
     d_one = [d_one[0], across(d_one[1], 1), across(near, 2)]
+    grad_attn = line(
+        lambda v, w: add(lax.dynamic_index_in_dim(v, core, 1, keepdims=False), w), grad_attn, theirs
+    )
     grad_in, gain_one = line(norm_one_back, d_one, x_q, d_mid, gains[0:1])
+    grad_attn, gain_one = lax.optimization_barrier((grad_attn, gain_one))
+    grad_attn = lax.optimization_barrier(lax.psum_scatter(grad_attn, FR, scatter_dimension=0, tiled=False))
     far = across(grad_in, 2)
-    near = across(grad_in, 1)
     placed = lax.dynamic_update_slice_in_dim(
         jnp.zeros((2, width), F32), gain_qk[:, 0, :], column * n, 1
     )
 
     small = line(lambda *v: jnp.concatenate(v, 0), grad_router[:experts], gain_one, gain_two, placed)
+    near, small = lax.optimization_barrier((grad_in, small))
+    near = across(near, 1)
     rows = small.shape[0]
     small = small.reshape(rows, p, ds).transpose(1, 0, 2)
     small = jnp.sum(lax.all_to_all(small, PLANE, 0, 0, tiled=True), 0)

time: 701 us -> 708 us (level)
    ppermute x15 -> x16, waiting for transfers between devices: 60.3 us -> 43.5 us  [swap(): return lax.ppermute(value, axis, [(0, 1), (1, 0)])]
    unnamed x8 -> x9, waiting for transfers between devices: 0.14 us -> 14.1 us
  transfers between devices with their start and end apart: 52 -> 53, of which waited for: 32 -> 31; matrix products, arithmetic and copies ran while one was open for 7% -> 8% of each run, Pallas kernels for 35% -> 34%
where the time goes in v5:
time: 708 us; the launch traced here: 699 us
  waiting for transfers between devices  275 us (39%)
  Pallas kernels  241 us (34%)
  starting transfers between devices  53.4 us (8%)
  local copies, waits for them, and re-layouts  43.2 us (6%)
  blocking collectives  35.4 us (5%)
  other arithmetic  28.2 us (4%)
  between operations  22.9 us (3%)
    ppermute x30, waiting for transfers between devices, across(): return lax.ppermute(value, 'tp', [(i, i ^ k) for i in range(size)])  182 us
    ppermute x16, waiting for transfers between devices, swap(): return lax.ppermute(value, axis, [(0, 1), (1, 0)])  43.5 us
    pallas_call x3, Pallas kernels, expert_down(): call(functools.partial(down_kernel, planes=planes, chunks=chunks, sides=l...  43.3 us
    ppermute x30, starting transfers between devices, across(): return lax.ppermute(value, 'tp', [(i, i ^ k) for i in range(size)])  42.4 us
    pallas_call x2, Pallas kernels, expert_up(): call(functools.partial(expert_kernel, parts=parts), 'expert_up', (e,), [f...  41.3 us
    pallas_call x2, Pallas kernels, expert_grads(): call(functools.partial(expert_grad_kernel, parts=parts), 'expert_grad', (...  40 us
    all_gather x2, waiting for transfers between devices, body(): lax.all_gather(mine, FR, axis=0, tiled=False).reshape(-1, e, 3, ds, f)  15.7 us
    all_to_all x2, blocking collectives, body(): mine = lax.all_to_all(grouped[:, begin:begin + e], 'core', 0, 0, tiled=True)  14.6 us
  transfers between devices with their start and end apart: 53, of which 31 were waited for; matrix products, arithmetic and copies ran while one was open for 8% of the time, Pallas kernels for 34%

profile of v5, /device:TPU:0, one launch (start us, length us, event | category | flops | bytes accessed | tf_op | source)
XLA Modules:
  0.0 698.6 jit_solution(17619589846445281011)
XLA Ops:
  11.9 8.6 %all_to_all.15 = bf16[2,6,3,256,256]{4,3,2,1,0:T(8,128)(2,1)} all-to-all(bf16[2,6,3,256,256]{4,3,2,1,0:T(8,128)(2,1)S(1)} %fusion.1), channel_id=1, replica_groups=mesh['fsdp'=2,'row'=2,'core'=2,'tp'=4] {'core'}, dimensions={0} | all-to-all | bytes 9437184 | tf_op jit(solution)/shard_map/all_to_all | solution.py:835
  29.6 10.3 %all_gather.26 = bf16[4,2048]{1,0:T(4,128)(2,1)S(1)} all-gather(bf16[4,256]{1,0:T(4,128)(2,1)S(1)} %copy-done.35), channel_id=1, replica_groups=mesh['fsdp'=2,'row'=2,'core'=2,'tp'=4] {'fsdp','row','core'}, dimensions={1}, use_global_device_ids=true | all-gather | bytes 18432 | tf_op jit(solution)/shard_map/all_gather | solution.py:837
  39.9 10.5 %all_gather.27 = bf16[2048,16]{0,1:T(8,128)(2,1)} all-gather(bf16[256,16]{0,1:T(8,128)(2,1)S(1)} %copy-done.31), channel_id=1, replica_groups=mesh['fsdp'=2,'row'=2,'core'=2,'tp'=4] {'fsdp','row','core'}, dimensions={0}, use_global_device_ids=true | all-gather | bytes 73728 | tf_op jit(solution)/shard_map/all_gather | solution.py:838
  54.7 13.1 %all-gather.7.cloned.1.call-done = bf16[32,256,512]{2,1,0:T(8,128)(2,1)} async-done(((bf16[4,256,512]{2,1,0:T(8,128)(2,1)}), bf16[32,256,512]{2,1,0:T(8,128)(2,1)}) %all-gather.7.cloned.1.call-update) | async-done | bytes 8388624 | tf_op jit(solution)/shard_map/all_gather | solution.py:829
  68.4 10.4 %qkv.1 = (bf16[512,2048]{1,0:T(8,128)(2,1)}, f32[2,512,512]{2,1,0:T(8,128)}, bf16[512,512]{1,0:T(8,128)(2,1)}, f32[2,512,128]{2,1,0:T(8,128)}) custom-call(bf16[512,2048]{1,0:T(8,128)(2,1)} %bitcast.91, f32[1,2048]{1,0:T(1,128)} %get-tuple-element.464.g_ref, bf16[8,4,256,512]{3,2,1,0:T(8,128)(2,1)} %bitcast.67), custom_call_target="tpu_custom_call" | custom-call | flops 3221225472 | bytes 13107200 | tf_op jit(solution)/shard_map/qkv/pallas_call | solution.py:87
  91.1 9.7 %collective-permute-done.2.refs_6_ = bf16[512,512]{1,0:T(8,128)(2,1)S(1)} collective-permute-done((bf16[512,512]{1,0:T(8,128)(2,1)}, bf16[512,512]{1,0:T(8,128)(2,1)S(1)}, u32[]{:S(2)}, u32[]{:S(2)}) %collective-permute-start.2) | collective-permute-done | bytes 524320 | tf_op jit(solution)/shard_map/ppermute | solution.py:711
  101.8 4.4 prep.1
  108.8 22.9 %collective-permute-done.4.refs_2_ = bf16[512,512]{1,0:T(8,128)(2,1)} collective-permute-done((bf16[512,512]{1,0:T(8,128)(2,1)}, bf16[512,512]{1,0:T(8,128)(2,1)}, u32[]{:S(2)}, u32[]{:S(2)}) %collective-permute-start.4) | collective-permute-done | bytes 524320 | tf_op jit(solution)/shard_map/ppermute | solution.py:711
  134.0 9.9 %attend.1.h_ref = bf16[512,512]{1,0:T(8,128)(2,1)} custom-call(s32[7]{0:T(128)} %pad_add_fusion.scal_ref, bf16[512,512]{1,0:T(8,128)(2,1)} %get-tuple-element.387.q_ref, bf16[512,512]{1,0:T(8,128)(2,1)} %get-tuple-element.388.refs_0_, bf16[512,512]{1,0:T(8,128)(2,1)} %collective-permute-done.3.refs_1_, bf16[512,512]{1,0:T(8,128)(2,1)} %collective-permute-done.4.refs_2_, ...), custom_call_target="tpu_custom_call" | custom-call | flops 1073741824 | bytes 6291456 | tf_op jit(solution)/shard_map/attend/pallas_call | solution.py:171
  143.9 5.4 outproj.1
  151.3 13.0 %collective-permute-done.9 = bf16[128,2048]{1,0:T(8,128)(2,1)S(1)} collective-permute-done((bf16[128,2048]{1,0:T(8,128)(2,1)}, bf16[128,2048]{1,0:T(8,128)(2,1)S(1)}, u32[]{:S(2)}, u32[]{:S(2)}) %collective-permute-start.9) | collective-permute-done | bytes 524320 | tf_op jit(solution)/shard_map/ppermute | solution.py:721
  171.6 11.9 %collective-permute-done.8.b_ref = bf16[128,2048]{1,0:T(8,128)(2,1)S(1)} collective-permute-done((bf16[128,2048]{1,0:T(8,128)(2,1)}, bf16[128,2048]{1,0:T(8,128)(2,1)S(1)}, u32[]{:S(2)}, u32[]{:S(2)}) %collective-permute-start.8) | collective-permute-done | bytes 524320 | tf_op jit(solution)/shard_map/ppermute | solution.py:721
  183.5 6.8 collective-permute-done.10.c_ref
  193.9 6.0 all_to_all.16
  200.1 3.8 collective-permute-start.11
  203.9 12.2 %collective-permute-done.12 = bf16[128,2176]{1,0:T(8,128)(2,1)S(1)} collective-permute-done((bf16[128,2176]{1,0:T(8,128)(2,1)}, bf16[128,2176]{1,0:T(8,128)(2,1)S(1)}, u32[]{:S(2)}, u32[]{:S(2)}) %collective-permute-start.12) | collective-permute-done | bytes 557088 | tf_op jit(solution)/shard_map/ppermute | solution.py:721
  216.8 8.8 %collective-permute-done.11 = bf16[128,2176]{1,0:T(8,128)(2,1)S(1)} collective-permute-done((bf16[128,2176]{1,0:T(8,128)(2,1)S(1)}, bf16[128,2176]{1,0:T(8,128)(2,1)S(1)}, u32[]{:S(2)}, u32[]{:S(2)}) %collective-permute-start.11) | collective-permute-done | bytes 557088 | tf_op jit(solution)/shard_map/ppermute | solution.py:721
  225.6 11.5 %collective-permute-done.13 = bf16[128,2176]{1,0:T(8,128)(2,1)S(1)} collective-permute-done((bf16[128,2176]{1,0:T(8,128)(2,1)S(1)}, bf16[128,2176]{1,0:T(8,128)(2,1)S(1)}, u32[]{:S(2)}, u32[]{:S(2)}) %collective-permute-start.13) | collective-permute-done | bytes 557088 | tf_op jit(solution)/shard_map/ppermute | solution.py:721
  241.1 6.8 collective-permute-done.15.refs_3_
  248.2 15.7 %all-gather.9.cloned.1.call-done.refs_4_.refs_1_.refs_2_ = bf16[8,6,3,256,256]{4,3,2,1,0:T(8,128)(2,1)} async-done(((bf16[2,6,3,256,256]{4,3,2,1,0:T(8,128)(2,1)}), bf16[8,6,3,256,256]{4,3,2,1,0:T(8,128)(2,1)}) %all-gather.9.cloned.1.call-update) | async-done | bytes 18874384 | tf_op jit(solution)/shard_map/all_gather | solution.py:836
  263.9 28.1 %expert_up.2 = (bf16[1024,1536]{1,0:T(8,128)(2,1)}, bf16[1024,3072]{1,0:T(8,128)(2,1)}, f32[1024,128]{1,0:T(8,128)}) custom-call(s32[1]{0:T(128)} %bitcast.19.first_ref, bf16[512,2176]{1,0:T(8,128)(2,1)} %constant_dynamic-update-slice_fusion.refs_0_, bf16[512,2176]{1,0:T(8,128)(2,1)} %collective-permute-done.14.refs_1_, ...), custom_call_target="tpu_custom_call" | custom-call | flops 19327352832 | bytes 36700160 | tf_op jit(solution)/shard_map/expert_up/pallas_call | solution.py:438
  292.0 18.9 %expert_dx.2 = (bf16[512,2048]{1,0:T(8,128)(2,1)}, bf16[512,2048]{1,0:T(8,128)(2,1)}) custom-call(bf16[1024,3072]{1,0:T(8,128)(2,1)} %get-tuple-element.324.refs_0_.refs_5_, bf16[8,6,3,256,256]{4,3,2,1,0:T(8,128)(2,1)} %all-gather.9.cloned.1.call-done.refs_4_.refs_1_.refs_2_), custom_call_target="tpu_custom_call" | custom-call | flops 12884901888 | bytes 23068672 | tf_op jit(solution)/shard_map/expert_dx/pallas_call | solution.py:562
  311.0 27.0 %expert_grad.2 = bf16[8,6,3,256,256]{4,3,2,1,0:T(8,128)(2,1)} custom-call(bf16[512,2176]{1,0:T(8,128)(2,1)} %constant_dynamic-update-slice_fusion.refs_0_, bf16[512,2176]{1,0:T(8,128)(2,1)} %collective-permute-done.14.refs_1_, bf16[512,2048]{1,0:T(8,128)(2,1)} %pad_maximum_fusion.refs_2_, bf16[512,2048]{1,0:T(8,128)(2,1)} %collective-permute-done.15.refs_3_, ...), custom_call_target="tpu_custom_call" | custom-call | flops 19327352832 | bytes 36700160 | tf_op jit(solution)/shard_map/expert_grad/pallas_call | solution.py:477
  338.2 13.2 %expert_up.3 = (bf16[1024,512]{1,0:T(8,128)(2,1)}, bf16[1024,1024]{1,0:T(8,128)(2,1)}, f32[1024,128]{1,0:T(8,128)}) custom-call(s32[1]{0:T(128)} %bitcast.22.first_ref, bf16[512,2176]{1,0:T(8,128)(2,1)} %constant_dynamic-update-slice_fusion.refs_0_, bf16[512,2176]{1,0:T(8,128)(2,1)} %collective-permute-done.14.refs_1_, ...), custom_call_target="tpu_custom_call" | custom-call | flops 6442450944 | bytes 17825792 | tf_op jit(solution)/shard_map/expert_up/pallas_call | solution.py:438
  351.4 10.5 %expert_dx.3 = (bf16[512,2176]{1,0:T(8,128)(2,1)}, bf16[512,2176]{1,0:T(8,128)(2,1)}) custom-call(bf16[1024,1024]{1,0:T(8,128)(2,1)} %get-tuple-element.362.refs_0_.refs_5_, bf16[8,2,3,256,256]{4,3,2,1,0:T(8,128)(2,1)} %all-gather.11.cloned.1.call-done.refs_4_.refs_1_.refs_3_, f32[1024,128]{1,0:T(8,128)} %get-tuple-element.336.refs_2_, ...), custom_call_target="tpu_custom_call" | custom-call | flops 4294967296 | bytes 10747904 | tf_op jit(solution)/shard_map/expert_dx/pallas_call | solution.py:562
  368.4 13.2 %collective-permute-done.17 = bf16[128,2176]{1,0:T(8,128)(2,1)S(1)} collective-permute-done((bf16[128,2176]{1,0:T(8,128)(2,1)S(1)}, bf16[128,2176]{1,0:T(8,128)(2,1)S(1)}, u32[]{:S(2)}, u32[]{:S(2)}) %collective-permute-start.17) | collective-permute-done | bytes 557088 | tf_op jit(solution)/shard_map/ppermute | solution.py:721
  386.8 13.8 %expert_out.1 = (bf16[512,2048]{1,0:T(8,128)(2,1)}, bf16[512,2048]{1,0:T(8,128)(2,1)}) custom-call(bf16[1024,1536]{1,0:T(8,128)(2,1)} %get-tuple-element.351.refs_4_.refs_0_, bf16[1024,512]{1,0:T(8,128)(2,1)} %get-tuple-element.361.refs_1_.refs_4_, bf16[8,6,3,256,256]{4,3,2,1,0:T(8,128)(2,1)} %all-gather.9.cloned.1.call-done.refs_4_.refs_1_.refs_2_, ...), custom_call_target="tpu_custom_call" | custom-call | flops 8589934592 | bytes 16777216 | tf_op jit(solution)/shard_map/expert_out/pallas_call | solution.py:562
  400.6 13.0 %expert_grad.3 = bf16[8,2,3,256,256]{4,3,2,1,0:T(8,128)(2,1)} custom-call(bf16[512,2176]{1,0:T(8,128)(2,1)} %constant_dynamic-update-slice_fusion.refs_0_, bf16[512,2176]{1,0:T(8,128)(2,1)} %collective-permute-done.14.refs_1_, bf16[512,2048]{1,0:T(8,128)(2,1)} %pad_maximum_fusion.refs_2_, bf16[512,2048]{1,0:T(8,128)(2,1)} %collective-permute-done.15.refs_3_, ...), custom_call_target="tpu_custom_call" | custom-call | flops 6442450944 | bytes 17825792 | tf_op jit(solution)/shard_map/expert_grad/pallas_call | solution.py:477
  415.3 4.6 norm_two_back.1
  421.0 25.7 %collective-permute-done.22 = bf16[128,2048]{1,0:T(8,128)(2,1)S(1)} collective-permute-done((bf16[128,2048]{1,0:T(8,128)(2,1)}, bf16[128,2048]{1,0:T(8,128)(2,1)S(1)}, u32[]{:S(2)}, u32[]{:S(2)}) %collective-permute-start.22) | collective-permute-done | bytes 524320 | tf_op jit(solution)/shard_map/ppermute | solution.py:721
  446.9 13.7 %collective-permute-done.23 = bf16[128,2048]{1,0:T(8,128)(2,1)S(1)} collective-permute-done((bf16[128,2048]{1,0:T(8,128)(2,1)S(1)}, bf16[128,2048]{1,0:T(8,128)(2,1)S(1)}, u32[]{:S(2)}, u32[]{:S(2)}) %collective-permute-start.23) | collective-permute-done | bytes 524320 | tf_op jit(solution)/shard_map/ppermute | solution.py:721
  463.0 5.0 dheads.1.refs_8_
  468.7 13.2 %attend_back.1 = (f32[512,512]{1,0:T(8,128)}, bf16[2,512,512]{2,1,0:T(8,128)(2,1)}, bf16[2,512,512]{2,1,0:T(8,128)(2,1)}, bf16[2,512,512]{2,1,0:T(8,128)(2,1)}, bf16[2,512,512]{2,1,0:T(8,128)(2,1)}) custom-call(s32[7]{0:T(128)} %pad_add_fusion.scal_ref, bf16[512,512]{1,0:T(8,128)(2,1)} %get-tuple-element.387.q_ref, ...), custom_call_target="tpu_custom_call" | custom-call | flops 2684354560 | bytes 12582912 | tf_op jit(solution)/shard_map/attend_back/pallas_call | solution.py:209
  488.0 7.8 %gradout.1.kept_ref = bf16[8,4,256,512]{3,2,1,0:T(8,128)(2,1)} custom-call(s32[4]{0:T(128)} %copy-done.28, bf16[512,2048]{1,0:T(8,128)(2,1)} %copy-done.2, bf16[512,512]{1,0:T(8,128)(2,1)} %attend.1.h_ref), custom_call_target="tpu_custom_call" | custom-call | flops 1073741824 | bytes 4718592 | tf_op jit(solution)/shard_map/gradout/pallas_call | solution.py:288
  495.8 12.3 %collective-permute-done.25 = bf16[128,2048]{1,0:T(8,128)(2,1)} collective-permute-done((bf16[128,2048]{1,0:T(8,128)(2,1)}, bf16[128,2048]{1,0:T(8,128)(2,1)}, u32[]{:S(2)}, u32[]{:S(2)}) %collective-permute-start.25) | collective-permute-done | bytes 524320 | tf_op jit(solution)/shard_map/ppermute | solution.py:721
  514.7 14.0 %reduce-scatter.10.cloned.1.call-done = bf16[1,2,6,3,256,256]{5,4,3,2,1,0:T(8,128)(2,1)} async-done(((bf16[4,2,6,3,256,256]{5,4,3,2,1,0:T(8,128)(2,1)}), bf16[1,2,6,3,256,256]{5,4,3,2,1,0:T(8,128)(2,1)}) %reduce-scatter.10.cloned.1.call-update) | async-done | bytes 4718608
  528.8 5.1 dynamic-slice_bitcast_fusion.1
  539.4 6.3 unturn.1
  555.4 4.1 inplace.3
  561.6 11.0 %raw_back.1 = (bf16[512,1536]{1,0:T(8,128)(2,1)}, bf16[128,2048]{1,0:T(8,128)(2,1)}, bf16[128,2048]{1,0:T(8,128)(2,1)}, bf16[128,2048]{1,0:T(8,128)(2,1)}, bf16[128,2048]{1,0:T(8,128)(2,1)}) custom-call(s32[4]{0:T(128)} %copy-done.28, f32[2,512,512]{2,1,0:T(8,128)} %get-tuple-element.439.u_ref, f32[2,512,512]{2,1,0:T(8,128)} %get-tuple-element.440.raw_ref, ...), custom_call_target="tpu_custom_call" | custom-call | flops 3221225472 | bytes 13631488 | tf_op jit(solution)/shard_map/raw_back/pallas_call | solution.py:659
  572.7 9.3 %qkv_grad.1 = bf16[8,4,256,512]{3,2,1,0:T(8,128)(2,1)} custom-call(bf16[512,2048]{1,0:T(8,128)(2,1)} %get-tuple-element.451.n_ref, bf16[512,1536]{1,0:T(8,128)(2,1)} %get-tuple-element.452.d_ref, bf16[8,4,256,512]{3,2,1,0:T(8,128)(2,1)} %gradout.1.kept_ref), custom_call_target="tpu_custom_call", output_to_operand_aliasing={{}: (2, {})} | custom-call | flops 3221225472 | bytes 9961472 | tf_op jit(solution)/shard_map/qkv_grad/pallas_call | solution.py:693
  587.4 12.7 %collective-permute-done.36 = bf16[128,2048]{1,0:T(8,128)(2,1)S(1)} collective-permute-done((bf16[128,2048]{1,0:T(8,128)(2,1)S(1)}, bf16[128,2048]{1,0:T(8,128)(2,1)S(1)}, u32[]{:S(2)}, u32[]{:S(2)}) %collective-permute-start.36) | collective-permute-done | bytes 524320 | tf_op jit(solution)/shard_map/ppermute | solution.py:721
  606.6 14.2 %collective-permute-done.37.b_ref = bf16[128,2048]{1,0:T(8,128)(2,1)S(1)} collective-permute-done((bf16[128,2048]{1,0:T(8,128)(2,1)S(1)}, bf16[128,2048]{1,0:T(8,128)(2,1)S(1)}, u32[]{:S(2)}, u32[]{:S(2)}) %collective-permute-start.37) | collective-permute-done | bytes 524320 | tf_op jit(solution)/shard_map/ppermute | solution.py:721
  620.8 5.0 collective-permute-done.38.c_ref
  638.0 8.0 %settle.2 = (f32[16,2,256,256]{3,2,1,0:T(8,128)}, f32[16,256,256]{2,1,0:T(8,128)}) custom-call(s32[6]{0:T(128)} %pad_add_fusion.1.spot_ref, bf16[6,3,256,256]{3,2,1,0:T(8,128)(2,1)} %get-tuple-element.475.refs_0_, bf16[6,3,256,256]{3,2,1,0:T(8,128)(2,1)} %collective-permute-done.42.refs_1_), custom_call_target="tpu_custom_call" | custom-call | bytes 14155776 | tf_op jit(solution)/shard_map/settle/pallas_call | solution.py:508
  646.0 11.7 %collective-permute-done.41.refs_1_ = bf16[128,2048]{1,0:T(8,128)(2,1)} collective-permute-done((bf16[128,2048]{1,0:T(8,128)(2,1)S(1)}, bf16[128,2048]{1,0:T(8,128)(2,1)}, u32[]{:S(2)}, u32[]{:S(2)}) %collective-permute-start.41) | collective-permute-done | bytes 524320 | tf_op jit(solution)/shard_map/ppermute | solution.py:721
  666.2 7.1 %all-to-all-done.2 = f32[8,20,256]{2,1,0:T(8,128)S(1)} async-done(((f32[8,20,256]{2,1,0:T(8,128)}), f32[8,20,256]{2,1,0:T(8,128)S(1)}, u32[]{:S(2)}, u32[]{:S(2)}) %all-to-all-start.2) | async-done | bytes 163872 | tf_op jit(solution)/shard_map/all_to_all | solution.py:976
  677.2 3.9 settle.3
  (249 shorter events, 141.8 us)
Async XLA Ops:
  7.2 60.6 %all-gather.7.cloned.1.call-start = ((), (), s32[]{:S(2)}) async-start(), calls=%async_computation.6 | async-start | bytes 9437184 | tf_op jit(solution)/shard_map/all_gather | solution.py:829
  9.7 254.3 %all-gather.9.cloned.1.call-start = ((), (), s32[]{:S(2)}) async-start(), calls=%async_computation.7 | async-start | bytes 23592960 | tf_op jit(solution)/shard_map/all_gather | solution.py:836
  20.5 317.7 %all-gather.11.cloned.1.call-start = ((), (), s32[]{:S(2)}) async-start(), calls=%async_computation.8 | async-start | bytes 7864320 | tf_op jit(solution)/shard_map/all_gather | solution.py:836
  78.8 22.0 %collective-permute-start.2 = (bf16[512,512]{1,0:T(8,128)(2,1)}, bf16[512,512]{1,0:T(8,128)(2,1)S(1)}, u32[]{:S(2)}, u32[]{:S(2)}) collective-permute-start(bf16[512,512]{1,0:T(8,128)(2,1)} %get-tuple-element.392.refs_4_), channel_id=1, source_target_pairs={{0,8},{8,0},{1,9},{9,1},{2,10},{10,2},{3,11},{11,3},{4,12},{12,4},... | collective-permute-start | bytes 1572872 | tf_op jit(solution)/shard_map/ppermute | solution.py:711
  106.2 25.5 %collective-permute-start.4 = (bf16[512,512]{1,0:T(8,128)(2,1)}, bf16[512,512]{1,0:T(8,128)(2,1)}, u32[]{:S(2)}, u32[]{:S(2)}) collective-permute-start(bf16[512,512]{1,0:T(8,128)(2,1)} %get-tuple-element.388.refs_0_), channel_id=1, source_target_pairs={{0,8},{8,0},{1,9},{9,1},{2,10},{10,2},{3,11},{11,3},{4,12},{12,4},... | collective-permute-start | bytes 1572872 | tf_op jit(solution)/shard_map/ppermute | solution.py:711
  108.3 24.9 %collective-permute-start.6 = (bf16[512,512]{1,0:T(8,128)(2,1)S(1)}, bf16[512,512]{1,0:T(8,128)(2,1)}, u32[]{:S(2)}, u32[]{:S(2)}) collective-permute-start(bf16[512,512]{1,0:T(8,128)(2,1)S(1)} %copy-done.24), channel_id=1, source_target_pairs={{0,4},{4,0},{1,5},{5,1},{2,6},{6,2},{3,7},{7,3},{8,12},{12,8},{9,1... | collective-permute-start | bytes 1572872 | tf_op jit(solution)/shard_map/ppermute | solution.py:711
  108.3 24.9 %collective-permute-start.3 = (bf16[512,512]{1,0:T(8,128)(2,1)}, bf16[512,512]{1,0:T(8,128)(2,1)}, u32[]{:S(2)}, u32[]{:S(2)}) collective-permute-start(bf16[512,512]{1,0:T(8,128)(2,1)} %get-tuple-element.388.refs_0_), channel_id=1, source_target_pairs={{0,4},{4,0},{1,5},{5,1},{2,6},{6,2},{3,7},{7,3},{8,12},{12,8},{9,1... | collective-permute-start | bytes 1572872 | tf_op jit(solution)/shard_map/ppermute | solution.py:711
  108.8 24.3 %collective-permute-start.7 = (bf16[512,512]{1,0:T(8,128)(2,1)S(1)}, bf16[512,512]{1,0:T(8,128)(2,1)}, u32[]{:S(2)}, u32[]{:S(2)}) collective-permute-start(bf16[512,512]{1,0:T(8,128)(2,1)S(1)} %collective-permute-done.2.refs_6_), channel_id=1, source_target_pairs={{0,4},{4,0},{1,5},{5,1},{2,6},{6,2},{3,7},{7,3},{8,12},{12,8},{9,1... | collective-permute-start | bytes 1572872 | tf_op jit(solution)/shard_map/ppermute | solution.py:711
  149.3 15.0 %collective-permute-start.9 = (bf16[128,2048]{1,0:T(8,128)(2,1)}, bf16[128,2048]{1,0:T(8,128)(2,1)S(1)}, u32[]{:S(2)}, u32[]{:S(2)}) collective-permute-start(bf16[128,2048]{1,0:T(8,128)(2,1)} %get-tuple-element.286), channel_id=1, source_target_pairs={{0,1},{1,0},{2,3},{3,2},{4,5},{5,4},{6,7},{7,6},{8,9},{9,8},{10,11... | collective-permute-start | bytes 1572872 | tf_op jit(solution)/shard_map/ppermute | solution.py:721
  150.6 32.9 %collective-permute-start.8 = (bf16[128,2048]{1,0:T(8,128)(2,1)}, bf16[128,2048]{1,0:T(8,128)(2,1)S(1)}, u32[]{:S(2)}, u32[]{:S(2)}) collective-permute-start(bf16[128,2048]{1,0:T(8,128)(2,1)} %get-tuple-element.284), channel_id=1, source_target_pairs={{0,1},{1,0},{2,3},{3,2},{4,5},{5,4},{6,7},{7,6},{8,9},{9,8},{10,11... | collective-permute-start | bytes 1572872 | tf_op jit(solution)/shard_map/ppermute | solution.py:721
  165.6 24.7 %collective-permute-start.10 = (bf16[128,2048]{1,0:T(8,128)(2,1)S(1)}, bf16[128,2048]{1,0:T(8,128)(2,1)}, u32[]{:S(2)}, u32[]{:S(2)}) collective-permute-start(bf16[128,2048]{1,0:T(8,128)(2,1)S(1)} %add_convert_fusion.10), channel_id=1, source_target_pairs={{0,2},{1,3},{2,0},{3,1},{4,6},{5,7},{6,4},{7,5},{8,10},{9,11},{10,... | collective-permute-start | bytes 1572872 | tf_op jit(solution)/shard_map/ppermute | solution.py:721
  193.7 22.4 %collective-permute-start.12 = (bf16[128,2176]{1,0:T(8,128)(2,1)}, bf16[128,2176]{1,0:T(8,128)(2,1)S(1)}, u32[]{:S(2)}, u32[]{:S(2)}) collective-permute-start(bf16[128,2176]{1,0:T(8,128)(2,1)} %get-tuple-element.367.ext_ref), channel_id=1, source_target_pairs={{0,2},{1,3},{2,0},{3,1},{4,6},{5,7},{6,4},{7,5},{8,10},{9,11},{10,... | collective-permute-start | bytes 1671176 | tf_op jit(solution)/shard_map/ppermute | solution.py:721
  199.9 328.9 %reduce-scatter.10.cloned.1.call-start = ((), (), s32[]{:S(2)}) async-start(), calls=%async_computation.9 | async-start | bytes 23592960
  200.1 25.5 %collective-permute-start.11 = (bf16[128,2176]{1,0:T(8,128)(2,1)S(1)}, bf16[128,2176]{1,0:T(8,128)(2,1)S(1)}, u32[]{:S(2)}, u32[]{:S(2)}) collective-permute-start(bf16[128,2176]{1,0:T(8,128)(2,1)S(1)} %copy-done.7), channel_id=1, source_target_pairs={{0,1},{1,0},{2,3},{3,2},{4,5},{5,4},{6,7},{7,6},{8,9},{9,8},{10,11... | collective-permute-start | bytes 1671176 | tf_op jit(solution)/shard_map/ppermute | solution.py:721
  216.1 21.0 %collective-permute-start.13 = (bf16[128,2176]{1,0:T(8,128)(2,1)S(1)}, bf16[128,2176]{1,0:T(8,128)(2,1)S(1)}, u32[]{:S(2)}, u32[]{:S(2)}) collective-permute-start(bf16[128,2176]{1,0:T(8,128)(2,1)S(1)} %collective-permute-done.12), channel_id=1, source_target_pairs={{0,1},{1,0},{2,3},{3,2},{4,5},{5,4},{6,7},{7,6},{8,9},{9,8},{10,11... | collective-permute-start | bytes 1671176 | tf_op jit(solution)/shard_map/ppermute | solution.py:721
  240.6 7.7 %collective-permute-start.14 = (bf16[512,2176]{1,0:T(8,128)(2,1)}, bf16[512,2176]{1,0:T(8,128)(2,1)}, u32[]{:S(2)}, u32[]{:S(2)}) collective-permute-start(bf16[512,2176]{1,0:T(8,128)(2,1)} %constant_dynamic-update-slice_fusion.refs_0_), channel_id=1, source_target_pairs={{0,4},{4,0},{1,5},{5,1},{2,6},{6,2},{3,7},{7,3},{8,12},{12,8},{9,1... | collective-permute-start | bytes 6684680 | tf_op jit(solution)/shard_map/ppermute | solution.py:711
  240.6 7.3 %collective-permute-start.15 = (bf16[512,2048]{1,0:T(8,128)(2,1)S(1)}, bf16[512,2048]{1,0:T(8,128)(2,1)}, u32[]{:S(2)}, u32[]{:S(2)}) collective-permute-start(bf16[512,2048]{1,0:T(8,128)(2,1)S(1)} %copy-done.9), channel_id=1, source_target_pairs={{0,4},{4,0},{1,5},{5,1},{2,6},{6,2},{3,7},{7,3},{8,12},{12,8},{9,1... | collective-permute-start | bytes 6291464 | tf_op jit(solution)/shard_map/ppermute | solution.py:711
  337.9 300.1 %reduce-scatter.14.cloned.1.call-start = ((), (), s32[]{:S(2)}) async-start(), calls=%async_computation.11 | async-start | bytes 7864320
  361.9 4.6 collective-permute-start.16
  366.8 14.7 %collective-permute-start.17 = (bf16[128,2176]{1,0:T(8,128)(2,1)S(1)}, bf16[128,2176]{1,0:T(8,128)(2,1)S(1)}, u32[]{:S(2)}, u32[]{:S(2)}) collective-permute-start(bf16[128,2176]{1,0:T(8,128)(2,1)S(1)} %add_convert_fusion.4), channel_id=1, source_target_pairs={{0,1},{1,0},{2,3},{3,2},{4,5},{5,4},{6,7},{7,6},{8,9},{9,8},{10,11... | collective-permute-start | bytes 1671176 | tf_op jit(solution)/shard_map/ppermute | solution.py:721
  381.8 31.9 %collective-permute-start.20 = (bf16[128,2176]{1,0:T(8,128)(2,1)S(1)}, bf16[128,2176]{1,0:T(8,128)(2,1)S(1)}, u32[]{:S(2)}, u32[]{:S(2)}) collective-permute-start(bf16[128,2176]{1,0:T(8,128)(2,1)S(1)} %add_convert_fusion.3), channel_id=1, source_target_pairs={{0,2},{1,3},{2,0},{3,1},{4,6},{5,7},{6,4},{7,5},{8,10},{9,11},{10,... | collective-permute-start | bytes 1671176 | tf_op jit(solution)/shard_map/ppermute | solution.py:721
  384.4 29.3 %collective-permute-start.19 = (bf16[128,2176]{1,0:T(8,128)(2,1)S(1)}, bf16[128,2176]{1,0:T(8,128)(2,1)S(1)}, u32[]{:S(2)}, u32[]{:S(2)}) collective-permute-start(bf16[128,2176]{1,0:T(8,128)(2,1)S(1)} %add_convert_fusion.2), channel_id=1, source_target_pairs={{0,1},{1,0},{2,3},{3,2},{4,5},{5,4},{6,7},{7,6},{8,9},{9,8},{10,11... | collective-permute-start | bytes 1671176 | tf_op jit(solution)/shard_map/ppermute | solution.py:721
  400.6 60.2 %collective-permute-start.18 = (bf16[512,2048]{1,0:T(8,128)(2,1)}, bf16[512,2048]{1,0:T(8,128)(2,1)S(1)}, u32[]{:S(2)}, u32[]{:S(2)}) collective-permute-start(bf16[512,2048]{1,0:T(8,128)(2,1)} %get-tuple-element.356), channel_id=1, source_target_pairs={{0,4},{4,0},{1,5},{5,1},{2,6},{6,2},{3,7},{7,3},{8,12},{12,8},{9,1... | collective-permute-start | bytes 6291464 | tf_op jit(solution)/shard_map/ppermute | solution.py:711
  419.9 26.8 %collective-permute-start.22 = (bf16[128,2048]{1,0:T(8,128)(2,1)}, bf16[128,2048]{1,0:T(8,128)(2,1)S(1)}, u32[]{:S(2)}, u32[]{:S(2)}) collective-permute-start(bf16[128,2048]{1,0:T(8,128)(2,1)} %get-tuple-element.377), channel_id=1, source_target_pairs={{0,2},{1,3},{2,0},{3,1},{4,6},{5,7},{6,4},{7,5},{8,10},{9,11},{10,... | collective-permute-start | bytes 1572872 | tf_op jit(solution)/shard_map/ppermute | solution.py:721
  421.0 25.8 %collective-permute-start.21 = (bf16[128,2048]{1,0:T(8,128)(2,1)}, bf16[128,2048]{1,0:T(8,128)(2,1)S(1)}, u32[]{:S(2)}, u32[]{:S(2)}) collective-permute-start(bf16[128,2048]{1,0:T(8,128)(2,1)} %get-tuple-element.377), channel_id=1, source_target_pairs={{0,1},{1,0},{2,3},{3,2},{4,5},{5,4},{6,7},{7,6},{8,9},{9,8},{10,11... | collective-permute-start | bytes 1572872 | tf_op jit(solution)/shard_map/ppermute | solution.py:721
  446.7 13.9 %collective-permute-start.23 = (bf16[128,2048]{1,0:T(8,128)(2,1)S(1)}, bf16[128,2048]{1,0:T(8,128)(2,1)S(1)}, u32[]{:S(2)}, u32[]{:S(2)}) collective-permute-start(bf16[128,2048]{1,0:T(8,128)(2,1)S(1)} %collective-permute-done.22), channel_id=1, source_target_pairs={{0,1},{1,0},{2,3},{3,2},{4,5},{5,4},{6,7},{7,6},{8,9},{9,8},{10,11... | collective-permute-start | bytes 1572872 | tf_op jit(solution)/shard_map/ppermute | solution.py:721
  468.0 219.0 %reduce-scatter.12.cloned.1.call-start = ((), (), s32[]{:S(2)}) async-start(), calls=%async_computation.10 | async-start | bytes 5242880
  468.3 14.1 %collective-permute-start.24 = (bf16[128,2048]{1,0:T(8,128)(2,1)}, bf16[128,2048]{1,0:T(8,128)(2,1)S(1)}, u32[]{:S(2)}, u32[]{:S(2)}) collective-permute-start(bf16[128,2048]{1,0:T(8,128)(2,1)} %add_convert_fusion.9), channel_id=1, source_target_pairs={{0,1},{1,0},{2,3},{3,2},{4,5},{5,4},{6,7},{7,6},{8,9},{9,8},{10,11... | collective-permute-start | bytes 1572872 | tf_op jit(solution)/shard_map/ppermute | solution.py:721
  481.9 52.0 %collective-permute-start.30 = (bf16[2,512,512]{2,1,0:T(8,128)(2,1)}, bf16[2,512,512]{2,1,0:T(8,128)(2,1)}, u32[]{:S(2)}, u32[]{:S(2)}) collective-permute-start(bf16[2,512,512]{2,1,0:T(8,128)(2,1)} %get-tuple-element.399), channel_id=1, source_target_pairs={{0,4},{4,0},{1,5},{5,1},{2,6},{6,2},{3,7},{7,3},{8,12},{12,8},{9,1... | collective-permute-start | bytes 3145736 | tf_op jit(solution)/shard_map/ppermute | solution.py:711
  483.5 26.3 %collective-permute-start.26 = (bf16[128,2048]{1,0:T(8,128)(2,1)}, bf16[128,2048]{1,0:T(8,128)(2,1)S(1)}, u32[]{:S(2)}, u32[]{:S(2)}) collective-permute-start(bf16[128,2048]{1,0:T(8,128)(2,1)} %add_convert_fusion.8), channel_id=1, source_target_pairs={{0,2},{1,3},{2,0},{3,1},{4,6},{5,7},{6,4},{7,5},{8,10},{9,11},{10,... | collective-permute-start | bytes 1572872 | tf_op jit(solution)/shard_map/ppermute | solution.py:721
  485.9 22.1 %collective-permute-start.25 = (bf16[128,2048]{1,0:T(8,128)(2,1)}, bf16[128,2048]{1,0:T(8,128)(2,1)}, u32[]{:S(2)}, u32[]{:S(2)}) collective-permute-start(bf16[128,2048]{1,0:T(8,128)(2,1)} %add_convert_fusion.7), channel_id=1, source_target_pairs={{0,1},{1,0},{2,3},{3,2},{4,5},{5,4},{6,7},{7,6},{8,9},{9,8},{10,11... | collective-permute-start | bytes 1572872 | tf_op jit(solution)/shard_map/ppermute | solution.py:721
  486.5 47.4 %collective-permute-start.31 = (bf16[2,512,512]{2,1,0:T(8,128)(2,1)S(1)}, bf16[2,512,512]{2,1,0:T(8,128)(2,1)}, u32[]{:S(2)}, u32[]{:S(2)}) collective-permute-start(bf16[2,512,512]{2,1,0:T(8,128)(2,1)S(1)} %add_convert_fusion), channel_id=1, source_target_pairs={{0,8},{8,0},{1,9},{9,1},{2,10},{10,2},{3,11},{11,3},{4,12},{12,4},... | collective-permute-start | bytes 3145736 | tf_op jit(solution)/shard_map/ppermute | solution.py:711
  511.2 25.4 %collective-permute-start.29 = (bf16[128,2048]{1,0:T(8,128)(2,1)S(1)}, bf16[128,2048]{1,0:T(8,128)(2,1)S(1)}, u32[]{:S(2)}, u32[]{:S(2)}) collective-permute-start(bf16[128,2048]{1,0:T(8,128)(2,1)S(1)} %add_convert_fusion.6.refs_0_), channel_id=1, source_target_pairs={{0,2},{1,3},{2,0},{3,1},{4,6},{5,7},{6,4},{7,5},{8,10},{9,11},{10,... | collective-permute-start | bytes 1572872 | tf_op jit(solution)/shard_map/ppermute | solution.py:721
  513.2 42.2 %collective-permute-start.28 = (bf16[128,2048]{1,0:T(8,128)(2,1)S(1)}, bf16[128,2048]{1,0:T(8,128)(2,1)}, u32[]{:S(2)}, u32[]{:S(2)}) collective-permute-start(bf16[128,2048]{1,0:T(8,128)(2,1)S(1)} %add_convert_fusion.6.refs_0_), channel_id=1, source_target_pairs={{0,1},{1,0},{2,3},{3,2},{4,5},{5,4},{6,7},{7,6},{8,9},{9,8},{10,11... | collective-permute-start | bytes 1572872 | tf_op jit(solution)/shard_map/ppermute | solution.py:721
  536.6 18.9 %collective-permute-start.32 = (bf16[128,2048]{1,0:T(8,128)(2,1)S(1)}, bf16[128,2048]{1,0:T(8,128)(2,1)}, u32[]{:S(2)}, u32[]{:S(2)}) collective-permute-start(bf16[128,2048]{1,0:T(8,128)(2,1)S(1)} %collective-permute-done.29.refs_2_), channel_id=1, source_target_pairs={{0,1},{1,0},{2,3},{3,2},{4,5},{5,4},{6,7},{7,6},{8,9},{9,8},{10,11... | collective-permute-start | bytes 1572872 | tf_op jit(solution)/shard_map/ppermute | solution.py:721
  550.6 4.8 collective-permute-start.34
  585.2 17.9 %collective-permute-start.35 = (bf16[4,4,256,512]{3,2,1,0:T(8,128)(2,1)S(1)}, bf16[4,4,256,512]{3,2,1,0:T(8,128)(2,1)S(1)}, u32[]{:S(2)}, u32[]{:S(2)}) collective-permute-start(bf16[4,4,256,512]{3,2,1,0:T(8,128)(2,1)S(1)} %dynamic-slice_bitcast_fusion), channel_id=1, source_target_pairs={{0,4},{4,0},{1,5},{5,1},{2,6},{6,2},{3,7},{7,3},{8,12},{12,8},{9,1... | collective-permute-start | bytes 12582920 | tf_op jit(solution)/shard_map/ppermute | solution.py:711
  585.3 14.8 %collective-permute-start.36 = (bf16[128,2048]{1,0:T(8,128)(2,1)S(1)}, bf16[128,2048]{1,0:T(8,128)(2,1)S(1)}, u32[]{:S(2)}, u32[]{:S(2)}) collective-permute-start(bf16[128,2048]{1,0:T(8,128)(2,1)S(1)} %copy-done.37), channel_id=1, source_target_pairs={{0,1},{1,0},{2,3},{3,2},{4,5},{5,4},{6,7},{7,6},{8,9},{9,8},{10,11... | collective-permute-start | bytes 1572872 | tf_op jit(solution)/shard_map/ppermute | solution.py:721
  587.1 33.7 %collective-permute-start.37 = (bf16[128,2048]{1,0:T(8,128)(2,1)S(1)}, bf16[128,2048]{1,0:T(8,128)(2,1)S(1)}, u32[]{:S(2)}, u32[]{:S(2)}) collective-permute-start(bf16[128,2048]{1,0:T(8,128)(2,1)S(1)} %copy-done.36), channel_id=1, source_target_pairs={{0,1},{1,0},{2,3},{3,2},{4,5},{5,4},{6,7},{7,6},{8,9},{9,8},{10,11... | collective-permute-start | bytes 1572872 | tf_op jit(solution)/shard_map/ppermute | solution.py:721
  600.2 25.5 %collective-permute-start.38 = (bf16[128,2048]{1,0:T(8,128)(2,1)S(1)}, bf16[128,2048]{1,0:T(8,128)(2,1)S(1)}, u32[]{:S(2)}, u32[]{:S(2)}) collective-permute-start(bf16[128,2048]{1,0:T(8,128)(2,1)S(1)} %add_convert_fusion.5), channel_id=1, source_target_pairs={{0,2},{1,3},{2,0},{3,1},{4,6},{5,7},{6,4},{7,5},{8,10},{9,11},{10,... | collective-permute-start | bytes 1572872 | tf_op jit(solution)/shard_map/ppermute | solution.py:721
  631.8 6.2 collective-permute-start.42
  632.8 24.9 %collective-permute-start.41 = (bf16[128,2048]{1,0:T(8,128)(2,1)S(1)}, bf16[128,2048]{1,0:T(8,128)(2,1)}, u32[]{:S(2)}, u32[]{:S(2)}) collective-permute-start(bf16[128,2048]{1,0:T(8,128)(2,1)S(1)} %copy-done.20), channel_id=1, source_target_pairs={{0,1},{1,0},{2,3},{3,2},{4,5},{5,4},{6,7},{7,6},{8,9},{9,8},{10,11... | collective-permute-start | bytes 1572872 | tf_op jit(solution)/shard_map/ppermute | solution.py:721
  634.1 27.6 %collective-permute-start.39 = (bf16[128,2048]{1,0:T(8,128)(2,1)S(1)}, bf16[128,2048]{1,0:T(8,128)(2,1)}, u32[]{:S(2)}, u32[]{:S(2)}) collective-permute-start(bf16[128,2048]{1,0:T(8,128)(2,1)S(1)} %copy-done.20), channel_id=1, source_target_pairs={{0,2},{1,3},{2,0},{3,1},{4,6},{5,7},{6,4},{7,5},{8,10},{9,11},{10,... | collective-permute-start | bytes 1572872 | tf_op jit(solution)/shard_map/ppermute | solution.py:721
  661.7 14.6 %collective-permute-start.44 = (bf16[2,3,256,256]{3,2,1,0:T(8,128)(2,1)S(1)}, bf16[2,3,256,256]{3,2,1,0:T(8,128)(2,1)S(1)}, u32[]{:S(2)}, u32[]{:S(2)}) collective-permute-start(bf16[2,3,256,256]{3,2,1,0:T(8,128)(2,1)S(1)} %get-tuple-element.524), channel_id=1, source_target_pairs={{0,4},{4,0},{1,5},{5,1},{2,6},{6,2},{3,7},{7,3},{8,12},{12,8},{9,1... | collective-permute-start | bytes 2359304 | tf_op jit(solution)/shard_map/ppermute | solution.py:711
  661.7 19.5 %collective-permute-start.40 = (bf16[128,2048]{1,0:T(8,128)(2,1)}, bf16[128,2048]{1,0:T(8,128)(2,1)S(1)}, u32[]{:S(2)}, u32[]{:S(2)}) collective-permute-start(bf16[128,2048]{1,0:T(8,128)(2,1)} %collective-permute-done.39.refs_0_), channel_id=1, source_target_pairs={{0,1},{1,0},{2,3},{3,2},{4,5},{5,4},{6,7},{7,6},{8,9},{9,8},{10,11... | collective-permute-start | bytes 1572872 | tf_op jit(solution)/shard_map/ppermute | solution.py:721
  662.5 10.8 %all-to-all-start.2 = ((f32[8,20,256]{2,1,0:T(8,128)}), f32[8,20,256]{2,1,0:T(8,128)S(1)}, u32[]{:S(2)}, u32[]{:S(2)}) async-start(f32[8,20,256]{2,1,0:T(8,128)} %bitcast.66), calls=%async_computation.2 | async-start | bytes 393216 | tf_op jit(solution)/shard_map/all_to_all | solution.py:976
  673.4 7.7 %collective-permute-start.43 = (f32[20,256]{1,0:T(8,128)S(1)}, f32[20,256]{1,0:T(8,128)S(1)}, u32[]{:S(2)}, u32[]{:S(2)}) collective-permute-start(f32[20,256]{1,0:T(8,128)S(1)} %reduce_sum.9), channel_id=1, source_target_pairs={{0,1},{1,0},{2,3},{3,2},{4,5},{5,4},{6,7},{7,6},{8,9},{9,8},{10,11... | collective-permute-start | bytes 61448 | tf_op jit(solution)/shard_map/ppermute | solution.py:721
  681.1 4.8 collective-permute-start.45
  (43 other events, 451.6 us)
Sparse Core Ops, SparseCore 0:
  10.5 57.2 all-gather.6
  69.6 194.2 all-gather.8
  265.8 70.1 all-gather.10
  338.9 189.7 reduce-scatter.9
  531.9 71.1 reduce-scatter.13
  630.3 54.0 reduce-scatter.11

commit v6 on v5

--- a/solution.py
+++ b/solution.py
@@ -642,7 +642,6 @@
     w = jnp.concatenate([w_ref[:, c].reshape(pb * ds, n) for c in range(3)], 1)
     y = nt(d_ref[...], w).astype(BF16)
     rows = outs[0].shape[0]
-    outs[0][...] = y[:rows]
     for r, o in enumerate(outs):
         for q in range(len(outs)):
 
@@ -952,25 +951,17 @@
     )
     last = across(d_one[3], 1)
     grad_attn = line(qkv_grads, normed_one, d_raw, grad_attn, p)
-    grad_attn = grad_attn.reshape((-1, 2) + grad_attn.shape[1:])
-    theirs = line(lambda v: lax.dynamic_index_in_dim(v, core ^ 1, 1, keepdims=False), grad_attn)
-    theirs = swap(theirs, "core")
+    grad_attn = lax.psum_scatter(grad_attn, PLANE, scatter_dimension=0, tiled=False)
     near = line(add, d_one[2], last)
     d_one = [d_one[0], across(d_one[1], 1), across(near, 2)]
-    grad_attn = line(
-        lambda v, w: add(lax.dynamic_index_in_dim(v, core, 1, keepdims=False), w), grad_attn, theirs
-    )
     grad_in, gain_one = line(norm_one_back, d_one, x_q, d_mid, gains[0:1])
-    grad_attn, gain_one = lax.optimization_barrier((grad_attn, gain_one))
-    grad_attn = lax.optimization_barrier(lax.psum_scatter(grad_attn, FR, scatter_dimension=0, tiled=False))
     far = across(grad_in, 2)
+    near = across(grad_in, 1)
     placed = lax.dynamic_update_slice_in_dim(
         jnp.zeros((2, width), F32), gain_qk[:, 0, :], column * n, 1
     )
 
     small = line(lambda *v: jnp.concatenate(v, 0), grad_router[:experts], gain_one, gain_two, placed)
-    near, small = lax.optimization_barrier((grad_in, small))
-    near = across(near, 1)
     rows = small.shape[0]
     small = small.reshape(rows, p, ds).transpose(1, 0, 2)
     small = jnp.sum(lax.all_to_all(small, PLANE, 0, 0, tiled=True), 0)

time: 708 us -> 701 us (level)
    ppermute x16 -> x15, waiting for transfers between devices: 43.5 us -> 43.5 us  [swap(): return lax.ppermute(value, axis, [(0, 1), (1, 0)])]
  transfers between devices with their start and end apart: 53 -> 52, of which waited for: 31 -> 32; matrix products, arithmetic and copies ran while one was open for 8% -> 7% of each run, Pallas kernels for 34% -> 35%
where the time goes in v6:
time: 701 us; the launch traced here: 691 us
  waiting for transfers between devices  272 us (39%)
  Pallas kernels  241 us (34%)
  starting transfers between devices  52.8 us (8%)
  local copies, waits for them, and re-layouts  41.6 us (6%)
  blocking collectives  35.3 us (5%)
  other arithmetic  25.4 us (4%)
  between operations  22.9 us (3%)
    ppermute x30, waiting for transfers between devices, across(): return lax.ppermute(value, 'tp', [(i, i ^ k) for i in range(size)])  181 us
    ppermute x15, waiting for transfers between devices, swap(): return lax.ppermute(value, axis, [(0, 1), (1, 0)])  43.5 us
    pallas_call x3, Pallas kernels, expert_down(): call(functools.partial(down_kernel, planes=planes, chunks=chunks, sides=l...  43.2 us
    ppermute x30, starting transfers between devices, across(): return lax.ppermute(value, 'tp', [(i, i ^ k) for i in range(size)])  42.1 us
    pallas_call x2, Pallas kernels, expert_up(): call(functools.partial(expert_kernel, parts=parts), 'expert_up', (e,), [f...  41.4 us
    pallas_call x2, Pallas kernels, expert_grads(): call(functools.partial(expert_grad_kernel, parts=parts), 'expert_grad', (...  40 us
    all_gather x2, waiting for transfers between devices, body(): lax.all_gather(mine, FR, axis=0, tiled=False).reshape(-1, e, 3, ds, f)  15.7 us
    all_to_all x2, blocking collectives, body(): mine = lax.all_to_all(grouped[:, begin:begin + e], 'core', 0, 0, tiled=True)  14.5 us
  transfers between devices with their start and end apart: 52, of which 32 were waited for; matrix products, arithmetic and copies ran while one was open for 7% of the time, Pallas kernels for 35%

profile of v6, /device:TPU:0, one launch (start us, length us, event | category | flops | bytes accessed | tf_op | source)
XLA Modules:
  0.0 691.2 jit_solution(9667911742036243754)
XLA Ops:
  11.9 8.6 %all_to_all.15 = bf16[2,6,3,256,256]{4,3,2,1,0:T(8,128)(2,1)} all-to-all(bf16[2,6,3,256,256]{4,3,2,1,0:T(8,128)(2,1)S(1)} %fusion), channel_id=1, replica_groups=mesh['fsdp'=2,'row'=2,'core'=2,'tp'=4] {'core'}, dimensions={0} | all-to-all | bytes 9437184 | tf_op jit(solution)/shard_map/all_to_all | solution.py:834
  29.6 10.3 %all_gather.26 = bf16[4,2048]{1,0:T(4,128)(2,1)S(1)} all-gather(bf16[4,256]{1,0:T(4,128)(2,1)S(1)} %copy-done.33), channel_id=1, replica_groups=mesh['fsdp'=2,'row'=2,'core'=2,'tp'=4] {'fsdp','row','core'}, dimensions={1}, use_global_device_ids=true | all-gather | bytes 18432 | tf_op jit(solution)/shard_map/all_gather | solution.py:836
  39.9 10.4 %all_gather.27 = bf16[2048,16]{0,1:T(8,128)(2,1)} all-gather(bf16[256,16]{0,1:T(8,128)(2,1)S(1)} %copy-done.30), channel_id=1, replica_groups=mesh['fsdp'=2,'row'=2,'core'=2,'tp'=4] {'fsdp','row','core'}, dimensions={0}, use_global_device_ids=true | all-gather | bytes 73728 | tf_op jit(solution)/shard_map/all_gather | solution.py:837
  54.6 13.2 %all-gather.7.cloned.1.call-done = bf16[32,256,512]{2,1,0:T(8,128)(2,1)} async-done(((bf16[4,256,512]{2,1,0:T(8,128)(2,1)}), bf16[32,256,512]{2,1,0:T(8,128)(2,1)}) %all-gather.7.cloned.1.call-update) | async-done | bytes 8388624 | tf_op jit(solution)/shard_map/all_gather | solution.py:828
  68.4 10.4 %qkv.1 = (bf16[512,2048]{1,0:T(8,128)(2,1)}, f32[2,512,512]{2,1,0:T(8,128)}, bf16[512,512]{1,0:T(8,128)(2,1)}, f32[2,512,128]{2,1,0:T(8,128)}) custom-call(bf16[512,2048]{1,0:T(8,128)(2,1)} %bitcast.83, f32[1,2048]{1,0:T(1,128)} %get-tuple-element.454.g_ref, bf16[8,4,256,512]{3,2,1,0:T(8,128)(2,1)} %bitcast.61), custom_call_target="tpu_custom_call" | custom-call | flops 3221225472 | bytes 13107200 | tf_op jit(solution)/shard_map/qkv/pallas_call | solution.py:87
  91.1 9.7 %collective-permute-done.2.refs_6_ = bf16[512,512]{1,0:T(8,128)(2,1)S(1)} collective-permute-done((bf16[512,512]{1,0:T(8,128)(2,1)}, bf16[512,512]{1,0:T(8,128)(2,1)S(1)}, u32[]{:S(2)}, u32[]{:S(2)}) %collective-permute-start.2) | collective-permute-done | bytes 524320 | tf_op jit(solution)/shard_map/ppermute | solution.py:710
  101.8 4.4 prep.1
  108.8 22.9 %collective-permute-done.4.refs_2_ = bf16[512,512]{1,0:T(8,128)(2,1)} collective-permute-done((bf16[512,512]{1,0:T(8,128)(2,1)}, bf16[512,512]{1,0:T(8,128)(2,1)}, u32[]{:S(2)}, u32[]{:S(2)}) %collective-permute-start.4) | collective-permute-done | bytes 524320 | tf_op jit(solution)/shard_map/ppermute | solution.py:710
  134.0 9.9 %attend.1.h_ref = bf16[512,512]{1,0:T(8,128)(2,1)} custom-call(s32[7]{0:T(128)} %pad_add_fusion.scal_ref, bf16[512,512]{1,0:T(8,128)(2,1)} %get-tuple-element.380.q_ref, bf16[512,512]{1,0:T(8,128)(2,1)} %get-tuple-element.381.refs_0_, bf16[512,512]{1,0:T(8,128)(2,1)} %collective-permute-done.3.refs_1_, bf16[512,512]{1,0:T(8,128)(2,1)} %collective-permute-done.4.refs_2_, ...), custom_call_target="tpu_custom_call" | custom-call | flops 1073741824 | bytes 6291456 | tf_op jit(solution)/shard_map/attend/pallas_call | solution.py:171
  143.9 5.4 outproj.1
  151.4 12.9 %collective-permute-done.9 = bf16[128,2048]{1,0:T(8,128)(2,1)S(1)} collective-permute-done((bf16[128,2048]{1,0:T(8,128)(2,1)}, bf16[128,2048]{1,0:T(8,128)(2,1)S(1)}, u32[]{:S(2)}, u32[]{:S(2)}) %collective-permute-start.9) | collective-permute-done | bytes 524320 | tf_op jit(solution)/shard_map/ppermute | solution.py:720
  171.6 11.9 %collective-permute-done.8.b_ref = bf16[128,2048]{1,0:T(8,128)(2,1)S(1)} collective-permute-done((bf16[128,2048]{1,0:T(8,128)(2,1)}, bf16[128,2048]{1,0:T(8,128)(2,1)S(1)}, u32[]{:S(2)}, u32[]{:S(2)}) %collective-permute-start.8) | collective-permute-done | bytes 524320 | tf_op jit(solution)/shard_map/ppermute | solution.py:720
  183.5 6.8 collective-permute-done.10.c_ref
  193.9 6.0 all_to_all.16
  200.1 3.7 collective-permute-start.11
  203.9 12.2 %collective-permute-done.12 = bf16[128,2176]{1,0:T(8,128)(2,1)S(1)} collective-permute-done((bf16[128,2176]{1,0:T(8,128)(2,1)}, bf16[128,2176]{1,0:T(8,128)(2,1)S(1)}, u32[]{:S(2)}, u32[]{:S(2)}) %collective-permute-start.12) | collective-permute-done | bytes 557088 | tf_op jit(solution)/shard_map/ppermute | solution.py:720
  216.9 8.9 %collective-permute-done.11 = bf16[128,2176]{1,0:T(8,128)(2,1)S(1)} collective-permute-done((bf16[128,2176]{1,0:T(8,128)(2,1)S(1)}, bf16[128,2176]{1,0:T(8,128)(2,1)S(1)}, u32[]{:S(2)}, u32[]{:S(2)}) %collective-permute-start.11) | collective-permute-done | bytes 557088 | tf_op jit(solution)/shard_map/ppermute | solution.py:720
  225.7 11.5 %collective-permute-done.13 = bf16[128,2176]{1,0:T(8,128)(2,1)S(1)} collective-permute-done((bf16[128,2176]{1,0:T(8,128)(2,1)S(1)}, bf16[128,2176]{1,0:T(8,128)(2,1)S(1)}, u32[]{:S(2)}, u32[]{:S(2)}) %collective-permute-start.13) | collective-permute-done | bytes 557088 | tf_op jit(solution)/shard_map/ppermute | solution.py:720
  241.1 6.8 collective-permute-done.15.refs_3_
  248.3 15.6 %all-gather.9.cloned.1.call-done.refs_4_.refs_1_.refs_2_ = bf16[8,6,3,256,256]{4,3,2,1,0:T(8,128)(2,1)} async-done(((bf16[2,6,3,256,256]{4,3,2,1,0:T(8,128)(2,1)}), bf16[8,6,3,256,256]{4,3,2,1,0:T(8,128)(2,1)}) %all-gather.9.cloned.1.call-update) | async-done | bytes 18874384 | tf_op jit(solution)/shard_map/all_gather | solution.py:835
  263.9 28.1 %expert_up.2 = (bf16[1024,1536]{1,0:T(8,128)(2,1)}, bf16[1024,3072]{1,0:T(8,128)(2,1)}, f32[1024,128]{1,0:T(8,128)}) custom-call(s32[1]{0:T(128)} %bitcast.19.first_ref, bf16[512,2176]{1,0:T(8,128)(2,1)} %constant_dynamic-update-slice_fusion.refs_0_, bf16[512,2176]{1,0:T(8,128)(2,1)} %collective-permute-done.14.refs_1_, ...), custom_call_target="tpu_custom_call" | custom-call | flops 19327352832 | bytes 36700160 | tf_op jit(solution)/shard_map/expert_up/pallas_call | solution.py:438
  292.0 18.9 %expert_dx.2 = (bf16[512,2048]{1,0:T(8,128)(2,1)}, bf16[512,2048]{1,0:T(8,128)(2,1)}) custom-call(bf16[1024,3072]{1,0:T(8,128)(2,1)} %get-tuple-element.317.refs_0_.refs_5_, bf16[8,6,3,256,256]{4,3,2,1,0:T(8,128)(2,1)} %all-gather.9.cloned.1.call-done.refs_4_.refs_1_.refs_2_), custom_call_target="tpu_custom_call" | custom-call | flops 12884901888 | bytes 23068672 | tf_op jit(solution)/shard_map/expert_dx/pallas_call | solution.py:562
  311.0 27.0 %expert_grad.2 = bf16[8,6,3,256,256]{4,3,2,1,0:T(8,128)(2,1)} custom-call(bf16[512,2176]{1,0:T(8,128)(2,1)} %constant_dynamic-update-slice_fusion.refs_0_, bf16[512,2176]{1,0:T(8,128)(2,1)} %collective-permute-done.14.refs_1_, bf16[512,2048]{1,0:T(8,128)(2,1)} %pad_maximum_fusion.refs_2_, bf16[512,2048]{1,0:T(8,128)(2,1)} %collective-permute-done.15.refs_3_, ...), custom_call_target="tpu_custom_call" | custom-call | flops 19327352832 | bytes 36700160 | tf_op jit(solution)/shard_map/expert_grad/pallas_call | solution.py:477
  338.3 13.3 %expert_up.3 = (bf16[1024,512]{1,0:T(8,128)(2,1)}, bf16[1024,1024]{1,0:T(8,128)(2,1)}, f32[1024,128]{1,0:T(8,128)}) custom-call(s32[1]{0:T(128)} %bitcast.22.first_ref, bf16[512,2176]{1,0:T(8,128)(2,1)} %constant_dynamic-update-slice_fusion.refs_0_, bf16[512,2176]{1,0:T(8,128)(2,1)} %collective-permute-done.14.refs_1_, ...), custom_call_target="tpu_custom_call" | custom-call | flops 6442450944 | bytes 17825792 | tf_op jit(solution)/shard_map/expert_up/pallas_call | solution.py:438
  351.5 10.5 %expert_dx.3 = (bf16[512,2176]{1,0:T(8,128)(2,1)}, bf16[512,2176]{1,0:T(8,128)(2,1)}) custom-call(bf16[1024,1024]{1,0:T(8,128)(2,1)} %get-tuple-element.355.refs_0_.refs_5_, bf16[8,2,3,256,256]{4,3,2,1,0:T(8,128)(2,1)} %all-gather.11.cloned.1.call-done.refs_4_.refs_1_.refs_3_, f32[1024,128]{1,0:T(8,128)} %get-tuple-element.329.refs_2_, ...), custom_call_target="tpu_custom_call" | custom-call | flops 4294967296 | bytes 10747904 | tf_op jit(solution)/shard_map/expert_dx/pallas_call | solution.py:562
  368.4 13.2 %collective-permute-done.17 = bf16[128,2176]{1,0:T(8,128)(2,1)S(1)} collective-permute-done((bf16[128,2176]{1,0:T(8,128)(2,1)S(1)}, bf16[128,2176]{1,0:T(8,128)(2,1)S(1)}, u32[]{:S(2)}, u32[]{:S(2)}) %collective-permute-start.17) | collective-permute-done | bytes 557088 | tf_op jit(solution)/shard_map/ppermute | solution.py:720
  386.9 13.8 %expert_out.1 = (bf16[512,2048]{1,0:T(8,128)(2,1)}, bf16[512,2048]{1,0:T(8,128)(2,1)}) custom-call(bf16[1024,1536]{1,0:T(8,128)(2,1)} %get-tuple-element.344.refs_4_.refs_0_, bf16[1024,512]{1,0:T(8,128)(2,1)} %get-tuple-element.354.refs_1_.refs_4_, bf16[8,6,3,256,256]{4,3,2,1,0:T(8,128)(2,1)} %all-gather.9.cloned.1.call-done.refs_4_.refs_1_.refs_2_, ...), custom_call_target="tpu_custom_call" | custom-call | flops 8589934592 | bytes 16777216 | tf_op jit(solution)/shard_map/expert_out/pallas_call | solution.py:562
  400.7 13.1 %expert_grad.3 = bf16[8,2,3,256,256]{4,3,2,1,0:T(8,128)(2,1)} custom-call(bf16[512,2176]{1,0:T(8,128)(2,1)} %constant_dynamic-update-slice_fusion.refs_0_, bf16[512,2176]{1,0:T(8,128)(2,1)} %collective-permute-done.14.refs_1_, bf16[512,2048]{1,0:T(8,128)(2,1)} %pad_maximum_fusion.refs_2_, bf16[512,2048]{1,0:T(8,128)(2,1)} %collective-permute-done.15.refs_3_, ...), custom_call_target="tpu_custom_call" | custom-call | flops 6442450944 | bytes 17825792 | tf_op jit(solution)/shard_map/expert_grad/pallas_call | solution.py:477
  415.4 4.5 norm_two_back.1
  421.1 25.6 %collective-permute-done.22 = bf16[128,2048]{1,0:T(8,128)(2,1)S(1)} collective-permute-done((bf16[128,2048]{1,0:T(8,128)(2,1)}, bf16[128,2048]{1,0:T(8,128)(2,1)S(1)}, u32[]{:S(2)}, u32[]{:S(2)}) %collective-permute-start.22) | collective-permute-done | bytes 524320 | tf_op jit(solution)/shard_map/ppermute | solution.py:720
  446.9 13.7 %collective-permute-done.23 = bf16[128,2048]{1,0:T(8,128)(2,1)S(1)} collective-permute-done((bf16[128,2048]{1,0:T(8,128)(2,1)S(1)}, bf16[128,2048]{1,0:T(8,128)(2,1)S(1)}, u32[]{:S(2)}, u32[]{:S(2)}) %collective-permute-start.23) | collective-permute-done | bytes 524320 | tf_op jit(solution)/shard_map/ppermute | solution.py:720
  463.1 5.0 dheads.1.refs_8_
  468.8 13.2 %attend_back.1 = (f32[512,512]{1,0:T(8,128)}, bf16[2,512,512]{2,1,0:T(8,128)(2,1)}, bf16[2,512,512]{2,1,0:T(8,128)(2,1)}, bf16[2,512,512]{2,1,0:T(8,128)(2,1)}, bf16[2,512,512]{2,1,0:T(8,128)(2,1)}) custom-call(s32[7]{0:T(128)} %pad_add_fusion.scal_ref, bf16[512,512]{1,0:T(8,128)(2,1)} %get-tuple-element.380.q_ref, ...), custom_call_target="tpu_custom_call" | custom-call | flops 2684354560 | bytes 12582912 | tf_op jit(solution)/shard_map/attend_back/pallas_call | solution.py:209
  488.2 7.8 %gradout.1.kept_ref = bf16[8,4,256,512]{3,2,1,0:T(8,128)(2,1)} custom-call(s32[4]{0:T(128)} %copy-done.27, bf16[512,2048]{1,0:T(8,128)(2,1)} %copy-done.1, bf16[512,512]{1,0:T(8,128)(2,1)} %attend.1.h_ref), custom_call_target="tpu_custom_call" | custom-call | flops 1073741824 | bytes 4718592 | tf_op jit(solution)/shard_map/gradout/pallas_call | solution.py:288
  496.0 12.1 %collective-permute-done.25 = bf16[128,2048]{1,0:T(8,128)(2,1)} collective-permute-done((bf16[128,2048]{1,0:T(8,128)(2,1)}, bf16[128,2048]{1,0:T(8,128)(2,1)}, u32[]{:S(2)}, u32[]{:S(2)}) %collective-permute-start.25) | collective-permute-done | bytes 524320 | tf_op jit(solution)/shard_map/ppermute | solution.py:720
  514.9 13.6 %reduce-scatter.10.cloned.1.call-done = bf16[1,2,6,3,256,256]{5,4,3,2,1,0:T(8,128)(2,1)} async-done(((bf16[4,2,6,3,256,256]{5,4,3,2,1,0:T(8,128)(2,1)}), bf16[1,2,6,3,256,256]{5,4,3,2,1,0:T(8,128)(2,1)}) %reduce-scatter.10.cloned.1.call-update) | async-done | bytes 4718608
  528.6 5.1 dynamic-slice_bitcast_fusion
  539.3 6.6 unturn.1
  555.4 4.2 inplace.3
  561.7 11.1 %raw_back.1 = (bf16[512,1536]{1,0:T(8,128)(2,1)}, bf16[128,2048]{1,0:T(8,128)(2,1)}, bf16[128,2048]{1,0:T(8,128)(2,1)}, bf16[128,2048]{1,0:T(8,128)(2,1)}, bf16[128,2048]{1,0:T(8,128)(2,1)}) custom-call(s32[4]{0:T(128)} %copy-done.27, f32[2,512,512]{2,1,0:T(8,128)} %get-tuple-element.432.u_ref, f32[2,512,512]{2,1,0:T(8,128)} %get-tuple-element.433.raw_ref, ...), custom_call_target="tpu_custom_call" | custom-call | flops 3221225472 | bytes 13631488 | tf_op jit(solution)/shard_map/raw_back/pallas_call | solution.py:658
  572.8 9.2 %qkv_grad.1 = bf16[8,4,256,512]{3,2,1,0:T(8,128)(2,1)} custom-call(bf16[512,2048]{1,0:T(8,128)(2,1)} %get-tuple-element.444.n_ref, bf16[512,1536]{1,0:T(8,128)(2,1)} %get-tuple-element.445.d_ref, bf16[8,4,256,512]{3,2,1,0:T(8,128)(2,1)} %gradout.1.kept_ref), custom_call_target="tpu_custom_call", output_to_operand_aliasing={{}: (2, {})} | custom-call | flops 3221225472 | bytes 9961472 | tf_op jit(solution)/shard_map/qkv_grad/pallas_call | solution.py:692
  586.6 12.7 %collective-permute-done.36 = bf16[128,2048]{1,0:T(8,128)(2,1)S(1)} collective-permute-done((bf16[128,2048]{1,0:T(8,128)(2,1)S(1)}, bf16[128,2048]{1,0:T(8,128)(2,1)S(1)}, u32[]{:S(2)}, u32[]{:S(2)}) %collective-permute-start.36) | collective-permute-done | bytes 524320 | tf_op jit(solution)/shard_map/ppermute | solution.py:720
  602.9 17.2 %collective-permute-done.35.b_ref = bf16[128,2048]{1,0:T(8,128)(2,1)} collective-permute-done((bf16[128,2048]{1,0:T(8,128)(2,1)}, bf16[128,2048]{1,0:T(8,128)(2,1)}, u32[]{:S(2)}, u32[]{:S(2)}) %collective-permute-start.35) | collective-permute-done | bytes 524320 | tf_op jit(solution)/shard_map/ppermute | solution.py:720
  620.1 4.5 collective-permute-done.37.c_ref
  634.6 7.9 %settle.2 = (f32[16,2,256,256]{3,2,1,0:T(8,128)}, f32[16,256,256]{2,1,0:T(8,128)}) custom-call(s32[6]{0:T(128)} %pad_add_fusion.1.spot_ref, bf16[6,3,256,256]{3,2,1,0:T(8,128)(2,1)} %get-tuple-element.462.refs_0_, bf16[6,3,256,256]{3,2,1,0:T(8,128)(2,1)} %collective-permute-done.41.refs_1_), custom_call_target="tpu_custom_call" | custom-call | bytes 14155776 | tf_op jit(solution)/shard_map/settle/pallas_call | solution.py:508
  642.5 7.2 %collective-permute-done.40.refs_1_ = bf16[128,2048]{1,0:T(8,128)(2,1)S(1)} collective-permute-done((bf16[128,2048]{1,0:T(8,128)(2,1)}, bf16[128,2048]{1,0:T(8,128)(2,1)S(1)}, u32[]{:S(2)}, u32[]{:S(2)}) %collective-permute-start.40) | collective-permute-done | bytes 524320 | tf_op jit(solution)/shard_map/ppermute | solution.py:720
  660.3 5.6 all-to-all-done.2
  669.8 3.8 settle.3
  (239 shorter events, 138.2 us)
Async XLA Ops:
  7.2 60.6 %all-gather.7.cloned.1.call-start = ((), (), s32[]{:S(2)}) async-start(), calls=%async_computation.7 | async-start | bytes 9437184 | tf_op jit(solution)/shard_map/all_gather | solution.py:828
  9.7 254.3 %all-gather.9.cloned.1.call-start = ((), (), s32[]{:S(2)}) async-start(), calls=%async_computation.8 | async-start | bytes 23592960 | tf_op jit(solution)/shard_map/all_gather | solution.py:835
  20.5 317.8 %all-gather.11.cloned.1.call-start = ((), (), s32[]{:S(2)}) async-start(), calls=%async_computation.9 | async-start | bytes 7864320 | tf_op jit(solution)/shard_map/all_gather | solution.py:835
  78.8 22.0 %collective-permute-start.2 = (bf16[512,512]{1,0:T(8,128)(2,1)}, bf16[512,512]{1,0:T(8,128)(2,1)S(1)}, u32[]{:S(2)}, u32[]{:S(2)}) collective-permute-start(bf16[512,512]{1,0:T(8,128)(2,1)} %get-tuple-element.385.refs_4_), channel_id=1, source_target_pairs={{0,8},{8,0},{1,9},{9,1},{2,10},{10,2},{3,11},{11,3},{4,12},{12,4},... | collective-permute-start | bytes 1572872 | tf_op jit(solution)/shard_map/ppermute | solution.py:710
  86.6 4.5 collective-permute-start.1
  106.2 25.5 %collective-permute-start.4 = (bf16[512,512]{1,0:T(8,128)(2,1)}, bf16[512,512]{1,0:T(8,128)(2,1)}, u32[]{:S(2)}, u32[]{:S(2)}) collective-permute-start(bf16[512,512]{1,0:T(8,128)(2,1)} %get-tuple-element.381.refs_0_), channel_id=1, source_target_pairs={{0,8},{8,0},{1,9},{9,1},{2,10},{10,2},{3,11},{11,3},{4,12},{12,4},... | collective-permute-start | bytes 1572872 | tf_op jit(solution)/shard_map/ppermute | solution.py:710
  108.3 24.8 %collective-permute-start.6 = (bf16[512,512]{1,0:T(8,128)(2,1)S(1)}, bf16[512,512]{1,0:T(8,128)(2,1)}, u32[]{:S(2)}, u32[]{:S(2)}) collective-permute-start(bf16[512,512]{1,0:T(8,128)(2,1)S(1)} %copy-done.22), channel_id=1, source_target_pairs={{0,4},{4,0},{1,5},{5,1},{2,6},{6,2},{3,7},{7,3},{8,12},{12,8},{9,1... | collective-permute-start | bytes 1572872 | tf_op jit(solution)/shard_map/ppermute | solution.py:710
  108.3 24.8 %collective-permute-start.3 = (bf16[512,512]{1,0:T(8,128)(2,1)}, bf16[512,512]{1,0:T(8,128)(2,1)}, u32[]{:S(2)}, u32[]{:S(2)}) collective-permute-start(bf16[512,512]{1,0:T(8,128)(2,1)} %get-tuple-element.381.refs_0_), channel_id=1, source_target_pairs={{0,4},{4,0},{1,5},{5,1},{2,6},{6,2},{3,7},{7,3},{8,12},{12,8},{9,1... | collective-permute-start | bytes 1572872 | tf_op jit(solution)/shard_map/ppermute | solution.py:710
  108.8 24.3 %collective-permute-start.7 = (bf16[512,512]{1,0:T(8,128)(2,1)S(1)}, bf16[512,512]{1,0:T(8,128)(2,1)}, u32[]{:S(2)}, u32[]{:S(2)}) collective-permute-start(bf16[512,512]{1,0:T(8,128)(2,1)S(1)} %collective-permute-done.2.refs_6_), channel_id=1, source_target_pairs={{0,4},{4,0},{1,5},{5,1},{2,6},{6,2},{3,7},{7,3},{8,12},{12,8},{9,1... | collective-permute-start | bytes 1572872 | tf_op jit(solution)/shard_map/ppermute | solution.py:710
  149.3 15.0 %collective-permute-start.9 = (bf16[128,2048]{1,0:T(8,128)(2,1)}, bf16[128,2048]{1,0:T(8,128)(2,1)S(1)}, u32[]{:S(2)}, u32[]{:S(2)}) collective-permute-start(bf16[128,2048]{1,0:T(8,128)(2,1)} %get-tuple-element.279), channel_id=1, source_target_pairs={{0,1},{1,0},{2,3},{3,2},{4,5},{5,4},{6,7},{7,6},{8,9},{9,8},{10,11... | collective-permute-start | bytes 1572872 | tf_op jit(solution)/shard_map/ppermute | solution.py:720
  150.6 32.9 %collective-permute-start.8 = (bf16[128,2048]{1,0:T(8,128)(2,1)}, bf16[128,2048]{1,0:T(8,128)(2,1)S(1)}, u32[]{:S(2)}, u32[]{:S(2)}) collective-permute-start(bf16[128,2048]{1,0:T(8,128)(2,1)} %get-tuple-element.277), channel_id=1, source_target_pairs={{0,1},{1,0},{2,3},{3,2},{4,5},{5,4},{6,7},{7,6},{8,9},{9,8},{10,11... | collective-permute-start | bytes 1572872 | tf_op jit(solution)/shard_map/ppermute | solution.py:720
  165.7 24.7 %collective-permute-start.10 = (bf16[128,2048]{1,0:T(8,128)(2,1)S(1)}, bf16[128,2048]{1,0:T(8,128)(2,1)}, u32[]{:S(2)}, u32[]{:S(2)}) collective-permute-start(bf16[128,2048]{1,0:T(8,128)(2,1)S(1)} %add_convert_fusion.10), channel_id=1, source_target_pairs={{0,2},{1,3},{2,0},{3,1},{4,6},{5,7},{6,4},{7,5},{8,10},{9,11},{10,... | collective-permute-start | bytes 1572872 | tf_op jit(solution)/shard_map/ppermute | solution.py:720
  193.7 22.4 %collective-permute-start.12 = (bf16[128,2176]{1,0:T(8,128)(2,1)}, bf16[128,2176]{1,0:T(8,128)(2,1)S(1)}, u32[]{:S(2)}, u32[]{:S(2)}) collective-permute-start(bf16[128,2176]{1,0:T(8,128)(2,1)} %get-tuple-element.360.ext_ref), channel_id=1, source_target_pairs={{0,2},{1,3},{2,0},{3,1},{4,6},{5,7},{6,4},{7,5},{8,10},{9,11},{10,... | collective-permute-start | bytes 1671176 | tf_op jit(solution)/shard_map/ppermute | solution.py:720
  199.9 328.7 %reduce-scatter.10.cloned.1.call-start = ((), (), s32[]{:S(2)}) async-start(), calls=%async_computation.10 | async-start | bytes 23592960
  200.1 25.6 %collective-permute-start.11 = (bf16[128,2176]{1,0:T(8,128)(2,1)S(1)}, bf16[128,2176]{1,0:T(8,128)(2,1)S(1)}, u32[]{:S(2)}, u32[]{:S(2)}) collective-permute-start(bf16[128,2176]{1,0:T(8,128)(2,1)S(1)} %copy-done.6), channel_id=1, source_target_pairs={{0,1},{1,0},{2,3},{3,2},{4,5},{5,4},{6,7},{7,6},{8,9},{9,8},{10,11... | collective-permute-start | bytes 1671176 | tf_op jit(solution)/shard_map/ppermute | solution.py:720
  216.1 21.1 %collective-permute-start.13 = (bf16[128,2176]{1,0:T(8,128)(2,1)S(1)}, bf16[128,2176]{1,0:T(8,128)(2,1)S(1)}, u32[]{:S(2)}, u32[]{:S(2)}) collective-permute-start(bf16[128,2176]{1,0:T(8,128)(2,1)S(1)} %collective-permute-done.12), channel_id=1, source_target_pairs={{0,1},{1,0},{2,3},{3,2},{4,5},{5,4},{6,7},{7,6},{8,9},{9,8},{10,11... | collective-permute-start | bytes 1671176 | tf_op jit(solution)/shard_map/ppermute | solution.py:720
  240.6 7.7 %collective-permute-start.14 = (bf16[512,2176]{1,0:T(8,128)(2,1)}, bf16[512,2176]{1,0:T(8,128)(2,1)}, u32[]{:S(2)}, u32[]{:S(2)}) collective-permute-start(bf16[512,2176]{1,0:T(8,128)(2,1)} %constant_dynamic-update-slice_fusion.refs_0_), channel_id=1, source_target_pairs={{0,4},{4,0},{1,5},{5,1},{2,6},{6,2},{3,7},{7,3},{8,12},{12,8},{9,1... | collective-permute-start | bytes 6684680 | tf_op jit(solution)/shard_map/ppermute | solution.py:710
  240.6 7.3 %collective-permute-start.15 = (bf16[512,2048]{1,0:T(8,128)(2,1)S(1)}, bf16[512,2048]{1,0:T(8,128)(2,1)}, u32[]{:S(2)}, u32[]{:S(2)}) collective-permute-start(bf16[512,2048]{1,0:T(8,128)(2,1)S(1)} %copy-done.8), channel_id=1, source_target_pairs={{0,4},{4,0},{1,5},{5,1},{2,6},{6,2},{3,7},{7,3},{8,12},{12,8},{9,1... | collective-permute-start | bytes 6291464 | tf_op jit(solution)/shard_map/ppermute | solution.py:710
  338.0 292.5 %reduce-scatter.12.cloned.1.call-start = ((), (), s32[]{:S(2)}) async-start(), calls=%async_computation.11 | async-start | bytes 7864320
  362.0 4.6 collective-permute-start.16
  366.9 14.7 %collective-permute-start.17 = (bf16[128,2176]{1,0:T(8,128)(2,1)S(1)}, bf16[128,2176]{1,0:T(8,128)(2,1)S(1)}, u32[]{:S(2)}, u32[]{:S(2)}) collective-permute-start(bf16[128,2176]{1,0:T(8,128)(2,1)S(1)} %add_convert_fusion.4), channel_id=1, source_target_pairs={{0,1},{1,0},{2,3},{3,2},{4,5},{5,4},{6,7},{7,6},{8,9},{9,8},{10,11... | collective-permute-start | bytes 1671176 | tf_op jit(solution)/shard_map/ppermute | solution.py:720
  381.8 31.9 %collective-permute-start.20 = (bf16[128,2176]{1,0:T(8,128)(2,1)S(1)}, bf16[128,2176]{1,0:T(8,128)(2,1)S(1)}, u32[]{:S(2)}, u32[]{:S(2)}) collective-permute-start(bf16[128,2176]{1,0:T(8,128)(2,1)S(1)} %add_convert_fusion.3), channel_id=1, source_target_pairs={{0,2},{1,3},{2,0},{3,1},{4,6},{5,7},{6,4},{7,5},{8,10},{9,11},{10,... | collective-permute-start | bytes 1671176 | tf_op jit(solution)/shard_map/ppermute | solution.py:720
  384.4 29.3 %collective-permute-start.19 = (bf16[128,2176]{1,0:T(8,128)(2,1)S(1)}, bf16[128,2176]{1,0:T(8,128)(2,1)S(1)}, u32[]{:S(2)}, u32[]{:S(2)}) collective-permute-start(bf16[128,2176]{1,0:T(8,128)(2,1)S(1)} %add_convert_fusion.2), channel_id=1, source_target_pairs={{0,1},{1,0},{2,3},{3,2},{4,5},{5,4},{6,7},{7,6},{8,9},{9,8},{10,11... | collective-permute-start | bytes 1671176 | tf_op jit(solution)/shard_map/ppermute | solution.py:720
  400.7 60.2 %collective-permute-start.18 = (bf16[512,2048]{1,0:T(8,128)(2,1)}, bf16[512,2048]{1,0:T(8,128)(2,1)S(1)}, u32[]{:S(2)}, u32[]{:S(2)}) collective-permute-start(bf16[512,2048]{1,0:T(8,128)(2,1)} %get-tuple-element.349), channel_id=1, source_target_pairs={{0,4},{4,0},{1,5},{5,1},{2,6},{6,2},{3,7},{7,3},{8,12},{12,8},{9,1... | collective-permute-start | bytes 6291464 | tf_op jit(solution)/shard_map/ppermute | solution.py:710
  419.9 26.8 %collective-permute-start.22 = (bf16[128,2048]{1,0:T(8,128)(2,1)}, bf16[128,2048]{1,0:T(8,128)(2,1)S(1)}, u32[]{:S(2)}, u32[]{:S(2)}) collective-permute-start(bf16[128,2048]{1,0:T(8,128)(2,1)} %get-tuple-element.370), channel_id=1, source_target_pairs={{0,2},{1,3},{2,0},{3,1},{4,6},{5,7},{6,4},{7,5},{8,10},{9,11},{10,... | collective-permute-start | bytes 1572872 | tf_op jit(solution)/shard_map/ppermute | solution.py:720
  421.1 25.8 %collective-permute-start.21 = (bf16[128,2048]{1,0:T(8,128)(2,1)}, bf16[128,2048]{1,0:T(8,128)(2,1)S(1)}, u32[]{:S(2)}, u32[]{:S(2)}) collective-permute-start(bf16[128,2048]{1,0:T(8,128)(2,1)} %get-tuple-element.370), channel_id=1, source_target_pairs={{0,1},{1,0},{2,3},{3,2},{4,5},{5,4},{6,7},{7,6},{8,9},{9,8},{10,11... | collective-permute-start | bytes 1572872 | tf_op jit(solution)/shard_map/ppermute | solution.py:720
  446.7 13.9 %collective-permute-start.23 = (bf16[128,2048]{1,0:T(8,128)(2,1)S(1)}, bf16[128,2048]{1,0:T(8,128)(2,1)S(1)}, u32[]{:S(2)}, u32[]{:S(2)}) collective-permute-start(bf16[128,2048]{1,0:T(8,128)(2,1)S(1)} %collective-permute-done.22), channel_id=1, source_target_pairs={{0,1},{1,0},{2,3},{3,2},{4,5},{5,4},{6,7},{7,6},{8,9},{9,8},{10,11... | collective-permute-start | bytes 1572872 | tf_op jit(solution)/shard_map/ppermute | solution.py:720
  468.2 211.5 %reduce-scatter.8.cloned.1.call-start = ((), (), s32[]{:S(2)}) async-start(), calls=%async_computation.6 | async-start | bytes 9437184 | tf_op jit(solution)/shard_map/reduce_scatter | solution.py:954
  468.5 14.1 %collective-permute-start.24 = (bf16[128,2048]{1,0:T(8,128)(2,1)}, bf16[128,2048]{1,0:T(8,128)(2,1)S(1)}, u32[]{:S(2)}, u32[]{:S(2)}) collective-permute-start(bf16[128,2048]{1,0:T(8,128)(2,1)} %add_convert_fusion.9), channel_id=1, source_target_pairs={{0,1},{1,0},{2,3},{3,2},{4,5},{5,4},{6,7},{7,6},{8,9},{9,8},{10,11... | collective-permute-start | bytes 1572872 | tf_op jit(solution)/shard_map/ppermute | solution.py:720
  482.1 51.7 %collective-permute-start.30 = (bf16[2,512,512]{2,1,0:T(8,128)(2,1)}, bf16[2,512,512]{2,1,0:T(8,128)(2,1)}, u32[]{:S(2)}, u32[]{:S(2)}) collective-permute-start(bf16[2,512,512]{2,1,0:T(8,128)(2,1)} %get-tuple-element.392), channel_id=1, source_target_pairs={{0,4},{4,0},{1,5},{5,1},{2,6},{6,2},{3,7},{7,3},{8,12},{12,8},{9,1... | collective-permute-start | bytes 3145736 | tf_op jit(solution)/shard_map/ppermute | solution.py:710
  483.6 26.3 %collective-permute-start.26 = (bf16[128,2048]{1,0:T(8,128)(2,1)}, bf16[128,2048]{1,0:T(8,128)(2,1)S(1)}, u32[]{:S(2)}, u32[]{:S(2)}) collective-permute-start(bf16[128,2048]{1,0:T(8,128)(2,1)} %add_convert_fusion.8), channel_id=1, source_target_pairs={{0,2},{1,3},{2,0},{3,1},{4,6},{5,7},{6,4},{7,5},{8,10},{9,11},{10,... | collective-permute-start | bytes 1572872 | tf_op jit(solution)/shard_map/ppermute | solution.py:720
  486.1 22.1 %collective-permute-start.25 = (bf16[128,2048]{1,0:T(8,128)(2,1)}, bf16[128,2048]{1,0:T(8,128)(2,1)}, u32[]{:S(2)}, u32[]{:S(2)}) collective-permute-start(bf16[128,2048]{1,0:T(8,128)(2,1)} %add_convert_fusion.7), channel_id=1, source_target_pairs={{0,1},{1,0},{2,3},{3,2},{4,5},{5,4},{6,7},{7,6},{8,9},{9,8},{10,11... | collective-permute-start | bytes 1572872 | tf_op jit(solution)/shard_map/ppermute | solution.py:720
  486.7 47.1 %collective-permute-start.31 = (bf16[2,512,512]{2,1,0:T(8,128)(2,1)S(1)}, bf16[2,512,512]{2,1,0:T(8,128)(2,1)}, u32[]{:S(2)}, u32[]{:S(2)}) collective-permute-start(bf16[2,512,512]{2,1,0:T(8,128)(2,1)S(1)} %add_convert_fusion), channel_id=1, source_target_pairs={{0,8},{8,0},{1,9},{9,1},{2,10},{10,2},{3,11},{11,3},{4,12},{12,4},... | collective-permute-start | bytes 3145736 | tf_op jit(solution)/shard_map/ppermute | solution.py:710
  511.3 25.4 %collective-permute-start.29 = (bf16[128,2048]{1,0:T(8,128)(2,1)S(1)}, bf16[128,2048]{1,0:T(8,128)(2,1)S(1)}, u32[]{:S(2)}, u32[]{:S(2)}) collective-permute-start(bf16[128,2048]{1,0:T(8,128)(2,1)S(1)} %add_convert_fusion.6.refs_0_), channel_id=1, source_target_pairs={{0,2},{1,3},{2,0},{3,1},{4,6},{5,7},{6,4},{7,5},{8,10},{9,11},{10,... | collective-permute-start | bytes 1572872 | tf_op jit(solution)/shard_map/ppermute | solution.py:720
  513.3 42.1 %collective-permute-start.28 = (bf16[128,2048]{1,0:T(8,128)(2,1)S(1)}, bf16[128,2048]{1,0:T(8,128)(2,1)}, u32[]{:S(2)}, u32[]{:S(2)}) collective-permute-start(bf16[128,2048]{1,0:T(8,128)(2,1)S(1)} %add_convert_fusion.6.refs_0_), channel_id=1, source_target_pairs={{0,1},{1,0},{2,3},{3,2},{4,5},{5,4},{6,7},{7,6},{8,9},{9,8},{10,11... | collective-permute-start | bytes 1572872 | tf_op jit(solution)/shard_map/ppermute | solution.py:720
  536.7 18.7 %collective-permute-start.32 = (bf16[128,2048]{1,0:T(8,128)(2,1)S(1)}, bf16[128,2048]{1,0:T(8,128)(2,1)}, u32[]{:S(2)}, u32[]{:S(2)}) collective-permute-start(bf16[128,2048]{1,0:T(8,128)(2,1)S(1)} %collective-permute-done.29.refs_2_), channel_id=1, source_target_pairs={{0,1},{1,0},{2,3},{3,2},{4,5},{5,4},{6,7},{7,6},{8,9},{9,8},{10,11... | collective-permute-start | bytes 1572872 | tf_op jit(solution)/shard_map/ppermute | solution.py:720
  550.8 4.5 collective-permute-start.34
  584.3 50.2 %collective-permute-start.41 = (bf16[6,3,256,256]{3,2,1,0:T(8,128)(2,1)S(1)}, bf16[6,3,256,256]{3,2,1,0:T(8,128)(2,1)}, u32[]{:S(2)}, u32[]{:S(2)}) collective-permute-start(bf16[6,3,256,256]{3,2,1,0:T(8,128)(2,1)S(1)} %copy-done.5), channel_id=1, source_target_pairs={{0,4},{4,0},{1,5},{5,1},{2,6},{6,2},{3,7},{7,3},{8,12},{12,8},{9,1... | collective-permute-start | bytes 7077896 | tf_op jit(solution)/shard_map/ppermute | solution.py:710
  584.6 14.7 %collective-permute-start.36 = (bf16[128,2048]{1,0:T(8,128)(2,1)S(1)}, bf16[128,2048]{1,0:T(8,128)(2,1)S(1)}, u32[]{:S(2)}, u32[]{:S(2)}) collective-permute-start(bf16[128,2048]{1,0:T(8,128)(2,1)S(1)} %copy-done.34), channel_id=1, source_target_pairs={{0,1},{1,0},{2,3},{3,2},{4,5},{5,4},{6,7},{7,6},{8,9},{9,8},{10,11... | collective-permute-start | bytes 1572872 | tf_op jit(solution)/shard_map/ppermute | solution.py:720
  586.0 34.1 %collective-permute-start.35 = (bf16[128,2048]{1,0:T(8,128)(2,1)}, bf16[128,2048]{1,0:T(8,128)(2,1)}, u32[]{:S(2)}, u32[]{:S(2)}) collective-permute-start(bf16[128,2048]{1,0:T(8,128)(2,1)} %get-tuple-element.441), channel_id=1, source_target_pairs={{0,1},{1,0},{2,3},{3,2},{4,5},{5,4},{6,7},{7,6},{8,9},{9,8},{10,11... | collective-permute-start | bytes 1572872 | tf_op jit(solution)/shard_map/ppermute | solution.py:720
  599.5 25.1 %collective-permute-start.37 = (bf16[128,2048]{1,0:T(8,128)(2,1)S(1)}, bf16[128,2048]{1,0:T(8,128)(2,1)S(1)}, u32[]{:S(2)}, u32[]{:S(2)}) collective-permute-start(bf16[128,2048]{1,0:T(8,128)(2,1)S(1)} %add_convert_fusion.5), channel_id=1, source_target_pairs={{0,2},{1,3},{2,0},{3,1},{4,6},{5,7},{6,4},{7,5},{8,10},{9,11},{10,... | collective-permute-start | bytes 1572872 | tf_op jit(solution)/shard_map/ppermute | solution.py:720
  629.0 20.6 %collective-permute-start.40 = (bf16[128,2048]{1,0:T(8,128)(2,1)}, bf16[128,2048]{1,0:T(8,128)(2,1)S(1)}, u32[]{:S(2)}, u32[]{:S(2)}) collective-permute-start(bf16[128,2048]{1,0:T(8,128)(2,1)} %get-tuple-element.467.refs_0_), channel_id=1, source_target_pairs={{0,1},{1,0},{2,3},{3,2},{4,5},{5,4},{6,7},{7,6},{8,9},{9,8},{10,11... | collective-permute-start | bytes 1572872 | tf_op jit(solution)/shard_map/ppermute | solution.py:720
  630.6 25.4 %collective-permute-start.38 = (bf16[128,2048]{1,0:T(8,128)(2,1)}, bf16[128,2048]{1,0:T(8,128)(2,1)S(1)}, u32[]{:S(2)}, u32[]{:S(2)}) collective-permute-start(bf16[128,2048]{1,0:T(8,128)(2,1)} %get-tuple-element.467.refs_0_), channel_id=1, source_target_pairs={{0,2},{1,3},{2,0},{3,1},{4,6},{5,7},{6,4},{7,5},{8,10},{9,11},{10,... | collective-permute-start | bytes 1572872 | tf_op jit(solution)/shard_map/ppermute | solution.py:720
  654.3 14.6 %collective-permute-start.43 = (bf16[2,3,256,256]{3,2,1,0:T(8,128)(2,1)S(1)}, bf16[2,3,256,256]{3,2,1,0:T(8,128)(2,1)S(1)}, u32[]{:S(2)}, u32[]{:S(2)}) collective-permute-start(bf16[2,3,256,256]{3,2,1,0:T(8,128)(2,1)S(1)} %get-tuple-element.510), channel_id=1, source_target_pairs={{0,4},{4,0},{1,5},{5,1},{2,6},{6,2},{3,7},{7,3},{8,12},{12,8},{9,1... | collective-permute-start | bytes 2359304 | tf_op jit(solution)/shard_map/ppermute | solution.py:710
  656.0 18.6 %collective-permute-start.39 = (bf16[128,2048]{1,0:T(8,128)(2,1)S(1)}, bf16[128,2048]{1,0:T(8,128)(2,1)S(1)}, u32[]{:S(2)}, u32[]{:S(2)}) collective-permute-start(bf16[128,2048]{1,0:T(8,128)(2,1)S(1)} %collective-permute-done.38.refs_0_), channel_id=1, source_target_pairs={{0,1},{1,0},{2,3},{3,2},{4,5},{5,4},{6,7},{7,6},{8,9},{9,8},{10,11... | collective-permute-start | bytes 1572872 | tf_op jit(solution)/shard_map/ppermute | solution.py:720
  656.8 9.0 %all-to-all-start.2 = ((f32[8,20,256]{2,1,0:T(8,128)}), f32[8,20,256]{2,1,0:T(8,128)S(1)}, u32[]{:S(2)}, u32[]{:S(2)}) async-start(f32[8,20,256]{2,1,0:T(8,128)} %bitcast.60), calls=%async_computation.3 | async-start | bytes 393216 | tf_op jit(solution)/shard_map/all_to_all | solution.py:967
  665.8 7.8 %collective-permute-start.42 = (f32[20,256]{1,0:T(8,128)S(1)}, f32[20,256]{1,0:T(8,128)S(1)}, u32[]{:S(2)}, u32[]{:S(2)}) collective-permute-start(f32[20,256]{1,0:T(8,128)S(1)} %reduce_sum.9), channel_id=1, source_target_pairs={{0,1},{1,0},{2,3},{3,2},{4,5},{5,4},{6,7},{7,6},{8,9},{9,8},{10,11... | collective-permute-start | bytes 61448 | tf_op jit(solution)/shard_map/ppermute | solution.py:720
  673.7 4.8 collective-permute-start.44
  (39 other events, 473.4 us)
Sparse Core Ops, SparseCore 0:
  10.5 57.2 all-gather.6
  69.6 194.2 all-gather.8
  265.8 70.1 all-gather.10
  338.9 189.5 reduce-scatter.9
  532.3 71.0 reduce-scatter.11
  607.1 71.2 reduce-scatter.7

commit v7 on v6

--- a/solution.py
+++ b/solution.py
@@ -903,13 +903,13 @@
             grads.append(to_owners(made, k, ()))
     d_normed = line.sums(*dx, tp)
     moe = line(expert_down, hid, ws, 2, 1, [], [], 2, "expert_out")
-    late = weight_grad(len(chunks) - 1)
 
     d_mid, d_mid_low, gain_two, grad_router = line(
         norm_two_back, d_normed, mid, ext, probs, chosen, cots[0], gains[1:2], router_rows
     )
     far = across(d_mid_low, 2)
     near = across(d_mid_low, 1)
+    late = weight_grad(len(chunks) - 1)
     d_mid_low = line(join, d_mid_low, near, far, across(far, 1))
     own, beside = cut(moe[0], tp), cut(swap(moe[1], "core"), tp)
     last = across(line(add, own[3], beside[3]), 1)

time: 701 us -> 703 us (level)
    unnamed x8, waiting for transfers between devices: 13.8 us -> 24.1 us
    ppermute x30, waiting for transfers between devices: 181 us -> 171 us  [across(): return lax.ppermute(value, 'tp', [(i, i ^ k) for i in range(size)])]
  transfers between devices with their start and end apart: 52 -> 52, of which waited for: 32 -> 30; matrix products, arithmetic and copies ran while one was open for 7% -> 7% of each run, Pallas kernels for 35% -> 35%
where the time goes in v7:
time: 703 us; the launch traced here: 693 us
  waiting for transfers between devices  273 us (39%)
  Pallas kernels  241 us (34%)
  starting transfers between devices  55.7 us (8%)
  local copies, waits for them, and re-layouts  40.9 us (6%)
  blocking collectives  35.3 us (5%)
  other arithmetic  25.4 us (4%)
  between operations  22.9 us (3%)
    ppermute x30, waiting for transfers between devices, across(): return lax.ppermute(value, 'tp', [(i, i ^ k) for i in range(size)])  171 us
    ppermute x30, starting transfers between devices, across(): return lax.ppermute(value, 'tp', [(i, i ^ k) for i in range(size)])  45 us
    ppermute x15, waiting for transfers between devices, swap(): return lax.ppermute(value, axis, [(0, 1), (1, 0)])  43.5 us
    pallas_call x3, Pallas kernels, expert_down(): call(functools.partial(down_kernel, planes=planes, chunks=chunks, sides=l...  43.2 us
    pallas_call x2, Pallas kernels, expert_up(): call(functools.partial(expert_kernel, parts=parts), 'expert_up', (e,), [f...  41.3 us
    pallas_call x2, Pallas kernels, expert_grads(): call(functools.partial(expert_grad_kernel, parts=parts), 'expert_grad', (...  40.1 us
    unnamed x8, waiting for transfers between devices  24.1 us
    all_gather x2, waiting for transfers between devices, body(): lax.all_gather(mine, FR, axis=0, tiled=False).reshape(-1, e, 3, ds, f)  15.7 us
  transfers between devices with their start and end apart: 52, of which 30 were waited for; matrix products, arithmetic and copies ran while one was open for 7% of the time, Pallas kernels for 35%

profile of v7, /device:TPU:0, one launch (start us, length us, event | category | flops | bytes accessed | tf_op | source)
XLA Modules:
  0.0 693.4 jit_solution(7193650349399598956)
XLA Ops:
  11.9 8.6 %all_to_all.15 = bf16[2,6,3,256,256]{4,3,2,1,0:T(8,128)(2,1)} all-to-all(bf16[2,6,3,256,256]{4,3,2,1,0:T(8,128)(2,1)S(1)} %fusion), channel_id=1, replica_groups=mesh['fsdp'=2,'row'=2,'core'=2,'tp'=4] {'core'}, dimensions={0} | all-to-all | bytes 9437184 | tf_op jit(solution)/shard_map/all_to_all | solution.py:834
  29.6 10.3 %all_gather.26 = bf16[4,2048]{1,0:T(4,128)(2,1)S(1)} all-gather(bf16[4,256]{1,0:T(4,128)(2,1)S(1)} %copy-done.33), channel_id=1, replica_groups=mesh['fsdp'=2,'row'=2,'core'=2,'tp'=4] {'fsdp','row','core'}, dimensions={1}, use_global_device_ids=true | all-gather | bytes 18432 | tf_op jit(solution)/shard_map/all_gather | solution.py:836
  39.9 10.4 %all_gather.27 = bf16[2048,16]{0,1:T(8,128)(2,1)} all-gather(bf16[256,16]{0,1:T(8,128)(2,1)S(1)} %copy-done.30), channel_id=1, replica_groups=mesh['fsdp'=2,'row'=2,'core'=2,'tp'=4] {'fsdp','row','core'}, dimensions={0}, use_global_device_ids=true | all-gather | bytes 73728 | tf_op jit(solution)/shard_map/all_gather | solution.py:837
  54.6 13.2 %all-gather.7.cloned.1.call-done = bf16[32,256,512]{2,1,0:T(8,128)(2,1)} async-done(((bf16[4,256,512]{2,1,0:T(8,128)(2,1)}), bf16[32,256,512]{2,1,0:T(8,128)(2,1)}) %all-gather.7.cloned.1.call-update) | async-done | bytes 8388624 | tf_op jit(solution)/shard_map/all_gather | solution.py:828
  68.4 10.4 %qkv.1 = (bf16[512,2048]{1,0:T(8,128)(2,1)}, f32[2,512,512]{2,1,0:T(8,128)}, bf16[512,512]{1,0:T(8,128)(2,1)}, f32[2,512,128]{2,1,0:T(8,128)}) custom-call(bf16[512,2048]{1,0:T(8,128)(2,1)} %bitcast.83, f32[1,2048]{1,0:T(1,128)} %get-tuple-element.454.g_ref, bf16[8,4,256,512]{3,2,1,0:T(8,128)(2,1)} %bitcast.61), custom_call_target="tpu_custom_call" | custom-call | flops 3221225472 | bytes 13107200 | tf_op jit(solution)/shard_map/qkv/pallas_call | solution.py:87
  91.1 9.7 %collective-permute-done.2.refs_6_ = bf16[512,512]{1,0:T(8,128)(2,1)S(1)} collective-permute-done((bf16[512,512]{1,0:T(8,128)(2,1)}, bf16[512,512]{1,0:T(8,128)(2,1)S(1)}, u32[]{:S(2)}, u32[]{:S(2)}) %collective-permute-start.2) | collective-permute-done | bytes 524320 | tf_op jit(solution)/shard_map/ppermute | solution.py:710
  101.8 4.4 prep.1
  108.8 22.9 %collective-permute-done.4.refs_2_ = bf16[512,512]{1,0:T(8,128)(2,1)} collective-permute-done((bf16[512,512]{1,0:T(8,128)(2,1)}, bf16[512,512]{1,0:T(8,128)(2,1)}, u32[]{:S(2)}, u32[]{:S(2)}) %collective-permute-start.4) | collective-permute-done | bytes 524320 | tf_op jit(solution)/shard_map/ppermute | solution.py:710
  134.0 9.9 %attend.1.h_ref = bf16[512,512]{1,0:T(8,128)(2,1)} custom-call(s32[7]{0:T(128)} %pad_add_fusion.scal_ref, bf16[512,512]{1,0:T(8,128)(2,1)} %get-tuple-element.380.q_ref, bf16[512,512]{1,0:T(8,128)(2,1)} %get-tuple-element.381.refs_0_, bf16[512,512]{1,0:T(8,128)(2,1)} %collective-permute-done.3.refs_1_, bf16[512,512]{1,0:T(8,128)(2,1)} %collective-permute-done.4.refs_2_, ...), custom_call_target="tpu_custom_call" | custom-call | flops 1073741824 | bytes 6291456 | tf_op jit(solution)/shard_map/attend/pallas_call | solution.py:171
  143.9 5.4 outproj.1
  151.4 12.9 %collective-permute-done.9 = bf16[128,2048]{1,0:T(8,128)(2,1)S(1)} collective-permute-done((bf16[128,2048]{1,0:T(8,128)(2,1)}, bf16[128,2048]{1,0:T(8,128)(2,1)S(1)}, u32[]{:S(2)}, u32[]{:S(2)}) %collective-permute-start.9) | collective-permute-done | bytes 524320 | tf_op jit(solution)/shard_map/ppermute | solution.py:720
  171.6 11.9 %collective-permute-done.8.b_ref = bf16[128,2048]{1,0:T(8,128)(2,1)S(1)} collective-permute-done((bf16[128,2048]{1,0:T(8,128)(2,1)}, bf16[128,2048]{1,0:T(8,128)(2,1)S(1)}, u32[]{:S(2)}, u32[]{:S(2)}) %collective-permute-start.8) | collective-permute-done | bytes 524320 | tf_op jit(solution)/shard_map/ppermute | solution.py:720
  183.5 6.8 collective-permute-done.10.c_ref
  193.9 6.0 all_to_all.16
  200.1 3.7 collective-permute-start.11
  203.8 12.2 %collective-permute-done.12 = bf16[128,2176]{1,0:T(8,128)(2,1)S(1)} collective-permute-done((bf16[128,2176]{1,0:T(8,128)(2,1)}, bf16[128,2176]{1,0:T(8,128)(2,1)S(1)}, u32[]{:S(2)}, u32[]{:S(2)}) %collective-permute-start.12) | collective-permute-done | bytes 557088 | tf_op jit(solution)/shard_map/ppermute | solution.py:720
  216.9 8.9 %collective-permute-done.11 = bf16[128,2176]{1,0:T(8,128)(2,1)S(1)} collective-permute-done((bf16[128,2176]{1,0:T(8,128)(2,1)S(1)}, bf16[128,2176]{1,0:T(8,128)(2,1)S(1)}, u32[]{:S(2)}, u32[]{:S(2)}) %collective-permute-start.11) | collective-permute-done | bytes 557088 | tf_op jit(solution)/shard_map/ppermute | solution.py:720
  225.7 11.5 %collective-permute-done.13 = bf16[128,2176]{1,0:T(8,128)(2,1)S(1)} collective-permute-done((bf16[128,2176]{1,0:T(8,128)(2,1)S(1)}, bf16[128,2176]{1,0:T(8,128)(2,1)S(1)}, u32[]{:S(2)}, u32[]{:S(2)}) %collective-permute-start.13) | collective-permute-done | bytes 557088 | tf_op jit(solution)/shard_map/ppermute | solution.py:720
  241.1 6.8 collective-permute-done.15.refs_3_
  248.3 15.6 %all-gather.9.cloned.1.call-done.refs_4_.refs_1_.refs_2_ = bf16[8,6,3,256,256]{4,3,2,1,0:T(8,128)(2,1)} async-done(((bf16[2,6,3,256,256]{4,3,2,1,0:T(8,128)(2,1)}), bf16[8,6,3,256,256]{4,3,2,1,0:T(8,128)(2,1)}) %all-gather.9.cloned.1.call-update) | async-done | bytes 18874384 | tf_op jit(solution)/shard_map/all_gather | solution.py:835
  263.9 28.1 %expert_up.2 = (bf16[1024,1536]{1,0:T(8,128)(2,1)}, bf16[1024,3072]{1,0:T(8,128)(2,1)}, f32[1024,128]{1,0:T(8,128)}) custom-call(s32[1]{0:T(128)} %bitcast.19.first_ref, bf16[512,2176]{1,0:T(8,128)(2,1)} %constant_dynamic-update-slice_fusion.refs_0_, bf16[512,2176]{1,0:T(8,128)(2,1)} %collective-permute-done.14.refs_1_, ...), custom_call_target="tpu_custom_call" | custom-call | flops 19327352832 | bytes 36700160 | tf_op jit(solution)/shard_map/expert_up/pallas_call | solution.py:438
  292.0 18.9 %expert_dx.2 = (bf16[512,2048]{1,0:T(8,128)(2,1)}, bf16[512,2048]{1,0:T(8,128)(2,1)}) custom-call(bf16[1024,3072]{1,0:T(8,128)(2,1)} %get-tuple-element.317.refs_0_.refs_5_, bf16[8,6,3,256,256]{4,3,2,1,0:T(8,128)(2,1)} %all-gather.9.cloned.1.call-done.refs_4_.refs_1_.refs_2_), custom_call_target="tpu_custom_call" | custom-call | flops 12884901888 | bytes 23068672 | tf_op jit(solution)/shard_map/expert_dx/pallas_call | solution.py:562
  311.0 27.0 %expert_grad.2 = bf16[8,6,3,256,256]{4,3,2,1,0:T(8,128)(2,1)} custom-call(bf16[512,2176]{1,0:T(8,128)(2,1)} %constant_dynamic-update-slice_fusion.refs_0_, bf16[512,2176]{1,0:T(8,128)(2,1)} %collective-permute-done.14.refs_1_, bf16[512,2048]{1,0:T(8,128)(2,1)} %pad_maximum_fusion.refs_2_, bf16[512,2048]{1,0:T(8,128)(2,1)} %collective-permute-done.15.refs_3_, ...), custom_call_target="tpu_custom_call" | custom-call | flops 19327352832 | bytes 36700160 | tf_op jit(solution)/shard_map/expert_grad/pallas_call | solution.py:477
  338.3 13.2 %expert_up.3 = (bf16[1024,512]{1,0:T(8,128)(2,1)}, bf16[1024,1024]{1,0:T(8,128)(2,1)}, f32[1024,128]{1,0:T(8,128)}) custom-call(s32[1]{0:T(128)} %bitcast.22.first_ref, bf16[512,2176]{1,0:T(8,128)(2,1)} %constant_dynamic-update-slice_fusion.refs_0_, bf16[512,2176]{1,0:T(8,128)(2,1)} %collective-permute-done.14.refs_1_, ...), custom_call_target="tpu_custom_call" | custom-call | flops 6442450944 | bytes 17825792 | tf_op jit(solution)/shard_map/expert_up/pallas_call | solution.py:438
  351.5 10.5 %expert_dx.3 = (bf16[512,2176]{1,0:T(8,128)(2,1)}, bf16[512,2176]{1,0:T(8,128)(2,1)}) custom-call(bf16[1024,1024]{1,0:T(8,128)(2,1)} %get-tuple-element.369.refs_0_.refs_5_, bf16[8,2,3,256,256]{4,3,2,1,0:T(8,128)(2,1)} %all-gather.11.cloned.1.call-done.refs_4_.refs_1_.refs_3_, f32[1024,128]{1,0:T(8,128)} %get-tuple-element.329.refs_2_, ...), custom_call_target="tpu_custom_call" | custom-call | flops 4294967296 | bytes 10747904 | tf_op jit(solution)/shard_map/expert_dx/pallas_call | solution.py:562
  368.4 13.2 %collective-permute-done.17 = bf16[128,2176]{1,0:T(8,128)(2,1)S(1)} collective-permute-done((bf16[128,2176]{1,0:T(8,128)(2,1)S(1)}, bf16[128,2176]{1,0:T(8,128)(2,1)S(1)}, u32[]{:S(2)}, u32[]{:S(2)}) %collective-permute-start.17) | collective-permute-done | bytes 557088 | tf_op jit(solution)/shard_map/ppermute | solution.py:720
  386.9 13.8 %expert_out.1 = (bf16[512,2048]{1,0:T(8,128)(2,1)}, bf16[512,2048]{1,0:T(8,128)(2,1)}) custom-call(bf16[1024,1536]{1,0:T(8,128)(2,1)} %get-tuple-element.344.refs_4_.refs_0_, bf16[1024,512]{1,0:T(8,128)(2,1)} %get-tuple-element.368.refs_1_.refs_4_, bf16[8,6,3,256,256]{4,3,2,1,0:T(8,128)(2,1)} %all-gather.9.cloned.1.call-done.refs_4_.refs_1_.refs_2_, ...), custom_call_target="tpu_custom_call" | custom-call | flops 8589934592 | bytes 16777216 | tf_op jit(solution)/shard_map/expert_out/pallas_call | solution.py:562
  400.6 8.4 %collective-permute-done.19.b_ref = bf16[128,2176]{1,0:T(8,128)(2,1)S(1)} collective-permute-done((bf16[128,2176]{1,0:T(8,128)(2,1)S(1)}, bf16[128,2176]{1,0:T(8,128)(2,1)S(1)}, u32[]{:S(2)}, u32[]{:S(2)}) %collective-permute-start.19) | collective-permute-done | bytes 557088 | tf_op jit(solution)/shard_map/ppermute | solution.py:720
  410.1 4.5 norm_two_back.1
  418.2 21.3 %collective-permute-done.22 = bf16[128,2048]{1,0:T(8,128)(2,1)S(1)} collective-permute-done((bf16[128,2048]{1,0:T(8,128)(2,1)}, bf16[128,2048]{1,0:T(8,128)(2,1)S(1)}, u32[]{:S(2)}, u32[]{:S(2)}) %collective-permute-start.22) | collective-permute-done | bytes 524320 | tf_op jit(solution)/shard_map/ppermute | solution.py:720
  439.5 13.1 %expert_grad.3 = bf16[8,2,3,256,256]{4,3,2,1,0:T(8,128)(2,1)} custom-call(bf16[512,2176]{1,0:T(8,128)(2,1)} %constant_dynamic-update-slice_fusion.refs_0_, bf16[512,2176]{1,0:T(8,128)(2,1)} %collective-permute-done.14.refs_1_, bf16[512,2048]{1,0:T(8,128)(2,1)} %pad_maximum_fusion.refs_2_, bf16[512,2048]{1,0:T(8,128)(2,1)} %collective-permute-done.15.refs_3_, ...), custom_call_target="tpu_custom_call" | custom-call | flops 6442450944 | bytes 17825792 | tf_op jit(solution)/shard_map/expert_grad/pallas_call | solution.py:477
  455.1 5.0 dheads.1.refs_8_
  462.4 13.2 %attend_back.1 = (f32[512,512]{1,0:T(8,128)}, bf16[2,512,512]{2,1,0:T(8,128)(2,1)}, bf16[2,512,512]{2,1,0:T(8,128)(2,1)}, bf16[2,512,512]{2,1,0:T(8,128)(2,1)}, bf16[2,512,512]{2,1,0:T(8,128)(2,1)}) custom-call(s32[7]{0:T(128)} %pad_add_fusion.scal_ref, bf16[512,512]{1,0:T(8,128)(2,1)} %get-tuple-element.380.q_ref, ...), custom_call_target="tpu_custom_call" | custom-call | flops 2684354560 | bytes 12582912 | tf_op jit(solution)/shard_map/attend_back/pallas_call | solution.py:209
  483.1 7.9 %gradout.1.kept_ref = bf16[8,4,256,512]{3,2,1,0:T(8,128)(2,1)} custom-call(s32[4]{0:T(128)} %copy-done.27, bf16[512,2048]{1,0:T(8,128)(2,1)} %copy-done.1, bf16[512,512]{1,0:T(8,128)(2,1)} %attend.1.h_ref), custom_call_target="tpu_custom_call" | custom-call | flops 1073741824 | bytes 4718592 | tf_op jit(solution)/shard_map/gradout/pallas_call | solution.py:288
  491.1 14.4 %collective-permute-done.25 = bf16[128,2048]{1,0:T(8,128)(2,1)} collective-permute-done((bf16[128,2048]{1,0:T(8,128)(2,1)}, bf16[128,2048]{1,0:T(8,128)(2,1)}, u32[]{:S(2)}, u32[]{:S(2)}) %collective-permute-start.25) | collective-permute-done | bytes 524320 | tf_op jit(solution)/shard_map/ppermute | solution.py:720
  508.2 24.0 %reduce-scatter.10.cloned.1.call-done = bf16[1,2,6,3,256,256]{5,4,3,2,1,0:T(8,128)(2,1)} async-done(((bf16[4,2,6,3,256,256]{5,4,3,2,1,0:T(8,128)(2,1)}), bf16[1,2,6,3,256,256]{5,4,3,2,1,0:T(8,128)(2,1)}) %reduce-scatter.10.cloned.1.call-update) | async-done | bytes 4718608
  532.2 5.1 dynamic-slice_bitcast_fusion
  542.9 6.1 unturn.1
  558.5 4.1 inplace.3
  564.7 11.0 %raw_back.1 = (bf16[512,1536]{1,0:T(8,128)(2,1)}, bf16[128,2048]{1,0:T(8,128)(2,1)}, bf16[128,2048]{1,0:T(8,128)(2,1)}, bf16[128,2048]{1,0:T(8,128)(2,1)}, bf16[128,2048]{1,0:T(8,128)(2,1)}) custom-call(s32[4]{0:T(128)} %copy-done.27, f32[2,512,512]{2,1,0:T(8,128)} %get-tuple-element.432.u_ref, f32[2,512,512]{2,1,0:T(8,128)} %get-tuple-element.433.raw_ref, ...), custom_call_target="tpu_custom_call" | custom-call | flops 3221225472 | bytes 13631488 | tf_op jit(solution)/shard_map/raw_back/pallas_call | solution.py:658
  575.7 9.2 %qkv_grad.1 = bf16[8,4,256,512]{3,2,1,0:T(8,128)(2,1)} custom-call(bf16[512,2048]{1,0:T(8,128)(2,1)} %get-tuple-element.444.n_ref, bf16[512,1536]{1,0:T(8,128)(2,1)} %get-tuple-element.445.d_ref, bf16[8,4,256,512]{3,2,1,0:T(8,128)(2,1)} %gradout.1.kept_ref), custom_call_target="tpu_custom_call", output_to_operand_aliasing={{}: (2, {})} | custom-call | flops 3221225472 | bytes 9961472 | tf_op jit(solution)/shard_map/qkv_grad/pallas_call | solution.py:692
  589.3 12.7 %collective-permute-done.36 = bf16[128,2048]{1,0:T(8,128)(2,1)S(1)} collective-permute-done((bf16[128,2048]{1,0:T(8,128)(2,1)S(1)}, bf16[128,2048]{1,0:T(8,128)(2,1)S(1)}, u32[]{:S(2)}, u32[]{:S(2)}) %collective-permute-start.36) | collective-permute-done | bytes 524320 | tf_op jit(solution)/shard_map/ppermute | solution.py:720
  605.6 17.1 %collective-permute-done.35.b_ref = bf16[128,2048]{1,0:T(8,128)(2,1)} collective-permute-done((bf16[128,2048]{1,0:T(8,128)(2,1)}, bf16[128,2048]{1,0:T(8,128)(2,1)}, u32[]{:S(2)}, u32[]{:S(2)}) %collective-permute-start.35) | collective-permute-done | bytes 524320 | tf_op jit(solution)/shard_map/ppermute | solution.py:720
  622.7 4.8 collective-permute-done.37.c_ref
  637.8 7.9 %settle.2 = (f32[16,2,256,256]{3,2,1,0:T(8,128)}, f32[16,256,256]{2,1,0:T(8,128)}) custom-call(s32[6]{0:T(128)} %pad_add_fusion.1.spot_ref, bf16[6,3,256,256]{3,2,1,0:T(8,128)(2,1)} %get-tuple-element.462.refs_0_, bf16[6,3,256,256]{3,2,1,0:T(8,128)(2,1)} %collective-permute-done.41.refs_1_), custom_call_target="tpu_custom_call" | custom-call | bytes 14155776 | tf_op jit(solution)/shard_map/settle/pallas_call | solution.py:508
  645.7 6.6 collective-permute-done.40.refs_1_
  662.8 5.6 all-to-all-done.2
  672.0 3.8 settle.3
  (239 shorter events, 138.3 us)
Async XLA Ops:
  7.2 60.6 %all-gather.7.cloned.1.call-start = ((), (), s32[]{:S(2)}) async-start(), calls=%async_computation.7 | async-start | bytes 9437184 | tf_op jit(solution)/shard_map/all_gather | solution.py:828
  9.7 254.3 %all-gather.9.cloned.1.call-start = ((), (), s32[]{:S(2)}) async-start(), calls=%async_computation.8 | async-start | bytes 23592960 | tf_op jit(solution)/shard_map/all_gather | solution.py:835
  20.5 317.8 %all-gather.11.cloned.1.call-start = ((), (), s32[]{:S(2)}) async-start(), calls=%async_computation.9 | async-start | bytes 7864320 | tf_op jit(solution)/shard_map/all_gather | solution.py:835
  78.8 22.0 %collective-permute-start.2 = (bf16[512,512]{1,0:T(8,128)(2,1)}, bf16[512,512]{1,0:T(8,128)(2,1)S(1)}, u32[]{:S(2)}, u32[]{:S(2)}) collective-permute-start(bf16[512,512]{1,0:T(8,128)(2,1)} %get-tuple-element.385.refs_4_), channel_id=1, source_target_pairs={{0,8},{8,0},{1,9},{9,1},{2,10},{10,2},{3,11},{11,3},{4,12},{12,4},... | collective-permute-start | bytes 1572872 | tf_op jit(solution)/shard_map/ppermute | solution.py:710
  86.6 4.5 collective-permute-start.1
  106.2 25.5 %collective-permute-start.4 = (bf16[512,512]{1,0:T(8,128)(2,1)}, bf16[512,512]{1,0:T(8,128)(2,1)}, u32[]{:S(2)}, u32[]{:S(2)}) collective-permute-start(bf16[512,512]{1,0:T(8,128)(2,1)} %get-tuple-element.381.refs_0_), channel_id=1, source_target_pairs={{0,8},{8,0},{1,9},{9,1},{2,10},{10,2},{3,11},{11,3},{4,12},{12,4},... | collective-permute-start | bytes 1572872 | tf_op jit(solution)/shard_map/ppermute | solution.py:710
  108.3 24.8 %collective-permute-start.6 = (bf16[512,512]{1,0:T(8,128)(2,1)S(1)}, bf16[512,512]{1,0:T(8,128)(2,1)}, u32[]{:S(2)}, u32[]{:S(2)}) collective-permute-start(bf16[512,512]{1,0:T(8,128)(2,1)S(1)} %copy-done.22), channel_id=1, source_target_pairs={{0,4},{4,0},{1,5},{5,1},{2,6},{6,2},{3,7},{7,3},{8,12},{12,8},{9,1... | collective-permute-start | bytes 1572872 | tf_op jit(solution)/shard_map/ppermute | solution.py:710
  108.3 24.8 %collective-permute-start.3 = (bf16[512,512]{1,0:T(8,128)(2,1)}, bf16[512,512]{1,0:T(8,128)(2,1)}, u32[]{:S(2)}, u32[]{:S(2)}) collective-permute-start(bf16[512,512]{1,0:T(8,128)(2,1)} %get-tuple-element.381.refs_0_), channel_id=1, source_target_pairs={{0,4},{4,0},{1,5},{5,1},{2,6},{6,2},{3,7},{7,3},{8,12},{12,8},{9,1... | collective-permute-start | bytes 1572872 | tf_op jit(solution)/shard_map/ppermute | solution.py:710
  108.8 24.3 %collective-permute-start.7 = (bf16[512,512]{1,0:T(8,128)(2,1)S(1)}, bf16[512,512]{1,0:T(8,128)(2,1)}, u32[]{:S(2)}, u32[]{:S(2)}) collective-permute-start(bf16[512,512]{1,0:T(8,128)(2,1)S(1)} %collective-permute-done.2.refs_6_), channel_id=1, source_target_pairs={{0,4},{4,0},{1,5},{5,1},{2,6},{6,2},{3,7},{7,3},{8,12},{12,8},{9,1... | collective-permute-start | bytes 1572872 | tf_op jit(solution)/shard_map/ppermute | solution.py:710
  149.3 15.0 %collective-permute-start.9 = (bf16[128,2048]{1,0:T(8,128)(2,1)}, bf16[128,2048]{1,0:T(8,128)(2,1)S(1)}, u32[]{:S(2)}, u32[]{:S(2)}) collective-permute-start(bf16[128,2048]{1,0:T(8,128)(2,1)} %get-tuple-element.279), channel_id=1, source_target_pairs={{0,1},{1,0},{2,3},{3,2},{4,5},{5,4},{6,7},{7,6},{8,9},{9,8},{10,11... | collective-permute-start | bytes 1572872 | tf_op jit(solution)/shard_map/ppermute | solution.py:720
  150.6 32.9 %collective-permute-start.8 = (bf16[128,2048]{1,0:T(8,128)(2,1)}, bf16[128,2048]{1,0:T(8,128)(2,1)S(1)}, u32[]{:S(2)}, u32[]{:S(2)}) collective-permute-start(bf16[128,2048]{1,0:T(8,128)(2,1)} %get-tuple-element.277), channel_id=1, source_target_pairs={{0,1},{1,0},{2,3},{3,2},{4,5},{5,4},{6,7},{7,6},{8,9},{9,8},{10,11... | collective-permute-start | bytes 1572872 | tf_op jit(solution)/shard_map/ppermute | solution.py:720
  165.7 24.7 %collective-permute-start.10 = (bf16[128,2048]{1,0:T(8,128)(2,1)S(1)}, bf16[128,2048]{1,0:T(8,128)(2,1)}, u32[]{:S(2)}, u32[]{:S(2)}) collective-permute-start(bf16[128,2048]{1,0:T(8,128)(2,1)S(1)} %add_convert_fusion.10), channel_id=1, source_target_pairs={{0,2},{1,3},{2,0},{3,1},{4,6},{5,7},{6,4},{7,5},{8,10},{9,11},{10,... | collective-permute-start | bytes 1572872 | tf_op jit(solution)/shard_map/ppermute | solution.py:720
  193.7 22.4 %collective-permute-start.12 = (bf16[128,2176]{1,0:T(8,128)(2,1)}, bf16[128,2176]{1,0:T(8,128)(2,1)S(1)}, u32[]{:S(2)}, u32[]{:S(2)}) collective-permute-start(bf16[128,2176]{1,0:T(8,128)(2,1)} %get-tuple-element.354.ext_ref), channel_id=1, source_target_pairs={{0,2},{1,3},{2,0},{3,1},{4,6},{5,7},{6,4},{7,5},{8,10},{9,11},{10,... | collective-permute-start | bytes 1671176 | tf_op jit(solution)/shard_map/ppermute | solution.py:720
  199.9 332.3 %reduce-scatter.10.cloned.1.call-start = ((), (), s32[]{:S(2)}) async-start(), calls=%async_computation.10 | async-start | bytes 23592960
  200.1 25.6 %collective-permute-start.11 = (bf16[128,2176]{1,0:T(8,128)(2,1)S(1)}, bf16[128,2176]{1,0:T(8,128)(2,1)S(1)}, u32[]{:S(2)}, u32[]{:S(2)}) collective-permute-start(bf16[128,2176]{1,0:T(8,128)(2,1)S(1)} %copy-done.6), channel_id=1, source_target_pairs={{0,1},{1,0},{2,3},{3,2},{4,5},{5,4},{6,7},{7,6},{8,9},{9,8},{10,11... | collective-permute-start | bytes 1671176 | tf_op jit(solution)/shard_map/ppermute | solution.py:720
  216.1 21.1 %collective-permute-start.13 = (bf16[128,2176]{1,0:T(8,128)(2,1)S(1)}, bf16[128,2176]{1,0:T(8,128)(2,1)S(1)}, u32[]{:S(2)}, u32[]{:S(2)}) collective-permute-start(bf16[128,2176]{1,0:T(8,128)(2,1)S(1)} %collective-permute-done.12), channel_id=1, source_target_pairs={{0,1},{1,0},{2,3},{3,2},{4,5},{5,4},{6,7},{7,6},{8,9},{9,8},{10,11... | collective-permute-start | bytes 1671176 | tf_op jit(solution)/shard_map/ppermute | solution.py:720
  240.6 7.7 %collective-permute-start.14 = (bf16[512,2176]{1,0:T(8,128)(2,1)}, bf16[512,2176]{1,0:T(8,128)(2,1)}, u32[]{:S(2)}, u32[]{:S(2)}) collective-permute-start(bf16[512,2176]{1,0:T(8,128)(2,1)} %constant_dynamic-update-slice_fusion.refs_0_), channel_id=1, source_target_pairs={{0,4},{4,0},{1,5},{5,1},{2,6},{6,2},{3,7},{7,3},{8,12},{12,8},{9,1... | collective-permute-start | bytes 6684680 | tf_op jit(solution)/shard_map/ppermute | solution.py:710
  240.6 7.3 %collective-permute-start.15 = (bf16[512,2048]{1,0:T(8,128)(2,1)S(1)}, bf16[512,2048]{1,0:T(8,128)(2,1)}, u32[]{:S(2)}, u32[]{:S(2)}) collective-permute-start(bf16[512,2048]{1,0:T(8,128)(2,1)S(1)} %copy-done.8), channel_id=1, source_target_pairs={{0,4},{4,0},{1,5},{5,1},{2,6},{6,2},{3,7},{7,3},{8,12},{12,8},{9,1... | collective-permute-start | bytes 6291464 | tf_op jit(solution)/shard_map/ppermute | solution.py:710
  338.0 295.6 %reduce-scatter.12.cloned.1.call-start = ((), (), s32[]{:S(2)}) async-start(), calls=%async_computation.11 | async-start | bytes 7864320
  362.0 4.6 collective-permute-start.16
  366.8 14.7 %collective-permute-start.17 = (bf16[128,2176]{1,0:T(8,128)(2,1)S(1)}, bf16[128,2176]{1,0:T(8,128)(2,1)S(1)}, u32[]{:S(2)}, u32[]{:S(2)}) collective-permute-start(bf16[128,2176]{1,0:T(8,128)(2,1)S(1)} %add_convert_fusion.4), channel_id=1, source_target_pairs={{0,1},{1,0},{2,3},{3,2},{4,5},{5,4},{6,7},{7,6},{8,9},{9,8},{10,11... | collective-permute-start | bytes 1671176 | tf_op jit(solution)/shard_map/ppermute | solution.py:720
  381.8 27.3 %collective-permute-start.20 = (bf16[128,2176]{1,0:T(8,128)(2,1)S(1)}, bf16[128,2176]{1,0:T(8,128)(2,1)S(1)}, u32[]{:S(2)}, u32[]{:S(2)}) collective-permute-start(bf16[128,2176]{1,0:T(8,128)(2,1)S(1)} %add_convert_fusion.3), channel_id=1, source_target_pairs={{0,2},{1,3},{2,0},{3,1},{4,6},{5,7},{6,4},{7,5},{8,10},{9,11},{10,... | collective-permute-start | bytes 1671176 | tf_op jit(solution)/shard_map/ppermute | solution.py:720
  384.4 24.6 %collective-permute-start.19 = (bf16[128,2176]{1,0:T(8,128)(2,1)S(1)}, bf16[128,2176]{1,0:T(8,128)(2,1)S(1)}, u32[]{:S(2)}, u32[]{:S(2)}) collective-permute-start(bf16[128,2176]{1,0:T(8,128)(2,1)S(1)} %add_convert_fusion.2), channel_id=1, source_target_pairs={{0,1},{1,0},{2,3},{3,2},{4,5},{5,4},{6,7},{7,6},{8,9},{9,8},{10,11... | collective-permute-start | bytes 1671176 | tf_op jit(solution)/shard_map/ppermute | solution.py:720
  400.6 52.2 %collective-permute-start.18 = (bf16[512,2048]{1,0:T(8,128)(2,1)}, bf16[512,2048]{1,0:T(8,128)(2,1)S(1)}, u32[]{:S(2)}, u32[]{:S(2)}) collective-permute-start(bf16[512,2048]{1,0:T(8,128)(2,1)} %get-tuple-element.349), channel_id=1, source_target_pairs={{0,4},{4,0},{1,5},{5,1},{2,6},{6,2},{3,7},{7,3},{8,12},{12,8},{9,1... | collective-permute-start | bytes 6291464 | tf_op jit(solution)/shard_map/ppermute | solution.py:710
  414.6 24.9 %collective-permute-start.22 = (bf16[128,2048]{1,0:T(8,128)(2,1)}, bf16[128,2048]{1,0:T(8,128)(2,1)S(1)}, u32[]{:S(2)}, u32[]{:S(2)}) collective-permute-start(bf16[128,2048]{1,0:T(8,128)(2,1)} %get-tuple-element.370), channel_id=1, source_target_pairs={{0,2},{1,3},{2,0},{3,1},{4,6},{5,7},{6,4},{7,5},{8,10},{9,11},{10,... | collective-permute-start | bytes 1572872 | tf_op jit(solution)/shard_map/ppermute | solution.py:720
  416.1 36.5 %collective-permute-start.21 = (bf16[128,2048]{1,0:T(8,128)(2,1)S(1)}, bf16[128,2048]{1,0:T(8,128)(2,1)S(1)}, u32[]{:S(2)}, u32[]{:S(2)}) collective-permute-start(bf16[128,2048]{1,0:T(8,128)(2,1)S(1)} %copy-done.18), channel_id=1, source_target_pairs={{0,1},{1,0},{2,3},{3,2},{4,5},{5,4},{6,7},{7,6},{8,9},{9,8},{10,11... | collective-permute-start | bytes 1572872 | tf_op jit(solution)/shard_map/ppermute | solution.py:720
  439.5 13.2 %collective-permute-start.23 = (bf16[128,2048]{1,0:T(8,128)(2,1)S(1)}, bf16[128,2048]{1,0:T(8,128)(2,1)S(1)}, u32[]{:S(2)}, u32[]{:S(2)}) collective-permute-start(bf16[128,2048]{1,0:T(8,128)(2,1)S(1)} %collective-permute-done.22), channel_id=1, source_target_pairs={{0,1},{1,0},{2,3},{3,2},{4,5},{5,4},{6,7},{7,6},{8,9},{9,8},{10,11... | collective-permute-start | bytes 1572872 | tf_op jit(solution)/shard_map/ppermute | solution.py:720
  460.1 221.7 %reduce-scatter.8.cloned.1.call-start = ((), (), s32[]{:S(2)}) async-start(), calls=%async_computation.6 | async-start | bytes 9437184 | tf_op jit(solution)/shard_map/reduce_scatter | solution.py:954
  460.4 15.8 %collective-permute-start.24 = (bf16[128,2048]{1,0:T(8,128)(2,1)}, bf16[128,2048]{1,0:T(8,128)(2,1)S(1)}, u32[]{:S(2)}, u32[]{:S(2)}) collective-permute-start(bf16[128,2048]{1,0:T(8,128)(2,1)} %add_convert_fusion.9), channel_id=1, source_target_pairs={{0,1},{1,0},{2,3},{3,2},{4,5},{5,4},{6,7},{7,6},{8,9},{9,8},{10,11... | collective-permute-start | bytes 1572872 | tf_op jit(solution)/shard_map/ppermute | solution.py:720
  475.7 5.7 collective-permute-start.27
  475.7 61.6 %collective-permute-start.30 = (bf16[2,512,512]{2,1,0:T(8,128)(2,1)}, bf16[2,512,512]{2,1,0:T(8,128)(2,1)}, u32[]{:S(2)}, u32[]{:S(2)}) collective-permute-start(bf16[2,512,512]{2,1,0:T(8,128)(2,1)} %get-tuple-element.392), channel_id=1, source_target_pairs={{0,4},{4,0},{1,5},{5,1},{2,6},{6,2},{3,7},{7,3},{8,12},{12,8},{9,1... | collective-permute-start | bytes 3145736 | tf_op jit(solution)/shard_map/ppermute | solution.py:710
  477.3 28.2 %collective-permute-start.26 = (bf16[128,2048]{1,0:T(8,128)(2,1)}, bf16[128,2048]{1,0:T(8,128)(2,1)S(1)}, u32[]{:S(2)}, u32[]{:S(2)}) collective-permute-start(bf16[128,2048]{1,0:T(8,128)(2,1)} %add_convert_fusion.8), channel_id=1, source_target_pairs={{0,2},{1,3},{2,0},{3,1},{4,6},{5,7},{6,4},{7,5},{8,10},{9,11},{10,... | collective-permute-start | bytes 1572872 | tf_op jit(solution)/shard_map/ppermute | solution.py:720
  480.4 25.1 %collective-permute-start.25 = (bf16[128,2048]{1,0:T(8,128)(2,1)}, bf16[128,2048]{1,0:T(8,128)(2,1)}, u32[]{:S(2)}, u32[]{:S(2)}) collective-permute-start(bf16[128,2048]{1,0:T(8,128)(2,1)} %add_convert_fusion.7), channel_id=1, source_target_pairs={{0,1},{1,0},{2,3},{3,2},{4,5},{5,4},{6,7},{7,6},{8,9},{9,8},{10,11... | collective-permute-start | bytes 1572872 | tf_op jit(solution)/shard_map/ppermute | solution.py:720
  481.7 55.6 %collective-permute-start.31 = (bf16[2,512,512]{2,1,0:T(8,128)(2,1)S(1)}, bf16[2,512,512]{2,1,0:T(8,128)(2,1)}, u32[]{:S(2)}, u32[]{:S(2)}) collective-permute-start(bf16[2,512,512]{2,1,0:T(8,128)(2,1)S(1)} %add_convert_fusion), channel_id=1, source_target_pairs={{0,8},{8,0},{1,9},{9,1},{2,10},{10,2},{3,11},{11,3},{4,12},{12,4},... | collective-permute-start | bytes 3145736 | tf_op jit(solution)/shard_map/ppermute | solution.py:710
  506.9 32.4 %collective-permute-start.29 = (bf16[128,2048]{1,0:T(8,128)(2,1)S(1)}, bf16[128,2048]{1,0:T(8,128)(2,1)S(1)}, u32[]{:S(2)}, u32[]{:S(2)}) collective-permute-start(bf16[128,2048]{1,0:T(8,128)(2,1)S(1)} %add_convert_fusion.6.refs_0_), channel_id=1, source_target_pairs={{0,2},{1,3},{2,0},{3,1},{4,6},{5,7},{6,4},{7,5},{8,10},{9,11},{10,... | collective-permute-start | bytes 1572872 | tf_op jit(solution)/shard_map/ppermute | solution.py:720
  507.0 51.5 %collective-permute-start.28 = (bf16[128,2048]{1,0:T(8,128)(2,1)S(1)}, bf16[128,2048]{1,0:T(8,128)(2,1)}, u32[]{:S(2)}, u32[]{:S(2)}) collective-permute-start(bf16[128,2048]{1,0:T(8,128)(2,1)S(1)} %add_convert_fusion.6.refs_0_), channel_id=1, source_target_pairs={{0,1},{1,0},{2,3},{3,2},{4,5},{5,4},{6,7},{7,6},{8,9},{9,8},{10,11... | collective-permute-start | bytes 1572872 | tf_op jit(solution)/shard_map/ppermute | solution.py:720
  539.3 19.2 %collective-permute-start.32 = (bf16[128,2048]{1,0:T(8,128)(2,1)S(1)}, bf16[128,2048]{1,0:T(8,128)(2,1)}, u32[]{:S(2)}, u32[]{:S(2)}) collective-permute-start(bf16[128,2048]{1,0:T(8,128)(2,1)S(1)} %collective-permute-done.29.refs_2_), channel_id=1, source_target_pairs={{0,1},{1,0},{2,3},{3,2},{4,5},{5,4},{6,7},{7,6},{8,9},{9,8},{10,11... | collective-permute-start | bytes 1572872 | tf_op jit(solution)/shard_map/ppermute | solution.py:720
  587.2 50.6 %collective-permute-start.41 = (bf16[6,3,256,256]{3,2,1,0:T(8,128)(2,1)S(1)}, bf16[6,3,256,256]{3,2,1,0:T(8,128)(2,1)}, u32[]{:S(2)}, u32[]{:S(2)}) collective-permute-start(bf16[6,3,256,256]{3,2,1,0:T(8,128)(2,1)S(1)} %copy-done.5), channel_id=1, source_target_pairs={{0,4},{4,0},{1,5},{5,1},{2,6},{6,2},{3,7},{7,3},{8,12},{12,8},{9,1... | collective-permute-start | bytes 7077896 | tf_op jit(solution)/shard_map/ppermute | solution.py:710
  587.3 14.7 %collective-permute-start.36 = (bf16[128,2048]{1,0:T(8,128)(2,1)S(1)}, bf16[128,2048]{1,0:T(8,128)(2,1)S(1)}, u32[]{:S(2)}, u32[]{:S(2)}) collective-permute-start(bf16[128,2048]{1,0:T(8,128)(2,1)S(1)} %copy-done.34), channel_id=1, source_target_pairs={{0,1},{1,0},{2,3},{3,2},{4,5},{5,4},{6,7},{7,6},{8,9},{9,8},{10,11... | collective-permute-start | bytes 1572872 | tf_op jit(solution)/shard_map/ppermute | solution.py:720
  588.7 34.0 %collective-permute-start.35 = (bf16[128,2048]{1,0:T(8,128)(2,1)}, bf16[128,2048]{1,0:T(8,128)(2,1)}, u32[]{:S(2)}, u32[]{:S(2)}) collective-permute-start(bf16[128,2048]{1,0:T(8,128)(2,1)} %get-tuple-element.441), channel_id=1, source_target_pairs={{0,1},{1,0},{2,3},{3,2},{4,5},{5,4},{6,7},{7,6},{8,9},{9,8},{10,11... | collective-permute-start | bytes 1572872 | tf_op jit(solution)/shard_map/ppermute | solution.py:720
  602.1 25.3 %collective-permute-start.37 = (bf16[128,2048]{1,0:T(8,128)(2,1)S(1)}, bf16[128,2048]{1,0:T(8,128)(2,1)S(1)}, u32[]{:S(2)}, u32[]{:S(2)}) collective-permute-start(bf16[128,2048]{1,0:T(8,128)(2,1)S(1)} %add_convert_fusion.5), channel_id=1, source_target_pairs={{0,2},{1,3},{2,0},{3,1},{4,6},{5,7},{6,4},{7,5},{8,10},{9,11},{10,... | collective-permute-start | bytes 1572872 | tf_op jit(solution)/shard_map/ppermute | solution.py:720
  631.9 20.4 %collective-permute-start.40 = (bf16[128,2048]{1,0:T(8,128)(2,1)}, bf16[128,2048]{1,0:T(8,128)(2,1)S(1)}, u32[]{:S(2)}, u32[]{:S(2)}) collective-permute-start(bf16[128,2048]{1,0:T(8,128)(2,1)} %get-tuple-element.467.refs_0_), channel_id=1, source_target_pairs={{0,1},{1,0},{2,3},{3,2},{4,5},{5,4},{6,7},{7,6},{8,9},{9,8},{10,11... | collective-permute-start | bytes 1572872 | tf_op jit(solution)/shard_map/ppermute | solution.py:720
  633.6 24.9 %collective-permute-start.38 = (bf16[128,2048]{1,0:T(8,128)(2,1)}, bf16[128,2048]{1,0:T(8,128)(2,1)S(1)}, u32[]{:S(2)}, u32[]{:S(2)}) collective-permute-start(bf16[128,2048]{1,0:T(8,128)(2,1)} %get-tuple-element.467.refs_0_), channel_id=1, source_target_pairs={{0,2},{1,3},{2,0},{3,1},{4,6},{5,7},{6,4},{7,5},{8,10},{9,11},{10,... | collective-permute-start | bytes 1572872 | tf_op jit(solution)/shard_map/ppermute | solution.py:720
  657.0 14.1 %collective-permute-start.43 = (bf16[2,3,256,256]{3,2,1,0:T(8,128)(2,1)S(1)}, bf16[2,3,256,256]{3,2,1,0:T(8,128)(2,1)S(1)}, u32[]{:S(2)}, u32[]{:S(2)}) collective-permute-start(bf16[2,3,256,256]{3,2,1,0:T(8,128)(2,1)S(1)} %get-tuple-element.510), channel_id=1, source_target_pairs={{0,4},{4,0},{1,5},{5,1},{2,6},{6,2},{3,7},{7,3},{8,12},{12,8},{9,1... | collective-permute-start | bytes 2359304 | tf_op jit(solution)/shard_map/ppermute | solution.py:710
  658.5 18.3 %collective-permute-start.39 = (bf16[128,2048]{1,0:T(8,128)(2,1)S(1)}, bf16[128,2048]{1,0:T(8,128)(2,1)S(1)}, u32[]{:S(2)}, u32[]{:S(2)}) collective-permute-start(bf16[128,2048]{1,0:T(8,128)(2,1)S(1)} %collective-permute-done.38.refs_0_), channel_id=1, source_target_pairs={{0,1},{1,0},{2,3},{3,2},{4,5},{5,4},{6,7},{7,6},{8,9},{9,8},{10,11... | collective-permute-start | bytes 1572872 | tf_op jit(solution)/shard_map/ppermute | solution.py:720
  659.4 9.0 %all-to-all-start.2 = ((f32[8,20,256]{2,1,0:T(8,128)}), f32[8,20,256]{2,1,0:T(8,128)S(1)}, u32[]{:S(2)}, u32[]{:S(2)}) async-start(f32[8,20,256]{2,1,0:T(8,128)} %bitcast.60), calls=%async_computation.3 | async-start | bytes 393216 | tf_op jit(solution)/shard_map/all_to_all | solution.py:967
  668.4 7.5 %collective-permute-start.42 = (f32[20,256]{1,0:T(8,128)S(1)}, f32[20,256]{1,0:T(8,128)S(1)}, u32[]{:S(2)}, u32[]{:S(2)}) collective-permute-start(f32[20,256]{1,0:T(8,128)S(1)} %reduce_sum.9), channel_id=1, source_target_pairs={{0,1},{1,0},{2,3},{3,2},{4,5},{5,4},{6,7},{7,6},{8,9},{9,8},{10,11... | collective-permute-start | bytes 61448 | tf_op jit(solution)/shard_map/ppermute | solution.py:720
  675.9 4.8 collective-permute-start.44
  (39 other events, 417.1 us)
Sparse Core Ops, SparseCore 0:
  10.5 57.2 all-gather.6
  69.6 194.2 all-gather.8
  265.8 70.1 all-gather.10
  338.9 193.1 reduce-scatter.9
  535.8 70.1 reduce-scatter.11
  609.8 71.2 reduce-scatter.7

commit v8 on v4

--- a/solution.py
+++ b/solution.py
@@ -642,7 +642,6 @@
     w = jnp.concatenate([w_ref[:, c].reshape(pb * ds, n) for c in range(3)], 1)
     y = nt(d_ref[...], w).astype(BF16)
     rows = outs[0].shape[0]
-    outs[0][...] = y[:rows]
     for r, o in enumerate(outs):
         for q in range(len(outs)):
 
@@ -904,13 +903,13 @@
             grads.append(to_owners(made, k, ()))
     d_normed = line.sums(*dx, tp)
     moe = line(expert_down, hid, ws, 2, 1, [], [], 2, "expert_out")
-    late = weight_grad(len(chunks) - 1)
 
     d_mid, d_mid_low, gain_two, grad_router = line(
         norm_two_back, d_normed, mid, ext, probs, chosen, cots[0], gains[1:2], router_rows
     )
     far = across(d_mid_low, 2)
     near = across(d_mid_low, 1)
+    late = weight_grad(len(chunks) - 1)
     d_mid_low = line(join, d_mid_low, near, far, across(far, 1))
     own, beside = cut(moe[0], tp), cut(swap(moe[1], "core"), tp)
     last = across(line(add, own[3], beside[3]), 1)

time: 701 us -> 705 us (level)
    ppermute x30, waiting for transfers between devices: 185 us -> 175 us  [across(): return lax.ppermute(value, 'tp', [(i, i ^ k) for i in range(size)])]
    reduce_scatter x1, waiting for transfers between devices: 0.69 us -> 8.87 us  [body(): lax.psum_scatter(grad_attn, PLANE, scatter_dimension=0, tiled=False)]
  transfers between devices with their start and end apart: 52 -> 52, of which waited for: 32 -> 30; matrix products, arithmetic and copies ran while one was open for 7% -> 7% of each run, Pallas kernels for 35% -> 35%
where the time goes in v8:
time: 705 us; the launch traced here: 696 us
  waiting for transfers between devices  285 us (40%)
  Pallas kernels  241 us (34%)
  starting transfers between devices  51.8 us (7%)
  local copies, waits for them, and re-layouts  36.8 us (5%)
  blocking collectives  35.3 us (5%)
  between operations  22.9 us (3%)
  other arithmetic  22.8 us (3%)
    ppermute x30, waiting for transfers between devices, across(): return lax.ppermute(value, 'tp', [(i, i ^ k) for i in range(size)])  175 us
    ppermute x15, waiting for transfers between devices, swap(): return lax.ppermute(value, axis, [(0, 1), (1, 0)])  66.1 us
    pallas_call x3, Pallas kernels, expert_down(): call(functools.partial(down_kernel, planes=planes, chunks=chunks, sides=l...  43.2 us
    pallas_call x2, Pallas kernels, expert_up(): call(functools.partial(expert_kernel, parts=parts), 'expert_up', (e,), [f...  41.3 us
    ppermute x30, starting transfers between devices, across(): return lax.ppermute(value, 'tp', [(i, i ^ k) for i in range(size)])  41.2 us
    pallas_call x2, Pallas kernels, expert_grads(): call(functools.partial(expert_grad_kernel, parts=parts), 'expert_grad', (...  40.1 us
    all_gather x2, waiting for transfers between devices, body(): lax.all_gather(mine, FR, axis=0, tiled=False).reshape(-1, e, 3, ds, f)  15.7 us
    all_to_all x2, blocking collectives, body(): mine = lax.all_to_all(grouped[:, begin:begin + e], 'core', 0, 0, tiled=True)  14.5 us
  transfers between devices with their start and end apart: 52, of which 30 were waited for; matrix products, arithmetic and copies ran while one was open for 7% of the time, Pallas kernels for 35%

profile of v8, /device:TPU:0, one launch (start us, length us, event | category | flops | bytes accessed | tf_op | source)
XLA Modules:
  0.0 696.1 jit_solution(3814823592160749155)
XLA Ops:
  11.9 8.6 %all_to_all.15 = bf16[2,6,3,256,256]{4,3,2,1,0:T(8,128)(2,1)} all-to-all(bf16[2,6,3,256,256]{4,3,2,1,0:T(8,128)(2,1)S(1)} %fusion), channel_id=1, replica_groups=mesh['fsdp'=2,'row'=2,'core'=2,'tp'=4] {'core'}, dimensions={0} | all-to-all | bytes 9437184 | tf_op jit(solution)/shard_map/all_to_all | solution.py:834
  29.5 10.3 %all_gather.26 = bf16[4,2048]{1,0:T(4,128)(2,1)S(1)} all-gather(bf16[4,256]{1,0:T(4,128)(2,1)S(1)} %copy-done.31), channel_id=1, replica_groups=mesh['fsdp'=2,'row'=2,'core'=2,'tp'=4] {'fsdp','row','core'}, dimensions={1}, use_global_device_ids=true | all-gather | bytes 18432 | tf_op jit(solution)/shard_map/all_gather | solution.py:836
  39.9 10.4 %all_gather.27 = bf16[2048,16]{0,1:T(8,128)(2,1)} all-gather(bf16[256,16]{0,1:T(8,128)(2,1)S(1)} %copy-done.29), channel_id=1, replica_groups=mesh['fsdp'=2,'row'=2,'core'=2,'tp'=4] {'fsdp','row','core'}, dimensions={0}, use_global_device_ids=true | all-gather | bytes 73728 | tf_op jit(solution)/shard_map/all_gather | solution.py:837
  54.6 13.2 %all-gather.7.cloned.1.call-done = bf16[32,256,512]{2,1,0:T(8,128)(2,1)} async-done(((bf16[4,256,512]{2,1,0:T(8,128)(2,1)}), bf16[32,256,512]{2,1,0:T(8,128)(2,1)}) %all-gather.7.cloned.1.call-update) | async-done | bytes 8388624 | tf_op jit(solution)/shard_map/all_gather | solution.py:828
  68.4 10.4 %qkv.1 = (bf16[512,2048]{1,0:T(8,128)(2,1)}, f32[2,512,512]{2,1,0:T(8,128)}, bf16[512,512]{1,0:T(8,128)(2,1)}, f32[2,512,128]{2,1,0:T(8,128)}) custom-call(bf16[512,2048]{1,0:T(8,128)(2,1)} %bitcast.83, f32[1,2048]{1,0:T(1,128)} %get-tuple-element.454.g_ref, bf16[8,4,256,512]{3,2,1,0:T(8,128)(2,1)} %bitcast.61), custom_call_target="tpu_custom_call" | custom-call | flops 3221225472 | bytes 13107200 | tf_op jit(solution)/shard_map/qkv/pallas_call | solution.py:87
  91.1 9.7 %collective-permute-done.2.refs_6_ = bf16[512,512]{1,0:T(8,128)(2,1)S(1)} collective-permute-done((bf16[512,512]{1,0:T(8,128)(2,1)}, bf16[512,512]{1,0:T(8,128)(2,1)S(1)}, u32[]{:S(2)}, u32[]{:S(2)}) %collective-permute-start.2) | collective-permute-done | bytes 524320 | tf_op jit(solution)/shard_map/ppermute | solution.py:710
  101.8 4.4 prep.1
  108.8 22.9 %collective-permute-done.4.refs_2_ = bf16[512,512]{1,0:T(8,128)(2,1)} collective-permute-done((bf16[512,512]{1,0:T(8,128)(2,1)}, bf16[512,512]{1,0:T(8,128)(2,1)}, u32[]{:S(2)}, u32[]{:S(2)}) %collective-permute-start.4) | collective-permute-done | bytes 524320 | tf_op jit(solution)/shard_map/ppermute | solution.py:710
  134.0 9.9 %attend.1.h_ref = bf16[512,512]{1,0:T(8,128)(2,1)} custom-call(s32[7]{0:T(128)} %pad_add_fusion.scal_ref, bf16[512,512]{1,0:T(8,128)(2,1)} %get-tuple-element.380.q_ref, bf16[512,512]{1,0:T(8,128)(2,1)} %get-tuple-element.381.refs_0_, bf16[512,512]{1,0:T(8,128)(2,1)} %collective-permute-done.3.refs_1_, bf16[512,512]{1,0:T(8,128)(2,1)} %collective-permute-done.4.refs_2_, ...), custom_call_target="tpu_custom_call" | custom-call | flops 1073741824 | bytes 6291456 | tf_op jit(solution)/shard_map/attend/pallas_call | solution.py:171
  143.9 5.4 outproj.1
  151.4 12.9 %collective-permute-done.9 = bf16[128,2048]{1,0:T(8,128)(2,1)S(1)} collective-permute-done((bf16[128,2048]{1,0:T(8,128)(2,1)}, bf16[128,2048]{1,0:T(8,128)(2,1)S(1)}, u32[]{:S(2)}, u32[]{:S(2)}) %collective-permute-start.9) | collective-permute-done | bytes 524320 | tf_op jit(solution)/shard_map/ppermute | solution.py:720
  171.6 11.9 %collective-permute-done.8.b_ref = bf16[128,2048]{1,0:T(8,128)(2,1)S(1)} collective-permute-done((bf16[128,2048]{1,0:T(8,128)(2,1)}, bf16[128,2048]{1,0:T(8,128)(2,1)S(1)}, u32[]{:S(2)}, u32[]{:S(2)}) %collective-permute-start.8) | collective-permute-done | bytes 524320 | tf_op jit(solution)/shard_map/ppermute | solution.py:720
  183.5 6.8 collective-permute-done.10.c_ref
  193.9 6.0 all_to_all.16
  203.9 12.2 %collective-permute-done.12 = bf16[128,2176]{1,0:T(8,128)(2,1)S(1)} collective-permute-done((bf16[128,2176]{1,0:T(8,128)(2,1)}, bf16[128,2176]{1,0:T(8,128)(2,1)S(1)}, u32[]{:S(2)}, u32[]{:S(2)}) %collective-permute-start.12) | collective-permute-done | bytes 557088 | tf_op jit(solution)/shard_map/ppermute | solution.py:720
  216.9 8.8 %collective-permute-done.11 = bf16[128,2176]{1,0:T(8,128)(2,1)S(1)} collective-permute-done((bf16[128,2176]{1,0:T(8,128)(2,1)S(1)}, bf16[128,2176]{1,0:T(8,128)(2,1)S(1)}, u32[]{:S(2)}, u32[]{:S(2)}) %collective-permute-start.11) | collective-permute-done | bytes 557088 | tf_op jit(solution)/shard_map/ppermute | solution.py:720
  225.7 11.5 %collective-permute-done.13 = bf16[128,2176]{1,0:T(8,128)(2,1)S(1)} collective-permute-done((bf16[128,2176]{1,0:T(8,128)(2,1)S(1)}, bf16[128,2176]{1,0:T(8,128)(2,1)S(1)}, u32[]{:S(2)}, u32[]{:S(2)}) %collective-permute-start.13) | collective-permute-done | bytes 557088 | tf_op jit(solution)/shard_map/ppermute | solution.py:720
  241.1 6.8 collective-permute-done.15.refs_3_
  248.2 15.7 %all-gather.9.cloned.1.call-done.refs_4_.refs_1_.refs_2_ = bf16[8,6,3,256,256]{4,3,2,1,0:T(8,128)(2,1)} async-done(((bf16[2,6,3,256,256]{4,3,2,1,0:T(8,128)(2,1)}), bf16[8,6,3,256,256]{4,3,2,1,0:T(8,128)(2,1)}) %all-gather.9.cloned.1.call-update) | async-done | bytes 18874384 | tf_op jit(solution)/shard_map/all_gather | solution.py:835
  264.0 28.1 %expert_up.2 = (bf16[1024,1536]{1,0:T(8,128)(2,1)}, bf16[1024,3072]{1,0:T(8,128)(2,1)}, f32[1024,128]{1,0:T(8,128)}) custom-call(s32[1]{0:T(128)} %bitcast.19.first_ref, bf16[512,2176]{1,0:T(8,128)(2,1)} %constant_dynamic-update-slice_fusion.refs_0_, bf16[512,2176]{1,0:T(8,128)(2,1)} %collective-permute-done.14.refs_1_, ...), custom_call_target="tpu_custom_call" | custom-call | flops 19327352832 | bytes 36700160 | tf_op jit(solution)/shard_map/expert_up/pallas_call | solution.py:438
  292.0 18.9 %expert_dx.2 = (bf16[512,2048]{1,0:T(8,128)(2,1)}, bf16[512,2048]{1,0:T(8,128)(2,1)}) custom-call(bf16[1024,3072]{1,0:T(8,128)(2,1)} %get-tuple-element.317.refs_0_.refs_5_, bf16[8,6,3,256,256]{4,3,2,1,0:T(8,128)(2,1)} %all-gather.9.cloned.1.call-done.refs_4_.refs_1_.refs_2_), custom_call_target="tpu_custom_call" | custom-call | flops 12884901888 | bytes 23068672 | tf_op jit(solution)/shard_map/expert_dx/pallas_call | solution.py:562
  311.0 27.0 %expert_grad.2 = bf16[8,6,3,256,256]{4,3,2,1,0:T(8,128)(2,1)} custom-call(bf16[512,2176]{1,0:T(8,128)(2,1)} %constant_dynamic-update-slice_fusion.refs_0_, bf16[512,2176]{1,0:T(8,128)(2,1)} %collective-permute-done.14.refs_1_, bf16[512,2048]{1,0:T(8,128)(2,1)} %pad_maximum_fusion.refs_2_, bf16[512,2048]{1,0:T(8,128)(2,1)} %collective-permute-done.15.refs_3_, ...), custom_call_target="tpu_custom_call" | custom-call | flops 19327352832 | bytes 36700160 | tf_op jit(solution)/shard_map/expert_grad/pallas_call | solution.py:477
  338.3 13.2 %expert_up.3 = (bf16[1024,512]{1,0:T(8,128)(2,1)}, bf16[1024,1024]{1,0:T(8,128)(2,1)}, f32[1024,128]{1,0:T(8,128)}) custom-call(s32[1]{0:T(128)} %bitcast.22.first_ref, bf16[512,2176]{1,0:T(8,128)(2,1)} %constant_dynamic-update-slice_fusion.refs_0_, bf16[512,2176]{1,0:T(8,128)(2,1)} %collective-permute-done.14.refs_1_, ...), custom_call_target="tpu_custom_call" | custom-call | flops 6442450944 | bytes 17825792 | tf_op jit(solution)/shard_map/expert_up/pallas_call | solution.py:438
  351.5 10.5 %expert_dx.3 = (bf16[512,2176]{1,0:T(8,128)(2,1)}, bf16[512,2176]{1,0:T(8,128)(2,1)}) custom-call(bf16[1024,1024]{1,0:T(8,128)(2,1)} %get-tuple-element.369.refs_0_.refs_5_, bf16[8,2,3,256,256]{4,3,2,1,0:T(8,128)(2,1)} %all-gather.11.cloned.1.call-done.refs_4_.refs_1_.refs_3_, f32[1024,128]{1,0:T(8,128)} %get-tuple-element.329.refs_2_, ...), custom_call_target="tpu_custom_call" | custom-call | flops 4294967296 | bytes 10747904 | tf_op jit(solution)/shard_map/expert_dx/pallas_call | solution.py:562
  368.4 13.2 %collective-permute-done.17 = bf16[128,2176]{1,0:T(8,128)(2,1)S(1)} collective-permute-done((bf16[128,2176]{1,0:T(8,128)(2,1)S(1)}, bf16[128,2176]{1,0:T(8,128)(2,1)S(1)}, u32[]{:S(2)}, u32[]{:S(2)}) %collective-permute-start.17) | collective-permute-done | bytes 557088 | tf_op jit(solution)/shard_map/ppermute | solution.py:720
  386.9 13.8 %expert_out.1 = (bf16[512,2048]{1,0:T(8,128)(2,1)}, bf16[512,2048]{1,0:T(8,128)(2,1)}) custom-call(bf16[1024,1536]{1,0:T(8,128)(2,1)} %get-tuple-element.344.refs_4_.refs_0_, bf16[1024,512]{1,0:T(8,128)(2,1)} %get-tuple-element.368.refs_1_.refs_4_, bf16[8,6,3,256,256]{4,3,2,1,0:T(8,128)(2,1)} %all-gather.9.cloned.1.call-done.refs_4_.refs_1_.refs_2_, ...), custom_call_target="tpu_custom_call" | custom-call | flops 8589934592 | bytes 16777216 | tf_op jit(solution)/shard_map/expert_out/pallas_call | solution.py:562
  400.7 8.4 %collective-permute-done.19.b_ref = bf16[128,2176]{1,0:T(8,128)(2,1)S(1)} collective-permute-done((bf16[128,2176]{1,0:T(8,128)(2,1)S(1)}, bf16[128,2176]{1,0:T(8,128)(2,1)S(1)}, u32[]{:S(2)}, u32[]{:S(2)}) %collective-permute-start.19) | collective-permute-done | bytes 557088 | tf_op jit(solution)/shard_map/ppermute | solution.py:720
  410.0 4.6 norm_two_back.1
  418.2 21.3 %collective-permute-done.22 = bf16[128,2048]{1,0:T(8,128)(2,1)S(1)} collective-permute-done((bf16[128,2048]{1,0:T(8,128)(2,1)}, bf16[128,2048]{1,0:T(8,128)(2,1)S(1)}, u32[]{:S(2)}, u32[]{:S(2)}) %collective-permute-start.22) | collective-permute-done | bytes 524320 | tf_op jit(solution)/shard_map/ppermute | solution.py:720
  439.5 13.2 %expert_grad.3 = bf16[8,2,3,256,256]{4,3,2,1,0:T(8,128)(2,1)} custom-call(bf16[512,2176]{1,0:T(8,128)(2,1)} %constant_dynamic-update-slice_fusion.refs_0_, bf16[512,2176]{1,0:T(8,128)(2,1)} %collective-permute-done.14.refs_1_, bf16[512,2048]{1,0:T(8,128)(2,1)} %pad_maximum_fusion.refs_2_, bf16[512,2048]{1,0:T(8,128)(2,1)} %collective-permute-done.15.refs_3_, ...), custom_call_target="tpu_custom_call" | custom-call | flops 6442450944 | bytes 17825792 | tf_op jit(solution)/shard_map/expert_grad/pallas_call | solution.py:477
  455.1 5.0 dheads.1.refs_8_
  462.5 13.2 %attend_back.1 = (f32[512,512]{1,0:T(8,128)}, bf16[2,512,512]{2,1,0:T(8,128)(2,1)}, bf16[2,512,512]{2,1,0:T(8,128)(2,1)}, bf16[2,512,512]{2,1,0:T(8,128)(2,1)}, bf16[2,512,512]{2,1,0:T(8,128)(2,1)}) custom-call(s32[7]{0:T(128)} %pad_add_fusion.scal_ref, bf16[512,512]{1,0:T(8,128)(2,1)} %get-tuple-element.380.q_ref, ...), custom_call_target="tpu_custom_call" | custom-call | flops 2684354560 | bytes 12582912 | tf_op jit(solution)/shard_map/attend_back/pallas_call | solution.py:209
  483.1 7.7 %gradout.1.kept_ref = bf16[8,4,256,512]{3,2,1,0:T(8,128)(2,1)} custom-call(s32[4]{0:T(128)} %copy-done.26, bf16[512,2048]{1,0:T(8,128)(2,1)} %copy-done.1, bf16[512,512]{1,0:T(8,128)(2,1)} %attend.1.h_ref), custom_call_target="tpu_custom_call" | custom-call | flops 1073741824 | bytes 4718592 | tf_op jit(solution)/shard_map/gradout/pallas_call | solution.py:288
  490.8 14.5 %collective-permute-done.25 = bf16[128,2048]{1,0:T(8,128)(2,1)S(1)} collective-permute-done((bf16[128,2048]{1,0:T(8,128)(2,1)}, bf16[128,2048]{1,0:T(8,128)(2,1)S(1)}, u32[]{:S(2)}, u32[]{:S(2)}) %collective-permute-start.25) | collective-permute-done | bytes 524320 | tf_op jit(solution)/shard_map/ppermute | solution.py:720
  507.1 22.6 %collective-permute-done.31 = bf16[2,512,512]{2,1,0:T(8,128)(2,1)S(1)} collective-permute-done((bf16[2,512,512]{2,1,0:T(8,128)(2,1)S(1)}, bf16[2,512,512]{2,1,0:T(8,128)(2,1)S(1)}, u32[]{:S(2)}, u32[]{:S(2)}) %collective-permute-start.31) | collective-permute-done | bytes 1048608 | tf_op jit(solution)/shard_map/ppermute | solution.py:710
  533.3 6.0 unturn.1
  548.8 4.3 inplace.3
  555.2 10.9 %raw_back.1 = (bf16[512,1536]{1,0:T(8,128)(2,1)}, bf16[128,2048]{1,0:T(8,128)(2,1)}, bf16[128,2048]{1,0:T(8,128)(2,1)}, bf16[128,2048]{1,0:T(8,128)(2,1)}, bf16[128,2048]{1,0:T(8,128)(2,1)}) custom-call(s32[4]{0:T(128)} %copy-done.26, f32[2,512,512]{2,1,0:T(8,128)} %get-tuple-element.431.u_ref, f32[2,512,512]{2,1,0:T(8,128)} %get-tuple-element.432.raw_ref, ...), custom_call_target="tpu_custom_call" | custom-call | flops 3221225472 | bytes 13631488 | tf_op jit(solution)/shard_map/raw_back/pallas_call | solution.py:658
  566.1 9.2 %qkv_grad.1 = bf16[8,4,256,512]{3,2,1,0:T(8,128)(2,1)} custom-call(bf16[512,2048]{1,0:T(8,128)(2,1)} %get-tuple-element.443.n_ref, bf16[512,1536]{1,0:T(8,128)(2,1)} %get-tuple-element.444.d_ref, bf16[8,4,256,512]{3,2,1,0:T(8,128)(2,1)} %gradout.1.kept_ref), custom_call_target="tpu_custom_call", output_to_operand_aliasing={{}: (2, {})} | custom-call | flops 3221225472 | bytes 9961472 | tf_op jit(solution)/shard_map/qkv_grad/pallas_call | solution.py:692
  575.4 4.3 dynamic-slice_bitcast_fusion
  581.7 12.7 %collective-permute-done.36 = bf16[128,2048]{1,0:T(8,128)(2,1)S(1)} collective-permute-done((bf16[128,2048]{1,0:T(8,128)(2,1)S(1)}, bf16[128,2048]{1,0:T(8,128)(2,1)S(1)}, u32[]{:S(2)}, u32[]{:S(2)}) %collective-permute-start.36) | collective-permute-done | bytes 524320 | tf_op jit(solution)/shard_map/ppermute | solution.py:720
  596.5 17.2 %collective-permute-done.35.b_ref = bf16[128,2048]{1,0:T(8,128)(2,1)S(1)} collective-permute-done((bf16[128,2048]{1,0:T(8,128)(2,1)}, bf16[128,2048]{1,0:T(8,128)(2,1)S(1)}, u32[]{:S(2)}, u32[]{:S(2)}) %collective-permute-start.35) | collective-permute-done | bytes 524320 | tf_op jit(solution)/shard_map/ppermute | solution.py:720
  613.7 6.5 collective-permute-done.37.c_ref
  620.2 4.3 norm_one_back.1
  629.2 8.1 %settle.2 = (f32[16,2,256,256]{3,2,1,0:T(8,128)}, f32[16,256,256]{2,1,0:T(8,128)}) custom-call(s32[6]{0:T(128)} %pad_add_fusion.1.spot_ref, bf16[6,3,256,256]{3,2,1,0:T(8,128)(2,1)} %get-tuple-element.462.refs_0_, bf16[6,3,256,256]{3,2,1,0:T(8,128)(2,1)} %collective-permute-done.41.refs_1_), custom_call_target="tpu_custom_call" | custom-call | bytes 14155776 | tf_op jit(solution)/shard_map/settle/pallas_call | solution.py:508
  637.3 8.5 %collective-permute-done.40.refs_1_ = bf16[128,2048]{1,0:T(8,128)(2,1)S(1)} collective-permute-done((bf16[128,2048]{1,0:T(8,128)(2,1)}, bf16[128,2048]{1,0:T(8,128)(2,1)S(1)}, u32[]{:S(2)}, u32[]{:S(2)}) %collective-permute-start.40) | collective-permute-done | bytes 524320 | tf_op jit(solution)/shard_map/ppermute | solution.py:720
  655.1 6.7 all-to-all-done.2
  674.4 8.9 %reduce-scatter.8.cloned.1.call-done = bf16[1,4,256,512]{3,2,1,0:T(8,128)(2,1)} async-done(((bf16[8,4,256,512]{3,2,1,0:T(8,128)(2,1)}), bf16[1,4,256,512]{3,2,1,0:T(8,128)(2,1)}) %reduce-scatter.8.cloned.1.call-update) | async-done | bytes 1048592 | tf_op jit(solution)/shard_map/reduce_scatter | solution.py:953
  (235 shorter events, 132.5 us)
Async XLA Ops:
  7.2 60.6 %all-gather.7.cloned.1.call-start = ((), (), s32[]{:S(2)}) async-start(), calls=%async_computation.7 | async-start | bytes 9437184 | tf_op jit(solution)/shard_map/all_gather | solution.py:828
  9.7 254.3 %all-gather.9.cloned.1.call-start = ((), (), s32[]{:S(2)}) async-start(), calls=%async_computation.8 | async-start | bytes 23592960 | tf_op jit(solution)/shard_map/all_gather | solution.py:835
  20.5 317.8 %all-gather.11.cloned.1.call-start = ((), (), s32[]{:S(2)}) async-start(), calls=%async_computation.9 | async-start | bytes 7864320 | tf_op jit(solution)/shard_map/all_gather | solution.py:835
  78.8 22.0 %collective-permute-start.2 = (bf16[512,512]{1,0:T(8,128)(2,1)}, bf16[512,512]{1,0:T(8,128)(2,1)S(1)}, u32[]{:S(2)}, u32[]{:S(2)}) collective-permute-start(bf16[512,512]{1,0:T(8,128)(2,1)} %get-tuple-element.385.refs_4_), channel_id=1, source_target_pairs={{0,8},{8,0},{1,9},{9,1},{2,10},{10,2},{3,11},{11,3},{4,12},{12,4},... | collective-permute-start | bytes 1572872 | tf_op jit(solution)/shard_map/ppermute | solution.py:710
  86.6 4.5 collective-permute-start.1
  106.2 25.5 %collective-permute-start.4 = (bf16[512,512]{1,0:T(8,128)(2,1)}, bf16[512,512]{1,0:T(8,128)(2,1)}, u32[]{:S(2)}, u32[]{:S(2)}) collective-permute-start(bf16[512,512]{1,0:T(8,128)(2,1)} %get-tuple-element.381.refs_0_), channel_id=1, source_target_pairs={{0,8},{8,0},{1,9},{9,1},{2,10},{10,2},{3,11},{11,3},{4,12},{12,4},... | collective-permute-start | bytes 1572872 | tf_op jit(solution)/shard_map/ppermute | solution.py:710
  108.3 24.7 %collective-permute-start.6 = (bf16[512,512]{1,0:T(8,128)(2,1)S(1)}, bf16[512,512]{1,0:T(8,128)(2,1)}, u32[]{:S(2)}, u32[]{:S(2)}) collective-permute-start(bf16[512,512]{1,0:T(8,128)(2,1)S(1)} %copy-done.21), channel_id=1, source_target_pairs={{0,4},{4,0},{1,5},{5,1},{2,6},{6,2},{3,7},{7,3},{8,12},{12,8},{9,1... | collective-permute-start | bytes 1572872 | tf_op jit(solution)/shard_map/ppermute | solution.py:710
  108.3 24.7 %collective-permute-start.3 = (bf16[512,512]{1,0:T(8,128)(2,1)}, bf16[512,512]{1,0:T(8,128)(2,1)}, u32[]{:S(2)}, u32[]{:S(2)}) collective-permute-start(bf16[512,512]{1,0:T(8,128)(2,1)} %get-tuple-element.381.refs_0_), channel_id=1, source_target_pairs={{0,4},{4,0},{1,5},{5,1},{2,6},{6,2},{3,7},{7,3},{8,12},{12,8},{9,1... | collective-permute-start | bytes 1572872 | tf_op jit(solution)/shard_map/ppermute | solution.py:710
  108.8 24.2 %collective-permute-start.7 = (bf16[512,512]{1,0:T(8,128)(2,1)S(1)}, bf16[512,512]{1,0:T(8,128)(2,1)}, u32[]{:S(2)}, u32[]{:S(2)}) collective-permute-start(bf16[512,512]{1,0:T(8,128)(2,1)S(1)} %collective-permute-done.2.refs_6_), channel_id=1, source_target_pairs={{0,4},{4,0},{1,5},{5,1},{2,6},{6,2},{3,7},{7,3},{8,12},{12,8},{9,1... | collective-permute-start | bytes 1572872 | tf_op jit(solution)/shard_map/ppermute | solution.py:710
  149.3 15.0 %collective-permute-start.9 = (bf16[128,2048]{1,0:T(8,128)(2,1)}, bf16[128,2048]{1,0:T(8,128)(2,1)S(1)}, u32[]{:S(2)}, u32[]{:S(2)}) collective-permute-start(bf16[128,2048]{1,0:T(8,128)(2,1)} %get-tuple-element.279), channel_id=1, source_target_pairs={{0,1},{1,0},{2,3},{3,2},{4,5},{5,4},{6,7},{7,6},{8,9},{9,8},{10,11... | collective-permute-start | bytes 1572872 | tf_op jit(solution)/shard_map/ppermute | solution.py:720
  150.7 32.9 %collective-permute-start.8 = (bf16[128,2048]{1,0:T(8,128)(2,1)}, bf16[128,2048]{1,0:T(8,128)(2,1)S(1)}, u32[]{:S(2)}, u32[]{:S(2)}) collective-permute-start(bf16[128,2048]{1,0:T(8,128)(2,1)} %get-tuple-element.277), channel_id=1, source_target_pairs={{0,1},{1,0},{2,3},{3,2},{4,5},{5,4},{6,7},{7,6},{8,9},{9,8},{10,11... | collective-permute-start | bytes 1572872 | tf_op jit(solution)/shard_map/ppermute | solution.py:720
  165.7 24.7 %collective-permute-start.10 = (bf16[128,2048]{1,0:T(8,128)(2,1)S(1)}, bf16[128,2048]{1,0:T(8,128)(2,1)}, u32[]{:S(2)}, u32[]{:S(2)}) collective-permute-start(bf16[128,2048]{1,0:T(8,128)(2,1)S(1)} %add_convert_fusion.10), channel_id=1, source_target_pairs={{0,2},{1,3},{2,0},{3,1},{4,6},{5,7},{6,4},{7,5},{8,10},{9,11},{10,... | collective-permute-start | bytes 1572872 | tf_op jit(solution)/shard_map/ppermute | solution.py:720
  193.7 22.4 %collective-permute-start.12 = (bf16[128,2176]{1,0:T(8,128)(2,1)}, bf16[128,2176]{1,0:T(8,128)(2,1)S(1)}, u32[]{:S(2)}, u32[]{:S(2)}) collective-permute-start(bf16[128,2176]{1,0:T(8,128)(2,1)} %get-tuple-element.354.ext_ref), channel_id=1, source_target_pairs={{0,2},{1,3},{2,0},{3,1},{4,6},{5,7},{6,4},{7,5},{8,10},{9,11},{10,... | collective-permute-start | bytes 1671176 | tf_op jit(solution)/shard_map/ppermute | solution.py:720
  199.9 375.5 %reduce-scatter.10.cloned.1.call-start = ((), (), s32[]{:S(2)}) async-start(), calls=%async_computation.10 | async-start | bytes 23592960
  200.1 25.6 %collective-permute-start.11 = (bf16[128,2176]{1,0:T(8,128)(2,1)S(1)}, bf16[128,2176]{1,0:T(8,128)(2,1)S(1)}, u32[]{:S(2)}, u32[]{:S(2)}) collective-permute-start(bf16[128,2176]{1,0:T(8,128)(2,1)S(1)} %copy-done.5), channel_id=1, source_target_pairs={{0,1},{1,0},{2,3},{3,2},{4,5},{5,4},{6,7},{7,6},{8,9},{9,8},{10,11... | collective-permute-start | bytes 1671176 | tf_op jit(solution)/shard_map/ppermute | solution.py:720
  216.1 21.0 %collective-permute-start.13 = (bf16[128,2176]{1,0:T(8,128)(2,1)S(1)}, bf16[128,2176]{1,0:T(8,128)(2,1)S(1)}, u32[]{:S(2)}, u32[]{:S(2)}) collective-permute-start(bf16[128,2176]{1,0:T(8,128)(2,1)S(1)} %collective-permute-done.12), channel_id=1, source_target_pairs={{0,1},{1,0},{2,3},{3,2},{4,5},{5,4},{6,7},{7,6},{8,9},{9,8},{10,11... | collective-permute-start | bytes 1671176 | tf_op jit(solution)/shard_map/ppermute | solution.py:720
  240.6 7.7 %collective-permute-start.14 = (bf16[512,2176]{1,0:T(8,128)(2,1)}, bf16[512,2176]{1,0:T(8,128)(2,1)}, u32[]{:S(2)}, u32[]{:S(2)}) collective-permute-start(bf16[512,2176]{1,0:T(8,128)(2,1)} %constant_dynamic-update-slice_fusion.refs_0_), channel_id=1, source_target_pairs={{0,4},{4,0},{1,5},{5,1},{2,6},{6,2},{3,7},{7,3},{8,12},{12,8},{9,1... | collective-permute-start | bytes 6684680 | tf_op jit(solution)/shard_map/ppermute | solution.py:710
  240.6 7.3 %collective-permute-start.15 = (bf16[512,2048]{1,0:T(8,128)(2,1)S(1)}, bf16[512,2048]{1,0:T(8,128)(2,1)}, u32[]{:S(2)}, u32[]{:S(2)}) collective-permute-start(bf16[512,2048]{1,0:T(8,128)(2,1)S(1)} %copy-done.7), channel_id=1, source_target_pairs={{0,4},{4,0},{1,5},{5,1},{2,6},{6,2},{3,7},{7,3},{8,12},{12,8},{9,1... | collective-permute-start | bytes 6291464 | tf_op jit(solution)/shard_map/ppermute | solution.py:710
  338.0 288.1 %reduce-scatter.12.cloned.1.call-start = ((), (), s32[]{:S(2)}) async-start(), calls=%async_computation.11 | async-start | bytes 7864320
  362.0 4.6 collective-permute-start.16
  366.9 14.7 %collective-permute-start.17 = (bf16[128,2176]{1,0:T(8,128)(2,1)S(1)}, bf16[128,2176]{1,0:T(8,128)(2,1)S(1)}, u32[]{:S(2)}, u32[]{:S(2)}) collective-permute-start(bf16[128,2176]{1,0:T(8,128)(2,1)S(1)} %add_convert_fusion.4), channel_id=1, source_target_pairs={{0,1},{1,0},{2,3},{3,2},{4,5},{5,4},{6,7},{7,6},{8,9},{9,8},{10,11... | collective-permute-start | bytes 1671176 | tf_op jit(solution)/shard_map/ppermute | solution.py:720
  381.8 27.3 %collective-permute-start.20 = (bf16[128,2176]{1,0:T(8,128)(2,1)S(1)}, bf16[128,2176]{1,0:T(8,128)(2,1)S(1)}, u32[]{:S(2)}, u32[]{:S(2)}) collective-permute-start(bf16[128,2176]{1,0:T(8,128)(2,1)S(1)} %add_convert_fusion.3), channel_id=1, source_target_pairs={{0,2},{1,3},{2,0},{3,1},{4,6},{5,7},{6,4},{7,5},{8,10},{9,11},{10,... | collective-permute-start | bytes 1671176 | tf_op jit(solution)/shard_map/ppermute | solution.py:720
  384.4 24.6 %collective-permute-start.19 = (bf16[128,2176]{1,0:T(8,128)(2,1)S(1)}, bf16[128,2176]{1,0:T(8,128)(2,1)S(1)}, u32[]{:S(2)}, u32[]{:S(2)}) collective-permute-start(bf16[128,2176]{1,0:T(8,128)(2,1)S(1)} %add_convert_fusion.2), channel_id=1, source_target_pairs={{0,1},{1,0},{2,3},{3,2},{4,5},{5,4},{6,7},{7,6},{8,9},{9,8},{10,11... | collective-permute-start | bytes 1671176 | tf_op jit(solution)/shard_map/ppermute | solution.py:720
  400.7 52.2 %collective-permute-start.18 = (bf16[512,2048]{1,0:T(8,128)(2,1)}, bf16[512,2048]{1,0:T(8,128)(2,1)S(1)}, u32[]{:S(2)}, u32[]{:S(2)}) collective-permute-start(bf16[512,2048]{1,0:T(8,128)(2,1)} %get-tuple-element.349), channel_id=1, source_target_pairs={{0,4},{4,0},{1,5},{5,1},{2,6},{6,2},{3,7},{7,3},{8,12},{12,8},{9,1... | collective-permute-start | bytes 6291464 | tf_op jit(solution)/shard_map/ppermute | solution.py:710
  414.6 24.9 %collective-permute-start.22 = (bf16[128,2048]{1,0:T(8,128)(2,1)}, bf16[128,2048]{1,0:T(8,128)(2,1)S(1)}, u32[]{:S(2)}, u32[]{:S(2)}) collective-permute-start(bf16[128,2048]{1,0:T(8,128)(2,1)} %get-tuple-element.370), channel_id=1, source_target_pairs={{0,2},{1,3},{2,0},{3,1},{4,6},{5,7},{6,4},{7,5},{8,10},{9,11},{10,... | collective-permute-start | bytes 1572872 | tf_op jit(solution)/shard_map/ppermute | solution.py:720
  416.1 36.5 %collective-permute-start.21 = (bf16[128,2048]{1,0:T(8,128)(2,1)S(1)}, bf16[128,2048]{1,0:T(8,128)(2,1)S(1)}, u32[]{:S(2)}, u32[]{:S(2)}) collective-permute-start(bf16[128,2048]{1,0:T(8,128)(2,1)S(1)} %copy-done.17), channel_id=1, source_target_pairs={{0,1},{1,0},{2,3},{3,2},{4,5},{5,4},{6,7},{7,6},{8,9},{9,8},{10,11... | collective-permute-start | bytes 1572872 | tf_op jit(solution)/shard_map/ppermute | solution.py:720
  439.5 13.2 %collective-permute-start.23 = (bf16[128,2048]{1,0:T(8,128)(2,1)S(1)}, bf16[128,2048]{1,0:T(8,128)(2,1)S(1)}, u32[]{:S(2)}, u32[]{:S(2)}) collective-permute-start(bf16[128,2048]{1,0:T(8,128)(2,1)S(1)} %collective-permute-done.22), channel_id=1, source_target_pairs={{0,1},{1,0},{2,3},{3,2},{4,5},{5,4},{6,7},{7,6},{8,9},{9,8},{10,11... | collective-permute-start | bytes 1572872 | tf_op jit(solution)/shard_map/ppermute | solution.py:720
  460.2 223.1 %reduce-scatter.8.cloned.1.call-start = ((), (), s32[]{:S(2)}) async-start(), calls=%async_computation.6 | async-start | bytes 9437184 | tf_op jit(solution)/shard_map/reduce_scatter | solution.py:953
  460.5 15.8 %collective-permute-start.24 = (bf16[128,2048]{1,0:T(8,128)(2,1)}, bf16[128,2048]{1,0:T(8,128)(2,1)S(1)}, u32[]{:S(2)}, u32[]{:S(2)}) collective-permute-start(bf16[128,2048]{1,0:T(8,128)(2,1)} %add_convert_fusion.9), channel_id=1, source_target_pairs={{0,1},{1,0},{2,3},{3,2},{4,5},{5,4},{6,7},{7,6},{8,9},{9,8},{10,11... | collective-permute-start | bytes 1572872 | tf_op jit(solution)/shard_map/ppermute | solution.py:720
  475.6 5.7 collective-permute-start.27
  475.7 31.4 %collective-permute-start.30 = (bf16[2,512,512]{2,1,0:T(8,128)(2,1)}, bf16[2,512,512]{2,1,0:T(8,128)(2,1)S(1)}, u32[]{:S(2)}, u32[]{:S(2)}) collective-permute-start(bf16[2,512,512]{2,1,0:T(8,128)(2,1)} %get-tuple-element.392), channel_id=1, source_target_pairs={{0,4},{4,0},{1,5},{5,1},{2,6},{6,2},{3,7},{7,3},{8,12},{12,8},{9,1... | collective-permute-start | bytes 3145736 | tf_op jit(solution)/shard_map/ppermute | solution.py:710
  477.3 28.0 %collective-permute-start.26 = (bf16[128,2048]{1,0:T(8,128)(2,1)}, bf16[128,2048]{1,0:T(8,128)(2,1)S(1)}, u32[]{:S(2)}, u32[]{:S(2)}) collective-permute-start(bf16[128,2048]{1,0:T(8,128)(2,1)} %add_convert_fusion.8), channel_id=1, source_target_pairs={{0,2},{1,3},{2,0},{3,1},{4,6},{5,7},{6,4},{7,5},{8,10},{9,11},{10,... | collective-permute-start | bytes 1572872 | tf_op jit(solution)/shard_map/ppermute | solution.py:720
  480.3 25.0 %collective-permute-start.25 = (bf16[128,2048]{1,0:T(8,128)(2,1)}, bf16[128,2048]{1,0:T(8,128)(2,1)S(1)}, u32[]{:S(2)}, u32[]{:S(2)}) collective-permute-start(bf16[128,2048]{1,0:T(8,128)(2,1)} %add_convert_fusion.7), channel_id=1, source_target_pairs={{0,1},{1,0},{2,3},{3,2},{4,5},{5,4},{6,7},{7,6},{8,9},{9,8},{10,11... | collective-permute-start | bytes 1572872 | tf_op jit(solution)/shard_map/ppermute | solution.py:720
  481.6 48.0 %collective-permute-start.31 = (bf16[2,512,512]{2,1,0:T(8,128)(2,1)S(1)}, bf16[2,512,512]{2,1,0:T(8,128)(2,1)S(1)}, u32[]{:S(2)}, u32[]{:S(2)}) collective-permute-start(bf16[2,512,512]{2,1,0:T(8,128)(2,1)S(1)} %add_convert_fusion), channel_id=1, source_target_pairs={{0,8},{8,0},{1,9},{9,1},{2,10},{10,2},{3,11},{11,3},{4,12},{12,4},... | collective-permute-start | bytes 3145736 | tf_op jit(solution)/shard_map/ppermute | solution.py:710
  505.7 24.4 %collective-permute-start.29 = (bf16[128,2048]{1,0:T(8,128)(2,1)S(1)}, bf16[128,2048]{1,0:T(8,128)(2,1)S(1)}, u32[]{:S(2)}, u32[]{:S(2)}) collective-permute-start(bf16[128,2048]{1,0:T(8,128)(2,1)S(1)} %add_convert_fusion.6.refs_0_), channel_id=1, source_target_pairs={{0,2},{1,3},{2,0},{3,1},{4,6},{5,7},{6,4},{7,5},{8,10},{9,11},{10,... | collective-permute-start | bytes 1572872 | tf_op jit(solution)/shard_map/ppermute | solution.py:720
  505.8 43.0 %collective-permute-start.28 = (bf16[128,2048]{1,0:T(8,128)(2,1)S(1)}, bf16[128,2048]{1,0:T(8,128)(2,1)}, u32[]{:S(2)}, u32[]{:S(2)}) collective-permute-start(bf16[128,2048]{1,0:T(8,128)(2,1)S(1)} %add_convert_fusion.6.refs_0_), channel_id=1, source_target_pairs={{0,1},{1,0},{2,3},{3,2},{4,5},{5,4},{6,7},{7,6},{8,9},{9,8},{10,11... | collective-permute-start | bytes 1572872 | tf_op jit(solution)/shard_map/ppermute | solution.py:720
  530.2 18.6 %collective-permute-start.32 = (bf16[128,2048]{1,0:T(8,128)(2,1)S(1)}, bf16[128,2048]{1,0:T(8,128)(2,1)}, u32[]{:S(2)}, u32[]{:S(2)}) collective-permute-start(bf16[128,2048]{1,0:T(8,128)(2,1)S(1)} %collective-permute-done.29.refs_2_), channel_id=1, source_target_pairs={{0,1},{1,0},{2,3},{3,2},{4,5},{5,4},{6,7},{7,6},{8,9},{9,8},{10,11... | collective-permute-start | bytes 1572872 | tf_op jit(solution)/shard_map/ppermute | solution.py:720
  579.7 49.5 %collective-permute-start.41 = (bf16[6,3,256,256]{3,2,1,0:T(8,128)(2,1)S(1)}, bf16[6,3,256,256]{3,2,1,0:T(8,128)(2,1)}, u32[]{:S(2)}, u32[]{:S(2)}) collective-permute-start(bf16[6,3,256,256]{3,2,1,0:T(8,128)(2,1)S(1)} %get-tuple-element.488), channel_id=1, source_target_pairs={{0,4},{4,0},{1,5},{5,1},{2,6},{6,2},{3,7},{7,3},{8,12},{12,8},{9,1... | collective-permute-start | bytes 7077896 | tf_op jit(solution)/shard_map/ppermute | solution.py:710
  579.7 14.7 %collective-permute-start.36 = (bf16[128,2048]{1,0:T(8,128)(2,1)S(1)}, bf16[128,2048]{1,0:T(8,128)(2,1)S(1)}, u32[]{:S(2)}, u32[]{:S(2)}) collective-permute-start(bf16[128,2048]{1,0:T(8,128)(2,1)S(1)} %copy-done.32), channel_id=1, source_target_pairs={{0,1},{1,0},{2,3},{3,2},{4,5},{5,4},{6,7},{7,6},{8,9},{9,8},{10,11... | collective-permute-start | bytes 1572872 | tf_op jit(solution)/shard_map/ppermute | solution.py:720
  580.4 33.3 %collective-permute-start.35 = (bf16[128,2048]{1,0:T(8,128)(2,1)}, bf16[128,2048]{1,0:T(8,128)(2,1)S(1)}, u32[]{:S(2)}, u32[]{:S(2)}) collective-permute-start(bf16[128,2048]{1,0:T(8,128)(2,1)} %get-tuple-element.440), channel_id=1, source_target_pairs={{0,1},{1,0},{2,3},{3,2},{4,5},{5,4},{6,7},{7,6},{8,9},{9,8},{10,11... | collective-permute-start | bytes 1572872 | tf_op jit(solution)/shard_map/ppermute | solution.py:720
  594.6 25.6 %collective-permute-start.37 = (bf16[128,2048]{1,0:T(8,128)(2,1)S(1)}, bf16[128,2048]{1,0:T(8,128)(2,1)}, u32[]{:S(2)}, u32[]{:S(2)}) collective-permute-start(bf16[128,2048]{1,0:T(8,128)(2,1)S(1)} %add_convert_fusion.5), channel_id=1, source_target_pairs={{0,2},{1,3},{2,0},{3,1},{4,6},{5,7},{6,4},{7,5},{8,10},{9,11},{10,... | collective-permute-start | bytes 1572872 | tf_op jit(solution)/shard_map/ppermute | solution.py:720
  624.5 21.4 %collective-permute-start.40 = (bf16[128,2048]{1,0:T(8,128)(2,1)}, bf16[128,2048]{1,0:T(8,128)(2,1)S(1)}, u32[]{:S(2)}, u32[]{:S(2)}) collective-permute-start(bf16[128,2048]{1,0:T(8,128)(2,1)} %get-tuple-element.467.refs_0_), channel_id=1, source_target_pairs={{0,1},{1,0},{2,3},{3,2},{4,5},{5,4},{6,7},{7,6},{8,9},{9,8},{10,11... | collective-permute-start | bytes 1572872 | tf_op jit(solution)/shard_map/ppermute | solution.py:720
  626.1 24.8 %collective-permute-start.38 = (bf16[128,2048]{1,0:T(8,128)(2,1)}, bf16[128,2048]{1,0:T(8,128)(2,1)S(1)}, u32[]{:S(2)}, u32[]{:S(2)}) collective-permute-start(bf16[128,2048]{1,0:T(8,128)(2,1)} %get-tuple-element.467.refs_0_), channel_id=1, source_target_pairs={{0,2},{1,3},{2,0},{3,1},{4,6},{5,7},{6,4},{7,5},{8,10},{9,11},{10,... | collective-permute-start | bytes 1572872 | tf_op jit(solution)/shard_map/ppermute | solution.py:720
  650.6 13.4 %collective-permute-start.43 = (bf16[2,3,256,256]{3,2,1,0:T(8,128)(2,1)S(1)}, bf16[2,3,256,256]{3,2,1,0:T(8,128)(2,1)S(1)}, u32[]{:S(2)}, u32[]{:S(2)}) collective-permute-start(bf16[2,3,256,256]{3,2,1,0:T(8,128)(2,1)S(1)} %get-tuple-element.510), channel_id=1, source_target_pairs={{0,4},{4,0},{1,5},{5,1},{2,6},{6,2},{3,7},{7,3},{8,12},{12,8},{9,1... | collective-permute-start | bytes 2359304 | tf_op jit(solution)/shard_map/ppermute | solution.py:710
  650.8 19.8 %collective-permute-start.39 = (bf16[128,2048]{1,0:T(8,128)(2,1)S(1)}, bf16[128,2048]{1,0:T(8,128)(2,1)S(1)}, u32[]{:S(2)}, u32[]{:S(2)}) collective-permute-start(bf16[128,2048]{1,0:T(8,128)(2,1)S(1)} %collective-permute-done.38.refs_0_), channel_id=1, source_target_pairs={{0,1},{1,0},{2,3},{3,2},{4,5},{5,4},{6,7},{7,6},{8,9},{9,8},{10,11... | collective-permute-start | bytes 1572872 | tf_op jit(solution)/shard_map/ppermute | solution.py:720
  651.7 10.1 %all-to-all-start.2 = ((f32[8,20,256]{2,1,0:T(8,128)}), f32[8,20,256]{2,1,0:T(8,128)S(1)}, u32[]{:S(2)}, u32[]{:S(2)}) async-start(f32[8,20,256]{2,1,0:T(8,128)} %bitcast.60), calls=%async_computation.3 | async-start | bytes 393216 | tf_op jit(solution)/shard_map/all_to_all | solution.py:967
  661.8 6.8 collective-permute-start.42
  668.6 18.9 %collective-permute-start.44 = (f32[20,256]{1,0:T(8,128)S(1)}, f32[20,256]{1,0:T(8,128)S(1)}, u32[]{:S(2)}, u32[]{:S(2)}) collective-permute-start(f32[20,256]{1,0:T(8,128)S(1)} %add.201), channel_id=1, source_target_pairs={{0,2},{1,3},{2,0},{3,1},{4,6},{5,7},{6,4},{7,5},{8,10},{9,11},{10,... | collective-permute-start | bytes 61448 | tf_op jit(solution)/shard_map/ppermute | solution.py:720
  (37 other events, 420.8 us)
Sparse Core Ops, SparseCore 0:
  10.5 57.2 all-gather.6
  69.6 194.2 all-gather.8
  265.8 70.1 all-gather.10
  339.0 193.2 reduce-scatter.9
  535.9 70.1 reduce-scatter.11
  609.8 73.3 reduce-scatter.7
